TPU v7x, 128 devices: a whole 4x4x4 slice. The times are simulated.
128 devices in a mesh: tok: 32 (over y, z, core), mp: 4 (over x).
Axes of the slice: x: 4, y: 4, z: 4, core: 2. Of those that a mesh axis runs over, the one named last changes fastest.
Arguments:
- tokens: bfloat16 [32768, 2048], P('tok'), may hold values from -6 to 6
- norm_gain: float32 [2048], replicated, may hold values from 0.1 to 1.9
- w_query: bfloat16 [2048, 2048], P(None, 'mp'), may hold values from -2 to 2
- w_key: bfloat16 [2048, 2048], P(None, 'mp'), may hold values from -2 to 2
- w_value: bfloat16 [2048, 2048], P(None, 'mp'), may hold values from -0.125 to 0.125
- w_out: bfloat16 [2048, 2048], replicated, may hold values from -2.5 to 2.5
- kv_cache: bfloat16 [2, 32768, 2, 2048], P(None, 'tok', None, 'mp'), may hold values from -6 to 6
- wake_blocks: int32 [256, 8], replicated, may hold values from 0 to 255, as said below
- wake_frames: int32 [256, 8], replicated, may hold values from 0 to 1
- wake_counts: int32 [256], replicated, may hold values from 2 to 8, as said below
Outputs:
- advanced: bfloat16 [32768, 2048], P('tok', 'mp')
Inputs may be any that keep to these rules, and one draw needn't show every extreme that they name: `wake_blocks`: blocks i * 8 to (i + 1) * 8 - 1 are held by tok index i. Among the live slots (w below the block's count) of the 8 query blocks of one tok index, at most 2 name blocks held by any one tok index, and for every tok index some holder is named exactly 2 times. Slots at or past the count hold any block number. `wake_counts`: some query block has all 8 slots live.
All inputs are finite; a program needn't handle non-finite values.
Results may differ from a plain program's by a relative error of at most 0.005.
The roundings to bfloat16 on the way count: a program that leaves them out, or rounds other values in their place, can miss the bound.
Values may be sent and summed in bfloat16 or wider, within the bound.
No kernel may reach another device: no remote copies, remote signals or barrier semaphores. Data moves between devices by JAX's collectives and lax.ppermute only.
A program may use at most 192 MiB of HBM per device.

v0:
```python
import functools
import math

import jax
import jax.numpy as jnp
from jax import lax
from jax.experimental import pallas as pl
from jax.experimental.pallas import tpu as pltpu
from jax.sharding import PartitionSpec as P

HD = 128
BLOCK = 128
WMAX = 8
NEG = -1e30
SCALE = 1.0 / math.sqrt(HD)
NY, NZ, NC, NX = 4, 4, 2, 4
F32, BF16 = jnp.float32, jnp.bfloat16
ANY = pl.BlockSpec(memory_space=pl.ANY)
SMEM = pl.BlockSpec(memory_space=pltpu.SMEM)
OROWS = 2048 + 48
FROWS = 1024 + 8


def params(mib=48):
    return pltpu.CompilerParams(vmem_limit_bytes=mib << 20)


def tok_of(y, z, c):
    return ((y % NY) * NZ + z % NZ) * NC + c % NC


def chips():
    return [(y, z, c) for y in range(NY) for z in range(NZ) for c in range(NC)]


def rows_perm(x, d):
    pairs = [(tok_of(y, z, c), tok_of(y + d, z, c) if c == 0 else tok_of(y, z + d, c)) for y, z, c in chips()]
    return lax.ppermute(x, "tok", pairs)


def query_perm(x, d):
    pairs = [(tok_of(y, z, c), tok_of(y, z + d, c) if c == 0 else tok_of(y + d, z, c)) for y, z, c in chips()]
    return lax.ppermute(x, "tok", pairs)


def core_swap(x):
    return lax.ppermute(x, "tok", [(tok_of(y, z, c), tok_of(y, z, 1 - c)) for y, z, c in chips()])


def ring_perm(x, d):
    n = NY * NZ * NC
    return lax.ppermute(x, "tok", [(i, (i + d) % n) for i in range(n)])


def mp_perm(x, d):
    return lax.ppermute(x, "mp", [(i, (i + d) % NX) for i in range(NX)])


def nt(a, b):
    return lax.dot_general(a, b, (((1,), (1,)), ((), ())), preferred_element_type=F32)


def nn(a, b):
    return lax.dot_general(a, b, (((1,), (0,)), ((), ())), preferred_element_type=F32)


def split_cache_kernel(core_ref, keep_ref, send_ref, keep, send):
    for src, out in ((keep_ref, keep), (send_ref, send)):
        for b in range(2):
            rows = slice(b * BLOCK, (b + 1) * BLOCK)
            out[b, 0] = src[0, rows, 0, :]
            out[b, 1] = src[0, rows, 1, :].T


def split_cache(j, core, rows):
    out = jax.ShapeDtypeStruct((16, 2, BLOCK, HD), BF16)
    block = pl.BlockSpec((2, 2, BLOCK, HD), lambda i, c: (i, 0, 0, 0))
    return pl.pallas_call(
        split_cache_kernel,
        grid_spec=pltpu.PrefetchScalarGridSpec(
            num_scalar_prefetch=1,
            grid=(8,),
            in_specs=[
                pl.BlockSpec((1, 256, 2, HD), lambda i, c: (i // 4, i % 4, 0, 2 * c[0] + j)),
                pl.BlockSpec((1, 256, 2, HD), lambda i, c: (i // 4, i % 4, 0, 2 - 2 * c[0] + j)),
            ],
            out_specs=[block, block],
        ),
        out_shape=[out, out],
        compiler_params=params(),
        cost_estimate=pl.CostEstimate(flops=0, transcendentals=0, bytes_accessed=4 << 20),
        name="split_cache",
    )(core, rows, rows)


def project_kernel(core_ref, tok_ref, gain_ref, wq, wk, wv, q_all, q_send, k_all, v_all, first, last):
    step = pl.program_id(0)
    core = core_ref[0]
    x = tok_ref[...].astype(F32)
    inverse = lax.rsqrt(jnp.mean(x * x, axis=1, keepdims=True) + 1e-05)
    normed = (x * inverse * gain_ref[...]).astype(BF16)
    q = nn(normed, wq[...]).astype(BF16)
    k = nn(normed, wk[...]).astype(BF16)
    v = nn(normed, wv[...])

    def put(shift):
        for h in range(4):
            slot = (h - shift) % 4
            lanes = slice(h * HD, (h + 1) * HD)
            q_all[slot] = q[:, lanes]
            if slot >= 2:
                q_send[slot - 2] = q[:, lanes]
            for b in range(2):
                rows = slice(b * BLOCK, (b + 1) * BLOCK)
                kb = k[rows, lanes]
                vb = v[rows, lanes].T.astype(BF16)
                k_all[slot, b] = kb
                v_all[slot, b] = vb
                if b == 0:
                    @pl.when(step == 0)
                    def _():
                        first[0, slot] = kb
                        first[1, slot] = vb
                else:
                    @pl.when(step == pl.num_programs(0) - 1)
                    def _():
                        last[0, slot] = kb
                        last[1, slot] = vb

    @pl.when(core == 0)
    def _():
        put(0)

    @pl.when(core == 1)
    def _():
        put(2)


def project(core, tokens, gain, wq, wk, wv):
    n, d = tokens.shape
    w = wq.shape[1]
    weight = pl.BlockSpec((d, w), lambda i, c: (0, 0), pipeline_mode=pl.Buffered(1))
    edge = pl.BlockSpec((2, 4, BLOCK, HD), lambda i, c: (0, 0, 0, 0))
    blocks = pl.BlockSpec((4, 2, BLOCK, HD), lambda i, c: (0, i, 0, 0))
    return pl.pallas_call(
        project_kernel,
        grid_spec=pltpu.PrefetchScalarGridSpec(
            num_scalar_prefetch=1,
            grid=(n // 256,),
            in_specs=[
                pl.BlockSpec((256, d), lambda i, c: (i, 0)),
                pl.BlockSpec((1, d), lambda i, c: (0, 0)),
                weight,
                weight,
                weight,
            ],
            out_specs=[
                pl.BlockSpec((4, 256, HD), lambda i, c: (0, i, 0)),
                pl.BlockSpec((2, 256, HD), lambda i, c: (0, i, 0)),
                blocks,
                blocks,
                edge,
                edge,
            ],
        ),
        out_shape=[
            jax.ShapeDtypeStruct((4, n, HD), BF16),
            jax.ShapeDtypeStruct((2, n, HD), BF16),
            jax.ShapeDtypeStruct((4, 8, BLOCK, HD), BF16),
            jax.ShapeDtypeStruct((4, 8, HD, BLOCK), BF16),
            jax.ShapeDtypeStruct((2, 4, BLOCK, HD), BF16),
            jax.ShapeDtypeStruct((2, 4, BLOCK, HD), BF16),
        ],
        compiler_params=params(),
        cost_estimate=pl.CostEstimate(flops=2 * n * d * 3 * w, transcendentals=0, bytes_accessed=16 << 20),
        name="project",
    )(core, tokens, gain.reshape(1, d), wq, wk, wv)


def near_kernel(q_ref, k_ref, v_ref, lo_ref, hi_ref, o_ref, lse_ref):
    for b in range(8):
        q = q_ref[0, b * BLOCK : (b + 1) * BLOCK]
        ks = [lo_ref[0, 0] if b == 0 else k_ref[0, b - 1], k_ref[0, b], hi_ref[0, 0] if b == 7 else k_ref[0, b + 1]]
        vs = [lo_ref[1, 0] if b == 0 else v_ref[0, b - 1], v_ref[0, b], hi_ref[1, 0] if b == 7 else v_ref[0, b + 1]]
        s = [nt(k, q) * SCALE for k in ks]
        m = jnp.max(jnp.maximum(jnp.maximum(s[0], s[1]), s[2]), axis=0, keepdims=True)
        p = [jnp.exp(x - m) for x in s]
        total = jnp.sum(p[0] + p[1] + p[2], axis=0, keepdims=True)
        acc = nn(vs[0], p[0].astype(BF16)) + nn(vs[1], p[1].astype(BF16)) + nn(vs[2], p[2].astype(BF16))
        o_ref[0, b] = acc / total
        lse_ref[0, b : b + 1, :] = m + jnp.log(total)


def near(q, k, v, lo, hi):
    blocks = pl.BlockSpec((1, 8, BLOCK, HD), lambda s: (s, 0, 0, 0))
    edge = pl.BlockSpec((2, 1, BLOCK, HD), lambda s: (0, (s + 2) % 4, 0, 0))
    return pl.pallas_call(
        near_kernel,
        grid=(4,),
        in_specs=[pl.BlockSpec((1, 1024, HD), lambda s: (s, 0, 0)), blocks, blocks, edge, edge],
        out_specs=[blocks, pl.BlockSpec((1, 8, HD), lambda s: (s, 0, 0))],
        out_shape=[jax.ShapeDtypeStruct((4, 8, HD, BLOCK), F32), jax.ShapeDtypeStruct((4, 8, BLOCK), F32)],
        compiler_params=params(),
        cost_estimate=pl.CostEstimate(flops=32 * 384 * 128 * 512, transcendentals=32 * 384 * 128, bytes_accessed=6 << 20),
        name="near",
    )(q, k, v, lo, hi)


GROUP = 4
UNITS = 96 + GROUP


def far_kernel(
    j, cnt_ref, code_ref, *rest,
):
    sources, qs, outs = rest[:8], rest[8:12], rest[12:16]
    kvbuf, qbuf, acc_ref, stat_ref, list_ref, unit_ref, first_ref, kvsem, qsem, logs = rest[16:]
    for r in range(4):
        pltpu.make_async_copy(qs[r].at[:, j], qbuf.at[pl.ds(2 * r, 2)], qsem.at[r]).start()

    def scan(i, carry):
        e, u = carry
        n = cnt_ref[i]
        first_ref[i] = u

        def named(carry):
            e, u = carry
            at = e
            for w in range(WMAX):
                code = code_ref[i * WMAX + w]
                list_ref[at] = code
                at = at + (code >= 0).astype(jnp.int32)

            def unit(k, u):
                both = (2 * k + 1 < n).astype(jnp.int32)
                unit_ref[u] = i * 512 + (e + 2 * k) * 2 + both
                return u + 1

            return at, lax.fori_loop(0, lax.shift_right_logical(n + 1, 1), unit, u)

        return lax.cond(n > 0, named, lambda carry: carry, (e, u))

    entries, units = lax.fori_loop(0, 64, scan, (jnp.int32(0), jnp.int32(0)))
    for g in range(GROUP):
        unit_ref[units + g] = -1

    def fetch(e, _):
        code = list_ref[e]
        at = lax.bitwise_and(code, 15)
        source = lax.shift_right_logical(code, 4)

        def start(lo, hi):
            if hi - lo == 1:
                pltpu.make_async_copy(sources[lo].at[at], kvbuf.at[e], kvsem.at[e]).start()
                return
            mid = (lo + hi) // 2

            @pl.when(source < mid)
            def _():
                start(lo, mid)

            @pl.when(source >= mid)
            def _():
                start(mid, hi)

        start(0, 8)
        return 0

    lax.fori_loop(0, entries, fetch, 0)
    for r in range(4):
        pltpu.make_async_copy(qs[r].at[:, j], qbuf.at[pl.ds(2 * r, 2)], qsem.at[r]).wait()

    def landed(e):
        pltpu.make_async_copy(sources[0].at[0], kvbuf.at[e], kvsem.at[e]).wait()

    def group(g, _):
        live = []
        for t in range(GROUP):
            u = g * GROUP + t
            unit = unit_ref[u]
            here = unit >= 0
            unit = jnp.where(here, unit, unit_ref[g * GROUP])
            both = lax.bitwise_and(unit, 1)
            ea = lax.bitwise_and(lax.shift_right_logical(unit, 1), 255)
            i = lax.shift_right_logical(unit, 9)

            @pl.when(here)
            def _():
                landed(ea)

            @pl.when(jnp.logical_and(here, both == 1))
            def _():
                landed(ea + 1)

            live.append((u, i, ea, ea + both, both == 1))
        for u, i, ea, eb, both in live:
            q = qbuf[lax.shift_right_logical(i, 3), lax.bitwise_and(i, 7)]
            sa = nt(kvbuf[ea, 0], q) * SCALE
            sb = jnp.where(both, nt(kvbuf[eb, 0], q) * SCALE, NEG)
            m = jnp.max(jnp.maximum(sa, sb), axis=0, keepdims=True)
            pa, pb = jnp.exp(sa - m), jnp.exp(sb - m)
            stat_ref[u, 0:1, :] = m
            stat_ref[u, 1:2, :] = jnp.sum(pa + pb, axis=0, keepdims=True)
            acc_ref[u] = nn(kvbuf[ea, 1], pa.astype(BF16)) + nn(kvbuf[eb, 1], pb.astype(BF16))
        return 0

    lax.fori_loop(0, lax.div(units + GROUP - 1, GROUP), group, 0)

    for r in range(4):
        out = outs[r]

        def block(i, _):
            n = cnt_ref[r * 16 + i]
            u = first_ref[r * 16 + i]
            rows = pl.ds(pl.multiple_of(i * HD, HD), HD)

            def store(value, log):
                out[rows, :] = value
                logs[pl.ds(i, 1), :] = log

            @pl.when(n == 0)
            def _():
                store(jnp.zeros((HD, BLOCK), BF16), jnp.full((1, BLOCK), NEG, F32))

            @pl.when(jnp.logical_and(n > 0, n <= 2))
            def _():
                m, total = stat_ref[u, 0:1, :], stat_ref[u, 1:2, :]
                store((acc_ref[u] * (1.0 / total)).astype(BF16), m + jnp.log(total))

            @pl.when(n > 2)
            def _():
                def more(k, carry):
                    m, total, acc = carry
                    mk, tk = stat_ref[k, 0:1, :], stat_ref[k, 1:2, :]
                    top = jnp.maximum(m, mk)
                    old, new = jnp.exp(m - top), jnp.exp(mk - top)
                    return top, total * old + tk * new, acc * old + acc_ref[k] * new

                start = (stat_ref[u, 0:1, :], stat_ref[u, 1:2, :], acc_ref[u])
                m, total, acc = lax.fori_loop(u + 1, u + lax.shift_right_logical(n + 1, 1), more, start)
                store((acc * (1.0 / total)).astype(BF16), m + jnp.log(total))

            return 0

        lax.fori_loop(0, 16, block, 0)
        part = logs[...]
        for t in range(3):
            term = part.astype(BF16)
            out[2048 + t * 16 : 2064 + t * 16, :] = term
            part = part - term.astype(F32)


def far(j, cnt, code, sources, qs):
    out = jax.ShapeDtypeStruct((OROWS, BLOCK), BF16)
    return pl.pallas_call(
        functools.partial(far_kernel, j),
        in_specs=[SMEM, SMEM] + [ANY] * 12,
        out_specs=[pl.BlockSpec((OROWS, BLOCK), lambda: (0, 0))] * 4,
        out_shape=[out] * 4,
        scratch_shapes=[
            pltpu.VMEM((128, 2, BLOCK, HD), BF16),
            pltpu.VMEM((8, 8, BLOCK, HD), BF16),
            pltpu.VMEM((UNITS, HD, BLOCK), F32),
            pltpu.VMEM((UNITS, 8, BLOCK), F32),
            pltpu.SMEM((128 + WMAX,), jnp.int32),
            pltpu.SMEM((UNITS,), jnp.int32),
            pltpu.SMEM((64,), jnp.int32),
            pltpu.SemaphoreType.DMA((128,)),
            pltpu.SemaphoreType.DMA((4,)),
            pltpu.VMEM((16, BLOCK), F32),
        ],
        compiler_params=params(),
        cost_estimate=pl.CostEstimate(flops=64 * 128 * 128 * 512, transcendentals=64 * 128 * 128, bytes_accessed=10 << 20),
        name="far",
    )(cnt, code, *sources, *qs)


def merge_kernel(a, b, c, d, keep, send):
    parts = (a, b, c, d)
    logs = [sum(p[2048 + t * 16 : 2064 + t * 16, :].astype(F32) for t in range(3)) for p in parts]
    peak = functools.reduce(jnp.maximum, logs)
    shares = [jnp.exp(x - peak) for x in logs]
    total = sum(shares)
    shares = [x / total for x in shares]
    joint = peak + jnp.log(total)
    for s, out in enumerate((keep, send)):
        for i in range(8):
            row = s * 8 + i
            rows = slice(row * HD, (row + 1) * HD)
            out[i * HD : (i + 1) * HD, :] = sum(
                x[row : row + 1, :] * p[rows, :].astype(F32) for x, p in zip(shares, parts)
            )
        out[1024:1032, :] = joint[s * 8 : (s + 1) * 8, :]


def merge(parts):
    out = jax.ShapeDtypeStruct((FROWS, BLOCK), F32)
    return pl.pallas_call(
        merge_kernel,
        out_shape=[out, out],
        compiler_params=params(),
        cost_estimate=pl.CostEstimate(flops=1 << 21, transcendentals=1 << 13, bytes_accessed=3 << 20),
        name="merge",
    )(*parts)


def finish_kernel(near_a, lse_a, near_b, lse_b, far_a, far_b, out):
    for s, (o, log, f) in enumerate(((near_a, lse_a, far_a), (near_b, lse_b, far_b))):
        here, away = log[0], f[1024:1032, :]
        peak = jnp.maximum(here, away)
        wn, wf = jnp.exp(here - peak), jnp.exp(away - peak)
        total = wn + wf
        wn, wf = wn / total, wf / total
        for b in range(8):
            both = wn[b : b + 1, :] * o[0, b] + wf[b : b + 1, :] * f[b * HD : (b + 1) * HD, :]
            out[s, b * BLOCK : (b + 1) * BLOCK, :] = both.T.astype(BF16)


def finish(j, o, lse, far_keep, far_other):
    def at(slot):
        return [
            pl.BlockSpec((1, 8, HD, BLOCK), lambda i: (slot, 0, 0, 0)),
            pl.BlockSpec((1, 8, BLOCK), lambda i: (slot, 0, 0)),
        ]

    whole = pl.BlockSpec((FROWS, BLOCK), lambda i: (0, 0))
    return pl.pallas_call(
        finish_kernel,
        grid=(1,),
        in_specs=at(j) + at(2 + j) + [whole, whole],
        out_specs=pl.BlockSpec((2, 1024, HD), lambda i: (0, 0, 0)),
        out_shape=jax.ShapeDtypeStruct((2, 1024, HD), BF16),
        compiler_params=params(),
        cost_estimate=pl.CostEstimate(flops=1 << 21, transcendentals=1 << 13, bytes_accessed=3 << 20),
        name="finish",
    )(o, lse, o, lse, far_keep, far_other)


def mix_kernel(last, place_ref, a0, a1, a2, a3, *rest):
    weights, carried, out = rest[:8], rest[8], rest[-1]
    total = carried[...].astype(F32) if carried is not out else None
    left = jnp.concatenate([a[s] for a in (a0, a1, a2, a3) for s in range(2)], axis=1)
    term = nn(left, jnp.concatenate([w[...] for w in weights], axis=0))
    total = term if total is None else total + term
    if last:
        total = total + rest[9][...]
    out[...] = total.astype(out.dtype)


def mix(j, place, parts, w_out, carried, acc=None):
    n, cols = 1024, 512

    def weight(rel, s):
        def at(i, p):
            head = (2 * p[0] + 2 * s + j) % 4
            return ((p[1] + rel) % NX * 4 + head, p[1])

        return pl.BlockSpec((HD, cols), at)

    last = acc is not None
    in_specs = [pl.BlockSpec((2, 256, HD), lambda i, p: (0, i, 0))] * 4
    in_specs += [weight(rel, s) for rel in range(4) for s in range(2)]
    args = list(parts) + [w_out] * 8
    if last:
        in_specs.append(pl.BlockSpec((256, cols), lambda i, p: (i, p[1])))
        in_specs.append(pl.BlockSpec((256, cols), lambda i, p: (i, 0)))
        args += [carried, acc]
    return pl.pallas_call(
        functools.partial(mix_kernel, last),
        grid_spec=pltpu.PrefetchScalarGridSpec(
            num_scalar_prefetch=1,
            grid=(n // 256,),
            in_specs=in_specs,
            out_specs=pl.BlockSpec((256, cols), lambda i, p: (i, 0)),
        ),
        out_shape=jax.ShapeDtypeStruct((n, cols), BF16 if last else F32),
        compiler_params=params(),
        cost_estimate=pl.CostEstimate(flops=2 * n * 1024 * cols, transcendentals=0, bytes_accessed=6 << 20),
        name="mix",
    )(place, *args)


def line_codes(wake_blocks, wake_frames, wake_counts, y, z, c):
    live = jnp.arange(WMAX, dtype=jnp.int32)[None, :] < wake_counts[:, None]
    word = jnp.where(live, wake_frames * 256 + wake_blocks, -1).reshape(NY, NZ, NC, 8, WMAX)
    by_y = lax.dynamic_index_in_dim(word, y, 0, keepdims=False)
    by_z = lax.dynamic_index_in_dim(word, z, 1, keepdims=False)
    here = jnp.where(c == 0, by_y, by_z)
    here = lax.dynamic_slice_in_dim(jnp.concatenate([here, here], axis=0), jnp.where(c == 0, z, y), 4, 0)
    here = lax.dynamic_slice_in_dim(jnp.concatenate([here, here], axis=1), c, 2, 1)
    word = here.reshape(64, WMAX)
    block, frame = word & 255, word >> 8
    hc, hz, hy = (block >> 3) & 1, (block >> 4) & 3, (block >> 6) & 3
    in_line = (word >= 0) & (jnp.where(c == 0, hz, hy) == jnp.where(c == 0, z, y))
    piece = (jnp.where(c == 0, hy, hz) - jnp.where(c == 0, y, z)) & 3
    code = piece * 32 + (hc ^ c) * 16 + (frame & 1) * 8 + (block & 7)
    code = jnp.where(in_line, code, -1)
    return code.reshape(512), jnp.sum(in_line.astype(jnp.int32), axis=1)


def on_device(tokens, norm_gain, w_query, w_key, w_value, w_out, kv_cache, wake_blocks, wake_frames, wake_counts):
    tok = lax.axis_index("tok").astype(jnp.int32)
    mp = lax.axis_index("mp").astype(jnp.int32)
    c, z, y = tok % NC, (tok // NC) % NZ, tok // (NC * NZ)
    core = c.reshape(1)
    place = jnp.stack([c, mp])

    def after(x, *deps):
        return lax.optimization_barrier((x, *deps))[0]

    keep, send = [None, None], [None, None]
    keep[0], send[0] = split_cache(0, core, kv_cache)
    up_k, down_k = [rows_perm(keep[0], 1), None], [rows_perm(keep[0], -1), None]
    got = [core_swap(send[0]), None]
    up_r, down_r = [rows_perm(got[0], 1), None], [rows_perm(got[0], -1), None]
    keep[1], send[1] = split_cache(1, core, kv_cache)
    got[1] = core_swap(send[1])

    q_all, q_send, k_all, v_all, first, last = project(core, tokens, norm_gain, w_query, w_key, w_value)
    mine = jnp.concatenate([q_all[:2], core_swap(q_send)], axis=0).reshape(2, 2, 8, BLOCK, HD)
    qs = [mine, query_perm(mine, -1), query_perm(mine, 2), query_perm(mine, 1)]
    lo, hi = ring_perm(last, 1), ring_perm(first, -1)
    code, cnt = line_codes(wake_blocks, wake_frames, wake_counts, y, z, c)
    near_o, near_lse = near(q_all, k_all, v_all, lo, hi)

    keep[1], got[1] = lax.optimization_barrier((keep[1], got[1], up_k[0], down_r[0]))[:2]
    up_k[1], down_k[1] = rows_perm(keep[1], 1), rows_perm(keep[1], -1)
    up_r[1], down_r[1] = rows_perm(got[1], 1), rows_perm(got[1], -1)

    acc = None
    parts = None
    for j in range(2):
        if parts is not None:
            up_k[j], down_r[j] = lax.optimization_barrier((up_k[j], down_r[j], parts[0]))[:2]
        up2, down2 = rows_perm(up_k[j], 1), rows_perm(down_r[j], -1)
        sources = [keep[j], got[j], down_k[j], down_r[j], up2, down2, up_k[j], up_r[j]]
        if j == 0:
            near_o, near_lse, sources[0] = lax.optimization_barrier((near_o, near_lse, sources[0]))
        parts = far(j, cnt, code, sources, qs)
        back = [parts[0], query_perm(parts[1], 1), query_perm(parts[2], 2), query_perm(parts[3], -1)]
        own, other = merge(back)
        heads = finish(j, near_o, near_lse, own, core_swap(other))
        gathered = [heads, mp_perm(heads, -1), mp_perm(heads, 2), mp_perm(heads, 1)]
        acc = mix(j, place, gathered, w_out, tokens, acc)
    return acc


def solution(mesh):
    return jax.shard_map(
        on_device,
        mesh=mesh,
        in_specs=(
            P("tok", None),
            P(),
            P(None, "mp"),
            P(None, "mp"),
            P(None, "mp"),
            P(),
            P(None, "tok", None, "mp"),
            P(),
            P(),
            P(),
        ),
        out_specs=P("tok", "mp"),
        check_vma=False,
    )
```

profile of v0, /device:TPU:1, one launch (start us, length us, event | category | flops | bytes accessed | tf_op | source)
XLA Modules:
  0.0 264.7 jit_solution(9861543768813788232)
XLA Ops:
  0.0 8.7 %split_cache.2 = (bf16[16,2,128,128]{3,2,1,0:T(8,128)(2,1)S(1)}, bf16[16,2,128,128]{3,2,1,0:T(8,128)(2,1)S(1)}) custom-call(s32[1]{0:T(128)} %bitcast.core_ref, bf16[2,1024,2,512]{3,2,1,0:T(2,128)(2,1)} %send_ref.3, bf16[2,1024,2,512]{3,2,1,0:T(2,128)(2,1)} %send_ref.3), custom_call_target="tpu_custom_call" | custom-call | bytes 4194304 | tf_op jit(solution)/shard_map/split_cache/pallas_call | solution.py:78
  14.1 14.9 %project.1 = (bf16[4,1024,128]{2,1,0:T(8,128)(2,1)S(1)}, bf16[2,1024,128]{2,1,0:T(8,128)(2,1)S(1)}, bf16[4,8,128,128]{3,2,1,0:T(8,128)(2,1)S(1)}, bf16[4,8,128,1...) custom-call(s32[1]{0:T(128)} %bitcast.core_ref, ...), custom_call_target="tpu_custom_call" | custom-call | flops 6442450944 | bytes 16777216 | tf_op jit(solution)/shard_map/project/pallas_call | solution.py:145
  29.8 8.7 %split_cache.3 = (bf16[16,2,128,128]{3,2,1,0:T(8,128)(2,1)S(1)}, bf16[16,2,128,128]{3,2,1,0:T(8,128)(2,1)S(1)}) custom-call(s32[1]{0:T(128)} %bitcast.core_ref, bf16[2,1024,2,512]{3,2,1,0:T(2,128)(2,1)} %send_ref.3, bf16[2,1024,2,512]{3,2,1,0:T(2,128)(2,1)} %send_ref.3), custom_call_target="tpu_custom_call" | custom-call | bytes 4194304 | tf_op jit(solution)/shard_map/split_cache/pallas_call | solution.py:78
  43.9 7.2 %collective-permute-done.1.hi_ref = bf16[2,4,128,128]{3,2,1,0:T(8,128)(2,1)S(1)} collective-permute-done((bf16[2,4,128,128]{3,2,1,0:T(8,128)(2,1)S(1)}, bf16[2,4,128,128]{3,2,1,0:T(8,128)(2,1)S(1)}, u32[]{:S(2)}, u32[]{:S(2)}) %collective-permute-start.1) | collective-permute-done | bytes 262176 | tf_op jit(solution)/shard_map/ppermute | solution.py:52
  57.0 5.7 %collective-permute-start.12 = (bf16[16,2,128,128]{3,2,1,0:T(8,128)(2,1)}, bf16[16,2,128,128]{3,2,1,0:T(8,128)(2,1)}, u32[]{:S(2)}, u32[]{:S(2)}) collective-permute-start(bf16[16,2,128,128]{3,2,1,0:T(8,128)(2,1)} %collective-permute-done.4.rest_1_), channel_id=1, source_target_pairs={{0,32},{4,12},{8,40},{12,20},{16,48},{20,28},{24,56},{28,4},{32,64... | collective-permute-start | bytes 3145736 | tf_op jit(solution)/shard_map/ppermute | solution.py:38
  62.7 17.6 %collective-permute-done.14.rest_9_ = bf16[2,2,8,128,128]{4,3,2,1,0:T(8,128)(2,1)} collective-permute-done((bf16[2,2,8,128,128]{4,3,2,1,0:T(8,128)(2,1)}, bf16[2,2,8,128,128]{4,3,2,1,0:T(8,128)(2,1)}, u32[]{:S(2)}, u32[]{:S(2)}) %collective-permute-start.14) | collective-permute-done | bytes 1048608 | tf_op jit(solution)/shard_map/ppermute | solution.py:43
  80.4 14.1 %collective-permute-start.8 = (bf16[16,2,128,128]{3,2,1,0:T(8,128)(2,1)}, bf16[16,2,128,128]{3,2,1,0:T(8,128)(2,1)}, u32[]{:S(2)}, u32[]{:S(2)}) collective-permute-start(bf16[16,2,128,128]{3,2,1,0:T(8,128)(2,1)} %collective-permute-done.2.rest_1_), channel_id=1, source_target_pairs={{0,96},{4,28},{8,104},{12,4},{16,112},{20,12},{24,120},{28,20},{32... | collective-permute-start | bytes 3145736 | tf_op jit(solution)/shard_map/ppermute | solution.py:38
  94.5 18.5 %collective-permute-start.11 = (bf16[16,2,128,128]{3,2,1,0:T(8,128)(2,1)}, bf16[16,2,128,128]{3,2,1,0:T(8,128)(2,1)}, u32[]{:S(2)}, u32[]{:S(2)}) collective-permute-start(bf16[16,2,128,128]{3,2,1,0:T(8,128)(2,1)} %collective-permute-done.5.rest_3_), channel_id=1, source_target_pairs={{0,96},{4,28},{8,104},{12,4},{16,112},{20,12},{24,120},{28,20},{32... | collective-permute-start | bytes 3145736 | tf_op jit(solution)/shard_map/ppermute | solution.py:38
  116.9 2.7 %collective-permute-start.6 = (bf16[16,2,128,128]{3,2,1,0:T(8,128)(2,1)}, bf16[16,2,128,128]{3,2,1,0:T(8,128)(2,1)}, u32[]{:S(2)}, u32[]{:S(2)}) collective-permute-start(bf16[16,2,128,128]{3,2,1,0:T(8,128)(2,1)} %copy-done), channel_id=1, source_target_pairs={{0,96},{4,28},{8,104},{12,4},{16,112},{20,12},{24,120},{28,20},{32... | collective-permute-start | bytes 3145736 | tf_op jit(solution)/shard_map/ppermute | solution.py:38
  121.9 8.8 %near.1 = (f32[4,8,128,128]{3,2,1,0:T(8,128)S(1)}, f32[4,8,128]{2,1,0:T(8,128)S(1)}) custom-call(bf16[4,1024,128]{2,1,0:T(8,128)(2,1)S(1)} %get-tuple-element.36.q_ref, bf16[4,8,128,128]{3,2,1,0:T(8,128)(2,1)S(1)} %get-tuple-element.37.k_ref, bf16[4,8,128,128]{3,2,1,0:T(8,128)(2,1)S(1)} %get-tuple-element.38.v_ref, ...), custom_call_target="tpu_custom_call" | custom-call | flops 805306368 | bytes 6291456 | tf_op jit(solution)/shard_map/near/pallas_call | solution.py:197
  130.7 15.5 %far.2 = (bf16[2096,128]{1,0:T(8,128)(2,1)S(1)}, bf16[2096,128]{1,0:T(8,128)(2,1)S(1)}, bf16[2096,128]{1,0:T(8,128)(2,1)S(1)}, bf16[2096,128]{1,0:T(8,128)(2,1)S(1)}) custom-call(s32[64]{0:T(128)S(1)} %reduce_sum.12.cnt_ref, s32[512]{0:T(512)S(1)} %reshape.63.code_ref, bf16[16,2,128,128]{3,2,1,0:T(8,128)(2,1)S(1)} %copy-done.3, ...), custom_call_target="tpu_custom_call" | custom-call | flops 536870912 | bytes 10485760 | tf_op jit(solution)/shard_map/far/pallas_call | solution.py:355
  146.3 2.7 %collective-permute-start.18 = (bf16[16,2,128,128]{3,2,1,0:T(8,128)(2,1)}, bf16[16,2,128,128]{3,2,1,0:T(8,128)(2,1)S(1)}, u32[]{:S(2)}, u32[]{:S(2)}) collective-permute-start(bf16[16,2,128,128]{3,2,1,0:T(8,128)(2,1)} %collective-permute-done.8.rest_3_), channel_id=1, source_target_pairs={{0,96},{4,28},{8,104},{12,4},{16,112},{20,12},{24,120},{28,20},{32... | collective-permute-start | bytes 3145736 | tf_op jit(solution)/shard_map/ppermute | solution.py:38
  149.0 6.1 %collective-permute-start.28 = (bf16[2096,128]{1,0:T(8,128)(2,1)S(1)}, bf16[2096,128]{1,0:T(8,128)(2,1)S(1)}, u32[]{:S(2)}, u32[]{:S(2)}) collective-permute-start(bf16[2096,128]{1,0:T(8,128)(2,1)S(1)} %get-tuple-element.63), channel_id=1, source_target_pairs={{0,16},{4,68},{8,24},{12,76},{16,0},{20,84},{24,8},{28,92},{32,48}... | collective-permute-start | bytes 1609736 | tf_op jit(solution)/shard_map/ppermute | solution.py:43
  157.1 12.0 %collective-permute-done.17.rest_4_ = bf16[16,2,128,128]{3,2,1,0:T(8,128)(2,1)S(1)} collective-permute-done((bf16[16,2,128,128]{3,2,1,0:T(8,128)(2,1)}, bf16[16,2,128,128]{3,2,1,0:T(8,128)(2,1)S(1)}, u32[]{:S(2)}, u32[]{:S(2)}) %collective-permute-start.17) | collective-permute-done | bytes 1048608 | tf_op jit(solution)/shard_map/ppermute | solution.py:38
  172.0 14.9 %far.3 = (bf16[2096,128]{1,0:T(8,128)(2,1)S(1)}, bf16[2096,128]{1,0:T(8,128)(2,1)S(1)}, bf16[2096,128]{1,0:T(8,128)(2,1)S(1)}, bf16[2096,128]{1,0:T(8,128)(2,1)S(1)}) custom-call(s32[64]{0:T(128)S(1)} %reduce_sum.12.cnt_ref, s32[512]{0:T(512)S(1)} %reshape.63.code_ref, bf16[16,2,128,128]{3,2,1,0:T(8,128)(2,1)S(1)} %copy-done.1, ...), custom_call_target="tpu_custom_call" | custom-call | flops 536870912 | bytes 10485760 | tf_op jit(solution)/shard_map/far/pallas_call | solution.py:355
  187.0 7.4 %collective-permute-start.21 = (bf16[2096,128]{1,0:T(8,128)(2,1)S(1)}, bf16[2096,128]{1,0:T(8,128)(2,1)S(1)}, u32[]{:S(2)}, u32[]{:S(2)}) collective-permute-start(bf16[2096,128]{1,0:T(8,128)(2,1)S(1)} %get-tuple-element.58), channel_id=1, source_target_pairs={{0,16},{4,68},{8,24},{12,76},{16,0},{20,84},{24,8},{28,92},{32,48}... | collective-permute-start | bytes 1609736 | tf_op jit(solution)/shard_map/ppermute | solution.py:43
  197.0 9.8 %collective-permute-done.21.c = bf16[2096,128]{1,0:T(8,128)(2,1)S(1)} collective-permute-done((bf16[2096,128]{1,0:T(8,128)(2,1)S(1)}, bf16[2096,128]{1,0:T(8,128)(2,1)S(1)}, u32[]{:S(2)}, u32[]{:S(2)}) %collective-permute-start.21) | collective-permute-done | bytes 536608 | tf_op jit(solution)/shard_map/ppermute | solution.py:43
  207.6 2.4 collective-permute-start.31
  214.9 6.7 %collective-permute-done.31.a1 = bf16[2,1024,128]{2,1,0:T(8,128)(2,1)S(1)} collective-permute-done((bf16[2,1024,128]{2,1,0:T(8,128)(2,1)S(1)}, bf16[2,1024,128]{2,1,0:T(8,128)(2,1)S(1)}, u32[]{:S(2)}, u32[]{:S(2)}) %collective-permute-start.31) | collective-permute-done | bytes 524320 | tf_op jit(solution)/shard_map/ppermute | solution.py:56
  224.3 13.5 %collective-permute-done.33.a3 = bf16[2,1024,128]{2,1,0:T(8,128)(2,1)S(1)} collective-permute-done((bf16[2,1024,128]{2,1,0:T(8,128)(2,1)S(1)}, bf16[2,1024,128]{2,1,0:T(8,128)(2,1)S(1)}, u32[]{:S(2)}, u32[]{:S(2)}) %collective-permute-start.33) | collective-permute-done | bytes 524320 | tf_op jit(solution)/shard_map/ppermute | solution.py:56
  237.8 4.3 %mix.2.rest_9_ = f32[1024,512]{1,0:T(8,128)S(1)} custom-call(s32[2]{0:T(128)S(1)} %pad_add_fusion.place_ref, bf16[2,1024,128]{2,1,0:T(8,128)(2,1)S(1)} %finish.3.a0, bf16[2,1024,128]{2,1,0:T(8,128)(2,1)S(1)} %collective-permute-done.31.a1, bf16[2,1024,128]{2,1,0:T(8,128)(2,1)S(1)} %collective-permute-done.32.a2, ...), custom_call_target="tpu_custom_call" | custom-call | flops 1073741824 | bytes 6291456 | tf_op jit(solution)/shard_map/mix/pallas_call | solution.py:468
  244.0 2.9 %collective-permute-done.25.a2 = bf16[2,1024,128]{2,1,0:T(8,128)(2,1)} collective-permute-done((bf16[2,1024,128]{2,1,0:T(8,128)(2,1)S(1)}, bf16[2,1024,128]{2,1,0:T(8,128)(2,1)}, u32[]{:S(2)}, u32[]{:S(2)}) %collective-permute-start.25) | collective-permute-done | bytes 524320 | tf_op jit(solution)/shard_map/ppermute | solution.py:56
  246.9 12.2 %collective-permute-done.26.a3 = bf16[2,1024,128]{2,1,0:T(8,128)(2,1)} collective-permute-done((bf16[2,1024,128]{2,1,0:T(8,128)(2,1)S(1)}, bf16[2,1024,128]{2,1,0:T(8,128)(2,1)}, u32[]{:S(2)}, u32[]{:S(2)}) %collective-permute-start.26) | collective-permute-done | bytes 524320 | tf_op jit(solution)/shard_map/ppermute | solution.py:56
  259.1 5.6 %mix.3 = bf16[1024,512]{1,0:T(8,128)(2,1)} custom-call(s32[2]{0:T(128)S(1)} %pad_add_fusion.place_ref, bf16[2,1024,128]{2,1,0:T(8,128)(2,1)S(1)} %finish.2.a0, bf16[2,1024,128]{2,1,0:T(8,128)(2,1)S(1)} %collective-permute-done.24.a1, bf16[2,1024,128]{2,1,0:T(8,128)(2,1)} %collective-permute-done.25.a2, bf16[2,1024,128]{2,1,0:T(8,128)(2,1)} %collective-permute-done.26.a3, ...), custom_call_target="tpu_custom_call" | custom-call | flops 1073741824 | bytes 6291456 | tf_op jit(solution)/shard_map/mix/pallas_call | solution.py:468
  (99 shorter events, 41.6 us)
Async XLA Ops:
  8.7 31.4 %collective-permute-start.4 = (bf16[16,2,128,128]{3,2,1,0:T(8,128)(2,1)S(1)}, bf16[16,2,128,128]{3,2,1,0:T(8,128)(2,1)}, u32[]{:S(2)}, u32[]{:S(2)}) collective-permute-start(bf16[16,2,128,128]{3,2,1,0:T(8,128)(2,1)S(1)} %get-tuple-element.48), channel_id=1, source_target_pairs={{0,4},{4,0},{8,12},{12,8},{16,20},{20,16},{24,28},{28,24},{32,36},... | collective-permute-start | bytes 3145736 | tf_op jit(solution)/shard_map/ppermute | solution.py:47
  10.2 43.1 %collective-permute-start.3 = (bf16[16,2,128,128]{3,2,1,0:T(8,128)(2,1)S(1)}, bf16[16,2,128,128]{3,2,1,0:T(8,128)(2,1)}, u32[]{:S(2)}, u32[]{:S(2)}) collective-permute-start(bf16[16,2,128,128]{3,2,1,0:T(8,128)(2,1)S(1)} %get-tuple-element.51.rest_0_), channel_id=1, source_target_pairs={{0,32},{4,12},{8,40},{12,20},{16,48},{20,28},{24,56},{28,4},{32,64... | collective-permute-start | bytes 3145736 | tf_op jit(solution)/shard_map/ppermute | solution.py:38
  11.9 41.9 %collective-permute-start.9 = (bf16[16,2,128,128]{3,2,1,0:T(8,128)(2,1)S(1)}, bf16[16,2,128,128]{3,2,1,0:T(8,128)(2,1)S(1)}, u32[]{:S(2)}, u32[]{:S(2)}) collective-permute-start(bf16[16,2,128,128]{3,2,1,0:T(8,128)(2,1)S(1)} %get-tuple-element.51.rest_0_), channel_id=1, source_target_pairs={{0,96},{4,28},{8,104},{12,4},{16,112},{20,12},{24,120},{28,20},{32... | collective-permute-start | bytes 3145736 | tf_op jit(solution)/shard_map/ppermute | solution.py:38
  40.1 17.0 %collective-permute-start.5 = (bf16[16,2,128,128]{3,2,1,0:T(8,128)(2,1)}, bf16[16,2,128,128]{3,2,1,0:T(8,128)(2,1)}, u32[]{:S(2)}, u32[]{:S(2)}) collective-permute-start(bf16[16,2,128,128]{3,2,1,0:T(8,128)(2,1)} %collective-permute-done.4.rest_1_), channel_id=1, source_target_pairs={{0,96},{4,28},{8,104},{12,4},{16,112},{20,12},{24,120},{28,20},{32... | collective-permute-start | bytes 3145736 | tf_op jit(solution)/shard_map/ppermute | solution.py:38
  51.8 28.6 %collective-permute-start.14 = (bf16[2,2,8,128,128]{4,3,2,1,0:T(8,128)(2,1)}, bf16[2,2,8,128,128]{4,3,2,1,0:T(8,128)(2,1)}, u32[]{:S(2)}, u32[]{:S(2)}) collective-permute-start(bf16[2,2,8,128,128]{4,3,2,1,0:T(8,128)(2,1)} %bitcast.5.rest_8_), channel_id=1, source_target_pairs={{0,24},{4,100},{8,0},{12,108},{16,8},{20,116},{24,16},{28,124},{32... | collective-permute-start | bytes 3145736 | tf_op jit(solution)/shard_map/ppermute | solution.py:43
  53.4 27.0 %collective-permute-start.15 = (bf16[2,2,8,128,128]{4,3,2,1,0:T(8,128)(2,1)}, bf16[2,2,8,128,128]{4,3,2,1,0:T(8,128)(2,1)}, u32[]{:S(2)}, u32[]{:S(2)}) collective-permute-start(bf16[2,2,8,128,128]{4,3,2,1,0:T(8,128)(2,1)} %bitcast.5.rest_8_), channel_id=1, source_target_pairs={{0,16},{4,68},{8,24},{12,76},{16,0},{20,84},{24,8},{28,92},{32,48}... | collective-permute-start | bytes 3145736 | tf_op jit(solution)/shard_map/ppermute | solution.py:43
  54.8 39.7 %collective-permute-start.16 = (bf16[2,2,8,128,128]{4,3,2,1,0:T(8,128)(2,1)}, bf16[2,2,8,128,128]{4,3,2,1,0:T(8,128)(2,1)}, u32[]{:S(2)}, u32[]{:S(2)}) collective-permute-start(bf16[2,2,8,128,128]{4,3,2,1,0:T(8,128)(2,1)} %bitcast.5.rest_8_), channel_id=1, source_target_pairs={{0,8},{4,36},{8,16},{12,44},{16,24},{20,52},{24,0},{28,60},{32,40}... | collective-permute-start | bytes 3145736 | tf_op jit(solution)/shard_map/ppermute | solution.py:43
  55.4 61.4 %collective-permute-start.10 = (bf16[16,2,128,128]{3,2,1,0:T(8,128)(2,1)}, bf16[16,2,128,128]{3,2,1,0:T(8,128)(2,1)}, u32[]{:S(2)}, u32[]{:S(2)}) collective-permute-start(bf16[16,2,128,128]{3,2,1,0:T(8,128)(2,1)} %collective-permute-done.3.rest_6_), channel_id=1, source_target_pairs={{0,32},{4,12},{8,40},{12,20},{16,48},{20,28},{24,56},{28,4},{32,64... | collective-permute-start | bytes 3145736 | tf_op jit(solution)/shard_map/ppermute | solution.py:38
  57.0 59.8 %collective-permute-start.12 = (bf16[16,2,128,128]{3,2,1,0:T(8,128)(2,1)}, bf16[16,2,128,128]{3,2,1,0:T(8,128)(2,1)}, u32[]{:S(2)}, u32[]{:S(2)}) collective-permute-start(bf16[16,2,128,128]{3,2,1,0:T(8,128)(2,1)} %collective-permute-done.4.rest_1_), channel_id=1, source_target_pairs={{0,32},{4,12},{8,40},{12,20},{16,48},{20,28},{24,56},{28,4},{32,64... | collective-permute-start | bytes 3145736 | tf_op jit(solution)/shard_map/ppermute | solution.py:38
  80.4 65.9 %collective-permute-start.7 = (bf16[16,2,128,128]{3,2,1,0:T(8,128)(2,1)}, bf16[16,2,128,128]{3,2,1,0:T(8,128)(2,1)}, u32[]{:S(2)}, u32[]{:S(2)}) collective-permute-start(bf16[16,2,128,128]{3,2,1,0:T(8,128)(2,1)} %copy-done), channel_id=1, source_target_pairs={{0,32},{4,12},{8,40},{12,20},{16,48},{20,28},{24,56},{28,4},{32,64... | collective-permute-start | bytes 3145736 | tf_op jit(solution)/shard_map/ppermute | solution.py:38
  80.4 65.9 %collective-permute-start.8 = (bf16[16,2,128,128]{3,2,1,0:T(8,128)(2,1)}, bf16[16,2,128,128]{3,2,1,0:T(8,128)(2,1)}, u32[]{:S(2)}, u32[]{:S(2)}) collective-permute-start(bf16[16,2,128,128]{3,2,1,0:T(8,128)(2,1)} %collective-permute-done.2.rest_1_), channel_id=1, source_target_pairs={{0,96},{4,28},{8,104},{12,4},{16,112},{20,12},{24,120},{28,20},{32... | collective-permute-start | bytes 3145736 | tf_op jit(solution)/shard_map/ppermute | solution.py:38
  94.5 36.2 %collective-permute-start.11 = (bf16[16,2,128,128]{3,2,1,0:T(8,128)(2,1)}, bf16[16,2,128,128]{3,2,1,0:T(8,128)(2,1)}, u32[]{:S(2)}, u32[]{:S(2)}) collective-permute-start(bf16[16,2,128,128]{3,2,1,0:T(8,128)(2,1)} %collective-permute-done.5.rest_3_), channel_id=1, source_target_pairs={{0,96},{4,28},{8,104},{12,4},{16,112},{20,12},{24,120},{28,20},{32... | collective-permute-start | bytes 3145736 | tf_op jit(solution)/shard_map/ppermute | solution.py:38
  116.8 32.2 %collective-permute-start.19 = (bf16[16,2,128,128]{3,2,1,0:T(8,128)(2,1)}, bf16[16,2,128,128]{3,2,1,0:T(8,128)(2,1)}, u32[]{:S(2)}, u32[]{:S(2)}) collective-permute-start(bf16[16,2,128,128]{3,2,1,0:T(8,128)(2,1)} %collective-permute-done.2.rest_1_), channel_id=1, source_target_pairs={{0,32},{4,12},{8,40},{12,20},{16,48},{20,28},{24,56},{28,4},{32,64... | collective-permute-start | bytes 3145736 | tf_op jit(solution)/shard_map/ppermute | solution.py:38
  116.9 38.2 %collective-permute-start.6 = (bf16[16,2,128,128]{3,2,1,0:T(8,128)(2,1)}, bf16[16,2,128,128]{3,2,1,0:T(8,128)(2,1)}, u32[]{:S(2)}, u32[]{:S(2)}) collective-permute-start(bf16[16,2,128,128]{3,2,1,0:T(8,128)(2,1)} %copy-done), channel_id=1, source_target_pairs={{0,96},{4,28},{8,104},{12,4},{16,112},{20,12},{24,120},{28,20},{32... | collective-permute-start | bytes 3145736 | tf_op jit(solution)/shard_map/ppermute | solution.py:38
  146.2 22.9 %collective-permute-start.17 = (bf16[16,2,128,128]{3,2,1,0:T(8,128)(2,1)}, bf16[16,2,128,128]{3,2,1,0:T(8,128)(2,1)S(1)}, u32[]{:S(2)}, u32[]{:S(2)}) collective-permute-start(bf16[16,2,128,128]{3,2,1,0:T(8,128)(2,1)} %collective-permute-done.7.rest_6_), channel_id=1, source_target_pairs={{0,32},{4,12},{8,40},{12,20},{16,48},{20,28},{24,56},{28,4},{32,64... | collective-permute-start | bytes 3145736 | tf_op jit(solution)/shard_map/ppermute | solution.py:38
  146.3 24.7 %collective-permute-start.18 = (bf16[16,2,128,128]{3,2,1,0:T(8,128)(2,1)}, bf16[16,2,128,128]{3,2,1,0:T(8,128)(2,1)S(1)}, u32[]{:S(2)}, u32[]{:S(2)}) collective-permute-start(bf16[16,2,128,128]{3,2,1,0:T(8,128)(2,1)} %collective-permute-done.8.rest_3_), channel_id=1, source_target_pairs={{0,96},{4,28},{8,104},{12,4},{16,112},{20,12},{24,120},{28,20},{32... | collective-permute-start | bytes 3145736 | tf_op jit(solution)/shard_map/ppermute | solution.py:38
  149.0 45.5 %collective-permute-start.27 = (bf16[2096,128]{1,0:T(8,128)(2,1)S(1)}, bf16[2096,128]{1,0:T(8,128)(2,1)S(1)}, u32[]{:S(2)}, u32[]{:S(2)}) collective-permute-start(bf16[2096,128]{1,0:T(8,128)(2,1)S(1)} %get-tuple-element.62), channel_id=1, source_target_pairs={{0,8},{4,36},{8,16},{12,44},{16,24},{20,52},{24,0},{28,60},{32,40}... | collective-permute-start | bytes 1609736 | tf_op jit(solution)/shard_map/ppermute | solution.py:43
  149.0 47.5 %collective-permute-start.28 = (bf16[2096,128]{1,0:T(8,128)(2,1)S(1)}, bf16[2096,128]{1,0:T(8,128)(2,1)S(1)}, u32[]{:S(2)}, u32[]{:S(2)}) collective-permute-start(bf16[2096,128]{1,0:T(8,128)(2,1)S(1)} %get-tuple-element.63), channel_id=1, source_target_pairs={{0,16},{4,68},{8,24},{12,76},{16,0},{20,84},{24,8},{28,92},{32,48}... | collective-permute-start | bytes 1609736 | tf_op jit(solution)/shard_map/ppermute | solution.py:43
  155.1 41.4 %collective-permute-start.29 = (bf16[2096,128]{1,0:T(8,128)(2,1)S(1)}, bf16[2096,128]{1,0:T(8,128)(2,1)S(1)}, u32[]{:S(2)}, u32[]{:S(2)}) collective-permute-start(bf16[2096,128]{1,0:T(8,128)(2,1)S(1)} %get-tuple-element.64), channel_id=1, source_target_pairs={{0,24},{4,100},{8,0},{12,108},{16,8},{20,116},{24,16},{28,124},{32... | collective-permute-start | bytes 1609736 | tf_op jit(solution)/shard_map/ppermute | solution.py:43
  187.0 19.8 %collective-permute-start.21 = (bf16[2096,128]{1,0:T(8,128)(2,1)S(1)}, bf16[2096,128]{1,0:T(8,128)(2,1)S(1)}, u32[]{:S(2)}, u32[]{:S(2)}) collective-permute-start(bf16[2096,128]{1,0:T(8,128)(2,1)S(1)} %get-tuple-element.58), channel_id=1, source_target_pairs={{0,16},{4,68},{8,24},{12,76},{16,0},{20,84},{24,8},{28,92},{32,48}... | collective-permute-start | bytes 1609736 | tf_op jit(solution)/shard_map/ppermute | solution.py:43
  210.7 27.1 %collective-permute-start.33 = (bf16[2,1024,128]{2,1,0:T(8,128)(2,1)S(1)}, bf16[2,1024,128]{2,1,0:T(8,128)(2,1)S(1)}, u32[]{:S(2)}, u32[]{:S(2)}) collective-permute-start(bf16[2,1024,128]{2,1,0:T(8,128)(2,1)S(1)} %finish.3.a0), channel_id=1, source_target_pairs={{0,1},{1,2},{2,3},{3,0},{4,5},{5,6},{6,7},{7,4},{8,9},{9,10},{10,1... | collective-permute-start | bytes 1572872 | tf_op jit(solution)/shard_map/ppermute | solution.py:56
  211.6 32.4 %collective-permute-start.24 = (bf16[2,1024,128]{2,1,0:T(8,128)(2,1)S(1)}, bf16[2,1024,128]{2,1,0:T(8,128)(2,1)S(1)}, u32[]{:S(2)}, u32[]{:S(2)}) collective-permute-start(bf16[2,1024,128]{2,1,0:T(8,128)(2,1)S(1)} %finish.2.a0), channel_id=1, source_target_pairs={{0,3},{1,0},{2,1},{3,2},{4,7},{5,4},{6,5},{7,6},{8,11},{9,8},{10,9... | collective-permute-start | bytes 1572872 | tf_op jit(solution)/shard_map/ppermute | solution.py:56
  213.7 33.2 %collective-permute-start.25 = (bf16[2,1024,128]{2,1,0:T(8,128)(2,1)S(1)}, bf16[2,1024,128]{2,1,0:T(8,128)(2,1)}, u32[]{:S(2)}, u32[]{:S(2)}) collective-permute-start(bf16[2,1024,128]{2,1,0:T(8,128)(2,1)S(1)} %finish.2.a0), channel_id=1, source_target_pairs={{0,2},{1,3},{2,0},{3,1},{4,6},{5,7},{6,4},{7,5},{8,10},{9,11},{10,... | collective-permute-start | bytes 1572872 | tf_op jit(solution)/shard_map/ppermute | solution.py:56
  221.6 37.5 %collective-permute-start.26 = (bf16[2,1024,128]{2,1,0:T(8,128)(2,1)S(1)}, bf16[2,1024,128]{2,1,0:T(8,128)(2,1)}, u32[]{:S(2)}, u32[]{:S(2)}) collective-permute-start(bf16[2,1024,128]{2,1,0:T(8,128)(2,1)S(1)} %finish.2.a0), channel_id=1, source_target_pairs={{0,1},{1,2},{2,3},{3,0},{4,5},{5,6},{6,7},{7,4},{8,9},{9,10},{10,1... | collective-permute-start | bytes 1572872 | tf_op jit(solution)/shard_map/ppermute | solution.py:56
  (24 other events, 435.4 us)
where the time goes:
time: 267 us; the launch traced here: 265 us
  waiting for transfers between devices  89.6 us (34%)
  Pallas kernels  82.7 us (31%)
  starting transfers between devices  81.2 us (30%)
  local copies, waits for them, and re-layouts  8.7 us (3%)
    ppermute x12, starting transfers between devices, rows_perm(): return lax.ppermute(x, 'tok', pairs)  49.7 us
    ppermute x6, waiting for transfers between devices, mp_perm(): return lax.ppermute(x, 'mp', [(i, (i + d) % NX) for i in range(NX)])  39.6 us
    pallas_call x2, Pallas kernels, far(): pl.pallas_call(functools.partial(far_kernel, j), in_specs=[SMEM, SMEM] +...  30.4 us
    ppermute x9, waiting for transfers between devices, query_perm(): return lax.ppermute(x, 'tok', pairs)  27.5 us
    ppermute x9, starting transfers between devices, query_perm(): return lax.ppermute(x, 'tok', pairs)  20.3 us
    pallas_call x2, Pallas kernels, split_cache(): pl.pallas_call(split_cache_kernel, grid_spec=pltpu.PrefetchScalarGridSpec...  17.4 us
    ppermute x12, waiting for transfers between devices, rows_perm(): return lax.ppermute(x, 'tok', pairs)  15.3 us
    pallas_call x1, Pallas kernels, project(): pl.pallas_call(project_kernel, grid_spec=pltpu.PrefetchScalarGridSpec(num...  14.9 us
  transfers between devices with their start and end apart: 34, of which 12 were waited for; matrix products, arithmetic and copies ran while one was open for 2% of the time, Pallas kernels for 26%

commit v1 on v0

--- a/solution.py
+++ b/solution.py
@@ -17,6 +17,7 @@
 F32, BF16 = jnp.float32, jnp.bfloat16
 ANY = pl.BlockSpec(memory_space=pl.ANY)
 SMEM = pl.BlockSpec(memory_space=pltpu.SMEM)
+BRIEF = pl.CostEstimate(flops=1, transcendentals=0, bytes_accessed=1)
 OROWS = 2048 + 48
 FROWS = 1024 + 8
 
@@ -47,9 +48,9 @@
     return lax.ppermute(x, "tok", [(tok_of(y, z, c), tok_of(y, z, 1 - c)) for y, z, c in chips()])
 
 
-def ring_perm(x, d):
+def halo_perm(x):
     n = NY * NZ * NC
-    return lax.ppermute(x, "tok", [(i, (i + d) % n) for i in range(n)])
+    return lax.ppermute(x, "tok", [(i, (i + (1 if i % 2 else -1)) % n) for i in range(n)])
 
 
 def mp_perm(x, d):
@@ -88,12 +89,12 @@
         ),
         out_shape=[out, out],
         compiler_params=params(),
-        cost_estimate=pl.CostEstimate(flops=0, transcendentals=0, bytes_accessed=4 << 20),
+        cost_estimate=BRIEF,
         name="split_cache",
     )(core, rows, rows)
 
 
-def project_kernel(core_ref, tok_ref, gain_ref, wq, wk, wv, q_all, q_send, k_all, v_all, first, last):
+def project_kernel(core_ref, tok_ref, gain_ref, wq, wk, wv, q_all, swap, k_all, v_all, edge):
     step = pl.program_id(0)
     core = core_ref[0]
     x = tok_ref[...].astype(F32)
@@ -103,29 +104,28 @@
     k = nn(normed, wk[...]).astype(BF16)
     v = nn(normed, wv[...])
 
-    def put(shift):
+    def put(here):
+        to_first = swap if here else edge
+        to_last = edge if here else swap
         for h in range(4):
-            slot = (h - shift) % 4
+            slot = (h - 2 * here) % 4
             lanes = slice(h * HD, (h + 1) * HD)
             q_all[slot] = q[:, lanes]
             if slot >= 2:
-                q_send[slot - 2] = q[:, lanes]
+                swap[pl.ds((slot - 2) * 1024 + pl.multiple_of(step * 256, 256), 256), :] = q[:, lanes]
             for b in range(2):
                 rows = slice(b * BLOCK, (b + 1) * BLOCK)
                 kb = k[rows, lanes]
                 vb = v[rows, lanes].T.astype(BF16)
                 k_all[slot, b] = kb
                 v_all[slot, b] = vb
-                if b == 0:
-                    @pl.when(step == 0)
-                    def _():
-                        first[0, slot] = kb
-                        first[1, slot] = vb
-                else:
-                    @pl.when(step == pl.num_programs(0) - 1)
-                    def _():
-                        last[0, slot] = kb
-                        last[1, slot] = vb
+                out, when = (to_first, 0) if b == 0 else (to_last, pl.num_programs(0) - 1)
+                base = 2048 if out is swap else 0
+
+                @pl.when(step == when)
+                def _():
+                    out[base + slot * HD : base + (slot + 1) * HD, :] = kb
+                    out[base + (4 + slot) * HD : base + (5 + slot) * HD, :] = vb
 
     @pl.when(core == 0)
     def _():
@@ -133,14 +133,13 @@
 
     @pl.when(core == 1)
     def _():
-        put(2)
+        put(1)
 
 
 def project(core, tokens, gain, wq, wk, wv):
     n, d = tokens.shape
     w = wq.shape[1]
     weight = pl.BlockSpec((d, w), lambda i, c: (0, 0), pipeline_mode=pl.Buffered(1))
-    edge = pl.BlockSpec((2, 4, BLOCK, HD), lambda i, c: (0, 0, 0, 0))
     blocks = pl.BlockSpec((4, 2, BLOCK, HD), lambda i, c: (0, i, 0, 0))
     return pl.pallas_call(
         project_kernel,
@@ -156,32 +155,33 @@
             ],
             out_specs=[
                 pl.BlockSpec((4, 256, HD), lambda i, c: (0, i, 0)),
-                pl.BlockSpec((2, 256, HD), lambda i, c: (0, i, 0)),
+                pl.BlockSpec((3072, HD), lambda i, c: (0, 0)),
                 blocks,
                 blocks,
-                edge,
-                edge,
+                pl.BlockSpec((1024, HD), lambda i, c: (0, 0)),
             ],
         ),
         out_shape=[
             jax.ShapeDtypeStruct((4, n, HD), BF16),
-            jax.ShapeDtypeStruct((2, n, HD), BF16),
+            jax.ShapeDtypeStruct((3072, HD), BF16),
             jax.ShapeDtypeStruct((4, 8, BLOCK, HD), BF16),
             jax.ShapeDtypeStruct((4, 8, HD, BLOCK), BF16),
-            jax.ShapeDtypeStruct((2, 4, BLOCK, HD), BF16),
-            jax.ShapeDtypeStruct((2, 4, BLOCK, HD), BF16),
+            jax.ShapeDtypeStruct((1024, HD), BF16),
         ],
         compiler_params=params(),
-        cost_estimate=pl.CostEstimate(flops=2 * n * d * 3 * w, transcendentals=0, bytes_accessed=16 << 20),
+        cost_estimate=BRIEF,
         name="project",
     )(core, tokens, gain.reshape(1, d), wq, wk, wv)
 
 
-def near_kernel(q_ref, k_ref, v_ref, lo_ref, hi_ref, o_ref, lse_ref):
+def near_kernel(core_ref, q_ref, k_ref, v_ref, ka, va, kb, vb, o_ref, lse_ref):
+    first = core_ref[0] == 0
+    klo, khi = jnp.where(first, ka[0], kb[0]), jnp.where(first, kb[0], ka[0])
+    vlo, vhi = jnp.where(first, va[0], vb[0]), jnp.where(first, vb[0], va[0])
     for b in range(8):
         q = q_ref[0, b * BLOCK : (b + 1) * BLOCK]
-        ks = [lo_ref[0, 0] if b == 0 else k_ref[0, b - 1], k_ref[0, b], hi_ref[0, 0] if b == 7 else k_ref[0, b + 1]]
-        vs = [lo_ref[1, 0] if b == 0 else v_ref[0, b - 1], v_ref[0, b], hi_ref[1, 0] if b == 7 else v_ref[0, b + 1]]
+        ks = [klo if b == 0 else k_ref[0, b - 1], k_ref[0, b], khi if b == 7 else k_ref[0, b + 1]]
+        vs = [vlo if b == 0 else v_ref[0, b - 1], v_ref[0, b], vhi if b == 7 else v_ref[0, b + 1]]
         s = [nt(k, q) * SCALE for k in ks]
         m = jnp.max(jnp.maximum(jnp.maximum(s[0], s[1]), s[2]), axis=0, keepdims=True)
         p = [jnp.exp(x - m) for x in s]
@@ -191,33 +191,33 @@
         lse_ref[0, b : b + 1, :] = m + jnp.log(total)
 
 
-def near(q, k, v, lo, hi):
-    blocks = pl.BlockSpec((1, 8, BLOCK, HD), lambda s: (s, 0, 0, 0))
-    edge = pl.BlockSpec((2, 1, BLOCK, HD), lambda s: (0, (s + 2) % 4, 0, 0))
+def near(core, q, k, v, halo, swapped):
+    blocks = pl.BlockSpec((1, 8, BLOCK, HD), lambda s, c: (s, 0, 0, 0))
+
+    def edge(first):
+        return pl.BlockSpec((1, BLOCK, HD), lambda s, c: (first + (s + 2) % 4, 0, 0))
+
     return pl.pallas_call(
         near_kernel,
-        grid=(4,),
-        in_specs=[pl.BlockSpec((1, 1024, HD), lambda s: (s, 0, 0)), blocks, blocks, edge, edge],
-        out_specs=[blocks, pl.BlockSpec((1, 8, HD), lambda s: (s, 0, 0))],
+        grid_spec=pltpu.PrefetchScalarGridSpec(
+            num_scalar_prefetch=1,
+            grid=(4,),
+            in_specs=[pl.BlockSpec((1, 1024, HD), lambda s, c: (s, 0, 0)), blocks, blocks]
+            + [edge(0), edge(4), edge(16), edge(20)],
+            out_specs=[blocks, pl.BlockSpec((1, 8, HD), lambda s, c: (s, 0, 0))],
+        ),
         out_shape=[jax.ShapeDtypeStruct((4, 8, HD, BLOCK), F32), jax.ShapeDtypeStruct((4, 8, BLOCK), F32)],
         compiler_params=params(),
-        cost_estimate=pl.CostEstimate(flops=32 * 384 * 128 * 512, transcendentals=32 * 384 * 128, bytes_accessed=6 << 20),
+        cost_estimate=BRIEF,
         name="near",
-    )(q, k, v, lo, hi)
+    )(core, q, k, v, halo.reshape(8, BLOCK, HD), halo.reshape(8, BLOCK, HD), swapped.reshape(24, BLOCK, HD), swapped.reshape(24, BLOCK, HD))
 
 
 GROUP = 4
 UNITS = 96 + GROUP
 
 
-def far_kernel(
-    j, cnt_ref, code_ref, *rest,
-):
-    sources, qs, outs = rest[:8], rest[8:12], rest[12:16]
-    kvbuf, qbuf, acc_ref, stat_ref, list_ref, unit_ref, first_ref, kvsem, qsem, logs = rest[16:]
-    for r in range(4):
-        pltpu.make_async_copy(qs[r].at[:, j], qbuf.at[pl.ds(2 * r, 2)], qsem.at[r]).start()
-
+def plan_kernel(cnt_ref, code_ref, list_ref, unit_ref, first_ref, size_ref):
     def scan(i, carry):
         e, u = carry
         n = cnt_ref[i]
@@ -243,6 +243,31 @@
     entries, units = lax.fori_loop(0, 64, scan, (jnp.int32(0), jnp.int32(0)))
     for g in range(GROUP):
         unit_ref[units + g] = -1
+    size_ref[0] = entries
+    size_ref[1] = units
+
+
+def plan(cnt, code):
+    def out(n):
+        return jax.ShapeDtypeStruct((n,), jnp.int32)
+
+    return pl.pallas_call(
+        plan_kernel,
+        in_specs=[SMEM] * 2,
+        out_specs=[SMEM] * 4,
+        out_shape=[out(128 + WMAX), out(UNITS), out(64), out(2)],
+        compiler_params=params(16),
+        cost_estimate=BRIEF,
+        name="plan",
+    )(cnt, code)
+
+
+def far_kernel(j, cnt_ref, list_ref, unit_ref, first_ref, size_ref, *rest):
+    sources, qs, outs = rest[:8], rest[8:12], rest[12:16]
+    kvbuf, qbuf, acc_ref, stat_ref, kvsem, qsem, logs = rest[16:]
+    entries, units = size_ref[0], size_ref[1]
+    for r in range(4):
+        pltpu.make_async_copy(qs[r].at[:, j], qbuf.at[pl.ds(2 * r, 2)], qsem.at[r]).start()
 
     def fetch(e, _):
         code = list_ref[e]
@@ -350,11 +375,11 @@
             part = part - term.astype(F32)
 
 
-def far(j, cnt, code, sources, qs):
+def far(j, cnt, lists, sources, qs):
     out = jax.ShapeDtypeStruct((OROWS, BLOCK), BF16)
     return pl.pallas_call(
         functools.partial(far_kernel, j),
-        in_specs=[SMEM, SMEM] + [ANY] * 12,
+        in_specs=[SMEM] * 5 + [ANY] * 12,
         out_specs=[pl.BlockSpec((OROWS, BLOCK), lambda: (0, 0))] * 4,
         out_shape=[out] * 4,
         scratch_shapes=[
@@ -362,17 +387,14 @@
             pltpu.VMEM((8, 8, BLOCK, HD), BF16),
             pltpu.VMEM((UNITS, HD, BLOCK), F32),
             pltpu.VMEM((UNITS, 8, BLOCK), F32),
-            pltpu.SMEM((128 + WMAX,), jnp.int32),
-            pltpu.SMEM((UNITS,), jnp.int32),
-            pltpu.SMEM((64,), jnp.int32),
             pltpu.SemaphoreType.DMA((128,)),
             pltpu.SemaphoreType.DMA((4,)),
             pltpu.VMEM((16, BLOCK), F32),
         ],
         compiler_params=params(),
-        cost_estimate=pl.CostEstimate(flops=64 * 128 * 128 * 512, transcendentals=64 * 128 * 128, bytes_accessed=10 << 20),
+        cost_estimate=BRIEF,
         name="far",
-    )(cnt, code, *sources, *qs)
+    )(cnt, *lists, *sources, *qs)
 
 
 def merge_kernel(a, b, c, d, keep, send):
@@ -399,7 +421,7 @@
         merge_kernel,
         out_shape=[out, out],
         compiler_params=params(),
-        cost_estimate=pl.CostEstimate(flops=1 << 21, transcendentals=1 << 13, bytes_accessed=3 << 20),
+        cost_estimate=BRIEF,
         name="merge",
     )(*parts)
 
@@ -431,7 +453,7 @@
         out_specs=pl.BlockSpec((2, 1024, HD), lambda i: (0, 0, 0)),
         out_shape=jax.ShapeDtypeStruct((2, 1024, HD), BF16),
         compiler_params=params(),
-        cost_estimate=pl.CostEstimate(flops=1 << 21, transcendentals=1 << 13, bytes_accessed=3 << 20),
+        cost_estimate=BRIEF,
         name="finish",
     )(o, lse, o, lse, far_keep, far_other)
 
@@ -475,7 +497,7 @@
         ),
         out_shape=jax.ShapeDtypeStruct((n, cols), BF16 if last else F32),
         compiler_params=params(),
-        cost_estimate=pl.CostEstimate(flops=2 * n * 1024 * cols, transcendentals=0, bytes_accessed=6 << 20),
+        cost_estimate=BRIEF,
         name="mix",
     )(place, *args)
 
@@ -508,41 +530,57 @@
     def after(x, *deps):
         return lax.optimization_barrier((x, *deps))[0]
 
-    keep, send = [None, None], [None, None]
-    keep[0], send[0] = split_cache(0, core, kv_cache)
-    up_k, down_k = [rows_perm(keep[0], 1), None], [rows_perm(keep[0], -1), None]
-    got = [core_swap(send[0]), None]
-    up_r, down_r = [rows_perm(got[0], 1), None], [rows_perm(got[0], -1), None]
-    keep[1], send[1] = split_cache(1, core, kv_cache)
-    got[1] = core_swap(send[1])
-
-    q_all, q_send, k_all, v_all, first, last = project(core, tokens, norm_gain, w_query, w_key, w_value)
-    mine = jnp.concatenate([q_all[:2], core_swap(q_send)], axis=0).reshape(2, 2, 8, BLOCK, HD)
+    keep0, send0 = split_cache(0, core, kv_cache)
+    up_k0, down_k0 = rows_perm(keep0, 1), rows_perm(keep0, -1)
+    got0 = core_swap(send0)
+    up_r0, down_r0 = rows_perm(got0, 1), rows_perm(got0, -1)
+
+    gain = after(norm_gain, got0)
+    q_all, swap, k_all, v_all, edge = project(core, tokens, gain, w_query, w_key, w_value)
+    swapped, halo = core_swap(swap), halo_perm(edge)
+    up20 = rows_perm(after(up_k0, edge), 1)
+    mine = jnp.concatenate([q_all[:2], swapped[:2048].reshape(2, 1024, HD)], axis=0).reshape(2, 2, 8, BLOCK, HD)
+    mine, halo, down_k0, up_r0, down_r0 = lax.optimization_barrier((mine, halo, down_k0, up_r0, down_r0))
+    down20 = rows_perm(down_r0, -1)
     qs = [mine, query_perm(mine, -1), query_perm(mine, 2), query_perm(mine, 1)]
-    lo, hi = ring_perm(last, 1), ring_perm(first, -1)
+
+    core1 = after(core, mine)
+    keep1, send1 = split_cache(1, core1, kv_cache)
     code, cnt = line_codes(wake_blocks, wake_frames, wake_counts, y, z, c)
-    near_o, near_lse = near(q_all, k_all, v_all, lo, hi)
-
-    keep[1], got[1] = lax.optimization_barrier((keep[1], got[1], up_k[0], down_r[0]))[:2]
-    up_k[1], down_k[1] = rows_perm(keep[1], 1), rows_perm(keep[1], -1)
-    up_r[1], down_r[1] = rows_perm(got[1], 1), rows_perm(got[1], -1)
-
-    acc = None
-    parts = None
-    for j in range(2):
-        if parts is not None:
-            up_k[j], down_r[j] = lax.optimization_barrier((up_k[j], down_r[j], parts[0]))[:2]
-        up2, down2 = rows_perm(up_k[j], 1), rows_perm(down_r[j], -1)
-        sources = [keep[j], got[j], down_k[j], down_r[j], up2, down2, up_k[j], up_r[j]]
-        if j == 0:
-            near_o, near_lse, sources[0] = lax.optimization_barrier((near_o, near_lse, sources[0]))
-        parts = far(j, cnt, code, sources, qs)
-        back = [parts[0], query_perm(parts[1], 1), query_perm(parts[2], 2), query_perm(parts[3], -1)]
-        own, other = merge(back)
-        heads = finish(j, near_o, near_lse, own, core_swap(other))
-        gathered = [heads, mp_perm(heads, -1), mp_perm(heads, 2), mp_perm(heads, 1)]
-        acc = mix(j, place, gathered, w_out, tokens, acc)
-    return acc
+    lists = plan(cnt, code)
+    send1, up20, down20 = lax.optimization_barrier((send1, up20, down20))
+    got1 = core_swap(send1)
+    near_o, near_lse = near(core, q_all, k_all, v_all, after(halo, keep1), swapped)
+    keep1, got1, near_o, near_lse, *qs = lax.optimization_barrier((keep1, got1, near_o, near_lse, *qs))
+    up_k1, down_k1 = rows_perm(keep1, 1), rows_perm(keep1, -1)
+    up_r1, down_r1 = rows_perm(got1, 1), rows_perm(got1, -1)
+
+    def returned(parts):
+        return [parts[0], query_perm(parts[1], 1), query_perm(parts[2], 2), query_perm(parts[3], -1)]
+
+    def gather(heads):
+        return [heads, mp_perm(heads, -1), mp_perm(heads, 2), mp_perm(heads, 1)]
+
+    sources = [keep0, got0, down_k0, down_r0, up20, down20, up_k0, up_r0]
+    parts = far(0, cnt, lists, sources, qs)
+    *parts, up_k1, down_k1 = lax.optimization_barrier((*parts, up_k1, down_k1))
+    back = returned(parts)
+    up21 = rows_perm(up_k1, 1)
+    back[0], down_k1, up_r1, down_r1 = lax.optimization_barrier((back[0], down_k1, up_r1, down_r1))
+    down21 = rows_perm(down_r1, -1)
+    own, other = merge(back)
+    heads = finish(0, near_o, near_lse, own, core_swap(other))
+    gathered = gather(heads)
+
+    sources = [after(keep1, heads), got1, down_k1, down_r1, up21, down21, up_k1, up_r1]
+    parts = far(1, cnt, lists, sources, qs)
+    back = returned(parts)
+    gathered[0] = after(gathered[0], parts[0])
+    acc = mix(0, place, gathered, w_out, tokens, None)
+    back[0], acc = lax.optimization_barrier((back[0], acc))
+    own, other = merge(back)
+    heads = finish(1, near_o, near_lse, own, core_swap(other))
+    return mix(1, place, gather(heads), w_out, tokens, acc)
 
 
 def solution(mesh):

time: 267 us -> 245 us (0.918)
  waiting for transfers between devices: 89.6 us -> 77.7 us
  starting transfers between devices: 81.2 us -> 70.6 us
    ppermute x12, starting transfers between devices: 49.7 us -> 20.6 us  [rows_perm(): return lax.ppermute(x, 'tok', pairs)]
    ppermute x5, starting transfers between devices: 2.26 us -> 28.4 us  [core_swap(): lax.ppermute(x, 'tok', [(tok_of(y, z, c), tok_of(y, z, 1 - c)) for y, z,...]
    ppermute x9, waiting for transfers between devices: 27.5 us -> 12.3 us  [query_perm(): return lax.ppermute(x, 'tok', pairs)]
    ppermute x6, waiting for transfers between devices: 39.6 us -> 49.4 us  [mp_perm(): return lax.ppermute(x, 'mp', [(i, (i + d) % NX) for i in range(NX)])]
    ppermute x12, waiting for transfers between devices: 15.3 us -> 8.35 us  [rows_perm(): return lax.ppermute(x, 'tok', pairs)]
    ppermute x9, starting transfers between devices: 20.3 us -> 14.9 us  [query_perm(): return lax.ppermute(x, 'tok', pairs)]
    unnamed x28 -> x46, local copies, waits for them, and re-layouts: 4.73 us -> 10.1 us
    pallas_call x3 -> x4, Pallas kernels: 39.2 us -> 35.1 us  [the longest x2 23 us: far(): pl.pallas_call(functools.partial(far_kernel, j), in_specs=[SMEM] * 5 + [A...]
  transfers between devices with their start and end apart: 34 -> 33, of which waited for: 12 -> 12; matrix products, arithmetic and copies ran while one was open for 2% -> 0% of each run, Pallas kernels for 26% -> 27%
where the time goes in v1:
time: 245 us; the launch traced here: 240 us
  Pallas kernels  80.1 us (33%)
  waiting for transfers between devices  77.7 us (32%)
  starting transfers between devices  70.6 us (29%)
  local copies, waits for them, and re-layouts  10.7 us (4%)
    ppermute x6, waiting for transfers between devices, mp_perm(): return lax.ppermute(x, 'mp', [(i, (i + d) % NX) for i in range(NX)])  49.4 us
    ppermute x5, starting transfers between devices, core_swap(): lax.ppermute(x, 'tok', [(tok_of(y, z, c), tok_of(y, z, 1 - c)) for y, z,...  28.4 us
    pallas_call x2, Pallas kernels, far(): pl.pallas_call(functools.partial(far_kernel, j), in_specs=[SMEM] * 5 + [A...  23 us
    ppermute x12, starting transfers between devices, rows_perm(): return lax.ppermute(x, 'tok', pairs)  20.6 us
    pallas_call x2, Pallas kernels, split_cache(): pl.pallas_call(split_cache_kernel, grid_spec=pltpu.PrefetchScalarGridSpec...  17.4 us
    ppermute x9, starting transfers between devices, query_perm(): return lax.ppermute(x, 'tok', pairs)  14.9 us
    pallas_call x1, Pallas kernels, project(): pl.pallas_call(project_kernel, grid_spec=pltpu.PrefetchScalarGridSpec(num...  14.8 us
    ppermute x9, waiting for transfers between devices, query_perm(): return lax.ppermute(x, 'tok', pairs)  12.3 us
  transfers between devices with their start and end apart: 33, of which 12 were waited for; matrix products, arithmetic and copies ran while one was open for 0% of the time, Pallas kernels for 27%

profile of v1, /device:TPU:1, one launch (start us, length us, event | category | flops | bytes accessed | tf_op | source)
XLA Modules:
  0.0 240.1 jit_solution(9271501346579632535)
XLA Ops:
  0.0 8.7 %split_cache.2 = (bf16[16,2,128,128]{3,2,1,0:T(8,128)(2,1)S(1)}, bf16[16,2,128,128]{3,2,1,0:T(8,128)(2,1)S(1)}) custom-call(s32[1]{0:T(128)} %bitcast.core_ref, bf16[2,1024,2,512]{3,2,1,0:T(2,128)(2,1)} %send_ref.3, bf16[2,1024,2,512]{3,2,1,0:T(2,128)(2,1)} %send_ref.3), custom_call_target="tpu_custom_call" | custom-call | flops 1 | bytes 1 | tf_op jit(solution)/shard_map/split_cache/pallas_call | solution.py:79
  16.7 14.8 %project.1 = (bf16[4,1024,128]{2,1,0:T(8,128)(2,1)S(1)}, bf16[3072,128]{1,0:T(8,128)(2,1)S(1)}, bf16[4,8,128,128]{3,2,1,0:T(8,128)(2,1)S(1)}, bf16[4,8,128,128]{3,2,1,0:T(8,128)(2,1)S(1)}, bf16[1024,128]{1,0:T(8,128)(2,1)S(1)}) custom-call(s32[1]{0:T(128)} %bitcast.core_ref, bf16[1024,2048]{1,0:T(8,128)(2,1)} %rest_8_.1, f32[1,2048]{1,0:T(1,128)S(1)} %bitcast.19, ...), custom_call_target="tpu_custom_call" | custom-call | flops 1 | bytes 1 | tf_op jit(solution)/shard_map/project/pallas_call | solution.py:144
  36.3 3.8 %collective-permute-done.2 = bf16[1024,128]{1,0:T(8,128)(2,1)S(1)} collective-permute-done((bf16[1024,128]{1,0:T(8,128)(2,1)S(1)}, bf16[1024,128]{1,0:T(8,128)(2,1)S(1)}, u32[]{:S(2)}, u32[]{:S(2)}) %collective-permute-start.2) | collective-permute-done | bytes 262176 | tf_op jit(solution)/shard_map/ppermute | solution.py:53
  41.1 3.1 %collective-permute-start.8 = (bf16[16,2,128,128]{3,2,1,0:T(8,128)(2,1)S(1)}, bf16[16,2,128,128]{3,2,1,0:T(8,128)(2,1)S(1)}, u32[]{:S(2)}, u32[]{:S(2)}) collective-permute-start(bf16[16,2,128,128]{3,2,1,0:T(8,128)(2,1)S(1)} %collective-permute-done.5.rest_3_), channel_id=1, source_target_pairs={{0,96},{4,28},{8,104},{12,4},{16,112},{20,12},{24,120},{28,20},{32... | collective-permute-start | bytes 3145736 | tf_op jit(solution)/shard_map/ppermute | solution.py:39
  47.1 8.7 %split_cache.3 = (bf16[16,2,128,128]{3,2,1,0:T(8,128)(2,1)S(1)}, bf16[16,2,128,128]{3,2,1,0:T(8,128)(2,1)S(1)}) custom-call(s32[1]{0:T(128)} %bitcast.core_ref, bf16[2,1024,2,512]{3,2,1,0:T(2,128)(2,1)} %send_ref.3, bf16[2,1024,2,512]{3,2,1,0:T(2,128)(2,1)} %send_ref.3), custom_call_target="tpu_custom_call" | custom-call | flops 1 | bytes 1 | tf_op jit(solution)/shard_map/split_cache/pallas_call | solution.py:79
  55.8 8.3 %collective-permute-done.8.rest_5_ = bf16[16,2,128,128]{3,2,1,0:T(8,128)(2,1)S(1)} collective-permute-done((bf16[16,2,128,128]{3,2,1,0:T(8,128)(2,1)S(1)}, bf16[16,2,128,128]{3,2,1,0:T(8,128)(2,1)S(1)}, u32[]{:S(2)}, u32[]{:S(2)}) %collective-permute-start.8) | collective-permute-done | bytes 1048608 | tf_op jit(solution)/shard_map/ppermute | solution.py:39
  65.1 16.9 %collective-permute-start.9 = (bf16[16,2,128,128]{3,2,1,0:T(8,128)(2,1)S(1)}, bf16[16,2,128,128]{3,2,1,0:T(8,128)(2,1)S(1)}, u32[]{:S(2)}, u32[]{:S(2)}) collective-permute-start(bf16[16,2,128,128]{3,2,1,0:T(8,128)(2,1)S(1)} %get-tuple-element.78), channel_id=1, source_target_pairs={{0,4},{4,0},{8,12},{12,8},{16,20},{20,16},{24,28},{28,24},{32,36},... | collective-permute-start | bytes 3145736 | tf_op jit(solution)/shard_map/ppermute | solution.py:48
  82.0 9.5 %near.1 = (f32[4,8,128,128]{3,2,1,0:T(8,128)}, f32[4,8,128]{2,1,0:T(8,128)S(1)}) custom-call(s32[1]{0:T(128)} %bitcast.core_ref, bf16[4,1024,128]{2,1,0:T(8,128)(2,1)S(1)} %get-tuple-element.68.q_ref, bf16[4,8,128,128]{3,2,1,0:T(8,128)(2,1)S(1)} %get-tuple-element.79.k_ref, bf16[4,8,128,128]{3,2,1,0:T(8,128)(2,1)S(1)} %get-tuple-element.80.v_ref, ...), custom_call_target="tpu_custom_call" | custom-call | flops 1 | bytes 1 | tf_op jit(solution)/shard_map/near/pallas_call | solution.py:200
  95.8 2.7 %collective-permute-start.16 = (bf16[16,2,128,128]{3,2,1,0:T(8,128)(2,1)}, bf16[16,2,128,128]{3,2,1,0:T(8,128)(2,1)}, u32[]{:S(2)}, u32[]{:S(2)}) collective-permute-start(bf16[16,2,128,128]{3,2,1,0:T(8,128)(2,1)} %copy-done.3), channel_id=1, source_target_pairs={{0,96},{4,28},{8,104},{12,4},{16,112},{20,12},{24,120},{28,20},{32... | collective-permute-start | bytes 3145736 | tf_op jit(solution)/shard_map/ppermute | solution.py:39
  99.0 2.6 %plan.1 = (s32[136]{0:T(256)S(1)}, s32[100]{0:T(128)S(1)}, s32[64]{0:T(128)S(1)}, s32[2]{0:T(128)S(1)}) custom-call(s32[64]{0:T(128)S(1)} %reduce_sum.12.cnt_ref, s32[512]{0:T(512)S(1)} %reshape.77.code_ref), custom_call_target="tpu_custom_call" | custom-call | flops 1 | bytes 1 | tf_op jit(solution)/shard_map/plan/pallas_call | solution.py:254
  102.8 11.1 %far.2 = (bf16[2096,128]{1,0:T(8,128)(2,1)S(1)}, bf16[2096,128]{1,0:T(8,128)(2,1)S(1)}, bf16[2096,128]{1,0:T(8,128)(2,1)S(1)}, bf16[2096,128]{1,0:T(8,128)(2,1)S(1)}) custom-call(s32[64]{0:T(128)S(1)} %reduce_sum.12.cnt_ref, s32[136]{0:T(256)S(1)} %get-tuple-element.87.list_ref, s32[100]{0:T(128)S(1)} %get-tuple-element.88.unit_ref, ...), custom_call_target="tpu_custom_call" | custom-call | flops 1 | bytes 1 | tf_op jit(solution)/shard_map/far/pallas_call | solution.py:380
  114.1 7.7 %collective-permute-start.18 = (bf16[2096,128]{1,0:T(8,128)(2,1)S(1)}, bf16[2096,128]{1,0:T(8,128)(2,1)S(1)}, u32[]{:S(2)}, u32[]{:S(2)}) collective-permute-start(bf16[2096,128]{1,0:T(8,128)(2,1)S(1)} %get-tuple-element.109), channel_id=1, source_target_pairs={{0,16},{4,68},{8,24},{12,76},{16,0},{20,84},{24,8},{28,92},{32,48}... | collective-permute-start | bytes 1609736 | tf_op jit(solution)/shard_map/ppermute | solution.py:44
  121.9 5.2 %collective-permute-start.22 = (bf16[16,2,128,128]{3,2,1,0:T(8,128)(2,1)}, bf16[16,2,128,128]{3,2,1,0:T(8,128)(2,1)S(1)}, u32[]{:S(2)}, u32[]{:S(2)}) collective-permute-start(bf16[16,2,128,128]{3,2,1,0:T(8,128)(2,1)} %collective-permute-done.16.rest_3_), channel_id=1, source_target_pairs={{0,96},{4,28},{8,104},{12,4},{16,112},{20,12},{24,120},{28,20},{32... | collective-permute-start | bytes 3145736 | tf_op jit(solution)/shard_map/ppermute | solution.py:39
  127.6 11.8 %collective-permute-done.18.c = bf16[2096,128]{1,0:T(8,128)(2,1)S(1)} collective-permute-done((bf16[2096,128]{1,0:T(8,128)(2,1)S(1)}, bf16[2096,128]{1,0:T(8,128)(2,1)S(1)}, u32[]{:S(2)}, u32[]{:S(2)}) %collective-permute-start.18) | collective-permute-done | bytes 536608 | tf_op jit(solution)/shard_map/ppermute | solution.py:44
  139.8 8.7 %collective-permute-start.20 = (f32[1032,128]{1,0:T(8,128)S(1)}, f32[1032,128]{1,0:T(8,128)S(1)}, u32[]{:S(2)}, u32[]{:S(2)}) collective-permute-start(f32[1032,128]{1,0:T(8,128)S(1)} %get-tuple-element.112), channel_id=1, source_target_pairs={{0,4},{4,0},{8,12},{12,8},{16,20},{20,16},{24,28},{28,24},{32,36},... | collective-permute-start | bytes 1585160 | tf_op jit(solution)/shard_map/ppermute | solution.py:48
  150.3 2.5 %collective-permute-start.23 = (bf16[2,1024,128]{2,1,0:T(8,128)(2,1)S(1)}, bf16[2,1024,128]{2,1,0:T(8,128)(2,1)S(1)}, u32[]{:S(2)}, u32[]{:S(2)}) collective-permute-start(bf16[2,1024,128]{2,1,0:T(8,128)(2,1)S(1)} %finish.2.a0), channel_id=1, source_target_pairs={{0,3},{1,0},{2,1},{3,2},{4,7},{5,4},{6,5},{7,6},{8,11},{9,8},{10,9... | collective-permute-start | bytes 1572872 | tf_op jit(solution)/shard_map/ppermute | solution.py:57
  154.9 11.9 %far.3 = (bf16[2096,128]{1,0:T(8,128)(2,1)S(1)}, bf16[2096,128]{1,0:T(8,128)(2,1)}, bf16[2096,128]{1,0:T(8,128)(2,1)}, bf16[2096,128]{1,0:T(8,128)(2,1)}) custom-call(s32[64]{0:T(128)S(1)} %reduce_sum.12.cnt_ref, s32[136]{0:T(256)S(1)} %get-tuple-element.87.list_ref, s32[100]{0:T(128)S(1)} %get-tuple-element.88.unit_ref, s32[64]{0:T(128)S(1)} %get-tuple-element.89.first_ref, ...), custom_call_target="tpu_custom_call" | custom-call | flops 1 | bytes 1 | tf_op jit(solution)/shard_map/far/pallas_call | solution.py:380
  167.1 3.9 %collective-permute-start.27 = (bf16[2096,128]{1,0:T(8,128)(2,1)}, bf16[2096,128]{1,0:T(8,128)(2,1)}, u32[]{:S(2)}, u32[]{:S(2)}) collective-permute-start(bf16[2096,128]{1,0:T(8,128)(2,1)} %get-tuple-element.122), channel_id=1, source_target_pairs={{0,16},{4,68},{8,24},{12,76},{16,0},{20,84},{24,8},{28,92},{32,48}... | collective-permute-start | bytes 1609736 | tf_op jit(solution)/shard_map/ppermute | solution.py:44
  173.0 7.7 %collective-permute-done.24.a2 = bf16[2,1024,128]{2,1,0:T(8,128)(2,1)} collective-permute-done((bf16[2,1024,128]{2,1,0:T(8,128)(2,1)S(1)}, bf16[2,1024,128]{2,1,0:T(8,128)(2,1)}, u32[]{:S(2)}, u32[]{:S(2)}) %collective-permute-start.24) | collective-permute-done | bytes 524320 | tf_op jit(solution)/shard_map/ppermute | solution.py:57
  180.8 16.3 %collective-permute-done.25.a3 = bf16[2,1024,128]{2,1,0:T(8,128)(2,1)} collective-permute-done((bf16[2,1024,128]{2,1,0:T(8,128)(2,1)S(1)}, bf16[2,1024,128]{2,1,0:T(8,128)(2,1)}, u32[]{:S(2)}, u32[]{:S(2)}) %collective-permute-start.25) | collective-permute-done | bytes 524320 | tf_op jit(solution)/shard_map/ppermute | solution.py:57
  198.1 4.7 %mix.2.rest_9_ = f32[1024,512]{1,0:T(8,128)S(1)} custom-call(s32[2]{0:T(128)S(1)} %pad_add_fusion.place_ref, bf16[2,1024,128]{2,1,0:T(8,128)(2,1)S(1)} %finish.2.a0, bf16[2,1024,128]{2,1,0:T(8,128)(2,1)S(1)} %copy-done.8, bf16[2,1024,128]{2,1,0:T(8,128)(2,1)} %collective-permute-done.24.a2, bf16[2,1024,128]{2,1,0:T(8,128)(2,1)} %collective-permute-done.25.a3, ...), custom_call_target="tpu_custom_call" | custom-call | flops 1 | bytes 1 | tf_op jit(solution)/shard_map/mix/pallas_call | solution.py:490
  209.2 11.7 %collective-permute-done.30.a1 = bf16[2,1024,128]{2,1,0:T(8,128)(2,1)S(1)} collective-permute-done((bf16[2,1024,128]{2,1,0:T(8,128)(2,1)S(1)}, bf16[2,1024,128]{2,1,0:T(8,128)(2,1)S(1)}, u32[]{:S(2)}, u32[]{:S(2)}) %collective-permute-start.30) | collective-permute-done | bytes 524320 | tf_op jit(solution)/shard_map/ppermute | solution.py:57
  222.4 12.2 %collective-permute-done.32.a3 = bf16[2,1024,128]{2,1,0:T(8,128)(2,1)S(1)} collective-permute-done((bf16[2,1024,128]{2,1,0:T(8,128)(2,1)S(1)}, bf16[2,1024,128]{2,1,0:T(8,128)(2,1)S(1)}, u32[]{:S(2)}, u32[]{:S(2)}) %collective-permute-start.32) | collective-permute-done | bytes 524320 | tf_op jit(solution)/shard_map/ppermute | solution.py:57
  234.6 5.4 %mix.3 = bf16[1024,512]{1,0:T(8,128)(2,1)} custom-call(s32[2]{0:T(128)S(1)} %pad_add_fusion.place_ref, bf16[2,1024,128]{2,1,0:T(8,128)(2,1)S(1)} %finish.3.a0, bf16[2,1024,128]{2,1,0:T(8,128)(2,1)S(1)} %collective-permute-done.30.a1, bf16[2,1024,128]{2,1,0:T(8,128)(2,1)S(1)} %collective-permute-done.31.a2, ...), custom_call_target="tpu_custom_call" | custom-call | flops 1 | bytes 1 | tf_op jit(solution)/shard_map/mix/pallas_call | solution.py:490
  (117 shorter events, 39.9 us)
Async XLA Ops:
  10.2 21.4 %collective-permute-start.6 = (bf16[16,2,128,128]{3,2,1,0:T(8,128)(2,1)S(1)}, bf16[16,2,128,128]{3,2,1,0:T(8,128)(2,1)S(1)}, u32[]{:S(2)}, u32[]{:S(2)}) collective-permute-start(bf16[16,2,128,128]{3,2,1,0:T(8,128)(2,1)S(1)} %get-tuple-element.71.rest_0_), channel_id=1, source_target_pairs={{0,32},{4,12},{8,40},{12,20},{16,48},{20,28},{24,56},{28,4},{32,64... | collective-permute-start | bytes 3145736 | tf_op jit(solution)/shard_map/ppermute | solution.py:39
  11.9 23.3 %collective-permute-start.3 = (bf16[16,2,128,128]{3,2,1,0:T(8,128)(2,1)S(1)}, bf16[16,2,128,128]{3,2,1,0:T(8,128)(2,1)S(1)}, u32[]{:S(2)}, u32[]{:S(2)}) collective-permute-start(bf16[16,2,128,128]{3,2,1,0:T(8,128)(2,1)S(1)} %get-tuple-element.71.rest_0_), channel_id=1, source_target_pairs={{0,96},{4,28},{8,104},{12,4},{16,112},{20,12},{24,120},{28,20},{32... | collective-permute-start | bytes 3145736 | tf_op jit(solution)/shard_map/ppermute | solution.py:39
  14.0 26.0 %collective-permute-start.4 = (bf16[16,2,128,128]{3,2,1,0:T(8,128)(2,1)S(1)}, bf16[16,2,128,128]{3,2,1,0:T(8,128)(2,1)S(1)}, u32[]{:S(2)}, u32[]{:S(2)}) collective-permute-start(bf16[16,2,128,128]{3,2,1,0:T(8,128)(2,1)S(1)} %collective-permute-done.rest_1_), channel_id=1, source_target_pairs={{0,32},{4,12},{8,40},{12,20},{16,48},{20,28},{24,56},{28,4},{32,64... | collective-permute-start | bytes 3145736 | tf_op jit(solution)/shard_map/ppermute | solution.py:39
  14.2 25.9 %collective-permute-start.5 = (bf16[16,2,128,128]{3,2,1,0:T(8,128)(2,1)S(1)}, bf16[16,2,128,128]{3,2,1,0:T(8,128)(2,1)S(1)}, u32[]{:S(2)}, u32[]{:S(2)}) collective-permute-start(bf16[16,2,128,128]{3,2,1,0:T(8,128)(2,1)S(1)} %collective-permute-done.rest_1_), channel_id=1, source_target_pairs={{0,96},{4,28},{8,104},{12,4},{16,112},{20,12},{24,120},{28,20},{32... | collective-permute-start | bytes 3145736 | tf_op jit(solution)/shard_map/ppermute | solution.py:39
  33.9 21.9 %collective-permute-start.7 = (bf16[16,2,128,128]{3,2,1,0:T(8,128)(2,1)S(1)}, bf16[16,2,128,128]{3,2,1,0:T(8,128)(2,1)}, u32[]{:S(2)}, u32[]{:S(2)}) collective-permute-start(bf16[16,2,128,128]{3,2,1,0:T(8,128)(2,1)S(1)} %collective-permute-done.6.rest_6_), channel_id=1, source_target_pairs={{0,32},{4,12},{8,40},{12,20},{16,48},{20,28},{24,56},{28,4},{32,64... | collective-permute-start | bytes 3145736 | tf_op jit(solution)/shard_map/ppermute | solution.py:39
  41.1 23.0 %collective-permute-start.8 = (bf16[16,2,128,128]{3,2,1,0:T(8,128)(2,1)S(1)}, bf16[16,2,128,128]{3,2,1,0:T(8,128)(2,1)S(1)}, u32[]{:S(2)}, u32[]{:S(2)}) collective-permute-start(bf16[16,2,128,128]{3,2,1,0:T(8,128)(2,1)S(1)} %collective-permute-done.5.rest_3_), channel_id=1, source_target_pairs={{0,96},{4,28},{8,104},{12,4},{16,112},{20,12},{24,120},{28,20},{32... | collective-permute-start | bytes 3145736 | tf_op jit(solution)/shard_map/ppermute | solution.py:39
  44.2 47.3 %collective-permute-start.10 = (bf16[2,2,8,128,128]{4,3,2,1,0:T(8,128)(2,1)S(1)}, bf16[2,2,8,128,128]{4,3,2,1,0:T(8,128)(2,1)S(1)}, u32[]{:S(2)}, u32[]{:S(2)}) collective-permute-start(bf16[2,2,8,128,128]{4,3,2,1,0:T(8,128)(2,1)S(1)} %bitcast.20), channel_id=1, source_target_pairs={{0,24},{4,100},{8,0},{12,108},{16,8},{20,116},{24,16},{28,124},{32... | collective-permute-start | bytes 3145736 | tf_op jit(solution)/shard_map/ppermute | solution.py:44
  46.3 45.1 %collective-permute-start.11 = (bf16[2,2,8,128,128]{4,3,2,1,0:T(8,128)(2,1)S(1)}, bf16[2,2,8,128,128]{4,3,2,1,0:T(8,128)(2,1)S(1)}, u32[]{:S(2)}, u32[]{:S(2)}) collective-permute-start(bf16[2,2,8,128,128]{4,3,2,1,0:T(8,128)(2,1)S(1)} %bitcast.21), channel_id=1, source_target_pairs={{0,16},{4,68},{8,24},{12,76},{16,0},{20,84},{24,8},{28,92},{32,48}... | collective-permute-start | bytes 3145736 | tf_op jit(solution)/shard_map/ppermute | solution.py:44
  46.7 44.8 %collective-permute-start.12 = (bf16[2,2,8,128,128]{4,3,2,1,0:T(8,128)(2,1)S(1)}, bf16[2,2,8,128,128]{4,3,2,1,0:T(8,128)(2,1)S(1)}, u32[]{:S(2)}, u32[]{:S(2)}) collective-permute-start(bf16[2,2,8,128,128]{4,3,2,1,0:T(8,128)(2,1)S(1)} %bitcast.22), channel_id=1, source_target_pairs={{0,8},{4,36},{8,16},{12,44},{16,24},{20,52},{24,0},{28,60},{32,40}... | collective-permute-start | bytes 3145736 | tf_op jit(solution)/shard_map/ppermute | solution.py:44
  65.1 26.4 %collective-permute-start.9 = (bf16[16,2,128,128]{3,2,1,0:T(8,128)(2,1)S(1)}, bf16[16,2,128,128]{3,2,1,0:T(8,128)(2,1)S(1)}, u32[]{:S(2)}, u32[]{:S(2)}) collective-permute-start(bf16[16,2,128,128]{3,2,1,0:T(8,128)(2,1)S(1)} %get-tuple-element.78), channel_id=1, source_target_pairs={{0,4},{4,0},{8,12},{12,8},{16,20},{20,16},{24,28},{28,24},{32,36},... | collective-permute-start | bytes 3145736 | tf_op jit(solution)/shard_map/ppermute | solution.py:48
  92.6 21.4 %collective-permute-start.13 = (bf16[16,2,128,128]{3,2,1,0:T(8,128)(2,1)S(1)}, bf16[16,2,128,128]{3,2,1,0:T(8,128)(2,1)}, u32[]{:S(2)}, u32[]{:S(2)}) collective-permute-start(bf16[16,2,128,128]{3,2,1,0:T(8,128)(2,1)S(1)} %get-tuple-element.113.rest_0_), channel_id=1, source_target_pairs={{0,32},{4,12},{8,40},{12,20},{16,48},{20,28},{24,56},{28,4},{32,64... | collective-permute-start | bytes 3145736 | tf_op jit(solution)/shard_map/ppermute | solution.py:39
  93.5 20.5 %collective-permute-start.14 = (bf16[16,2,128,128]{3,2,1,0:T(8,128)(2,1)S(1)}, bf16[16,2,128,128]{3,2,1,0:T(8,128)(2,1)}, u32[]{:S(2)}, u32[]{:S(2)}) collective-permute-start(bf16[16,2,128,128]{3,2,1,0:T(8,128)(2,1)S(1)} %get-tuple-element.113.rest_0_), channel_id=1, source_target_pairs={{0,96},{4,28},{8,104},{12,4},{16,112},{20,12},{24,120},{28,20},{32... | collective-permute-start | bytes 3145736 | tf_op jit(solution)/shard_map/ppermute | solution.py:39
  95.8 26.0 %collective-permute-start.15 = (bf16[16,2,128,128]{3,2,1,0:T(8,128)(2,1)}, bf16[16,2,128,128]{3,2,1,0:T(8,128)(2,1)}, u32[]{:S(2)}, u32[]{:S(2)}) collective-permute-start(bf16[16,2,128,128]{3,2,1,0:T(8,128)(2,1)} %copy-done.3), channel_id=1, source_target_pairs={{0,32},{4,12},{8,40},{12,20},{16,48},{20,28},{24,56},{28,4},{32,64... | collective-permute-start | bytes 3145736 | tf_op jit(solution)/shard_map/ppermute | solution.py:39
  95.8 25.9 %collective-permute-start.16 = (bf16[16,2,128,128]{3,2,1,0:T(8,128)(2,1)}, bf16[16,2,128,128]{3,2,1,0:T(8,128)(2,1)}, u32[]{:S(2)}, u32[]{:S(2)}) collective-permute-start(bf16[16,2,128,128]{3,2,1,0:T(8,128)(2,1)} %copy-done.3), channel_id=1, source_target_pairs={{0,96},{4,28},{8,104},{12,4},{16,112},{20,12},{24,120},{28,20},{32... | collective-permute-start | bytes 3145736 | tf_op jit(solution)/shard_map/ppermute | solution.py:39
  114.1 25.3 %collective-permute-start.18 = (bf16[2096,128]{1,0:T(8,128)(2,1)S(1)}, bf16[2096,128]{1,0:T(8,128)(2,1)S(1)}, u32[]{:S(2)}, u32[]{:S(2)}) collective-permute-start(bf16[2096,128]{1,0:T(8,128)(2,1)S(1)} %get-tuple-element.109), channel_id=1, source_target_pairs={{0,16},{4,68},{8,24},{12,76},{16,0},{20,84},{24,8},{28,92},{32,48}... | collective-permute-start | bytes 1609736 | tf_op jit(solution)/shard_map/ppermute | solution.py:44
  121.8 17.6 %collective-permute-start.19 = (bf16[2096,128]{1,0:T(8,128)(2,1)S(1)}, bf16[2096,128]{1,0:T(8,128)(2,1)S(1)}, u32[]{:S(2)}, u32[]{:S(2)}) collective-permute-start(bf16[2096,128]{1,0:T(8,128)(2,1)S(1)} %get-tuple-element.110), channel_id=1, source_target_pairs={{0,24},{4,100},{8,0},{12,108},{16,8},{20,116},{24,16},{28,124},{32... | collective-permute-start | bytes 1609736 | tf_op jit(solution)/shard_map/ppermute | solution.py:44
  121.8 31.1 %collective-permute-start.21 = (bf16[16,2,128,128]{3,2,1,0:T(8,128)(2,1)}, bf16[16,2,128,128]{3,2,1,0:T(8,128)(2,1)S(1)}, u32[]{:S(2)}, u32[]{:S(2)}) collective-permute-start(bf16[16,2,128,128]{3,2,1,0:T(8,128)(2,1)} %collective-permute-done.13.rest_6_), channel_id=1, source_target_pairs={{0,32},{4,12},{8,40},{12,20},{16,48},{20,28},{24,56},{28,4},{32,64... | collective-permute-start | bytes 3145736 | tf_op jit(solution)/shard_map/ppermute | solution.py:39
  121.9 31.0 %collective-permute-start.22 = (bf16[16,2,128,128]{3,2,1,0:T(8,128)(2,1)}, bf16[16,2,128,128]{3,2,1,0:T(8,128)(2,1)S(1)}, u32[]{:S(2)}, u32[]{:S(2)}) collective-permute-start(bf16[16,2,128,128]{3,2,1,0:T(8,128)(2,1)} %collective-permute-done.16.rest_3_), channel_id=1, source_target_pairs={{0,96},{4,28},{8,104},{12,4},{16,112},{20,12},{24,120},{28,20},{32... | collective-permute-start | bytes 3145736 | tf_op jit(solution)/shard_map/ppermute | solution.py:39
  150.3 21.2 %collective-permute-start.23 = (bf16[2,1024,128]{2,1,0:T(8,128)(2,1)S(1)}, bf16[2,1024,128]{2,1,0:T(8,128)(2,1)S(1)}, u32[]{:S(2)}, u32[]{:S(2)}) collective-permute-start(bf16[2,1024,128]{2,1,0:T(8,128)(2,1)S(1)} %finish.2.a0), channel_id=1, source_target_pairs={{0,3},{1,0},{2,1},{3,2},{4,7},{5,4},{6,5},{7,6},{8,11},{9,8},{10,9... | collective-permute-start | bytes 1572872 | tf_op jit(solution)/shard_map/ppermute | solution.py:57
  166.8 36.0 %collective-permute-start.26 = (bf16[2096,128]{1,0:T(8,128)(2,1)}, bf16[2096,128]{1,0:T(8,128)(2,1)}, u32[]{:S(2)}, u32[]{:S(2)}) collective-permute-start(bf16[2096,128]{1,0:T(8,128)(2,1)} %get-tuple-element.121), channel_id=1, source_target_pairs={{0,8},{4,36},{8,16},{12,44},{16,24},{20,52},{24,0},{28,60},{32,40}... | collective-permute-start | bytes 1609736 | tf_op jit(solution)/shard_map/ppermute | solution.py:44
  167.1 35.7 %collective-permute-start.27 = (bf16[2096,128]{1,0:T(8,128)(2,1)}, bf16[2096,128]{1,0:T(8,128)(2,1)}, u32[]{:S(2)}, u32[]{:S(2)}) collective-permute-start(bf16[2096,128]{1,0:T(8,128)(2,1)} %get-tuple-element.122), channel_id=1, source_target_pairs={{0,16},{4,68},{8,24},{12,76},{16,0},{20,84},{24,8},{28,92},{32,48}... | collective-permute-start | bytes 1609736 | tf_op jit(solution)/shard_map/ppermute | solution.py:44
  171.0 31.8 %collective-permute-start.28 = (bf16[2096,128]{1,0:T(8,128)(2,1)}, bf16[2096,128]{1,0:T(8,128)(2,1)}, u32[]{:S(2)}, u32[]{:S(2)}) collective-permute-start(bf16[2096,128]{1,0:T(8,128)(2,1)} %get-tuple-element.123), channel_id=1, source_target_pairs={{0,24},{4,100},{8,0},{12,108},{16,8},{20,116},{24,16},{28,124},{32... | collective-permute-start | bytes 1609736 | tf_op jit(solution)/shard_map/ppermute | solution.py:44
  172.4 24.7 %collective-permute-start.25 = (bf16[2,1024,128]{2,1,0:T(8,128)(2,1)S(1)}, bf16[2,1024,128]{2,1,0:T(8,128)(2,1)}, u32[]{:S(2)}, u32[]{:S(2)}) collective-permute-start(bf16[2,1024,128]{2,1,0:T(8,128)(2,1)S(1)} %finish.2.a0), channel_id=1, source_target_pairs={{0,1},{1,2},{2,3},{3,0},{4,5},{5,6},{6,7},{7,4},{8,9},{9,10},{10,1... | collective-permute-start | bytes 1572872 | tf_op jit(solution)/shard_map/ppermute | solution.py:57
  208.6 26.0 %collective-permute-start.32 = (bf16[2,1024,128]{2,1,0:T(8,128)(2,1)S(1)}, bf16[2,1024,128]{2,1,0:T(8,128)(2,1)S(1)}, u32[]{:S(2)}, u32[]{:S(2)}) collective-permute-start(bf16[2,1024,128]{2,1,0:T(8,128)(2,1)S(1)} %finish.3.a0), channel_id=1, source_target_pairs={{0,1},{1,2},{2,3},{3,0},{4,5},{5,6},{6,7},{7,4},{8,9},{9,10},{10,1... | collective-permute-start | bytes 1572872 | tf_op jit(solution)/shard_map/ppermute | solution.py:57
  (32 other events, 309.2 us)

commit v2 on v1

--- a/solution.py
+++ b/solution.py
@@ -217,14 +217,14 @@
 UNITS = 96 + GROUP
 
 
-def plan_kernel(cnt_ref, code_ref, list_ref, unit_ref, first_ref, size_ref):
+def plan_kernel(cnt_ref, code_ref, list_ref, unit_ref, first_ref, long_ref, size_ref):
     def scan(i, carry):
-        e, u = carry
+        e, u, m = carry
         n = cnt_ref[i]
         first_ref[i] = u
 
         def named(carry):
-            e, u = carry
+            e, u, m = carry
             at = e
             for w in range(WMAX):
                 code = code_ref[i * WMAX + w]
@@ -236,15 +236,17 @@
                 unit_ref[u] = i * 512 + (e + 2 * k) * 2 + both
                 return u + 1
 
-            return at, lax.fori_loop(0, lax.shift_right_logical(n + 1, 1), unit, u)
-
-        return lax.cond(n > 0, named, lambda carry: carry, (e, u))
-
-    entries, units = lax.fori_loop(0, 64, scan, (jnp.int32(0), jnp.int32(0)))
+            long_ref[m] = i
+            return at, lax.fori_loop(0, lax.shift_right_logical(n + 1, 1), unit, u), m + (n > 2).astype(jnp.int32)
+
+        return lax.cond(n > 0, named, lambda carry: carry, (e, u, m))
+
+    entries, units, longs = lax.fori_loop(0, 64, scan, (jnp.int32(0), jnp.int32(0), jnp.int32(0)))
     for g in range(GROUP):
         unit_ref[units + g] = -1
     size_ref[0] = entries
     size_ref[1] = units
+    size_ref[2] = longs
 
 
 def plan(cnt, code):
@@ -254,17 +256,17 @@
     return pl.pallas_call(
         plan_kernel,
         in_specs=[SMEM] * 2,
-        out_specs=[SMEM] * 4,
-        out_shape=[out(128 + WMAX), out(UNITS), out(64), out(2)],
+        out_specs=[SMEM] * 5,
+        out_shape=[out(128 + WMAX), out(UNITS), out(64), out(64), out(3)],
         compiler_params=params(16),
         cost_estimate=BRIEF,
         name="plan",
     )(cnt, code)
 
 
-def far_kernel(j, cnt_ref, list_ref, unit_ref, first_ref, size_ref, *rest):
+def far_kernel(j, cnt_ref, list_ref, unit_ref, first_ref, long_ref, size_ref, *rest):
     sources, qs, outs = rest[:8], rest[8:12], rest[12:16]
-    kvbuf, qbuf, acc_ref, stat_ref, kvsem, qsem, logs = rest[16:]
+    kvbuf, qbuf, obuf, acc_ref, stat_ref, logs, kvsem, qsem, osem = rest[16:]
     entries, units = size_ref[0], size_ref[1]
     for r in range(4):
         pltpu.make_async_copy(qs[r].at[:, j], qbuf.at[pl.ds(2 * r, 2)], qsem.at[r]).start()
@@ -292,104 +294,93 @@
         return 0
 
     lax.fori_loop(0, entries, fetch, 0)
+    logs[...] = jnp.full((64, BLOCK), NEG, F32)
     for r in range(4):
         pltpu.make_async_copy(qs[r].at[:, j], qbuf.at[pl.ds(2 * r, 2)], qsem.at[r]).wait()
 
-    def landed(e):
+    def landed(e, _):
         pltpu.make_async_copy(sources[0].at[0], kvbuf.at[e], kvsem.at[e]).wait()
+        return 0
+
+    lax.fori_loop(0, entries, landed, 0)
+
+    def store(i, m, total, acc):
+        rows = pl.ds(pl.multiple_of(lax.bitwise_and(i, 15) * HD, HD), HD)
+        obuf[lax.shift_right_logical(i, 4), rows, :] = (acc * (1.0 / total)).astype(BF16)
+        logs[pl.ds(i, 1), :] = m + jnp.log(total)
 
     def group(g, _):
-        live = []
+        done = []
         for t in range(GROUP):
             u = g * GROUP + t
             unit = unit_ref[u]
-            here = unit >= 0
-            unit = jnp.where(here, unit, unit_ref[g * GROUP])
+            unit = jnp.where(unit >= 0, unit, unit_ref[g * GROUP])
             both = lax.bitwise_and(unit, 1)
             ea = lax.bitwise_and(lax.shift_right_logical(unit, 1), 255)
+            eb = ea + both
             i = lax.shift_right_logical(unit, 9)
-
-            @pl.when(here)
-            def _():
-                landed(ea)
-
-            @pl.when(jnp.logical_and(here, both == 1))
-            def _():
-                landed(ea + 1)
-
-            live.append((u, i, ea, ea + both, both == 1))
-        for u, i, ea, eb, both in live:
             q = qbuf[lax.shift_right_logical(i, 3), lax.bitwise_and(i, 7)]
             sa = nt(kvbuf[ea, 0], q) * SCALE
-            sb = jnp.where(both, nt(kvbuf[eb, 0], q) * SCALE, NEG)
+            sb = jnp.where(both == 1, nt(kvbuf[eb, 0], q) * SCALE, NEG)
             m = jnp.max(jnp.maximum(sa, sb), axis=0, keepdims=True)
             pa, pb = jnp.exp(sa - m), jnp.exp(sb - m)
+            total = jnp.sum(pa + pb, axis=0, keepdims=True)
+            acc = nn(kvbuf[ea, 1], pa.astype(BF16)) + nn(kvbuf[eb, 1], pb.astype(BF16))
+            done.append((u, i, m, total, acc))
+        for u, i, m, total, acc in done:
             stat_ref[u, 0:1, :] = m
-            stat_ref[u, 1:2, :] = jnp.sum(pa + pb, axis=0, keepdims=True)
-            acc_ref[u] = nn(kvbuf[ea, 1], pa.astype(BF16)) + nn(kvbuf[eb, 1], pb.astype(BF16))
+            stat_ref[u, 1:2, :] = total
+            acc_ref[u] = acc
+            store(i, m, total, acc)
         return 0
 
     lax.fori_loop(0, lax.div(units + GROUP - 1, GROUP), group, 0)
 
+    def join(k, _):
+        i = long_ref[k]
+        n = cnt_ref[i]
+        u = first_ref[i]
+
+        def more(k, carry):
+            m, total, acc = carry
+            mk, tk = stat_ref[k, 0:1, :], stat_ref[k, 1:2, :]
+            top = jnp.maximum(m, mk)
+            old, new = jnp.exp(m - top), jnp.exp(mk - top)
+            return top, total * old + tk * new, acc * old + acc_ref[k] * new
+
+        start = (stat_ref[u, 0:1, :], stat_ref[u, 1:2, :], acc_ref[u])
+        store(i, *lax.fori_loop(u + 1, u + lax.shift_right_logical(n + 1, 1), more, start))
+        return 0
+
+    lax.fori_loop(0, size_ref[2], join, 0)
     for r in range(4):
-        out = outs[r]
-
-        def block(i, _):
-            n = cnt_ref[r * 16 + i]
-            u = first_ref[r * 16 + i]
-            rows = pl.ds(pl.multiple_of(i * HD, HD), HD)
-
-            def store(value, log):
-                out[rows, :] = value
-                logs[pl.ds(i, 1), :] = log
-
-            @pl.when(n == 0)
-            def _():
-                store(jnp.zeros((HD, BLOCK), BF16), jnp.full((1, BLOCK), NEG, F32))
-
-            @pl.when(jnp.logical_and(n > 0, n <= 2))
-            def _():
-                m, total = stat_ref[u, 0:1, :], stat_ref[u, 1:2, :]
-                store((acc_ref[u] * (1.0 / total)).astype(BF16), m + jnp.log(total))
-
-            @pl.when(n > 2)
-            def _():
-                def more(k, carry):
-                    m, total, acc = carry
-                    mk, tk = stat_ref[k, 0:1, :], stat_ref[k, 1:2, :]
-                    top = jnp.maximum(m, mk)
-                    old, new = jnp.exp(m - top), jnp.exp(mk - top)
-                    return top, total * old + tk * new, acc * old + acc_ref[k] * new
-
-                start = (stat_ref[u, 0:1, :], stat_ref[u, 1:2, :], acc_ref[u])
-                m, total, acc = lax.fori_loop(u + 1, u + lax.shift_right_logical(n + 1, 1), more, start)
-                store((acc * (1.0 / total)).astype(BF16), m + jnp.log(total))
-
-            return 0
-
-        lax.fori_loop(0, 16, block, 0)
-        part = logs[...]
+        part = logs[r * 16 : (r + 1) * 16, :]
         for t in range(3):
             term = part.astype(BF16)
-            out[2048 + t * 16 : 2064 + t * 16, :] = term
+            obuf[r, 2048 + t * 16 : 2064 + t * 16, :] = term
             part = part - term.astype(F32)
+        pltpu.make_async_copy(obuf.at[r], outs[r], osem.at[r]).start()
+    for r in range(4):
+        pltpu.make_async_copy(obuf.at[r], outs[r], osem.at[r]).wait()
 
 
 def far(j, cnt, lists, sources, qs):
     out = jax.ShapeDtypeStruct((OROWS, BLOCK), BF16)
     return pl.pallas_call(
         functools.partial(far_kernel, j),
-        in_specs=[SMEM] * 5 + [ANY] * 12,
-        out_specs=[pl.BlockSpec((OROWS, BLOCK), lambda: (0, 0))] * 4,
+        in_specs=[SMEM] * 6 + [ANY] * 12,
+        out_specs=[ANY] * 4,
         out_shape=[out] * 4,
         scratch_shapes=[
             pltpu.VMEM((128, 2, BLOCK, HD), BF16),
             pltpu.VMEM((8, 8, BLOCK, HD), BF16),
+            pltpu.VMEM((4, OROWS, BLOCK), BF16),
             pltpu.VMEM((UNITS, HD, BLOCK), F32),
             pltpu.VMEM((UNITS, 8, BLOCK), F32),
+            pltpu.VMEM((64, BLOCK), F32),
             pltpu.SemaphoreType.DMA((128,)),
             pltpu.SemaphoreType.DMA((4,)),
-            pltpu.VMEM((16, BLOCK), F32),
+            pltpu.SemaphoreType.DMA((4,)),
         ],
         compiler_params=params(),
         cost_estimate=BRIEF,
@@ -401,16 +392,19 @@
     parts = (a, b, c, d)
     logs = [sum(p[2048 + t * 16 : 2064 + t * 16, :].astype(F32) for t in range(3)) for p in parts]
     peak = functools.reduce(jnp.maximum, logs)
-    shares = [jnp.exp(x - peak) for x in logs]
+    shares = [jnp.where(x > 0.5 * NEG, jnp.exp(x - peak), 0.0) for x in logs]
     total = sum(shares)
+    joint = jnp.where(total > 0.0, peak + jnp.log(total), NEG)
+    total = jnp.where(total > 0.0, total, 1.0)
+    live = [x > 0.5 * NEG for x in logs]
     shares = [x / total for x in shares]
-    joint = peak + jnp.log(total)
     for s, out in enumerate((keep, send)):
         for i in range(8):
             row = s * 8 + i
             rows = slice(row * HD, (row + 1) * HD)
             out[i * HD : (i + 1) * HD, :] = sum(
-                x[row : row + 1, :] * p[rows, :].astype(F32) for x, p in zip(shares, parts)
+                jnp.where(on[row : row + 1, :], x[row : row + 1, :] * p[rows, :].astype(F32), 0.0)
+                for on, x, p in zip(live, shares, parts)
             )
         out[1024:1032, :] = joint[s * 8 : (s + 1) * 8, :]
 
@@ -542,17 +536,17 @@
     mine = jnp.concatenate([q_all[:2], swapped[:2048].reshape(2, 1024, HD)], axis=0).reshape(2, 2, 8, BLOCK, HD)
     mine, halo, down_k0, up_r0, down_r0 = lax.optimization_barrier((mine, halo, down_k0, up_r0, down_r0))
     down20 = rows_perm(down_r0, -1)
-    qs = [mine, query_perm(mine, -1), query_perm(mine, 2), query_perm(mine, 1)]
-
-    core1 = after(core, mine)
-    keep1, send1 = split_cache(1, core1, kv_cache)
+    q1, q3, q2 = query_perm(mine, -1), query_perm(mine, 1), query_perm(mine, 2)
+
+    keep1, send1 = split_cache(1, after(core, mine), kv_cache)
+    near_o, near_lse = near(core, q_all, k_all, v_all, after(halo, keep1), swapped)
     code, cnt = line_codes(wake_blocks, wake_frames, wake_counts, y, z, c)
     lists = plan(cnt, code)
-    send1, up20, down20 = lax.optimization_barrier((send1, up20, down20))
+    keep1, near_o, near_lse, q1, q3, *lists = lax.optimization_barrier((keep1, near_o, near_lse, q1, q3, *lists))
+    up_k1, down_k1 = rows_perm(keep1, 1), rows_perm(keep1, -1)
+    send1, up20, down20, q2 = lax.optimization_barrier((send1, up20, down20, q2, near_o))[:4]
     got1 = core_swap(send1)
-    near_o, near_lse = near(core, q_all, k_all, v_all, after(halo, keep1), swapped)
-    keep1, got1, near_o, near_lse, *qs = lax.optimization_barrier((keep1, got1, near_o, near_lse, *qs))
-    up_k1, down_k1 = rows_perm(keep1, 1), rows_perm(keep1, -1)
+    qs = [after(mine, got1), q1, q2, q3]
     up_r1, down_r1 = rows_perm(got1, 1), rows_perm(got1, -1)
 
     def returned(parts):
@@ -566,14 +560,15 @@
     *parts, up_k1, down_k1 = lax.optimization_barrier((*parts, up_k1, down_k1))
     back = returned(parts)
     up21 = rows_perm(up_k1, 1)
-    back[0], down_k1, up_r1, down_r1 = lax.optimization_barrier((back[0], down_k1, up_r1, down_r1))
     down21 = rows_perm(down_r1, -1)
+    back[0], up_r1, up21, down21 = lax.optimization_barrier((back[0], up_r1, up21, down21))
     own, other = merge(back)
     heads = finish(0, near_o, near_lse, own, core_swap(other))
     gathered = gather(heads)
 
     sources = [after(keep1, heads), got1, down_k1, down_r1, up21, down21, up_k1, up_r1]
     parts = far(1, cnt, lists, sources, qs)
+    *parts, gathered[1], gathered[3] = lax.optimization_barrier((*parts, gathered[1], gathered[3]))
     back = returned(parts)
     gathered[0] = after(gathered[0], parts[0])
     acc = mix(0, place, gathered, w_out, tokens, None)

time: 245 us -> 243 us (level); the launches traced: 240 us -> 241 us
  starting transfers between devices: 70.6 us -> 46.4 us
  waiting for transfers between devices: 77.7 us -> 94 us
  Pallas kernels: 80.1 us -> 93 us
  local copies, waits for them, and re-layouts: 10.7 us -> 5.4 us
    ppermute x5, starting transfers between devices: 28.4 us -> 3.74 us  [core_swap(): lax.ppermute(x, 'tok', [(tok_of(y, z, c), tok_of(y, z, 1 - c)) for y, z,...]
    ppermute x12, waiting for transfers between devices: 8.35 us -> 30.8 us  [rows_perm(): return lax.ppermute(x, 'tok', pairs)]
    ppermute x6, waiting for transfers between devices: 49.4 us -> 36.3 us  [mp_perm(): return lax.ppermute(x, 'mp', [(i, (i + d) % NX) for i in range(NX)])]
    pallas_call x3, Pallas kernels: 25.6 us -> 37.7 us  [the longest x2 34.7 us: far(): pl.pallas_call(functools.partial(far_kernel, j), in_specs=[SMEM] * 6 + [A...]
    ppermute x1, waiting for transfers between devices: 3.79 us -> 11.5 us  [halo_perm(): lax.ppermute(x, 'tok', [(i, (i + (1 if i % 2 else -1)) % n) for i in rang...]
    unnamed x46 -> x44, local copies, waits for them, and re-layouts: 10.1 us -> 4.73 us
    ppermute x6, starting transfers between devices: 5.23 us -> 7.98 us  [mp_perm(): return lax.ppermute(x, 'mp', [(i, (i + d) % NX) for i in range(NX)])]
    ppermute x9, waiting for transfers between devices: 12.3 us -> 9.64 us  [query_perm(): return lax.ppermute(x, 'tok', pairs)]
  transfers between devices with their start and end apart: 33 -> 33, of which waited for: 12 -> 15; matrix products, arithmetic and copies ran while one was open for 0% -> 1% of each run, Pallas kernels for 27% -> 25%
where the time goes in v2:
time: 243 us; the launch traced here: 241 us
  waiting for transfers between devices  94 us (39%)
  Pallas kernels  93 us (38%)
  starting transfers between devices  46.4 us (19%)
  local copies, waits for them, and re-layouts  5.4 us (2%)
    ppermute x6, waiting for transfers between devices, mp_perm(): return lax.ppermute(x, 'mp', [(i, (i + d) % NX) for i in range(NX)])  36.3 us
    pallas_call x2, Pallas kernels, far(): pl.pallas_call(functools.partial(far_kernel, j), in_specs=[SMEM] * 6 + [A...  34.7 us
    ppermute x12, waiting for transfers between devices, rows_perm(): return lax.ppermute(x, 'tok', pairs)  30.8 us
    ppermute x12, starting transfers between devices, rows_perm(): return lax.ppermute(x, 'tok', pairs)  18.7 us
    pallas_call x2, Pallas kernels, split_cache(): pl.pallas_call(split_cache_kernel, grid_spec=pltpu.PrefetchScalarGridSpec...  17.5 us
    pallas_call x1, Pallas kernels, project(): pl.pallas_call(project_kernel, grid_spec=pltpu.PrefetchScalarGridSpec(num...  15.2 us
    ppermute x9, starting transfers between devices, query_perm(): return lax.ppermute(x, 'tok', pairs)  14.1 us
    ppermute x1, waiting for transfers between devices, halo_perm(): lax.ppermute(x, 'tok', [(i, (i + (1 if i % 2 else -1)) % n) for i in rang...  11.5 us
  transfers between devices with their start and end apart: 33, of which 15 were waited for; matrix products, arithmetic and copies ran while one was open for 1% of the time, Pallas kernels for 25%

profile of v2, /device:TPU:1, one launch (start us, length us, event | category | flops | bytes accessed | tf_op | source)
XLA Modules:
  0.0 240.6 jit_solution(9690135976274910581)
XLA Ops:
  0.0 8.7 %split_cache.2 = (bf16[16,2,128,128]{3,2,1,0:T(8,128)(2,1)S(1)}, bf16[16,2,128,128]{3,2,1,0:T(8,128)(2,1)S(1)}) custom-call(s32[1]{0:T(128)} %bitcast.core_ref, bf16[2,1024,2,512]{3,2,1,0:T(2,128)(2,1)} %send_ref.3, bf16[2,1024,2,512]{3,2,1,0:T(2,128)(2,1)} %send_ref.3), custom_call_target="tpu_custom_call" | custom-call | flops 1 | bytes 1 | tf_op jit(solution)/shard_map/split_cache/pallas_call | solution.py:79
  12.5 15.2 %project.1 = (bf16[4,1024,128]{2,1,0:T(8,128)(2,1)S(1)}, bf16[3072,128]{1,0:T(8,128)(2,1)S(1)}, bf16[4,8,128,128]{3,2,1,0:T(8,128)(2,1)S(1)}, bf16[4,8,128,128]{3,2,1,0:T(8,128)(2,1)S(1)}, bf16[1024,128]{1,0:T(8,128)(2,1)S(1)}) custom-call(s32[1]{0:T(128)} %bitcast.core_ref, bf16[1024,2048]{1,0:T(8,128)(2,1)} %rest_8_.1, f32[1,2048]{1,0:T(1,128)S(1)} %bitcast.19, ...), custom_call_target="tpu_custom_call" | custom-call | flops 1 | bytes 1 | tf_op jit(solution)/shard_map/project/pallas_call | solution.py:144
  27.9 3.8 %collective-permute-start.3 = (bf16[16,2,128,128]{3,2,1,0:T(8,128)(2,1)S(1)}, bf16[16,2,128,128]{3,2,1,0:T(8,128)(2,1)S(1)}, u32[]{:S(2)}, u32[]{:S(2)}) collective-permute-start(bf16[16,2,128,128]{3,2,1,0:T(8,128)(2,1)S(1)} %get-tuple-element.82.rest_0_), channel_id=1, source_target_pairs={{0,96},{4,28},{8,104},{12,4},{16,112},{20,12},{24,120},{28,20},{32... | collective-permute-start | bytes 3145736 | tf_op jit(solution)/shard_map/ppermute | solution.py:39
  37.4 7.6 %collective-permute-done.3.rest_2_ = bf16[16,2,128,128]{3,2,1,0:T(8,128)(2,1)S(1)} collective-permute-done((bf16[16,2,128,128]{3,2,1,0:T(8,128)(2,1)S(1)}, bf16[16,2,128,128]{3,2,1,0:T(8,128)(2,1)S(1)}, u32[]{:S(2)}, u32[]{:S(2)}) %collective-permute-start.3) | collective-permute-done | bytes 1048608 | tf_op jit(solution)/shard_map/ppermute | solution.py:39
  46.0 11.5 %collective-permute-done.2 = bf16[1024,128]{1,0:T(8,128)(2,1)S(1)} collective-permute-done((bf16[1024,128]{1,0:T(8,128)(2,1)S(1)}, bf16[1024,128]{1,0:T(8,128)(2,1)S(1)}, u32[]{:S(2)}, u32[]{:S(2)}) %collective-permute-start.2) | collective-permute-done | bytes 262176 | tf_op jit(solution)/shard_map/ppermute | solution.py:53
  60.7 2.9 %collective-permute-start.10 = (bf16[16,2,128,128]{3,2,1,0:T(8,128)(2,1)}, bf16[16,2,128,128]{3,2,1,0:T(8,128)(2,1)}, u32[]{:S(2)}, u32[]{:S(2)}) collective-permute-start(bf16[16,2,128,128]{3,2,1,0:T(8,128)(2,1)} %collective-permute-done.5.rest_3_), channel_id=1, source_target_pairs={{0,96},{4,28},{8,104},{12,4},{16,112},{20,12},{24,120},{28,20},{32... | collective-permute-start | bytes 3145736 | tf_op jit(solution)/shard_map/ppermute | solution.py:39
  67.3 2.9 %plan.1 = (s32[136]{0:T(256)S(1)}, s32[100]{0:T(128)S(1)}, s32[64]{0:T(128)S(1)}, s32[64]{0:T(128)S(1)}, s32[3]{0:T(128)S(1)}) custom-call(s32[64]{0:T(128)S(1)} %reduce_sum.12.cnt_ref, s32[512]{0:T(512)S(1)} %reshape.77.code_ref), custom_call_target="tpu_custom_call" | custom-call | flops 1 | bytes 1 | tf_op jit(solution)/shard_map/plan/pallas_call | solution.py:256
  70.3 8.8 %split_cache.3 = (bf16[16,2,128,128]{3,2,1,0:T(8,128)(2,1)S(1)}, bf16[16,2,128,128]{3,2,1,0:T(8,128)(2,1)S(1)}) custom-call(s32[1]{0:T(128)} %bitcast.core_ref, bf16[2,1024,2,512]{3,2,1,0:T(2,128)(2,1)} %send_ref.3, bf16[2,1024,2,512]{3,2,1,0:T(2,128)(2,1)} %send_ref.3), custom_call_target="tpu_custom_call" | custom-call | flops 1 | bytes 1 | tf_op jit(solution)/shard_map/split_cache/pallas_call | solution.py:79
  79.1 9.6 %near.1 = (f32[4,8,128,128]{3,2,1,0:T(8,128)}, f32[4,8,128]{2,1,0:T(8,128)S(1)}) custom-call(s32[1]{0:T(128)} %bitcast.core_ref, bf16[4,1024,128]{2,1,0:T(8,128)(2,1)S(1)} %get-tuple-element.79.q_ref, bf16[4,8,128,128]{3,2,1,0:T(8,128)(2,1)S(1)} %get-tuple-element.86.k_ref, bf16[4,8,128,128]{3,2,1,0:T(8,128)(2,1)S(1)} %copy-done.2, ...), custom_call_target="tpu_custom_call" | custom-call | flops 1 | bytes 1 | tf_op jit(solution)/shard_map/near/pallas_call | solution.py:200
  88.7 8.8 %collective-permute-done.7.rest_11_ = bf16[2,2,8,128,128]{4,3,2,1,0:T(8,128)(2,1)} collective-permute-done((bf16[2,2,8,128,128]{4,3,2,1,0:T(8,128)(2,1)}, bf16[2,2,8,128,128]{4,3,2,1,0:T(8,128)(2,1)}, u32[]{:S(2)}, u32[]{:S(2)}) %collective-permute-start.7) | collective-permute-done | bytes 1048608 | tf_op jit(solution)/shard_map/ppermute | solution.py:44
  104.1 16.9 %far.2 = (bf16[2096,128]{1,0:T(8,128)(2,1)S(1)}, bf16[2096,128]{1,0:T(8,128)(2,1)S(1)}, bf16[2096,128]{1,0:T(8,128)(2,1)S(1)}, bf16[2096,128]{1,0:T(8,128)(2,1)S(1)}) custom-call(s32[64]{0:T(128)S(1)} %reduce_sum.12.cnt_ref, s32[136]{0:T(256)S(1)} %get-tuple-element.99.list_ref, s32[100]{0:T(128)S(1)} %get-tuple-element.100.unit_ref, ...), custom_call_target="tpu_custom_call" | custom-call | flops 1 | bytes 1 | tf_op jit(solution)/shard_map/far/pallas_call | solution.py:369
  122.0 2.9 %collective-permute-done.17.rest_3_ = bf16[16,2,128,128]{3,2,1,0:T(8,128)(2,1)S(1)} collective-permute-done((bf16[16,2,128,128]{3,2,1,0:T(8,128)(2,1)S(1)}, bf16[16,2,128,128]{3,2,1,0:T(8,128)(2,1)S(1)}, u32[]{:S(2)}, u32[]{:S(2)}) %collective-permute-start.17) | collective-permute-done | bytes 1048608 | tf_op jit(solution)/shard_map/ppermute | solution.py:39
  125.0 3.5 %collective-permute-start.18 = (bf16[16,2,128,128]{3,2,1,0:T(8,128)(2,1)S(1)}, bf16[16,2,128,128]{3,2,1,0:T(8,128)(2,1)S(1)}, u32[]{:S(2)}, u32[]{:S(2)}) collective-permute-start(bf16[16,2,128,128]{3,2,1,0:T(8,128)(2,1)S(1)} %collective-permute-done.17.rest_3_), channel_id=1, source_target_pairs={{0,96},{4,28},{8,104},{12,4},{16,112},{20,12},{24,120},{28,20},{32... | collective-permute-start | bytes 3145736 | tf_op jit(solution)/shard_map/ppermute | solution.py:39
  129.2 2.9 %collective-permute-start.20 = (bf16[2096,128]{1,0:T(8,128)(2,1)S(1)}, bf16[2096,128]{1,0:T(8,128)(2,1)S(1)}, u32[]{:S(2)}, u32[]{:S(2)}) collective-permute-start(bf16[2096,128]{1,0:T(8,128)(2,1)S(1)} %get-tuple-element.125), channel_id=1, source_target_pairs={{0,16},{4,68},{8,24},{12,76},{16,0},{20,84},{24,8},{28,92},{32,48}... | collective-permute-start | bytes 1609736 | tf_op jit(solution)/shard_map/ppermute | solution.py:44
  132.9 6.6 %collective-permute-done.16.rest_4_ = bf16[16,2,128,128]{3,2,1,0:T(8,128)(2,1)S(1)} collective-permute-done((bf16[16,2,128,128]{3,2,1,0:T(8,128)(2,1)S(1)}, bf16[16,2,128,128]{3,2,1,0:T(8,128)(2,1)S(1)}, u32[]{:S(2)}, u32[]{:S(2)}) %collective-permute-start.16) | collective-permute-done | bytes 1048608 | tf_op jit(solution)/shard_map/ppermute | solution.py:39
  139.5 12.1 %collective-permute-done.18.rest_5_ = bf16[16,2,128,128]{3,2,1,0:T(8,128)(2,1)S(1)} collective-permute-done((bf16[16,2,128,128]{3,2,1,0:T(8,128)(2,1)S(1)}, bf16[16,2,128,128]{3,2,1,0:T(8,128)(2,1)S(1)}, u32[]{:S(2)}, u32[]{:S(2)}) %collective-permute-start.18) | collective-permute-done | bytes 1048608 | tf_op jit(solution)/shard_map/ppermute | solution.py:39
  158.8 17.9 %far.3 = (bf16[2096,128]{1,0:T(8,128)(2,1)S(1)}, bf16[2096,128]{1,0:T(8,128)(2,1)}, bf16[2096,128]{1,0:T(8,128)(2,1)}, bf16[2096,128]{1,0:T(8,128)(2,1)}) custom-call(s32[64]{0:T(128)S(1)} %reduce_sum.12.cnt_ref, s32[136]{0:T(256)S(1)} %get-tuple-element.99.list_ref, s32[100]{0:T(128)S(1)} %get-tuple-element.100.unit_ref, ...), custom_call_target="tpu_custom_call" | custom-call | flops 1 | bytes 1 | tf_op jit(solution)/shard_map/far/pallas_call | solution.py:369
  179.2 3.3 %collective-permute-start.27 = (bf16[2096,128]{1,0:T(8,128)(2,1)}, bf16[2096,128]{1,0:T(8,128)(2,1)}, u32[]{:S(2)}, u32[]{:S(2)}) collective-permute-start(bf16[2096,128]{1,0:T(8,128)(2,1)} %get-tuple-element.144), channel_id=1, source_target_pairs={{0,16},{4,68},{8,24},{12,76},{16,0},{20,84},{24,8},{28,92},{32,48}... | collective-permute-start | bytes 1609736 | tf_op jit(solution)/shard_map/ppermute | solution.py:44
  184.3 10.9 %collective-permute-done.25.a2 = bf16[2,1024,128]{2,1,0:T(8,128)(2,1)} collective-permute-done((bf16[2,1024,128]{2,1,0:T(8,128)(2,1)S(1)}, bf16[2,1024,128]{2,1,0:T(8,128)(2,1)}, u32[]{:S(2)}, u32[]{:S(2)}) %collective-permute-start.25) | collective-permute-done | bytes 524320 | tf_op jit(solution)/shard_map/ppermute | solution.py:57
  197.3 4.6 %mix.2.rest_9_ = f32[1024,512]{1,0:T(8,128)S(1)} custom-call(s32[2]{0:T(128)S(1)} %pad_add_fusion.place_ref, bf16[2,1024,128]{2,1,0:T(8,128)(2,1)S(1)} %finish.2.a0, bf16[2,1024,128]{2,1,0:T(8,128)(2,1)S(1)} %copy-done.10, bf16[2,1024,128]{2,1,0:T(8,128)(2,1)} %collective-permute-done.25.a2, bf16[2,1024,128]{2,1,0:T(8,128)(2,1)S(1)} %copy-done.12, ...), custom_call_target="tpu_custom_call" | custom-call | flops 1 | bytes 1 | tf_op jit(solution)/shard_map/mix/pallas_call | solution.py:484
  206.1 3.0 %collective-permute-start.30 = (bf16[2,1024,128]{2,1,0:T(8,128)(2,1)S(1)}, bf16[2,1024,128]{2,1,0:T(8,128)(2,1)S(1)}, u32[]{:S(2)}, u32[]{:S(2)}) collective-permute-start(bf16[2,1024,128]{2,1,0:T(8,128)(2,1)S(1)} %finish.3.a0), channel_id=1, source_target_pairs={{0,3},{1,0},{2,1},{3,2},{4,7},{5,4},{6,5},{7,6},{8,11},{9,8},{10,9... | collective-permute-start | bytes 1572872 | tf_op jit(solution)/shard_map/ppermute | solution.py:57
  209.8 21.6 %collective-permute-done.30.a1 = bf16[2,1024,128]{2,1,0:T(8,128)(2,1)S(1)} collective-permute-done((bf16[2,1024,128]{2,1,0:T(8,128)(2,1)S(1)}, bf16[2,1024,128]{2,1,0:T(8,128)(2,1)S(1)}, u32[]{:S(2)}, u32[]{:S(2)}) %collective-permute-start.30) | collective-permute-done | bytes 524320 | tf_op jit(solution)/shard_map/ppermute | solution.py:57
  231.4 3.7 %collective-permute-done.32.a3 = bf16[2,1024,128]{2,1,0:T(8,128)(2,1)S(1)} collective-permute-done((bf16[2,1024,128]{2,1,0:T(8,128)(2,1)S(1)}, bf16[2,1024,128]{2,1,0:T(8,128)(2,1)S(1)}, u32[]{:S(2)}, u32[]{:S(2)}) %collective-permute-start.32) | collective-permute-done | bytes 524320 | tf_op jit(solution)/shard_map/ppermute | solution.py:57
  235.2 5.4 %mix.3 = bf16[1024,512]{1,0:T(8,128)(2,1)} custom-call(s32[2]{0:T(128)S(1)} %pad_add_fusion.place_ref, bf16[2,1024,128]{2,1,0:T(8,128)(2,1)S(1)} %finish.3.a0, bf16[2,1024,128]{2,1,0:T(8,128)(2,1)S(1)} %collective-permute-done.30.a1, bf16[2,1024,128]{2,1,0:T(8,128)(2,1)S(1)} %collective-permute-done.31.a2, ...), custom_call_target="tpu_custom_call" | custom-call | flops 1 | bytes 1 | tf_op jit(solution)/shard_map/mix/pallas_call | solution.py:484
  (115 shorter events, 45.0 us)
Async XLA Ops:
  31.7 25.8 %collective-permute-start.4 = (bf16[16,2,128,128]{3,2,1,0:T(8,128)(2,1)S(1)}, bf16[16,2,128,128]{3,2,1,0:T(8,128)(2,1)S(1)}, u32[]{:S(2)}, u32[]{:S(2)}) collective-permute-start(bf16[16,2,128,128]{3,2,1,0:T(8,128)(2,1)S(1)} %collective-permute-done.rest_1_), channel_id=1, source_target_pairs={{0,32},{4,12},{8,40},{12,20},{16,48},{20,28},{24,56},{28,4},{32,64... | collective-permute-start | bytes 3145736 | tf_op jit(solution)/shard_map/ppermute | solution.py:39
  31.7 25.8 %collective-permute-start.5 = (bf16[16,2,128,128]{3,2,1,0:T(8,128)(2,1)S(1)}, bf16[16,2,128,128]{3,2,1,0:T(8,128)(2,1)}, u32[]{:S(2)}, u32[]{:S(2)}) collective-permute-start(bf16[16,2,128,128]{3,2,1,0:T(8,128)(2,1)S(1)} %collective-permute-done.rest_1_), channel_id=1, source_target_pairs={{0,96},{4,28},{8,104},{12,4},{16,112},{20,12},{24,120},{28,20},{32... | collective-permute-start | bytes 3145736 | tf_op jit(solution)/shard_map/ppermute | solution.py:39
  34.4 26.3 %collective-permute-start.8 = (bf16[16,2,128,128]{3,2,1,0:T(8,128)(2,1)S(1)}, bf16[16,2,128,128]{3,2,1,0:T(8,128)(2,1)}, u32[]{:S(2)}, u32[]{:S(2)}) collective-permute-start(bf16[16,2,128,128]{3,2,1,0:T(8,128)(2,1)S(1)} %get-tuple-element.82.rest_0_), channel_id=1, source_target_pairs={{0,32},{4,12},{8,40},{12,20},{16,48},{20,28},{24,56},{28,4},{32,64... | collective-permute-start | bytes 3145736 | tf_op jit(solution)/shard_map/ppermute | solution.py:39
  34.4 23.1 %collective-permute-start.2 = (bf16[1024,128]{1,0:T(8,128)(2,1)S(1)}, bf16[1024,128]{1,0:T(8,128)(2,1)S(1)}, u32[]{:S(2)}, u32[]{:S(2)}) collective-permute-start(bf16[1024,128]{1,0:T(8,128)(2,1)S(1)} %get-tuple-element.81), channel_id=1, source_target_pairs={{0,124},{4,8},{8,4},{12,16},{16,12},{20,24},{24,20},{28,32},{32,28... | collective-permute-start | bytes 786440 | tf_op jit(solution)/shard_map/ppermute | solution.py:53
  57.5 31.1 %collective-permute-start.6 = (bf16[2,2,8,128,128]{4,3,2,1,0:T(8,128)(2,1)}, bf16[2,2,8,128,128]{4,3,2,1,0:T(8,128)(2,1)}, u32[]{:S(2)}, u32[]{:S(2)}) collective-permute-start(bf16[2,2,8,128,128]{4,3,2,1,0:T(8,128)(2,1)} %bitcast.4.rest_8_), channel_id=1, source_target_pairs={{0,24},{4,100},{8,0},{12,108},{16,8},{20,116},{24,16},{28,124},{32... | collective-permute-start | bytes 3145736 | tf_op jit(solution)/shard_map/ppermute | solution.py:44
  60.3 37.2 %collective-permute-start.7 = (bf16[2,2,8,128,128]{4,3,2,1,0:T(8,128)(2,1)}, bf16[2,2,8,128,128]{4,3,2,1,0:T(8,128)(2,1)}, u32[]{:S(2)}, u32[]{:S(2)}) collective-permute-start(bf16[2,2,8,128,128]{4,3,2,1,0:T(8,128)(2,1)} %bitcast.4.rest_8_), channel_id=1, source_target_pairs={{0,8},{4,36},{8,16},{12,44},{16,24},{20,52},{24,0},{28,60},{32,40}... | collective-permute-start | bytes 3145736 | tf_op jit(solution)/shard_map/ppermute | solution.py:44
  60.7 37.9 %collective-permute-start.9 = (bf16[16,2,128,128]{3,2,1,0:T(8,128)(2,1)}, bf16[16,2,128,128]{3,2,1,0:T(8,128)(2,1)}, u32[]{:S(2)}, u32[]{:S(2)}) collective-permute-start(bf16[16,2,128,128]{3,2,1,0:T(8,128)(2,1)} %collective-permute-done.8.rest_6_), channel_id=1, source_target_pairs={{0,32},{4,12},{8,40},{12,20},{16,48},{20,28},{24,56},{28,4},{32,64... | collective-permute-start | bytes 3145736 | tf_op jit(solution)/shard_map/ppermute | solution.py:39
  60.7 37.9 %collective-permute-start.10 = (bf16[16,2,128,128]{3,2,1,0:T(8,128)(2,1)}, bf16[16,2,128,128]{3,2,1,0:T(8,128)(2,1)}, u32[]{:S(2)}, u32[]{:S(2)}) collective-permute-start(bf16[16,2,128,128]{3,2,1,0:T(8,128)(2,1)} %collective-permute-done.5.rest_3_), channel_id=1, source_target_pairs={{0,96},{4,28},{8,104},{12,4},{16,112},{20,12},{24,120},{28,20},{32... | collective-permute-start | bytes 3145736 | tf_op jit(solution)/shard_map/ppermute | solution.py:39
  63.6 35.0 %collective-permute-start.11 = (bf16[2,2,8,128,128]{4,3,2,1,0:T(8,128)(2,1)}, bf16[2,2,8,128,128]{4,3,2,1,0:T(8,128)(2,1)}, u32[]{:S(2)}, u32[]{:S(2)}) collective-permute-start(bf16[2,2,8,128,128]{4,3,2,1,0:T(8,128)(2,1)} %bitcast.4.rest_8_), channel_id=1, source_target_pairs={{0,16},{4,68},{8,24},{12,76},{16,0},{20,84},{24,8},{28,92},{32,48}... | collective-permute-start | bytes 3145736 | tf_op jit(solution)/shard_map/ppermute | solution.py:44
  99.3 21.7 %collective-permute-start.13 = (bf16[16,2,128,128]{3,2,1,0:T(8,128)(2,1)S(1)}, bf16[16,2,128,128]{3,2,1,0:T(8,128)(2,1)S(1)}, u32[]{:S(2)}, u32[]{:S(2)}) collective-permute-start(bf16[16,2,128,128]{3,2,1,0:T(8,128)(2,1)S(1)} %get-tuple-element.129.rest_0_), channel_id=1, source_target_pairs={{0,32},{4,12},{8,40},{12,20},{16,48},{20,28},{24,56},{28,4},{32,64... | collective-permute-start | bytes 3145736 | tf_op jit(solution)/shard_map/ppermute | solution.py:39
  99.3 21.7 %collective-permute-start.14 = (bf16[16,2,128,128]{3,2,1,0:T(8,128)(2,1)S(1)}, bf16[16,2,128,128]{3,2,1,0:T(8,128)(2,1)S(1)}, u32[]{:S(2)}, u32[]{:S(2)}) collective-permute-start(bf16[16,2,128,128]{3,2,1,0:T(8,128)(2,1)S(1)} %get-tuple-element.129.rest_0_), channel_id=1, source_target_pairs={{0,96},{4,28},{8,104},{12,4},{16,112},{20,12},{24,120},{28,20},{32... | collective-permute-start | bytes 3145736 | tf_op jit(solution)/shard_map/ppermute | solution.py:39
  102.0 23.0 %collective-permute-start.17 = (bf16[16,2,128,128]{3,2,1,0:T(8,128)(2,1)S(1)}, bf16[16,2,128,128]{3,2,1,0:T(8,128)(2,1)S(1)}, u32[]{:S(2)}, u32[]{:S(2)}) collective-permute-start(bf16[16,2,128,128]{3,2,1,0:T(8,128)(2,1)S(1)} %collective-permute-done.12.rest_1_), channel_id=1, source_target_pairs={{0,96},{4,28},{8,104},{12,4},{16,112},{20,12},{24,120},{28,20},{32... | collective-permute-start | bytes 3145736 | tf_op jit(solution)/shard_map/ppermute | solution.py:39
  104.1 28.1 %collective-permute-start.15 = (bf16[16,2,128,128]{3,2,1,0:T(8,128)(2,1)S(1)}, bf16[16,2,128,128]{3,2,1,0:T(8,128)(2,1)}, u32[]{:S(2)}, u32[]{:S(2)}) collective-permute-start(bf16[16,2,128,128]{3,2,1,0:T(8,128)(2,1)S(1)} %collective-permute-done.12.rest_1_), channel_id=1, source_target_pairs={{0,32},{4,12},{8,40},{12,20},{16,48},{20,28},{24,56},{28,4},{32,64... | collective-permute-start | bytes 3145736 | tf_op jit(solution)/shard_map/ppermute | solution.py:39
  125.0 26.7 %collective-permute-start.18 = (bf16[16,2,128,128]{3,2,1,0:T(8,128)(2,1)S(1)}, bf16[16,2,128,128]{3,2,1,0:T(8,128)(2,1)S(1)}, u32[]{:S(2)}, u32[]{:S(2)}) collective-permute-start(bf16[16,2,128,128]{3,2,1,0:T(8,128)(2,1)S(1)} %collective-permute-done.17.rest_3_), channel_id=1, source_target_pairs={{0,96},{4,28},{8,104},{12,4},{16,112},{20,12},{24,120},{28,20},{32... | collective-permute-start | bytes 3145736 | tf_op jit(solution)/shard_map/ppermute | solution.py:39
  128.5 23.2 %collective-permute-start.19 = (bf16[2096,128]{1,0:T(8,128)(2,1)S(1)}, bf16[2096,128]{1,0:T(8,128)(2,1)S(1)}, u32[]{:S(2)}, u32[]{:S(2)}) collective-permute-start(bf16[2096,128]{1,0:T(8,128)(2,1)S(1)} %get-tuple-element.124), channel_id=1, source_target_pairs={{0,8},{4,36},{8,16},{12,44},{16,24},{20,52},{24,0},{28,60},{32,40}... | collective-permute-start | bytes 1609736 | tf_op jit(solution)/shard_map/ppermute | solution.py:44
  129.2 22.4 %collective-permute-start.20 = (bf16[2096,128]{1,0:T(8,128)(2,1)S(1)}, bf16[2096,128]{1,0:T(8,128)(2,1)S(1)}, u32[]{:S(2)}, u32[]{:S(2)}) collective-permute-start(bf16[2096,128]{1,0:T(8,128)(2,1)S(1)} %get-tuple-element.125), channel_id=1, source_target_pairs={{0,16},{4,68},{8,24},{12,76},{16,0},{20,84},{24,8},{28,92},{32,48}... | collective-permute-start | bytes 1609736 | tf_op jit(solution)/shard_map/ppermute | solution.py:44
  132.2 20.3 %collective-permute-start.21 = (bf16[2096,128]{1,0:T(8,128)(2,1)S(1)}, bf16[2096,128]{1,0:T(8,128)(2,1)S(1)}, u32[]{:S(2)}, u32[]{:S(2)}) collective-permute-start(bf16[2096,128]{1,0:T(8,128)(2,1)S(1)} %get-tuple-element.126), channel_id=1, source_target_pairs={{0,24},{4,100},{8,0},{12,108},{16,8},{20,116},{24,16},{28,124},{32... | collective-permute-start | bytes 1609736 | tf_op jit(solution)/shard_map/ppermute | solution.py:44
  156.2 20.4 %collective-permute-start.23 = (bf16[2,1024,128]{2,1,0:T(8,128)(2,1)S(1)}, bf16[2,1024,128]{2,1,0:T(8,128)(2,1)S(1)}, u32[]{:S(2)}, u32[]{:S(2)}) collective-permute-start(bf16[2,1024,128]{2,1,0:T(8,128)(2,1)S(1)} %finish.2.a0), channel_id=1, source_target_pairs={{0,3},{1,0},{2,1},{3,2},{4,7},{5,4},{6,5},{7,6},{8,11},{9,8},{10,9... | collective-permute-start | bytes 1572872 | tf_op jit(solution)/shard_map/ppermute | solution.py:57
  178.3 23.6 %collective-permute-start.26 = (bf16[2096,128]{1,0:T(8,128)(2,1)}, bf16[2096,128]{1,0:T(8,128)(2,1)}, u32[]{:S(2)}, u32[]{:S(2)}) collective-permute-start(bf16[2096,128]{1,0:T(8,128)(2,1)} %get-tuple-element.143), channel_id=1, source_target_pairs={{0,8},{4,36},{8,16},{12,44},{16,24},{20,52},{24,0},{28,60},{32,40}... | collective-permute-start | bytes 1609736 | tf_op jit(solution)/shard_map/ppermute | solution.py:44
  179.2 22.7 %collective-permute-start.27 = (bf16[2096,128]{1,0:T(8,128)(2,1)}, bf16[2096,128]{1,0:T(8,128)(2,1)}, u32[]{:S(2)}, u32[]{:S(2)}) collective-permute-start(bf16[2096,128]{1,0:T(8,128)(2,1)} %get-tuple-element.144), channel_id=1, source_target_pairs={{0,16},{4,68},{8,24},{12,76},{16,0},{20,84},{24,8},{28,92},{32,48}... | collective-permute-start | bytes 1609736 | tf_op jit(solution)/shard_map/ppermute | solution.py:44
  182.5 19.4 %collective-permute-start.28 = (bf16[2096,128]{1,0:T(8,128)(2,1)}, bf16[2096,128]{1,0:T(8,128)(2,1)}, u32[]{:S(2)}, u32[]{:S(2)}) collective-permute-start(bf16[2096,128]{1,0:T(8,128)(2,1)} %get-tuple-element.145), channel_id=1, source_target_pairs={{0,24},{4,100},{8,0},{12,108},{16,8},{20,116},{24,16},{28,124},{32... | collective-permute-start | bytes 1609736 | tf_op jit(solution)/shard_map/ppermute | solution.py:44
  206.1 25.3 %collective-permute-start.30 = (bf16[2,1024,128]{2,1,0:T(8,128)(2,1)S(1)}, bf16[2,1024,128]{2,1,0:T(8,128)(2,1)S(1)}, u32[]{:S(2)}, u32[]{:S(2)}) collective-permute-start(bf16[2,1024,128]{2,1,0:T(8,128)(2,1)S(1)} %finish.3.a0), channel_id=1, source_target_pairs={{0,3},{1,0},{2,1},{3,2},{4,7},{5,4},{6,5},{7,6},{8,11},{9,8},{10,9... | collective-permute-start | bytes 1572872 | tf_op jit(solution)/shard_map/ppermute | solution.py:57
  209.2 22.3 %collective-permute-start.31 = (bf16[2,1024,128]{2,1,0:T(8,128)(2,1)S(1)}, bf16[2,1024,128]{2,1,0:T(8,128)(2,1)S(1)}, u32[]{:S(2)}, u32[]{:S(2)}) collective-permute-start(bf16[2,1024,128]{2,1,0:T(8,128)(2,1)S(1)} %finish.3.a0), channel_id=1, source_target_pairs={{0,2},{1,3},{2,0},{3,1},{4,6},{5,7},{6,4},{7,5},{8,10},{9,11},{10,... | collective-permute-start | bytes 1572872 | tf_op jit(solution)/shard_map/ppermute | solution.py:57
  209.2 26.0 %collective-permute-start.32 = (bf16[2,1024,128]{2,1,0:T(8,128)(2,1)S(1)}, bf16[2,1024,128]{2,1,0:T(8,128)(2,1)S(1)}, u32[]{:S(2)}, u32[]{:S(2)}) collective-permute-start(bf16[2,1024,128]{2,1,0:T(8,128)(2,1)S(1)} %finish.3.a0), channel_id=1, source_target_pairs={{0,1},{1,2},{2,3},{3,0},{4,5},{5,6},{6,7},{7,4},{8,9},{9,10},{10,1... | collective-permute-start | bytes 1572872 | tf_op jit(solution)/shard_map/ppermute | solution.py:57
  (31 other events, 457.0 us)

commit v3 on v2

--- a/solution.py
+++ b/solution.py
@@ -169,7 +169,7 @@
             jax.ShapeDtypeStruct((1024, HD), BF16),
         ],
         compiler_params=params(),
-        cost_estimate=BRIEF,
+        cost_estimate=pl.CostEstimate(flops=2 * n * d * 3 * w, transcendentals=0, bytes_accessed=16 << 20),
         name="project",
     )(core, tokens, gain.reshape(1, d), wq, wk, wv)
 
@@ -217,15 +217,15 @@
 UNITS = 96 + GROUP
 
 
-def plan_kernel(cnt_ref, code_ref, list_ref, unit_ref, first_ref, long_ref, size_ref):
+def plan_kernel(cnt_ref, code_ref, unit_ref, first_ref, long_ref, size_ref, list_ref):
     def scan(i, carry):
-        e, u, m = carry
+        u, m = carry
         n = cnt_ref[i]
         first_ref[i] = u
 
         def named(carry):
-            e, u, m = carry
-            at = e
+            u, m = carry
+            at = jnp.int32(0)
             for w in range(WMAX):
                 code = code_ref[i * WMAX + w]
                 list_ref[at] = code
@@ -233,20 +233,19 @@
 
             def unit(k, u):
                 both = (2 * k + 1 < n).astype(jnp.int32)
-                unit_ref[u] = i * 512 + (e + 2 * k) * 2 + both
+                unit_ref[u] = both * (1 << 22) + i * (1 << 16) + list_ref[2 * k] * 256 + list_ref[2 * k + both]
                 return u + 1
 
             long_ref[m] = i
-            return at, lax.fori_loop(0, lax.shift_right_logical(n + 1, 1), unit, u), m + (n > 2).astype(jnp.int32)
-
-        return lax.cond(n > 0, named, lambda carry: carry, (e, u, m))
-
-    entries, units, longs = lax.fori_loop(0, 64, scan, (jnp.int32(0), jnp.int32(0), jnp.int32(0)))
+            return lax.fori_loop(0, lax.shift_right_logical(n + 1, 1), unit, u), m + (n > 2).astype(jnp.int32)
+
+        return lax.cond(n > 0, named, lambda carry: carry, (u, m))
+
+    units, longs = lax.fori_loop(0, 64, scan, (jnp.int32(0), jnp.int32(0)))
     for g in range(GROUP):
         unit_ref[units + g] = -1
-    size_ref[0] = entries
-    size_ref[1] = units
-    size_ref[2] = longs
+    size_ref[0] = units
+    size_ref[1] = longs
 
 
 def plan(cnt, code):
@@ -256,53 +255,26 @@
     return pl.pallas_call(
         plan_kernel,
         in_specs=[SMEM] * 2,
-        out_specs=[SMEM] * 5,
-        out_shape=[out(128 + WMAX), out(UNITS), out(64), out(64), out(3)],
+        out_specs=[SMEM] * 4,
+        out_shape=[out(UNITS), out(64), out(64), out(2)],
+        scratch_shapes=[pltpu.SMEM((2 * WMAX,), jnp.int32)],
         compiler_params=params(16),
         cost_estimate=BRIEF,
         name="plan",
     )(cnt, code)
 
 
-def far_kernel(j, cnt_ref, list_ref, unit_ref, first_ref, long_ref, size_ref, *rest):
+def far_kernel(j, cnt_ref, unit_ref, first_ref, long_ref, size_ref, *rest):
     sources, qs, outs = rest[:8], rest[8:12], rest[12:16]
     kvbuf, qbuf, obuf, acc_ref, stat_ref, logs, kvsem, qsem, osem = rest[16:]
-    entries, units = size_ref[0], size_ref[1]
-    for r in range(4):
-        pltpu.make_async_copy(qs[r].at[:, j], qbuf.at[pl.ds(2 * r, 2)], qsem.at[r]).start()
-
-    def fetch(e, _):
-        code = list_ref[e]
-        at = lax.bitwise_and(code, 15)
-        source = lax.shift_right_logical(code, 4)
-
-        def start(lo, hi):
-            if hi - lo == 1:
-                pltpu.make_async_copy(sources[lo].at[at], kvbuf.at[e], kvsem.at[e]).start()
-                return
-            mid = (lo + hi) // 2
-
-            @pl.when(source < mid)
-            def _():
-                start(lo, mid)
-
-            @pl.when(source >= mid)
-            def _():
-                start(mid, hi)
-
-        start(0, 8)
-        return 0
-
-    lax.fori_loop(0, entries, fetch, 0)
+    units = size_ref[0]
+    copies = [pltpu.make_async_copy(qs[r].at[:, j], qbuf.at[pl.ds(2 * r, 2)], qsem.at[r]) for r in range(4)]
+    copies += [pltpu.make_async_copy(sources[k], kvbuf.at[pl.ds(16 * k, 16)], kvsem.at[k]) for k in range(8)]
+    for copy in copies:
+        copy.start()
     logs[...] = jnp.full((64, BLOCK), NEG, F32)
-    for r in range(4):
-        pltpu.make_async_copy(qs[r].at[:, j], qbuf.at[pl.ds(2 * r, 2)], qsem.at[r]).wait()
-
-    def landed(e, _):
-        pltpu.make_async_copy(sources[0].at[0], kvbuf.at[e], kvsem.at[e]).wait()
-        return 0
-
-    lax.fori_loop(0, entries, landed, 0)
+    for copy in copies:
+        copy.wait()
 
     def store(i, m, total, acc):
         rows = pl.ds(pl.multiple_of(lax.bitwise_and(i, 15) * HD, HD), HD)
@@ -310,24 +282,22 @@
         logs[pl.ds(i, 1), :] = m + jnp.log(total)
 
     def group(g, _):
-        done = []
         for t in range(GROUP):
             u = g * GROUP + t
             unit = unit_ref[u]
             unit = jnp.where(unit >= 0, unit, unit_ref[g * GROUP])
-            both = lax.bitwise_and(unit, 1)
-            ea = lax.bitwise_and(lax.shift_right_logical(unit, 1), 255)
-            eb = ea + both
-            i = lax.shift_right_logical(unit, 9)
+            both = lax.shift_right_logical(unit, 22) == 1
+            i = lax.bitwise_and(lax.shift_right_logical(unit, 16), 63)
+            ea = lax.bitwise_and(lax.shift_right_logical(unit, 8), 127)
+            eb = lax.bitwise_and(unit, 127)
             q = qbuf[lax.shift_right_logical(i, 3), lax.bitwise_and(i, 7)]
-            sa = nt(kvbuf[ea, 0], q) * SCALE
-            sb = jnp.where(both == 1, nt(kvbuf[eb, 0], q) * SCALE, NEG)
+            s = nt(jnp.concatenate([kvbuf[ea, 0], kvbuf[eb, 0]], axis=0), q) * SCALE
+            sa, sb = s[:BLOCK], jnp.where(both, s[BLOCK:], NEG)
             m = jnp.max(jnp.maximum(sa, sb), axis=0, keepdims=True)
             pa, pb = jnp.exp(sa - m), jnp.exp(sb - m)
             total = jnp.sum(pa + pb, axis=0, keepdims=True)
-            acc = nn(kvbuf[ea, 1], pa.astype(BF16)) + nn(kvbuf[eb, 1], pb.astype(BF16))
-            done.append((u, i, m, total, acc))
-        for u, i, m, total, acc in done:
+            p = jnp.concatenate([pa, pb], axis=0).astype(BF16)
+            acc = nn(jnp.concatenate([kvbuf[ea, 1], kvbuf[eb, 1]], axis=1), p)
             stat_ref[u, 0:1, :] = m
             stat_ref[u, 1:2, :] = total
             acc_ref[u] = acc
@@ -352,7 +322,7 @@
         store(i, *lax.fori_loop(u + 1, u + lax.shift_right_logical(n + 1, 1), more, start))
         return 0
 
-    lax.fori_loop(0, size_ref[2], join, 0)
+    lax.fori_loop(0, size_ref[1], join, 0)
     for r in range(4):
         part = logs[r * 16 : (r + 1) * 16, :]
         for t in range(3):
@@ -368,7 +338,7 @@
     out = jax.ShapeDtypeStruct((OROWS, BLOCK), BF16)
     return pl.pallas_call(
         functools.partial(far_kernel, j),
-        in_specs=[SMEM] * 6 + [ANY] * 12,
+        in_specs=[SMEM] * 5 + [ANY] * 12,
         out_specs=[ANY] * 4,
         out_shape=[out] * 4,
         scratch_shapes=[
@@ -378,7 +348,7 @@
             pltpu.VMEM((UNITS, HD, BLOCK), F32),
             pltpu.VMEM((UNITS, 8, BLOCK), F32),
             pltpu.VMEM((64, BLOCK), F32),
-            pltpu.SemaphoreType.DMA((128,)),
+            pltpu.SemaphoreType.DMA((8,)),
             pltpu.SemaphoreType.DMA((4,)),
             pltpu.SemaphoreType.DMA((4,)),
         ],
@@ -528,25 +498,25 @@
     up_k0, down_k0 = rows_perm(keep0, 1), rows_perm(keep0, -1)
     got0 = core_swap(send0)
     up_r0, down_r0 = rows_perm(got0, 1), rows_perm(got0, -1)
-
-    gain = after(norm_gain, got0)
+    keep1, send1 = split_cache(1, after(core, got0), kv_cache)
+    got1 = core_swap(send1)
+
+    gain, up_k0, down_k0 = lax.optimization_barrier((norm_gain, up_k0, down_k0, got1))[:3]
+    up20 = rows_perm(up_k0, 1)
     q_all, swap, k_all, v_all, edge = project(core, tokens, gain, w_query, w_key, w_value)
     swapped, halo = core_swap(swap), halo_perm(edge)
-    up20 = rows_perm(after(up_k0, edge), 1)
     mine = jnp.concatenate([q_all[:2], swapped[:2048].reshape(2, 1024, HD)], axis=0).reshape(2, 2, 8, BLOCK, HD)
-    mine, halo, down_k0, up_r0, down_r0 = lax.optimization_barrier((mine, halo, down_k0, up_r0, down_r0))
+    mine, halo, up_r0, down_r0 = lax.optimization_barrier((mine, halo, up_r0, down_r0))
     down20 = rows_perm(down_r0, -1)
     q1, q3, q2 = query_perm(mine, -1), query_perm(mine, 1), query_perm(mine, 2)
 
-    keep1, send1 = split_cache(1, after(core, mine), kv_cache)
-    near_o, near_lse = near(core, q_all, k_all, v_all, after(halo, keep1), swapped)
+    near_o, near_lse = near(core, q_all, k_all, v_all, after(halo, mine), swapped)
     code, cnt = line_codes(wake_blocks, wake_frames, wake_counts, y, z, c)
     lists = plan(cnt, code)
     keep1, near_o, near_lse, q1, q3, *lists = lax.optimization_barrier((keep1, near_o, near_lse, q1, q3, *lists))
     up_k1, down_k1 = rows_perm(keep1, 1), rows_perm(keep1, -1)
-    send1, up20, down20, q2 = lax.optimization_barrier((send1, up20, down20, q2, near_o))[:4]
-    got1 = core_swap(send1)
-    qs = [after(mine, got1), q1, q2, q3]
+    got1, up20, down20, q2 = lax.optimization_barrier((got1, up20, down20, q2, near_o))[:4]
+    qs = [mine, q1, q2, q3]
     up_r1, down_r1 = rows_perm(got1, 1), rows_perm(got1, -1)
 
     def returned(parts):

time: 243 us -> 228 us (0.938); the launches traced: 241 us -> 228 us
  waiting for transfers between devices: 94 us -> 80.6 us
  Pallas kernels: 93 us -> 80.2 us
  starting transfers between devices: 46.4 us -> 55.9 us
  local copies, waits for them, and re-layouts: 5.4 us -> 9.55 us
    pallas_call x3, Pallas kernels: 37.7 us -> 25 us  [the longest x2 22.1 us: far(): pl.pallas_call(functools.partial(far_kernel, j), in_specs=[SMEM] * 5 + [A...]
    ppermute x12, starting transfers between devices: 18.7 us -> 30.4 us  [rows_perm(): return lax.ppermute(x, 'tok', pairs)]
    ppermute x1, waiting for transfers between devices: 11.5 us -> 2.5 us  [halo_perm(): lax.ppermute(x, 'tok', [(i, (i + (1 if i % 2 else -1)) % n) for i in rang...]
    ppermute x9, waiting for transfers between devices: 9.64 us -> 3.01 us  [query_perm(): return lax.ppermute(x, 'tok', pairs)]
    ppermute x12, waiting for transfers between devices: 30.8 us -> 35.6 us  [rows_perm(): return lax.ppermute(x, 'tok', pairs)]
    unnamed x44 -> x54, local copies, waits for them, and re-layouts: 4.73 us -> 8.88 us
  transfers between devices with their start and end apart: 33 -> 33, of which waited for: 15 -> 15; matrix products, arithmetic and copies ran while one was open for 1% -> 1% of each run, Pallas kernels for 25% -> 28%
where the time goes in v3:
time: 228 us
  waiting for transfers between devices  80.6 us (35%)
  Pallas kernels  80.2 us (35%)
  starting transfers between devices  55.9 us (25%)
  local copies, waits for them, and re-layouts  9.55 us (4%)
    ppermute x6, waiting for transfers between devices, mp_perm(): return lax.ppermute(x, 'mp', [(i, (i + d) % NX) for i in range(NX)])  35.9 us
    ppermute x12, waiting for transfers between devices, rows_perm(): return lax.ppermute(x, 'tok', pairs)  35.6 us
    ppermute x12, starting transfers between devices, rows_perm(): return lax.ppermute(x, 'tok', pairs)  30.4 us
    pallas_call x2, Pallas kernels, far(): pl.pallas_call(functools.partial(far_kernel, j), in_specs=[SMEM] * 5 + [A...  22.1 us
    pallas_call x2, Pallas kernels, split_cache(): pl.pallas_call(split_cache_kernel, grid_spec=pltpu.PrefetchScalarGridSpec...  17.7 us
    pallas_call x1, Pallas kernels, project(): pl.pallas_call(project_kernel, grid_spec=pltpu.PrefetchScalarGridSpec(num...  14.8 us
    ppermute x9, starting transfers between devices, query_perm(): return lax.ppermute(x, 'tok', pairs)  12.8 us
    pallas_call x2, Pallas kernels, mix(): pl.pallas_call(functools.partial(mix_kernel, last), grid_spec=pltpu.Prefe...  10 us
  transfers between devices with their start and end apart: 33, of which 15 were waited for; matrix products, arithmetic and copies ran while one was open for 1% of the time, Pallas kernels for 28%

profile of v3, /device:TPU:1, one launch (start us, length us, event | category | flops | bytes accessed | tf_op | source)
XLA Modules:
  0.0 228.1 jit_solution(11166337091739743933)
XLA Ops:
  0.0 8.7 %split_cache.2 = (bf16[16,2,128,128]{3,2,1,0:T(8,128)(2,1)S(1)}, bf16[16,2,128,128]{3,2,1,0:T(8,128)(2,1)S(1)}) custom-call(s32[1]{0:T(128)} %bitcast.core_ref, bf16[2,1024,2,512]{3,2,1,0:T(2,128)(2,1)} %send_ref.3, bf16[2,1024,2,512]{3,2,1,0:T(2,128)(2,1)} %send_ref.3), custom_call_target="tpu_custom_call" | custom-call | flops 1 | bytes 1 | tf_op jit(solution)/shard_map/split_cache/pallas_call | solution.py:79
  10.2 3.8 %collective-permute-start.2 = (bf16[16,2,128,128]{3,2,1,0:T(8,128)(2,1)S(1)}, bf16[16,2,128,128]{3,2,1,0:T(8,128)(2,1)S(1)}, u32[]{:S(2)}, u32[]{:S(2)}) collective-permute-start(bf16[16,2,128,128]{3,2,1,0:T(8,128)(2,1)S(1)} %get-tuple-element.77.rest_0_), channel_id=1, source_target_pairs={{0,96},{4,28},{8,104},{12,4},{16,112},{20,12},{24,120},{28,20},{32... | collective-permute-start | bytes 3145736 | tf_op jit(solution)/shard_map/ppermute | solution.py:39
  14.0 9.0 %split_cache.3 = (bf16[16,2,128,128]{3,2,1,0:T(8,128)(2,1)S(1)}, bf16[16,2,128,128]{3,2,1,0:T(8,128)(2,1)S(1)}) custom-call(s32[1]{0:T(128)} %bitcast.core_ref, bf16[2,1024,2,512]{3,2,1,0:T(2,128)(2,1)} %send_ref.3, bf16[2,1024,2,512]{3,2,1,0:T(2,128)(2,1)} %send_ref.3), custom_call_target="tpu_custom_call" | custom-call | flops 1 | bytes 1 | tf_op jit(solution)/shard_map/split_cache/pallas_call | solution.py:79
  24.1 3.1 %collective-permute-start.7 = (bf16[16,2,128,128]{3,2,1,0:T(8,128)(2,1)S(1)}, bf16[16,2,128,128]{3,2,1,0:T(8,128)(2,1)}, u32[]{:S(2)}, u32[]{:S(2)}) collective-permute-start(bf16[16,2,128,128]{3,2,1,0:T(8,128)(2,1)S(1)} %collective-permute-done.rest_1_), channel_id=1, source_target_pairs={{0,96},{4,28},{8,104},{12,4},{16,112},{20,12},{24,120},{28,20},{32... | collective-permute-start | bytes 3145736 | tf_op jit(solution)/shard_map/ppermute | solution.py:39
  30.1 14.8 %project.1 = (bf16[4,1024,128]{2,1,0:T(8,128)(2,1)S(1)}, bf16[3072,128]{1,0:T(8,128)(2,1)S(1)}, bf16[4,8,128,128]{3,2,1,0:T(8,128)(2,1)S(1)}, bf16[4,8,128,128]{3,2,1,0:T(8,128)(2,1)S(1)}, bf16[1024,128]{1,0:T(8,128)(2,1)S(1)}) custom-call(s32[1]{0:T(128)} %bitcast.core_ref, bf16[1024,2048]{1,0:T(8,128)(2,1)} %rest_8_.1, f32[1,2048]{1,0:T(1,128)S(1)} %bitcast.19, ...), custom_call_target="tpu_custom_call" | custom-call | flops 6442450944 | bytes 16777216 | tf_op jit(solution)/shard_map/project/pallas_call | solution.py:144
  55.3 4.2 %collective-permute-start.11 = (bf16[16,2,128,128]{3,2,1,0:T(8,128)(2,1)}, bf16[16,2,128,128]{3,2,1,0:T(8,128)(2,1)}, u32[]{:S(2)}, u32[]{:S(2)}) collective-permute-start(bf16[16,2,128,128]{3,2,1,0:T(8,128)(2,1)} %collective-permute-done.7.rest_3_), channel_id=1, source_target_pairs={{0,96},{4,28},{8,104},{12,4},{16,112},{20,12},{24,120},{28,20},{32... | collective-permute-start | bytes 3145736 | tf_op jit(solution)/shard_map/ppermute | solution.py:39
  65.4 9.6 %near.1 = (f32[4,8,128,128]{3,2,1,0:T(8,128)}, f32[4,8,128]{2,1,0:T(8,128)S(1)}) custom-call(s32[1]{0:T(128)} %bitcast.core_ref, bf16[4,1024,128]{2,1,0:T(8,128)(2,1)S(1)} %get-tuple-element.80.q_ref, bf16[4,8,128,128]{3,2,1,0:T(8,128)(2,1)S(1)} %get-tuple-element.81.k_ref, bf16[4,8,128,128]{3,2,1,0:T(8,128)(2,1)S(1)} %copy-done.2, ...), custom_call_target="tpu_custom_call" | custom-call | flops 1 | bytes 1 | tf_op jit(solution)/shard_map/near/pallas_call | solution.py:200
  75.0 7.3 %collective-permute-start.14 = (bf16[16,2,128,128]{3,2,1,0:T(8,128)(2,1)S(1)}, bf16[16,2,128,128]{3,2,1,0:T(8,128)(2,1)S(1)}, u32[]{:S(2)}, u32[]{:S(2)}) collective-permute-start(bf16[16,2,128,128]{3,2,1,0:T(8,128)(2,1)S(1)} %copy-done.4), channel_id=1, source_target_pairs={{0,96},{4,28},{8,104},{12,4},{16,112},{20,12},{24,120},{28,20},{32... | collective-permute-start | bytes 3145736 | tf_op jit(solution)/shard_map/ppermute | solution.py:39
  82.2 5.4 %collective-permute-done.10.rest_4_ = bf16[16,2,128,128]{3,2,1,0:T(8,128)(2,1)} collective-permute-done((bf16[16,2,128,128]{3,2,1,0:T(8,128)(2,1)}, bf16[16,2,128,128]{3,2,1,0:T(8,128)(2,1)}, u32[]{:S(2)}, u32[]{:S(2)}) %collective-permute-start.10) | collective-permute-done | bytes 1048608 | tf_op jit(solution)/shard_map/ppermute | solution.py:39
  87.6 3.0 %collective-permute-done.12.rest_10_ = bf16[2,2,8,128,128]{4,3,2,1,0:T(8,128)(2,1)} collective-permute-done((bf16[2,2,8,128,128]{4,3,2,1,0:T(8,128)(2,1)}, bf16[2,2,8,128,128]{4,3,2,1,0:T(8,128)(2,1)}, u32[]{:S(2)}, u32[]{:S(2)}) %collective-permute-start.12) | collective-permute-done | bytes 1048608 | tf_op jit(solution)/shard_map/ppermute | solution.py:44
  90.6 7.5 %collective-permute-start.17 = (bf16[16,2,128,128]{3,2,1,0:T(8,128)(2,1)S(1)}, bf16[16,2,128,128]{3,2,1,0:T(8,128)(2,1)S(1)}, u32[]{:S(2)}, u32[]{:S(2)}) collective-permute-start(bf16[16,2,128,128]{3,2,1,0:T(8,128)(2,1)S(1)} %copy-done.6), channel_id=1, source_target_pairs={{0,96},{4,28},{8,104},{12,4},{16,112},{20,12},{24,120},{28,20},{32... | collective-permute-start | bytes 3145736 | tf_op jit(solution)/shard_map/ppermute | solution.py:39
  98.1 10.6 %far.2 = (bf16[2096,128]{1,0:T(8,128)(2,1)S(1)}, bf16[2096,128]{1,0:T(8,128)(2,1)S(1)}, bf16[2096,128]{1,0:T(8,128)(2,1)S(1)}, bf16[2096,128]{1,0:T(8,128)(2,1)S(1)}) custom-call(s32[64]{0:T(128)S(1)} %reduce_sum.12.cnt_ref, s32[100]{0:T(128)S(1)} %get-tuple-element.96.unit_ref, s32[64]{0:T(128)S(1)} %get-tuple-element.97.first_ref, ...), custom_call_target="tpu_custom_call" | custom-call | flops 1 | bytes 1 | tf_op jit(solution)/shard_map/far/pallas_call | solution.py:339
  108.7 6.3 %collective-permute-done.17.rest_3_ = bf16[16,2,128,128]{3,2,1,0:T(8,128)(2,1)S(1)} collective-permute-done((bf16[16,2,128,128]{3,2,1,0:T(8,128)(2,1)S(1)}, bf16[16,2,128,128]{3,2,1,0:T(8,128)(2,1)S(1)}, u32[]{:S(2)}, u32[]{:S(2)}) %collective-permute-start.17) | collective-permute-done | bytes 1048608 | tf_op jit(solution)/shard_map/ppermute | solution.py:39
  115.0 3.4 %collective-permute-start.18 = (bf16[16,2,128,128]{3,2,1,0:T(8,128)(2,1)S(1)}, bf16[16,2,128,128]{3,2,1,0:T(8,128)(2,1)S(1)}, u32[]{:S(2)}, u32[]{:S(2)}) collective-permute-start(bf16[16,2,128,128]{3,2,1,0:T(8,128)(2,1)S(1)} %collective-permute-done.17.rest_3_), channel_id=1, source_target_pairs={{0,96},{4,28},{8,104},{12,4},{16,112},{20,12},{24,120},{28,20},{32... | collective-permute-start | bytes 3145736 | tf_op jit(solution)/shard_map/ppermute | solution.py:39
  118.4 3.6 %collective-permute-start.20 = (bf16[2096,128]{1,0:T(8,128)(2,1)S(1)}, bf16[2096,128]{1,0:T(8,128)(2,1)S(1)}, u32[]{:S(2)}, u32[]{:S(2)}) collective-permute-start(bf16[2096,128]{1,0:T(8,128)(2,1)S(1)} %get-tuple-element.119), channel_id=1, source_target_pairs={{0,16},{4,68},{8,24},{12,76},{16,0},{20,84},{24,8},{28,92},{32,48}... | collective-permute-start | bytes 1609736 | tf_op jit(solution)/shard_map/ppermute | solution.py:44
  122.0 18.4 %collective-permute-done.18.rest_5_ = bf16[16,2,128,128]{3,2,1,0:T(8,128)(2,1)S(1)} collective-permute-done((bf16[16,2,128,128]{3,2,1,0:T(8,128)(2,1)S(1)}, bf16[16,2,128,128]{3,2,1,0:T(8,128)(2,1)S(1)}, u32[]{:S(2)}, u32[]{:S(2)}) %collective-permute-start.18) | collective-permute-done | bytes 1048608 | tf_op jit(solution)/shard_map/ppermute | solution.py:39
  140.5 4.6 %collective-permute-done.16.rest_4_ = bf16[16,2,128,128]{3,2,1,0:T(8,128)(2,1)S(1)} collective-permute-done((bf16[16,2,128,128]{3,2,1,0:T(8,128)(2,1)S(1)}, bf16[16,2,128,128]{3,2,1,0:T(8,128)(2,1)S(1)}, u32[]{:S(2)}, u32[]{:S(2)}) %collective-permute-start.16) | collective-permute-done | bytes 1048608 | tf_op jit(solution)/shard_map/ppermute | solution.py:39
  151.7 11.5 %far.3 = (bf16[2096,128]{1,0:T(8,128)(2,1)S(1)}, bf16[2096,128]{1,0:T(8,128)(2,1)}, bf16[2096,128]{1,0:T(8,128)(2,1)}, bf16[2096,128]{1,0:T(8,128)(2,1)}) custom-call(s32[64]{0:T(128)S(1)} %reduce_sum.12.cnt_ref, s32[100]{0:T(128)S(1)} %get-tuple-element.96.unit_ref, s32[64]{0:T(128)S(1)} %get-tuple-element.97.first_ref, s32[64]{0:T(128)S(1)} %get-tuple-element.98.long_ref, ...), custom_call_target="tpu_custom_call" | custom-call | flops 1 | bytes 1 | tf_op jit(solution)/shard_map/far/pallas_call | solution.py:339
  165.9 3.0 %collective-permute-start.27 = (bf16[2096,128]{1,0:T(8,128)(2,1)}, bf16[2096,128]{1,0:T(8,128)(2,1)}, u32[]{:S(2)}, u32[]{:S(2)}) collective-permute-start(bf16[2096,128]{1,0:T(8,128)(2,1)} %get-tuple-element.138), channel_id=1, source_target_pairs={{0,16},{4,68},{8,24},{12,76},{16,0},{20,84},{24,8},{28,92},{32,48}... | collective-permute-start | bytes 1609736 | tf_op jit(solution)/shard_map/ppermute | solution.py:44
  171.8 13.5 %collective-permute-done.25.a2 = bf16[2,1024,128]{2,1,0:T(8,128)(2,1)} collective-permute-done((bf16[2,1024,128]{2,1,0:T(8,128)(2,1)S(1)}, bf16[2,1024,128]{2,1,0:T(8,128)(2,1)}, u32[]{:S(2)}, u32[]{:S(2)}) %collective-permute-start.25) | collective-permute-done | bytes 524320 | tf_op jit(solution)/shard_map/ppermute | solution.py:57
  187.3 4.6 %mix.2.rest_9_ = f32[1024,512]{1,0:T(8,128)S(1)} custom-call(s32[2]{0:T(128)S(1)} %pad_add_fusion.place_ref, bf16[2,1024,128]{2,1,0:T(8,128)(2,1)S(1)} %finish.2.a0, bf16[2,1024,128]{2,1,0:T(8,128)(2,1)S(1)} %copy-done.16, bf16[2,1024,128]{2,1,0:T(8,128)(2,1)} %collective-permute-done.25.a2, bf16[2,1024,128]{2,1,0:T(8,128)(2,1)S(1)} %copy-done.14, ...), custom_call_target="tpu_custom_call" | custom-call | flops 1 | bytes 1 | tf_op jit(solution)/shard_map/mix/pallas_call | solution.py:454
  200.3 11.0 %collective-permute-done.32.a3 = bf16[2,1024,128]{2,1,0:T(8,128)(2,1)S(1)} collective-permute-done((bf16[2,1024,128]{2,1,0:T(8,128)(2,1)S(1)}, bf16[2,1024,128]{2,1,0:T(8,128)(2,1)S(1)}, u32[]{:S(2)}, u32[]{:S(2)}) %collective-permute-start.32) | collective-permute-done | bytes 524320 | tf_op jit(solution)/shard_map/ppermute | solution.py:57
  211.4 10.7 %collective-permute-done.31.a2 = bf16[2,1024,128]{2,1,0:T(8,128)(2,1)S(1)} collective-permute-done((bf16[2,1024,128]{2,1,0:T(8,128)(2,1)S(1)}, bf16[2,1024,128]{2,1,0:T(8,128)(2,1)S(1)}, u32[]{:S(2)}, u32[]{:S(2)}) %collective-permute-start.31) | collective-permute-done | bytes 524320 | tf_op jit(solution)/shard_map/ppermute | solution.py:57
  222.6 5.4 %mix.3 = bf16[1024,512]{1,0:T(8,128)(2,1)} custom-call(s32[2]{0:T(128)S(1)} %pad_add_fusion.place_ref, bf16[2,1024,128]{2,1,0:T(8,128)(2,1)S(1)} %finish.3.a0, bf16[2,1024,128]{2,1,0:T(8,128)(2,1)S(1)} %collective-permute-done.30.a1, bf16[2,1024,128]{2,1,0:T(8,128)(2,1)S(1)} %collective-permute-done.31.a2, ...), custom_call_target="tpu_custom_call" | custom-call | flops 1 | bytes 1 | tf_op jit(solution)/shard_map/mix/pallas_call | solution.py:454
  (125 shorter events, 44.7 us)
Async XLA Ops:
  10.2 17.0 %collective-permute-start.2 = (bf16[16,2,128,128]{3,2,1,0:T(8,128)(2,1)S(1)}, bf16[16,2,128,128]{3,2,1,0:T(8,128)(2,1)S(1)}, u32[]{:S(2)}, u32[]{:S(2)}) collective-permute-start(bf16[16,2,128,128]{3,2,1,0:T(8,128)(2,1)S(1)} %get-tuple-element.77.rest_0_), channel_id=1, source_target_pairs={{0,96},{4,28},{8,104},{12,4},{16,112},{20,12},{24,120},{28,20},{32... | collective-permute-start | bytes 3145736 | tf_op jit(solution)/shard_map/ppermute | solution.py:39
  14.0 15.1 %collective-permute-start.1 = (bf16[16,2,128,128]{3,2,1,0:T(8,128)(2,1)S(1)}, bf16[16,2,128,128]{3,2,1,0:T(8,128)(2,1)}, u32[]{:S(2)}, u32[]{:S(2)}) collective-permute-start(bf16[16,2,128,128]{3,2,1,0:T(8,128)(2,1)S(1)} %get-tuple-element.77.rest_0_), channel_id=1, source_target_pairs={{0,32},{4,12},{8,40},{12,20},{16,48},{20,28},{24,56},{28,4},{32,64... | collective-permute-start | bytes 3145736 | tf_op jit(solution)/shard_map/ppermute | solution.py:39
  24.1 24.4 %collective-permute-start.7 = (bf16[16,2,128,128]{3,2,1,0:T(8,128)(2,1)S(1)}, bf16[16,2,128,128]{3,2,1,0:T(8,128)(2,1)}, u32[]{:S(2)}, u32[]{:S(2)}) collective-permute-start(bf16[16,2,128,128]{3,2,1,0:T(8,128)(2,1)S(1)} %collective-permute-done.rest_1_), channel_id=1, source_target_pairs={{0,96},{4,28},{8,104},{12,4},{16,112},{20,12},{24,120},{28,20},{32... | collective-permute-start | bytes 3145736 | tf_op jit(solution)/shard_map/ppermute | solution.py:39
  27.2 21.3 %collective-permute-start.6 = (bf16[16,2,128,128]{3,2,1,0:T(8,128)(2,1)S(1)}, bf16[16,2,128,128]{3,2,1,0:T(8,128)(2,1)S(1)}, u32[]{:S(2)}, u32[]{:S(2)}) collective-permute-start(bf16[16,2,128,128]{3,2,1,0:T(8,128)(2,1)S(1)} %collective-permute-done.rest_1_), channel_id=1, source_target_pairs={{0,32},{4,12},{8,40},{12,20},{16,48},{20,28},{24,56},{28,4},{32,64... | collective-permute-start | bytes 3145736 | tf_op jit(solution)/shard_map/ppermute | solution.py:39
  50.9 24.0 %collective-permute-start.9 = (bf16[2,2,8,128,128]{4,3,2,1,0:T(8,128)(2,1)}, bf16[2,2,8,128,128]{4,3,2,1,0:T(8,128)(2,1)}, u32[]{:S(2)}, u32[]{:S(2)}) collective-permute-start(bf16[2,2,8,128,128]{4,3,2,1,0:T(8,128)(2,1)} %bitcast.4.rest_8_), channel_id=1, source_target_pairs={{0,8},{4,36},{8,16},{12,44},{16,24},{20,52},{24,0},{28,60},{32,40}... | collective-permute-start | bytes 3145736 | tf_op jit(solution)/shard_map/ppermute | solution.py:44
  52.4 22.6 %collective-permute-start.8 = (bf16[2,2,8,128,128]{4,3,2,1,0:T(8,128)(2,1)}, bf16[2,2,8,128,128]{4,3,2,1,0:T(8,128)(2,1)}, u32[]{:S(2)}, u32[]{:S(2)}) collective-permute-start(bf16[2,2,8,128,128]{4,3,2,1,0:T(8,128)(2,1)} %bitcast.4.rest_8_), channel_id=1, source_target_pairs={{0,24},{4,100},{8,0},{12,108},{16,8},{20,116},{24,16},{28,124},{32... | collective-permute-start | bytes 3145736 | tf_op jit(solution)/shard_map/ppermute | solution.py:44
  54.1 33.5 %collective-permute-start.10 = (bf16[16,2,128,128]{3,2,1,0:T(8,128)(2,1)}, bf16[16,2,128,128]{3,2,1,0:T(8,128)(2,1)}, u32[]{:S(2)}, u32[]{:S(2)}) collective-permute-start(bf16[16,2,128,128]{3,2,1,0:T(8,128)(2,1)} %collective-permute-done.1.rest_6_), channel_id=1, source_target_pairs={{0,32},{4,12},{8,40},{12,20},{16,48},{20,28},{24,56},{28,4},{32,64... | collective-permute-start | bytes 3145736 | tf_op jit(solution)/shard_map/ppermute | solution.py:39
  55.3 32.3 %collective-permute-start.11 = (bf16[16,2,128,128]{3,2,1,0:T(8,128)(2,1)}, bf16[16,2,128,128]{3,2,1,0:T(8,128)(2,1)}, u32[]{:S(2)}, u32[]{:S(2)}) collective-permute-start(bf16[16,2,128,128]{3,2,1,0:T(8,128)(2,1)} %collective-permute-done.7.rest_3_), channel_id=1, source_target_pairs={{0,96},{4,28},{8,104},{12,4},{16,112},{20,12},{24,120},{28,20},{32... | collective-permute-start | bytes 3145736 | tf_op jit(solution)/shard_map/ppermute | solution.py:39
  59.5 31.1 %collective-permute-start.12 = (bf16[2,2,8,128,128]{4,3,2,1,0:T(8,128)(2,1)}, bf16[2,2,8,128,128]{4,3,2,1,0:T(8,128)(2,1)}, u32[]{:S(2)}, u32[]{:S(2)}) collective-permute-start(bf16[2,2,8,128,128]{4,3,2,1,0:T(8,128)(2,1)} %bitcast.4.rest_8_), channel_id=1, source_target_pairs={{0,16},{4,68},{8,24},{12,76},{16,0},{20,84},{24,8},{28,92},{32,48}... | collective-permute-start | bytes 3145736 | tf_op jit(solution)/shard_map/ppermute | solution.py:44
  75.0 33.7 %collective-permute-start.14 = (bf16[16,2,128,128]{3,2,1,0:T(8,128)(2,1)S(1)}, bf16[16,2,128,128]{3,2,1,0:T(8,128)(2,1)S(1)}, u32[]{:S(2)}, u32[]{:S(2)}) collective-permute-start(bf16[16,2,128,128]{3,2,1,0:T(8,128)(2,1)S(1)} %copy-done.4), channel_id=1, source_target_pairs={{0,96},{4,28},{8,104},{12,4},{16,112},{20,12},{24,120},{28,20},{32... | collective-permute-start | bytes 3145736 | tf_op jit(solution)/shard_map/ppermute | solution.py:39
  82.2 26.4 %collective-permute-start.13 = (bf16[16,2,128,128]{3,2,1,0:T(8,128)(2,1)S(1)}, bf16[16,2,128,128]{3,2,1,0:T(8,128)(2,1)S(1)}, u32[]{:S(2)}, u32[]{:S(2)}) collective-permute-start(bf16[16,2,128,128]{3,2,1,0:T(8,128)(2,1)S(1)} %copy-done.4), channel_id=1, source_target_pairs={{0,32},{4,12},{8,40},{12,20},{16,48},{20,28},{24,56},{28,4},{32,64... | collective-permute-start | bytes 3145736 | tf_op jit(solution)/shard_map/ppermute | solution.py:39
  90.6 24.4 %collective-permute-start.17 = (bf16[16,2,128,128]{3,2,1,0:T(8,128)(2,1)S(1)}, bf16[16,2,128,128]{3,2,1,0:T(8,128)(2,1)S(1)}, u32[]{:S(2)}, u32[]{:S(2)}) collective-permute-start(bf16[16,2,128,128]{3,2,1,0:T(8,128)(2,1)S(1)} %copy-done.6), channel_id=1, source_target_pairs={{0,96},{4,28},{8,104},{12,4},{16,112},{20,12},{24,120},{28,20},{32... | collective-permute-start | bytes 3145736 | tf_op jit(solution)/shard_map/ppermute | solution.py:39
  98.1 24.0 %collective-permute-start.15 = (bf16[16,2,128,128]{3,2,1,0:T(8,128)(2,1)S(1)}, bf16[16,2,128,128]{3,2,1,0:T(8,128)(2,1)S(1)}, u32[]{:S(2)}, u32[]{:S(2)}) collective-permute-start(bf16[16,2,128,128]{3,2,1,0:T(8,128)(2,1)S(1)} %copy-done.6), channel_id=1, source_target_pairs={{0,32},{4,12},{8,40},{12,20},{16,48},{20,28},{24,56},{28,4},{32,64... | collective-permute-start | bytes 3145736 | tf_op jit(solution)/shard_map/ppermute | solution.py:39
  115.0 25.5 %collective-permute-start.18 = (bf16[16,2,128,128]{3,2,1,0:T(8,128)(2,1)S(1)}, bf16[16,2,128,128]{3,2,1,0:T(8,128)(2,1)S(1)}, u32[]{:S(2)}, u32[]{:S(2)}) collective-permute-start(bf16[16,2,128,128]{3,2,1,0:T(8,128)(2,1)S(1)} %collective-permute-done.17.rest_3_), channel_id=1, source_target_pairs={{0,96},{4,28},{8,104},{12,4},{16,112},{20,12},{24,120},{28,20},{32... | collective-permute-start | bytes 3145736 | tf_op jit(solution)/shard_map/ppermute | solution.py:39
  118.4 26.7 %collective-permute-start.16 = (bf16[16,2,128,128]{3,2,1,0:T(8,128)(2,1)S(1)}, bf16[16,2,128,128]{3,2,1,0:T(8,128)(2,1)S(1)}, u32[]{:S(2)}, u32[]{:S(2)}) collective-permute-start(bf16[16,2,128,128]{3,2,1,0:T(8,128)(2,1)S(1)} %collective-permute-done.13.rest_6_), channel_id=1, source_target_pairs={{0,32},{4,12},{8,40},{12,20},{16,48},{20,28},{24,56},{28,4},{32,64... | collective-permute-start | bytes 3145736 | tf_op jit(solution)/shard_map/ppermute | solution.py:39
  118.4 26.7 %collective-permute-start.19 = (bf16[2096,128]{1,0:T(8,128)(2,1)S(1)}, bf16[2096,128]{1,0:T(8,128)(2,1)S(1)}, u32[]{:S(2)}, u32[]{:S(2)}) collective-permute-start(bf16[2096,128]{1,0:T(8,128)(2,1)S(1)} %get-tuple-element.118), channel_id=1, source_target_pairs={{0,8},{4,36},{8,16},{12,44},{16,24},{20,52},{24,0},{28,60},{32,40}... | collective-permute-start | bytes 1609736 | tf_op jit(solution)/shard_map/ppermute | solution.py:44
  118.4 26.7 %collective-permute-start.20 = (bf16[2096,128]{1,0:T(8,128)(2,1)S(1)}, bf16[2096,128]{1,0:T(8,128)(2,1)S(1)}, u32[]{:S(2)}, u32[]{:S(2)}) collective-permute-start(bf16[2096,128]{1,0:T(8,128)(2,1)S(1)} %get-tuple-element.119), channel_id=1, source_target_pairs={{0,16},{4,68},{8,24},{12,76},{16,0},{20,84},{24,8},{28,92},{32,48}... | collective-permute-start | bytes 1609736 | tf_op jit(solution)/shard_map/ppermute | solution.py:44
  122.0 24.0 %collective-permute-start.21 = (bf16[2096,128]{1,0:T(8,128)(2,1)S(1)}, bf16[2096,128]{1,0:T(8,128)(2,1)S(1)}, u32[]{:S(2)}, u32[]{:S(2)}) collective-permute-start(bf16[2096,128]{1,0:T(8,128)(2,1)S(1)} %get-tuple-element.120), channel_id=1, source_target_pairs={{0,24},{4,100},{8,0},{12,108},{16,8},{20,116},{24,16},{28,124},{32... | collective-permute-start | bytes 1609736 | tf_op jit(solution)/shard_map/ppermute | solution.py:44
  165.0 27.0 %collective-permute-start.26 = (bf16[2096,128]{1,0:T(8,128)(2,1)}, bf16[2096,128]{1,0:T(8,128)(2,1)}, u32[]{:S(2)}, u32[]{:S(2)}) collective-permute-start(bf16[2096,128]{1,0:T(8,128)(2,1)} %get-tuple-element.137), channel_id=1, source_target_pairs={{0,8},{4,36},{8,16},{12,44},{16,24},{20,52},{24,0},{28,60},{32,40}... | collective-permute-start | bytes 1609736 | tf_op jit(solution)/shard_map/ppermute | solution.py:44
  165.9 26.1 %collective-permute-start.27 = (bf16[2096,128]{1,0:T(8,128)(2,1)}, bf16[2096,128]{1,0:T(8,128)(2,1)}, u32[]{:S(2)}, u32[]{:S(2)}) collective-permute-start(bf16[2096,128]{1,0:T(8,128)(2,1)} %get-tuple-element.138), channel_id=1, source_target_pairs={{0,16},{4,68},{8,24},{12,76},{16,0},{20,84},{24,8},{28,92},{32,48}... | collective-permute-start | bytes 1609736 | tf_op jit(solution)/shard_map/ppermute | solution.py:44
  168.9 23.1 %collective-permute-start.28 = (bf16[2096,128]{1,0:T(8,128)(2,1)}, bf16[2096,128]{1,0:T(8,128)(2,1)}, u32[]{:S(2)}, u32[]{:S(2)}) collective-permute-start(bf16[2096,128]{1,0:T(8,128)(2,1)} %get-tuple-element.139), channel_id=1, source_target_pairs={{0,24},{4,100},{8,0},{12,108},{16,8},{20,116},{24,16},{28,124},{32... | collective-permute-start | bytes 1609736 | tf_op jit(solution)/shard_map/ppermute | solution.py:44
  170.2 15.1 %collective-permute-start.25 = (bf16[2,1024,128]{2,1,0:T(8,128)(2,1)S(1)}, bf16[2,1024,128]{2,1,0:T(8,128)(2,1)}, u32[]{:S(2)}, u32[]{:S(2)}) collective-permute-start(bf16[2,1024,128]{2,1,0:T(8,128)(2,1)S(1)} %finish.2.a0), channel_id=1, source_target_pairs={{0,2},{1,3},{2,0},{3,1},{4,6},{5,7},{6,4},{7,5},{8,10},{9,11},{10,... | collective-permute-start | bytes 1572872 | tf_op jit(solution)/shard_map/ppermute | solution.py:57
  196.8 25.3 %collective-permute-start.31 = (bf16[2,1024,128]{2,1,0:T(8,128)(2,1)S(1)}, bf16[2,1024,128]{2,1,0:T(8,128)(2,1)S(1)}, u32[]{:S(2)}, u32[]{:S(2)}) collective-permute-start(bf16[2,1024,128]{2,1,0:T(8,128)(2,1)S(1)} %finish.3.a0), channel_id=1, source_target_pairs={{0,2},{1,3},{2,0},{3,1},{4,6},{5,7},{6,4},{7,5},{8,10},{9,11},{10,... | collective-permute-start | bytes 1572872 | tf_op jit(solution)/shard_map/ppermute | solution.py:57
  199.2 23.5 %collective-permute-start.30 = (bf16[2,1024,128]{2,1,0:T(8,128)(2,1)S(1)}, bf16[2,1024,128]{2,1,0:T(8,128)(2,1)S(1)}, u32[]{:S(2)}, u32[]{:S(2)}) collective-permute-start(bf16[2,1024,128]{2,1,0:T(8,128)(2,1)S(1)} %finish.3.a0), channel_id=1, source_target_pairs={{0,3},{1,0},{2,1},{3,2},{4,7},{5,4},{6,5},{7,6},{8,11},{9,8},{10,9... | collective-permute-start | bytes 1572872 | tf_op jit(solution)/shard_map/ppermute | solution.py:57
  (36 other events, 448.8 us)

commit v4 on v3

--- a/solution.py
+++ b/solution.py
@@ -65,33 +65,27 @@
     return lax.dot_general(a, b, (((1,), (0,)), ((), ())), preferred_element_type=F32)
 
 
-def split_cache_kernel(core_ref, keep_ref, send_ref, keep, send):
-    for src, out in ((keep_ref, keep), (send_ref, send)):
-        for b in range(2):
-            rows = slice(b * BLOCK, (b + 1) * BLOCK)
-            out[b, 0] = src[0, rows, 0, :]
-            out[b, 1] = src[0, rows, 1, :].T
-
-
-def split_cache(j, core, rows):
-    out = jax.ShapeDtypeStruct((16, 2, BLOCK, HD), BF16)
-    block = pl.BlockSpec((2, 2, BLOCK, HD), lambda i, c: (i, 0, 0, 0))
+def split_cache_kernel(head_ref, src, out):
+    for b in range(2):
+        rows = slice(b * BLOCK, (b + 1) * BLOCK)
+        out[b, 0] = src[0, rows, 0, :]
+        out[b, 1] = src[0, rows, 1, :].T
+
+
+def split_cache(head, rows, holders=1):
     return pl.pallas_call(
         split_cache_kernel,
         grid_spec=pltpu.PrefetchScalarGridSpec(
             num_scalar_prefetch=1,
             grid=(8,),
-            in_specs=[
-                pl.BlockSpec((1, 256, 2, HD), lambda i, c: (i // 4, i % 4, 0, 2 * c[0] + j)),
-                pl.BlockSpec((1, 256, 2, HD), lambda i, c: (i // 4, i % 4, 0, 2 - 2 * c[0] + j)),
-            ],
-            out_specs=[block, block],
+            in_specs=[pl.BlockSpec((1, 256, 2, HD), lambda i, h: (i // 4, i % 4, 0, h[0]))],
+            out_specs=pl.BlockSpec((2, 2, BLOCK, HD), lambda i, h: (i, 0, 0, 0)),
         ),
-        out_shape=[out, out],
+        out_shape=jax.ShapeDtypeStruct((16 * holders, 2, BLOCK, HD), BF16),
         compiler_params=params(),
         cost_estimate=BRIEF,
         name="split_cache",
-    )(core, rows, rows)
+    )(head, rows)
 
 
 def project_kernel(core_ref, tok_ref, gain_ref, wq, wk, wv, q_all, swap, k_all, v_all, edge):
@@ -169,7 +163,7 @@
             jax.ShapeDtypeStruct((1024, HD), BF16),
         ],
         compiler_params=params(),
-        cost_estimate=pl.CostEstimate(flops=2 * n * d * 3 * w, transcendentals=0, bytes_accessed=16 << 20),
+        cost_estimate=BRIEF,
         name="project",
     )(core, tokens, gain.reshape(1, d), wq, wk, wv)
 
@@ -265,11 +259,12 @@
 
 
 def far_kernel(j, cnt_ref, unit_ref, first_ref, long_ref, size_ref, *rest):
-    sources, qs, outs = rest[:8], rest[8:12], rest[12:16]
-    kvbuf, qbuf, obuf, acc_ref, stat_ref, logs, kvsem, qsem, osem = rest[16:]
+    sources, qs, outs = rest[:5], rest[5:9], rest[9:13]
+    kvbuf, qbuf, obuf, acc_ref, stat_ref, logs, kvsem, qsem, osem = rest[13:]
     units = size_ref[0]
     copies = [pltpu.make_async_copy(qs[r].at[:, j], qbuf.at[pl.ds(2 * r, 2)], qsem.at[r]) for r in range(4)]
-    copies += [pltpu.make_async_copy(sources[k], kvbuf.at[pl.ds(16 * k, 16)], kvsem.at[k]) for k in range(8)]
+    for k, (first, size) in enumerate(((0, 32), (32, 32), (64, 16), (80, 16), (96, 32))):
+        copies.append(pltpu.make_async_copy(sources[k], kvbuf.at[pl.ds(first, size)], kvsem.at[k]))
     for copy in copies:
         copy.start()
     logs[...] = jnp.full((64, BLOCK), NEG, F32)
@@ -338,7 +333,7 @@
     out = jax.ShapeDtypeStruct((OROWS, BLOCK), BF16)
     return pl.pallas_call(
         functools.partial(far_kernel, j),
-        in_specs=[SMEM] * 5 + [ANY] * 12,
+        in_specs=[SMEM] * 5 + [ANY] * 9,
         out_specs=[ANY] * 4,
         out_shape=[out] * 4,
         scratch_shapes=[
@@ -348,7 +343,7 @@
             pltpu.VMEM((UNITS, HD, BLOCK), F32),
             pltpu.VMEM((UNITS, 8, BLOCK), F32),
             pltpu.VMEM((64, BLOCK), F32),
-            pltpu.SemaphoreType.DMA((8,)),
+            pltpu.SemaphoreType.DMA((5,)),
             pltpu.SemaphoreType.DMA((4,)),
             pltpu.SemaphoreType.DMA((4,)),
         ],
@@ -422,48 +417,54 @@
     )(o, lse, o, lse, far_keep, far_other)
 
 
-def mix_kernel(last, place_ref, a0, a1, a2, a3, *rest):
-    weights, carried, out = rest[:8], rest[8], rest[-1]
-    total = carried[...].astype(F32) if carried is not out else None
-    left = jnp.concatenate([a[s] for a in (a0, a1, a2, a3) for s in range(2)], axis=1)
-    term = nn(left, jnp.concatenate([w[...] for w in weights], axis=0))
-    total = term if total is None else total + term
-    if last:
-        total = total + rest[9][...]
-    out[...] = total.astype(out.dtype)
-
-
-def mix(j, place, parts, w_out, carried, acc=None):
-    n, cols = 1024, 512
-
-    def weight(rel, s):
-        def at(i, p):
-            head = (2 * p[0] + 2 * s + j) % 4
-            return ((p[1] + rel) % NX * 4 + head, p[1])
-
-        return pl.BlockSpec((HD, cols), at)
-
-    last = acc is not None
-    in_specs = [pl.BlockSpec((2, 256, HD), lambda i, p: (0, i, 0))] * 4
-    in_specs += [weight(rel, s) for rel in range(4) for s in range(2)]
-    args = list(parts) + [w_out] * 8
-    if last:
-        in_specs.append(pl.BlockSpec((256, cols), lambda i, p: (i, p[1])))
-        in_specs.append(pl.BlockSpec((256, cols), lambda i, p: (i, 0)))
-        args += [carried, acc]
-    return pl.pallas_call(
-        functools.partial(mix_kernel, last),
+def pick_kernel(place_ref, *rest):
+    for j in range(2):
+        for k in range(8):
+            rest[16 + j][k * HD : (k + 1) * HD, :] = rest[j * 8 + k][...]
+
+
+def pick(place, w_out):
+    def weight(j, rel, s):
+        return pl.BlockSpec((HD, 512), lambda i, p: ((p[1] + rel) % NX * 4 + (2 * p[0] + 2 * s + j) % 4, p[1]))
+
+    out = jax.ShapeDtypeStruct((1024, 512), BF16)
+    return pl.pallas_call(
+        pick_kernel,
         grid_spec=pltpu.PrefetchScalarGridSpec(
             num_scalar_prefetch=1,
-            grid=(n // 256,),
-            in_specs=in_specs,
-            out_specs=pl.BlockSpec((256, cols), lambda i, p: (i, 0)),
+            grid=(1,),
+            in_specs=[weight(j, rel, s) for j in range(2) for rel in range(4) for s in range(2)],
+            out_specs=[pl.BlockSpec((1024, 512), lambda i, p: (0, 0))] * 2,
         ),
-        out_shape=jax.ShapeDtypeStruct((n, cols), BF16 if last else F32),
+        out_shape=[out, out],
+        compiler_params=params(),
+        cost_estimate=BRIEF,
+        name="pick",
+    )(place, *[w_out] * 16)
+
+
+def mix_kernel(place_ref, a0, a1, a2, a3, weight, carried, out):
+    left = jnp.concatenate([a[s] for a in (a0, a1, a2, a3) for s in range(2)], axis=1)
+    out[...] = (carried[...].astype(F32) + nn(left, weight[...])).astype(out.dtype)
+
+
+def mix(place, parts, weight, carried, kind):
+    column = 0 if carried.shape[1] == 512 else 1
+    return pl.pallas_call(
+        mix_kernel,
+        grid_spec=pltpu.PrefetchScalarGridSpec(
+            num_scalar_prefetch=1,
+            grid=(4,),
+            in_specs=[pl.BlockSpec((2, 256, HD), lambda i, p: (0, i, 0))] * 4
+            + [pl.BlockSpec((1024, 512), lambda i, p: (0, 0))]
+            + [pl.BlockSpec((256, 512), lambda i, p: (i, p[1] * column))],
+            out_specs=pl.BlockSpec((256, 512), lambda i, p: (i, 0)),
+        ),
+        out_shape=jax.ShapeDtypeStruct((1024, 512), kind),
         compiler_params=params(),
         cost_estimate=BRIEF,
         name="mix",
-    )(place, *args)
+    )(place, *parts, weight, carried)
 
 
 def line_codes(wake_blocks, wake_frames, wake_counts, y, z, c):
@@ -494,30 +495,31 @@
     def after(x, *deps):
         return lax.optimization_barrier((x, *deps))[0]
 
-    keep0, send0 = split_cache(0, core, kv_cache)
-    up_k0, down_k0 = rows_perm(keep0, 1), rows_perm(keep0, -1)
-    got0 = core_swap(send0)
-    up_r0, down_r0 = rows_perm(got0, 1), rows_perm(got0, -1)
-    keep1, send1 = split_cache(1, after(core, got0), kv_cache)
-    got1 = core_swap(send1)
-
-    gain, up_k0, down_k0 = lax.optimization_barrier((norm_gain, up_k0, down_k0, got1))[:3]
-    up20 = rows_perm(up_k0, 1)
+    def rows_of(j, gate):
+        got = core_swap(split_cache(2 - 2 * gate + j, kv_cache))
+        return lax.dynamic_update_slice(split_cache(2 * gate + j, kv_cache, 2), got, (16, 0, 0, 0))
+
+    rows0 = rows_of(0, core)
+    up0, down0 = rows_perm(rows0, 1), rows_perm(rows0, -1)
+    rows1 = rows_of(1, after(core, rows0))
+
+    gain, rows1 = lax.optimization_barrier((norm_gain, rows1))
     q_all, swap, k_all, v_all, edge = project(core, tokens, gain, w_query, w_key, w_value)
     swapped, halo = core_swap(swap), halo_perm(edge)
     mine = jnp.concatenate([q_all[:2], swapped[:2048].reshape(2, 1024, HD)], axis=0).reshape(2, 2, 8, BLOCK, HD)
-    mine, halo, up_r0, down_r0 = lax.optimization_barrier((mine, halo, up_r0, down_r0))
-    down20 = rows_perm(down_r0, -1)
+    mine, halo, up0, down0 = lax.optimization_barrier((mine, halo, up0, down0))
+    up20, down20 = rows_perm(up0[:16], 1), rows_perm(down0[16:], -1)
     q1, q3, q2 = query_perm(mine, -1), query_perm(mine, 1), query_perm(mine, 2)
 
     near_o, near_lse = near(core, q_all, k_all, v_all, after(halo, mine), swapped)
     code, cnt = line_codes(wake_blocks, wake_frames, wake_counts, y, z, c)
     lists = plan(cnt, code)
-    keep1, near_o, near_lse, q1, q3, *lists = lax.optimization_barrier((keep1, near_o, near_lse, q1, q3, *lists))
-    up_k1, down_k1 = rows_perm(keep1, 1), rows_perm(keep1, -1)
-    got1, up20, down20, q2 = lax.optimization_barrier((got1, up20, down20, q2, near_o))[:4]
+    weights = pick(after(place, mine), w_out)
+    held = (*weights, rows1, near_o, near_lse, up20, down20, q1, q2, q3, *lists)
+    *weights, rows1, near_o, near_lse, up20, down20, q1, q2, q3, e, f, g, h = lax.optimization_barrier(held)
+    lists = [e, f, g, h]
+    up1, down1 = rows_perm(rows1, 1), rows_perm(rows1, -1)
     qs = [mine, q1, q2, q3]
-    up_r1, down_r1 = rows_perm(got1, 1), rows_perm(got1, -1)
 
     def returned(parts):
         return [parts[0], query_perm(parts[1], 1), query_perm(parts[2], 2), query_perm(parts[3], -1)]
@@ -525,27 +527,24 @@
     def gather(heads):
         return [heads, mp_perm(heads, -1), mp_perm(heads, 2), mp_perm(heads, 1)]
 
-    sources = [keep0, got0, down_k0, down_r0, up20, down20, up_k0, up_r0]
-    parts = far(0, cnt, lists, sources, qs)
-    *parts, up_k1, down_k1 = lax.optimization_barrier((*parts, up_k1, down_k1))
+    parts = far(0, cnt, lists, [rows0, down0, up20, down20, up0], qs)
     back = returned(parts)
-    up21 = rows_perm(up_k1, 1)
-    down21 = rows_perm(down_r1, -1)
-    back[0], up_r1, up21, down21 = lax.optimization_barrier((back[0], up_r1, up21, down21))
+    back[1], back[3], up1, down1 = lax.optimization_barrier((back[1], back[3], up1, down1))
+    up21, down21 = rows_perm(up1[:16], 1), rows_perm(down1[16:], -1)
+    near_lse, up21, down21 = lax.optimization_barrier((near_lse, up21, down21))
     own, other = merge(back)
     heads = finish(0, near_o, near_lse, own, core_swap(other))
     gathered = gather(heads)
 
-    sources = [after(keep1, heads), got1, down_k1, down_r1, up21, down21, up_k1, up_r1]
-    parts = far(1, cnt, lists, sources, qs)
+    parts = far(1, cnt, lists, [after(rows1, heads), down1, up21, down21, up1], qs)
     *parts, gathered[1], gathered[3] = lax.optimization_barrier((*parts, gathered[1], gathered[3]))
     back = returned(parts)
     gathered[0] = after(gathered[0], parts[0])
-    acc = mix(0, place, gathered, w_out, tokens, None)
+    acc = mix(place, gathered, weights[0], tokens, F32)
     back[0], acc = lax.optimization_barrier((back[0], acc))
     own, other = merge(back)
     heads = finish(1, near_o, near_lse, own, core_swap(other))
-    return mix(1, place, gather(heads), w_out, tokens, acc)
+    return mix(place, gather(heads), weights[1], acc, BF16)
 
 
 def solution(mesh):

time: 228 us -> 228 us (level)
  starting transfers between devices: 55.9 us -> 44 us
  local copies, waits for them, and re-layouts: 9.55 us -> 18.7 us
    ppermute x12 -> x8, starting transfers between devices: 30.4 us -> 13.8 us  [rows_perm(): return lax.ppermute(x, 'tok', pairs)]
    ppermute x9, waiting for transfers between devices: 3.01 us -> 11.7 us  [query_perm(): return lax.ppermute(x, 'tok', pairs)]
    slice x0 -> x4, local copies, waits for them, and re-layouts: none -> 4.8 us  [the longest x2 4.63 us: on_device(): up20, down20 = (rows_perm(up0[:16], 1), rows_perm(down0[16:], -1))]
    pallas_call x2 -> x4, Pallas kernels: 17.7 us -> 22 us  [split_cache(): pl.pallas_call(split_cache_kernel, grid_spec=pltpu.PrefetchScalarGridSpec...]
    pallas_call x2, Pallas kernels: 22.1 us -> 18.5 us  [far(): pl.pallas_call(functools.partial(far_kernel, j), in_specs=[SMEM] * 5 + [A...]
    ppermute x12 -> x8, waiting for transfers between devices: 35.6 us -> 32.1 us  [rows_perm(): return lax.ppermute(x, 'tok', pairs)]
    ppermute x5, starting transfers between devices: 3.14 us -> 5.84 us  [core_swap(): lax.ppermute(x, 'tok', [(tok_of(y, z, c), tok_of(y, z, 1 - c)) for y, z,...]
    unnamed x54 -> x36, local copies, waits for them, and re-layouts: 8.88 us -> 7.6 us
  transfers between devices with their start and end apart: 33 -> 29, of which waited for: 15 -> 14; matrix products, arithmetic and copies ran while one was open for 1% -> 5% of each run, Pallas kernels for 28% -> 29%
where the time goes in v4:
time: 228 us; the launch traced here: 227 us
  waiting for transfers between devices  82.6 us (36%)
  Pallas kernels  80.4 us (35%)
  starting transfers between devices  44 us (19%)
  local copies, waits for them, and re-layouts  18.7 us (8%)
    ppermute x6, waiting for transfers between devices, mp_perm(): return lax.ppermute(x, 'mp', [(i, (i + d) % NX) for i in range(NX)])  34.2 us
    ppermute x8, waiting for transfers between devices, rows_perm(): return lax.ppermute(x, 'tok', pairs)  32.1 us
    pallas_call x4, Pallas kernels, split_cache(): pl.pallas_call(split_cache_kernel, grid_spec=pltpu.PrefetchScalarGridSpec...  22 us
    pallas_call x2, Pallas kernels, far(): pl.pallas_call(functools.partial(far_kernel, j), in_specs=[SMEM] * 5 + [A...  18.5 us
    pallas_call x1, Pallas kernels, project(): pl.pallas_call(project_kernel, grid_spec=pltpu.PrefetchScalarGridSpec(num...  15.7 us
    ppermute x8, starting transfers between devices, rows_perm(): return lax.ppermute(x, 'tok', pairs)  13.8 us
    ppermute x9, starting transfers between devices, query_perm(): return lax.ppermute(x, 'tok', pairs)  13.4 us
    ppermute x9, waiting for transfers between devices, query_perm(): return lax.ppermute(x, 'tok', pairs)  11.7 us
  transfers between devices with their start and end apart: 29, of which 14 were waited for; matrix products, arithmetic and copies ran while one was open for 5% of the time, Pallas kernels for 29%

profile of v4, /device:TPU:1, one launch (start us, length us, event | category | flops | bytes accessed | tf_op | source)
XLA Modules:
  0.0 227.2 jit_solution(823017488309154308)
XLA Ops:
  2.2 4.5 %split_cache.5 = bf16[16,2,128,128]{3,2,1,0:T(8,128)(2,1)S(1)} custom-call(s32[1]{0:T(128)S(6)} %sub.18.head_ref, bf16[2,1024,2,512]{3,2,1,0:T(2,128)(2,1)S(1)} %copy-done), custom_call_target="tpu_custom_call" | custom-call | flops 1 | bytes 1 | tf_op jit(solution)/shard_map/split_cache/pallas_call | solution.py:76
  8.2 6.1 %split_cache.4 = bf16[32,2,128,128]{3,2,1,0:T(8,128)(2,1)S(1)} custom-call(s32[1]{0:T(128)S(6)} %mul.35.head_ref, bf16[2,1024,2,512]{3,2,1,0:T(2,128)(2,1)} %src.7), custom_call_target="tpu_custom_call" | custom-call | flops 1 | bytes 1 | tf_op jit(solution)/shard_map/split_cache/pallas_call | solution.py:76
  14.6 4.5 %split_cache.7 = bf16[16,2,128,128]{3,2,1,0:T(8,128)(2,1)S(1)} custom-call(s32[1]{0:T(128)S(6)} %add.47.head_ref, bf16[2,1024,2,512]{3,2,1,0:T(2,128)(2,1)S(1)} %copy-done.1), custom_call_target="tpu_custom_call" | custom-call | flops 1 | bytes 1 | tf_op jit(solution)/shard_map/split_cache/pallas_call | solution.py:76
  19.2 3.9 %collective-permute-start.5 = (bf16[32,2,128,128]{3,2,1,0:T(8,128)(2,1)S(1)}, bf16[32,2,128,128]{3,2,1,0:T(8,128)(2,1)}, u32[]{:S(2)}, u32[]{:S(2)}) collective-permute-start(bf16[32,2,128,128]{3,2,1,0:T(8,128)(2,1)S(1)} %constant_dynamic-update-slice_fusion.1.rest_0_), channel_id=1, source_target_pairs={{0,96},{4,28},{8,104},{12,4},{16,112},{20,12},{24,120},{28,20},{32... | collective-permute-start | bytes 6291464 | tf_op jit(solution)/shard_map/ppermute | solution.py:39
  23.1 6.9 %split_cache.6 = bf16[32,2,128,128]{3,2,1,0:T(8,128)(2,1)} custom-call(s32[1]{0:T(128)S(6)} %add.46.head_ref, bf16[2,1024,2,512]{3,2,1,0:T(2,128)(2,1)} %src.7), custom_call_target="tpu_custom_call" | custom-call | flops 1 | bytes 1 | tf_op jit(solution)/shard_map/split_cache/pallas_call | solution.py:76
  31.1 15.7 %project.1 = (bf16[4,1024,128]{2,1,0:T(8,128)(2,1)S(1)}, bf16[3072,128]{1,0:T(8,128)(2,1)}, bf16[4,8,128,128]{3,2,1,0:T(8,128)(2,1)S(1)}, bf16[4,8,128,128]{3,2,1,0:T(8,128)(2,1)S(1)}, bf16[1024,128]{1,0:T(8,128)(2,1)}) custom-call(s32[1]{0:T(128)} %bitcast.core_ref, bf16[1024,2048]{1,0:T(8,128)(2,1)} %carried.1, f32[1,2048]{1,0:T(1,128)S(1)} %bitcast.24, ...), custom_call_target="tpu_custom_call" | custom-call | flops 1 | bytes 1 | tf_op jit(solution)/shard_map/project/pallas_call | solution.py:138
  65.8 5.3 %collective-permute-start.7 = (bf16[16,2,128,128]{3,2,1,0:T(8,128)(2,1)}, bf16[16,2,128,128]{3,2,1,0:T(8,128)(2,1)S(1)}, u32[]{:S(2)}, u32[]{:S(2)}) collective-permute-start(bf16[16,2,128,128]{3,2,1,0:T(8,128)(2,1)} %slice.21), channel_id=1, source_target_pairs={{0,96},{4,28},{8,104},{12,4},{16,112},{20,12},{24,120},{28,20},{32... | collective-permute-start | bytes 3145736 | tf_op jit(solution)/shard_map/ppermute | solution.py:39
  76.1 2.8 %plan.1 = (s32[100]{0:T(128)S(1)}, s32[64]{0:T(128)S(1)}, s32[64]{0:T(128)S(1)}, s32[2]{0:T(128)S(1)}) custom-call(s32[64]{0:T(128)S(1)} %reduce_sum.12.cnt_ref, s32[512]{0:T(512)S(1)} %reshape.77.code_ref), custom_call_target="tpu_custom_call" | custom-call | flops 1 | bytes 1 | tf_op jit(solution)/shard_map/plan/pallas_call | solution.py:249
  81.9 9.6 %near.1 = (f32[4,8,128,128]{3,2,1,0:T(8,128)}, f32[4,8,128]{2,1,0:T(8,128)S(1)}) custom-call(s32[1]{0:T(128)} %bitcast.core_ref, bf16[4,1024,128]{2,1,0:T(8,128)(2,1)S(1)} %copy-done.7, bf16[4,8,128,128]{3,2,1,0:T(8,128)(2,1)S(1)} %copy-done.9, bf16[4,8,128,128]{3,2,1,0:T(8,128)(2,1)S(1)} %copy-done.11, bf16[8,128,128]{2,1,0:T(8,128)(2,1)S(1)} %bitcast.22, ...), custom_call_target="tpu_custom_call" | custom-call | flops 1 | bytes 1 | tf_op jit(solution)/shard_map/near/pallas_call | solution.py:194
  91.4 6.6 %collective-permute-done.7.rest_3_ = bf16[16,2,128,128]{3,2,1,0:T(8,128)(2,1)S(1)} collective-permute-done((bf16[16,2,128,128]{3,2,1,0:T(8,128)(2,1)}, bf16[16,2,128,128]{3,2,1,0:T(8,128)(2,1)S(1)}, u32[]{:S(2)}, u32[]{:S(2)}) %collective-permute-start.7) | collective-permute-done | bytes 1048608 | tf_op jit(solution)/shard_map/ppermute | solution.py:39
  98.2 3.1 %collective-permute-start.14 = (bf16[32,2,128,128]{3,2,1,0:T(8,128)(2,1)}, bf16[32,2,128,128]{3,2,1,0:T(8,128)(2,1)S(1)}, u32[]{:S(2)}, u32[]{:S(2)}) collective-permute-start(bf16[32,2,128,128]{3,2,1,0:T(8,128)(2,1)} %constant_dynamic-update-slice_fusion.rest_0_), channel_id=1, source_target_pairs={{0,96},{4,28},{8,104},{12,4},{16,112},{20,12},{24,120},{28,20},{32... | collective-permute-start | bytes 6291464 | tf_op jit(solution)/shard_map/ppermute | solution.py:39
  101.2 9.3 %far.2 = (bf16[2096,128]{1,0:T(8,128)(2,1)S(1)}, bf16[2096,128]{1,0:T(8,128)(2,1)S(1)}, bf16[2096,128]{1,0:T(8,128)(2,1)S(1)}, bf16[2096,128]{1,0:T(8,128)(2,1)S(1)}) custom-call(s32[64]{0:T(128)S(1)} %reduce_sum.12.cnt_ref, s32[100]{0:T(128)S(1)} %get-tuple-element.94.unit_ref, s32[64]{0:T(128)S(1)} %get-tuple-element.95.first_ref, ...), custom_call_target="tpu_custom_call" | custom-call | flops 1 | bytes 1 | tf_op jit(solution)/shard_map/far/pallas_call | solution.py:334
  114.4 11.6 %collective-permute-done.11.b = bf16[2096,128]{1,0:T(8,128)(2,1)S(1)} collective-permute-done((bf16[2096,128]{1,0:T(8,128)(2,1)S(1)}, bf16[2096,128]{1,0:T(8,128)(2,1)S(1)}, u32[]{:S(2)}, u32[]{:S(2)}) %collective-permute-start.11) | collective-permute-done | bytes 536608 | tf_op jit(solution)/shard_map/ppermute | solution.py:44
  126.1 9.9 %collective-permute-done.14.rest_1_ = bf16[32,2,128,128]{3,2,1,0:T(8,128)(2,1)S(1)} collective-permute-done((bf16[32,2,128,128]{3,2,1,0:T(8,128)(2,1)}, bf16[32,2,128,128]{3,2,1,0:T(8,128)(2,1)S(1)}, u32[]{:S(2)}, u32[]{:S(2)}) %collective-permute-start.14) | collective-permute-done | bytes 2097184 | tf_op jit(solution)/shard_map/ppermute | solution.py:39
  136.0 3.3 %collective-permute-done.13.rest_4_ = bf16[32,2,128,128]{3,2,1,0:T(8,128)(2,1)S(1)} collective-permute-done((bf16[32,2,128,128]{3,2,1,0:T(8,128)(2,1)}, bf16[32,2,128,128]{3,2,1,0:T(8,128)(2,1)S(1)}, u32[]{:S(2)}, u32[]{:S(2)}) %collective-permute-start.13) | collective-permute-done | bytes 2097184 | tf_op jit(solution)/shard_map/ppermute | solution.py:39
  144.3 10.6 %collective-permute-done.16.rest_3_ = bf16[16,2,128,128]{3,2,1,0:T(8,128)(2,1)S(1)} collective-permute-done((bf16[16,2,128,128]{3,2,1,0:T(8,128)(2,1)S(1)}, bf16[16,2,128,128]{3,2,1,0:T(8,128)(2,1)S(1)}, u32[]{:S(2)}, u32[]{:S(2)}) %collective-permute-start.16) | collective-permute-done | bytes 1048608 | tf_op jit(solution)/shard_map/ppermute | solution.py:39
  159.5 9.3 %far.3 = (bf16[2096,128]{1,0:T(8,128)(2,1)S(1)}, bf16[2096,128]{1,0:T(8,128)(2,1)S(1)}, bf16[2096,128]{1,0:T(8,128)(2,1)S(1)}, bf16[2096,128]{1,0:T(8,128)(2,1)S(1)}) custom-call(s32[64]{0:T(128)S(1)} %reduce_sum.12.cnt_ref, s32[100]{0:T(128)S(1)} %get-tuple-element.94.unit_ref, s32[64]{0:T(128)S(1)} %get-tuple-element.95.first_ref, ...), custom_call_target="tpu_custom_call" | custom-call | flops 1 | bytes 1 | tf_op jit(solution)/shard_map/far/pallas_call | solution.py:334
  170.4 4.2 %collective-permute-start.23 = (bf16[2096,128]{1,0:T(8,128)(2,1)S(1)}, bf16[2096,128]{1,0:T(8,128)(2,1)S(1)}, u32[]{:S(2)}, u32[]{:S(2)}) collective-permute-start(bf16[2096,128]{1,0:T(8,128)(2,1)S(1)} %get-tuple-element.129), channel_id=1, source_target_pairs={{0,16},{4,68},{8,24},{12,76},{16,0},{20,84},{24,8},{28,92},{32,48}... | collective-permute-start | bytes 1609736 | tf_op jit(solution)/shard_map/ppermute | solution.py:44
  177.1 10.5 %collective-permute-done.21.a2 = bf16[2,1024,128]{2,1,0:T(8,128)(2,1)S(1)} collective-permute-done((bf16[2,1024,128]{2,1,0:T(8,128)(2,1)S(1)}, bf16[2,1024,128]{2,1,0:T(8,128)(2,1)S(1)}, u32[]{:S(2)}, u32[]{:S(2)}) %collective-permute-start.21) | collective-permute-done | bytes 524320 | tf_op jit(solution)/shard_map/ppermute | solution.py:57
  187.5 4.0 %mix.2.carried = f32[1024,512]{1,0:T(8,128)S(1)} custom-call(s32[2]{0:T(128)S(1)} %pad_add_fusion.place_ref, bf16[2,1024,128]{2,1,0:T(8,128)(2,1)S(1)} %finish.2.a0, bf16[2,1024,128]{2,1,0:T(8,128)(2,1)S(1)} %collective-permute-done.19.a1, bf16[2,1024,128]{2,1,0:T(8,128)(2,1)S(1)} %collective-permute-done.21.a2, ...), custom_call_target="tpu_custom_call" | custom-call | flops 1 | bytes 1 | tf_op jit(solution)/shard_map/mix/pallas_call | solution.py:453
  192.1 3.0 %collective-permute-start.25 = (f32[1032,128]{1,0:T(8,128)S(1)}, f32[1032,128]{1,0:T(8,128)S(1)}, u32[]{:S(2)}, u32[]{:S(2)}) collective-permute-start(f32[1032,128]{1,0:T(8,128)S(1)} %get-tuple-element.132), channel_id=1, source_target_pairs={{0,4},{4,0},{8,12},{12,8},{16,20},{20,16},{24,28},{28,24},{32,36},... | collective-permute-start | bytes 1585160 | tf_op jit(solution)/shard_map/ppermute | solution.py:48
  201.6 9.8 %collective-permute-done.28.a3 = bf16[2,1024,128]{2,1,0:T(8,128)(2,1)S(1)} collective-permute-done((bf16[2,1024,128]{2,1,0:T(8,128)(2,1)S(1)}, bf16[2,1024,128]{2,1,0:T(8,128)(2,1)S(1)}, u32[]{:S(2)}, u32[]{:S(2)}) %collective-permute-start.28) | collective-permute-done | bytes 524320 | tf_op jit(solution)/shard_map/ppermute | solution.py:57
  211.4 12.4 %collective-permute-done.27.a2 = bf16[2,1024,128]{2,1,0:T(8,128)(2,1)S(1)} collective-permute-done((bf16[2,1024,128]{2,1,0:T(8,128)(2,1)S(1)}, bf16[2,1024,128]{2,1,0:T(8,128)(2,1)S(1)}, u32[]{:S(2)}, u32[]{:S(2)}) %collective-permute-start.27) | collective-permute-done | bytes 524320 | tf_op jit(solution)/shard_map/ppermute | solution.py:57
  223.8 3.4 %mix.3 = bf16[1024,512]{1,0:T(8,128)(2,1)} custom-call(s32[2]{0:T(128)S(1)} %pad_add_fusion.place_ref, bf16[2,1024,128]{2,1,0:T(8,128)(2,1)S(1)} %finish.3.a0, bf16[2,1024,128]{2,1,0:T(8,128)(2,1)S(1)} %collective-permute-done.26.a1, bf16[2,1024,128]{2,1,0:T(8,128)(2,1)S(1)} %collective-permute-done.27.a2, ...), custom_call_target="tpu_custom_call" | custom-call | flops 1 | bytes 1 | tf_op jit(solution)/shard_map/mix/pallas_call | solution.py:453
  (108 shorter events, 56.6 us)
Async XLA Ops:
  19.2 36.6 %collective-permute-start.5 = (bf16[32,2,128,128]{3,2,1,0:T(8,128)(2,1)S(1)}, bf16[32,2,128,128]{3,2,1,0:T(8,128)(2,1)}, u32[]{:S(2)}, u32[]{:S(2)}) collective-permute-start(bf16[32,2,128,128]{3,2,1,0:T(8,128)(2,1)S(1)} %constant_dynamic-update-slice_fusion.1.rest_0_), channel_id=1, source_target_pairs={{0,96},{4,28},{8,104},{12,4},{16,112},{20,12},{24,120},{28,20},{32... | collective-permute-start | bytes 6291464 | tf_op jit(solution)/shard_map/ppermute | solution.py:39
  23.1 32.7 %collective-permute-start.4 = (bf16[32,2,128,128]{3,2,1,0:T(8,128)(2,1)S(1)}, bf16[32,2,128,128]{3,2,1,0:T(8,128)(2,1)}, u32[]{:S(2)}, u32[]{:S(2)}) collective-permute-start(bf16[32,2,128,128]{3,2,1,0:T(8,128)(2,1)S(1)} %constant_dynamic-update-slice_fusion.1.rest_0_), channel_id=1, source_target_pairs={{0,32},{4,12},{8,40},{12,20},{16,48},{20,28},{24,56},{28,4},{32,64... | collective-permute-start | bytes 6291464 | tf_op jit(solution)/shard_map/ppermute | solution.py:39
  55.8 42.3 %collective-permute-start.10 = (bf16[2,2,8,128,128]{4,3,2,1,0:T(8,128)(2,1)S(1)}, bf16[2,2,8,128,128]{4,3,2,1,0:T(8,128)(2,1)}, u32[]{:S(2)}, u32[]{:S(2)}) collective-permute-start(bf16[2,2,8,128,128]{4,3,2,1,0:T(8,128)(2,1)S(1)} %bitcast.15), channel_id=1, source_target_pairs={{0,8},{4,36},{8,16},{12,44},{16,24},{20,52},{24,0},{28,60},{32,40}... | collective-permute-start | bytes 3145736 | tf_op jit(solution)/shard_map/ppermute | solution.py:44
  57.5 40.7 %collective-permute-start.9 = (bf16[2,2,8,128,128]{4,3,2,1,0:T(8,128)(2,1)S(1)}, bf16[2,2,8,128,128]{4,3,2,1,0:T(8,128)(2,1)}, u32[]{:S(2)}, u32[]{:S(2)}) collective-permute-start(bf16[2,2,8,128,128]{4,3,2,1,0:T(8,128)(2,1)S(1)} %bitcast.16), channel_id=1, source_target_pairs={{0,16},{4,68},{8,24},{12,76},{16,0},{20,84},{24,8},{28,92},{32,48}... | collective-permute-start | bytes 3145736 | tf_op jit(solution)/shard_map/ppermute | solution.py:44
  60.1 38.1 %collective-permute-start.8 = (bf16[2,2,8,128,128]{4,3,2,1,0:T(8,128)(2,1)S(1)}, bf16[2,2,8,128,128]{4,3,2,1,0:T(8,128)(2,1)}, u32[]{:S(2)}, u32[]{:S(2)}) collective-permute-start(bf16[2,2,8,128,128]{4,3,2,1,0:T(8,128)(2,1)S(1)} %bitcast.17), channel_id=1, source_target_pairs={{0,24},{4,100},{8,0},{12,108},{16,8},{20,116},{24,16},{28,124},{32... | collective-permute-start | bytes 3145736 | tf_op jit(solution)/shard_map/ppermute | solution.py:44
  65.8 32.3 %collective-permute-start.7 = (bf16[16,2,128,128]{3,2,1,0:T(8,128)(2,1)}, bf16[16,2,128,128]{3,2,1,0:T(8,128)(2,1)S(1)}, u32[]{:S(2)}, u32[]{:S(2)}) collective-permute-start(bf16[16,2,128,128]{3,2,1,0:T(8,128)(2,1)} %slice.21), channel_id=1, source_target_pairs={{0,96},{4,28},{8,104},{12,4},{16,112},{20,12},{24,120},{28,20},{32... | collective-permute-start | bytes 3145736 | tf_op jit(solution)/shard_map/ppermute | solution.py:39
  71.1 27.0 %collective-permute-start.6 = (bf16[16,2,128,128]{3,2,1,0:T(8,128)(2,1)}, bf16[16,2,128,128]{3,2,1,0:T(8,128)(2,1)S(1)}, u32[]{:S(2)}, u32[]{:S(2)}) collective-permute-start(bf16[16,2,128,128]{3,2,1,0:T(8,128)(2,1)} %slice.20), channel_id=1, source_target_pairs={{0,32},{4,12},{8,40},{12,20},{16,48},{20,28},{24,56},{28,4},{32,64... | collective-permute-start | bytes 3145736 | tf_op jit(solution)/shard_map/ppermute | solution.py:39
  98.2 37.9 %collective-permute-start.14 = (bf16[32,2,128,128]{3,2,1,0:T(8,128)(2,1)}, bf16[32,2,128,128]{3,2,1,0:T(8,128)(2,1)S(1)}, u32[]{:S(2)}, u32[]{:S(2)}) collective-permute-start(bf16[32,2,128,128]{3,2,1,0:T(8,128)(2,1)} %constant_dynamic-update-slice_fusion.rest_0_), channel_id=1, source_target_pairs={{0,96},{4,28},{8,104},{12,4},{16,112},{20,12},{24,120},{28,20},{32... | collective-permute-start | bytes 6291464 | tf_op jit(solution)/shard_map/ppermute | solution.py:39
  101.2 38.1 %collective-permute-start.13 = (bf16[32,2,128,128]{3,2,1,0:T(8,128)(2,1)}, bf16[32,2,128,128]{3,2,1,0:T(8,128)(2,1)S(1)}, u32[]{:S(2)}, u32[]{:S(2)}) collective-permute-start(bf16[32,2,128,128]{3,2,1,0:T(8,128)(2,1)} %constant_dynamic-update-slice_fusion.rest_0_), channel_id=1, source_target_pairs={{0,32},{4,12},{8,40},{12,20},{16,48},{20,28},{24,56},{28,4},{32,64... | collective-permute-start | bytes 6291464 | tf_op jit(solution)/shard_map/ppermute | solution.py:39
  110.5 15.6 %collective-permute-start.11 = (bf16[2096,128]{1,0:T(8,128)(2,1)S(1)}, bf16[2096,128]{1,0:T(8,128)(2,1)S(1)}, u32[]{:S(2)}, u32[]{:S(2)}) collective-permute-start(bf16[2096,128]{1,0:T(8,128)(2,1)S(1)} %get-tuple-element.103), channel_id=1, source_target_pairs={{0,8},{4,36},{8,16},{12,44},{16,24},{20,52},{24,0},{28,60},{32,40}... | collective-permute-start | bytes 1609736 | tf_op jit(solution)/shard_map/ppermute | solution.py:44
  111.9 14.3 %collective-permute-start.12 = (bf16[2096,128]{1,0:T(8,128)(2,1)S(1)}, bf16[2096,128]{1,0:T(8,128)(2,1)S(1)}, u32[]{:S(2)}, u32[]{:S(2)}) collective-permute-start(bf16[2096,128]{1,0:T(8,128)(2,1)S(1)} %get-tuple-element.104), channel_id=1, source_target_pairs={{0,24},{4,100},{8,0},{12,108},{16,8},{20,116},{24,16},{28,124},{32... | collective-permute-start | bytes 1609736 | tf_op jit(solution)/shard_map/ppermute | solution.py:44
  113.3 29.1 %collective-permute-start.17 = (bf16[2096,128]{1,0:T(8,128)(2,1)S(1)}, bf16[2096,128]{1,0:T(8,128)(2,1)S(1)}, u32[]{:S(2)}, u32[]{:S(2)}) collective-permute-start(bf16[2096,128]{1,0:T(8,128)(2,1)S(1)} %get-tuple-element.111), channel_id=1, source_target_pairs={{0,16},{4,68},{8,24},{12,76},{16,0},{20,84},{24,8},{28,92},{32,48}... | collective-permute-start | bytes 1609736 | tf_op jit(solution)/shard_map/ppermute | solution.py:44
  140.9 14.0 %collective-permute-start.16 = (bf16[16,2,128,128]{3,2,1,0:T(8,128)(2,1)S(1)}, bf16[16,2,128,128]{3,2,1,0:T(8,128)(2,1)S(1)}, u32[]{:S(2)}, u32[]{:S(2)}) collective-permute-start(bf16[16,2,128,128]{3,2,1,0:T(8,128)(2,1)S(1)} %slice.23), channel_id=1, source_target_pairs={{0,96},{4,28},{8,104},{12,4},{16,112},{20,12},{24,120},{28,20},{32... | collective-permute-start | bytes 3145736 | tf_op jit(solution)/shard_map/ppermute | solution.py:39
  141.4 15.2 %collective-permute-start.15 = (bf16[16,2,128,128]{3,2,1,0:T(8,128)(2,1)S(1)}, bf16[16,2,128,128]{3,2,1,0:T(8,128)(2,1)S(1)}, u32[]{:S(2)}, u32[]{:S(2)}) collective-permute-start(bf16[16,2,128,128]{3,2,1,0:T(8,128)(2,1)S(1)} %slice.22), channel_id=1, source_target_pairs={{0,32},{4,12},{8,40},{12,20},{16,48},{20,28},{24,56},{28,4},{32,64... | collective-permute-start | bytes 3145736 | tf_op jit(solution)/shard_map/ppermute | solution.py:39
  143.0 13.5 %collective-permute-start.18 = (f32[1032,128]{1,0:T(8,128)S(1)}, f32[1032,128]{1,0:T(8,128)S(1)}, u32[]{:S(2)}, u32[]{:S(2)}) collective-permute-start(f32[1032,128]{1,0:T(8,128)S(1)} %get-tuple-element.114), channel_id=1, source_target_pairs={{0,4},{4,0},{8,12},{12,8},{16,20},{20,16},{24,28},{28,24},{32,36},... | collective-permute-start | bytes 1585160 | tf_op jit(solution)/shard_map/ppermute | solution.py:48
  156.8 13.6 %collective-permute-start.20 = (bf16[2,1024,128]{2,1,0:T(8,128)(2,1)S(1)}, bf16[2,1024,128]{2,1,0:T(8,128)(2,1)S(1)}, u32[]{:S(2)}, u32[]{:S(2)}) collective-permute-start(bf16[2,1024,128]{2,1,0:T(8,128)(2,1)S(1)} %finish.2.a0), channel_id=1, source_target_pairs={{0,1},{1,2},{2,3},{3,0},{4,5},{5,6},{6,7},{7,4},{8,9},{9,10},{10,1... | collective-permute-start | bytes 1572872 | tf_op jit(solution)/shard_map/ppermute | solution.py:57
  158.1 12.3 %collective-permute-start.19 = (bf16[2,1024,128]{2,1,0:T(8,128)(2,1)S(1)}, bf16[2,1024,128]{2,1,0:T(8,128)(2,1)S(1)}, u32[]{:S(2)}, u32[]{:S(2)}) collective-permute-start(bf16[2,1024,128]{2,1,0:T(8,128)(2,1)S(1)} %finish.2.a0), channel_id=1, source_target_pairs={{0,3},{1,0},{2,1},{3,2},{4,7},{5,4},{6,5},{7,6},{8,11},{9,8},{10,9... | collective-permute-start | bytes 1572872 | tf_op jit(solution)/shard_map/ppermute | solution.py:57
  170.4 21.1 %collective-permute-start.22 = (bf16[2096,128]{1,0:T(8,128)(2,1)S(1)}, bf16[2096,128]{1,0:T(8,128)(2,1)S(1)}, u32[]{:S(2)}, u32[]{:S(2)}) collective-permute-start(bf16[2096,128]{1,0:T(8,128)(2,1)S(1)} %get-tuple-element.128), channel_id=1, source_target_pairs={{0,8},{4,36},{8,16},{12,44},{16,24},{20,52},{24,0},{28,60},{32,40}... | collective-permute-start | bytes 1609736 | tf_op jit(solution)/shard_map/ppermute | solution.py:44
  170.4 21.1 %collective-permute-start.23 = (bf16[2096,128]{1,0:T(8,128)(2,1)S(1)}, bf16[2096,128]{1,0:T(8,128)(2,1)S(1)}, u32[]{:S(2)}, u32[]{:S(2)}) collective-permute-start(bf16[2096,128]{1,0:T(8,128)(2,1)S(1)} %get-tuple-element.129), channel_id=1, source_target_pairs={{0,16},{4,68},{8,24},{12,76},{16,0},{20,84},{24,8},{28,92},{32,48}... | collective-permute-start | bytes 1609736 | tf_op jit(solution)/shard_map/ppermute | solution.py:44
  174.5 17.0 %collective-permute-start.24 = (bf16[2096,128]{1,0:T(8,128)(2,1)S(1)}, bf16[2096,128]{1,0:T(8,128)(2,1)S(1)}, u32[]{:S(2)}, u32[]{:S(2)}) collective-permute-start(bf16[2096,128]{1,0:T(8,128)(2,1)S(1)} %get-tuple-element.130), channel_id=1, source_target_pairs={{0,24},{4,100},{8,0},{12,108},{16,8},{20,116},{24,16},{28,124},{32... | collective-permute-start | bytes 1609736 | tf_op jit(solution)/shard_map/ppermute | solution.py:44
  174.5 13.0 %collective-permute-start.21 = (bf16[2,1024,128]{2,1,0:T(8,128)(2,1)S(1)}, bf16[2,1024,128]{2,1,0:T(8,128)(2,1)S(1)}, u32[]{:S(2)}, u32[]{:S(2)}) collective-permute-start(bf16[2,1024,128]{2,1,0:T(8,128)(2,1)S(1)} %finish.2.a0), channel_id=1, source_target_pairs={{0,2},{1,3},{2,0},{3,1},{4,6},{5,7},{6,4},{7,5},{8,10},{9,11},{10,... | collective-permute-start | bytes 1572872 | tf_op jit(solution)/shard_map/ppermute | solution.py:57
  196.9 14.5 %collective-permute-start.28 = (bf16[2,1024,128]{2,1,0:T(8,128)(2,1)S(1)}, bf16[2,1024,128]{2,1,0:T(8,128)(2,1)S(1)}, u32[]{:S(2)}, u32[]{:S(2)}) collective-permute-start(bf16[2,1024,128]{2,1,0:T(8,128)(2,1)S(1)} %finish.3.a0), channel_id=1, source_target_pairs={{0,1},{1,2},{2,3},{3,0},{4,5},{5,6},{6,7},{7,4},{8,9},{9,10},{10,1... | collective-permute-start | bytes 1572872 | tf_op jit(solution)/shard_map/ppermute | solution.py:57
  198.3 25.5 %collective-permute-start.27 = (bf16[2,1024,128]{2,1,0:T(8,128)(2,1)S(1)}, bf16[2,1024,128]{2,1,0:T(8,128)(2,1)S(1)}, u32[]{:S(2)}, u32[]{:S(2)}) collective-permute-start(bf16[2,1024,128]{2,1,0:T(8,128)(2,1)S(1)} %finish.3.a0), channel_id=1, source_target_pairs={{0,2},{1,3},{2,0},{3,1},{4,6},{5,7},{6,4},{7,5},{8,10},{9,11},{10,... | collective-permute-start | bytes 1572872 | tf_op jit(solution)/shard_map/ppermute | solution.py:57
  200.9 22.9 %collective-permute-start.26 = (bf16[2,1024,128]{2,1,0:T(8,128)(2,1)S(1)}, bf16[2,1024,128]{2,1,0:T(8,128)(2,1)S(1)}, u32[]{:S(2)}, u32[]{:S(2)}) collective-permute-start(bf16[2,1024,128]{2,1,0:T(8,128)(2,1)S(1)} %finish.3.a0), channel_id=1, source_target_pairs={{0,3},{1,0},{2,1},{3,2},{4,7},{5,4},{6,5},{7,6},{8,11},{9,8},{10,9... | collective-permute-start | bytes 1572872 | tf_op jit(solution)/shard_map/ppermute | solution.py:57
  (23 other events, 132.3 us)

commit v5 on v4

--- a/solution.py
+++ b/solution.py
@@ -88,13 +88,57 @@
     )(head, rows)
 
 
-def project_kernel(core_ref, tok_ref, gain_ref, wq, wk, wv, q_all, swap, k_all, v_all, edge):
-    step = pl.program_id(0)
-    core = core_ref[0]
+def normalise(tok_ref, gain_ref):
     x = tok_ref[...].astype(F32)
     inverse = lax.rsqrt(jnp.mean(x * x, axis=1, keepdims=True) + 1e-05)
-    normed = (x * inverse * gain_ref[...]).astype(BF16)
+    return (x * inverse * gain_ref[...]).astype(BF16)
+
+
+def both_cores(core, put):
+    for here in range(2):
+        pl.when(core == here)(functools.partial(put, here))
+
+
+def query_kernel(core_ref, tok_ref, gain_ref, wq, normed_ref, keep, send):
+    normed = normalise(tok_ref, gain_ref)
+    normed_ref[...] = normed
     q = nn(normed, wq[...]).astype(BF16)
+
+    def put(here):
+        for h in range(4):
+            slot = (h - 2 * here) % 4
+            out = keep if slot < 2 else send
+            out[slot % 2] = q[:, h * HD : (h + 1) * HD]
+
+    both_cores(core_ref[0], put)
+
+
+def query(core, tokens, gain, wq):
+    n, d = tokens.shape
+    half = jax.ShapeDtypeStruct((2, n, HD), BF16)
+    heads = pl.BlockSpec((2, 256, HD), lambda i, c: (0, i, 0))
+    return pl.pallas_call(
+        query_kernel,
+        grid_spec=pltpu.PrefetchScalarGridSpec(
+            num_scalar_prefetch=1,
+            grid=(n // 256,),
+            in_specs=[
+                pl.BlockSpec((256, d), lambda i, c: (i, 0)),
+                pl.BlockSpec((1, d), lambda i, c: (0, 0)),
+                pl.BlockSpec((d, wq.shape[1]), lambda i, c: (0, 0), pipeline_mode=pl.Buffered(1)),
+            ],
+            out_specs=[pl.BlockSpec((256, d), lambda i, c: (i, 0)), heads, heads],
+        ),
+        out_shape=[jax.ShapeDtypeStruct((n, d), BF16), half, half],
+        compiler_params=params(),
+        cost_estimate=BRIEF,
+        name="query",
+    )(core, tokens, gain.reshape(1, d), wq)
+
+
+def project_kernel(core_ref, normed_ref, wk, wv, k_all, v_all, swap, edge):
+    step = pl.program_id(0)
+    normed = normed_ref[...]
     k = nn(normed, wk[...]).astype(BF16)
     v = nn(normed, wv[...])
 
@@ -104,9 +148,6 @@
         for h in range(4):
             slot = (h - 2 * here) % 4
             lanes = slice(h * HD, (h + 1) * HD)
-            q_all[slot] = q[:, lanes]
-            if slot >= 2:
-                swap[pl.ds((slot - 2) * 1024 + pl.multiple_of(step * 256, 256), 256), :] = q[:, lanes]
             for b in range(2):
                 rows = slice(b * BLOCK, (b + 1) * BLOCK)
                 kb = k[rows, lanes]
@@ -114,66 +155,48 @@
                 k_all[slot, b] = kb
                 v_all[slot, b] = vb
                 out, when = (to_first, 0) if b == 0 else (to_last, pl.num_programs(0) - 1)
-                base = 2048 if out is swap else 0
 
                 @pl.when(step == when)
                 def _():
-                    out[base + slot * HD : base + (slot + 1) * HD, :] = kb
-                    out[base + (4 + slot) * HD : base + (5 + slot) * HD, :] = vb
-
-    @pl.when(core == 0)
-    def _():
-        put(0)
-
-    @pl.when(core == 1)
-    def _():
-        put(1)
-
-
-def project(core, tokens, gain, wq, wk, wv):
-    n, d = tokens.shape
-    w = wq.shape[1]
-    weight = pl.BlockSpec((d, w), lambda i, c: (0, 0), pipeline_mode=pl.Buffered(1))
+                    out[slot * HD : (slot + 1) * HD, :] = kb
+                    out[(4 + slot) * HD : (5 + slot) * HD, :] = vb
+
+    both_cores(core_ref[0], put)
+
+
+def project(core, normed, wk, wv):
+    n, d = normed.shape
+    weight = pl.BlockSpec((d, wk.shape[1]), lambda i, c: (0, 0), pipeline_mode=pl.Buffered(1))
     blocks = pl.BlockSpec((4, 2, BLOCK, HD), lambda i, c: (0, i, 0, 0))
+    edge = pl.BlockSpec((1024, HD), lambda i, c: (0, 0))
     return pl.pallas_call(
         project_kernel,
         grid_spec=pltpu.PrefetchScalarGridSpec(
             num_scalar_prefetch=1,
             grid=(n // 256,),
-            in_specs=[
-                pl.BlockSpec((256, d), lambda i, c: (i, 0)),
-                pl.BlockSpec((1, d), lambda i, c: (0, 0)),
-                weight,
-                weight,
-                weight,
-            ],
-            out_specs=[
-                pl.BlockSpec((4, 256, HD), lambda i, c: (0, i, 0)),
-                pl.BlockSpec((3072, HD), lambda i, c: (0, 0)),
-                blocks,
-                blocks,
-                pl.BlockSpec((1024, HD), lambda i, c: (0, 0)),
-            ],
+            in_specs=[pl.BlockSpec((256, d), lambda i, c: (i, 0)), weight, weight],
+            out_specs=[blocks, blocks, edge, edge],
         ),
         out_shape=[
-            jax.ShapeDtypeStruct((4, n, HD), BF16),
-            jax.ShapeDtypeStruct((3072, HD), BF16),
             jax.ShapeDtypeStruct((4, 8, BLOCK, HD), BF16),
             jax.ShapeDtypeStruct((4, 8, HD, BLOCK), BF16),
             jax.ShapeDtypeStruct((1024, HD), BF16),
+            jax.ShapeDtypeStruct((1024, HD), BF16),
         ],
         compiler_params=params(),
         cost_estimate=BRIEF,
         name="project",
-    )(core, tokens, gain.reshape(1, d), wq, wk, wv)
-
-
-def near_kernel(core_ref, q_ref, k_ref, v_ref, ka, va, kb, vb, o_ref, lse_ref):
+    )(core, normed, wk, wv)
+
+
+def near_kernel(core_ref, qa_ref, qb_ref, k_ref, v_ref, ka, va, kb, vb, o_ref, lse_ref):
     first = core_ref[0] == 0
     klo, khi = jnp.where(first, ka[0], kb[0]), jnp.where(first, kb[0], ka[0])
     vlo, vhi = jnp.where(first, va[0], vb[0]), jnp.where(first, vb[0], va[0])
+    mine = pl.program_id(0) < 2
     for b in range(8):
-        q = q_ref[0, b * BLOCK : (b + 1) * BLOCK]
+        rows = slice(b * BLOCK, (b + 1) * BLOCK)
+        q = jnp.where(mine, qa_ref[0, rows], qb_ref[0, rows])
         ks = [klo if b == 0 else k_ref[0, b - 1], k_ref[0, b], khi if b == 7 else k_ref[0, b + 1]]
         vs = [vlo if b == 0 else v_ref[0, b - 1], v_ref[0, b], vhi if b == 7 else v_ref[0, b + 1]]
         s = [nt(k, q) * SCALE for k in ks]
@@ -185,7 +208,7 @@
         lse_ref[0, b : b + 1, :] = m + jnp.log(total)
 
 
-def near(core, q, k, v, halo, swapped):
+def near(core, keep, send, k, v, halo, swapped):
     blocks = pl.BlockSpec((1, 8, BLOCK, HD), lambda s, c: (s, 0, 0, 0))
 
     def edge(first):
@@ -196,15 +219,15 @@
         grid_spec=pltpu.PrefetchScalarGridSpec(
             num_scalar_prefetch=1,
             grid=(4,),
-            in_specs=[pl.BlockSpec((1, 1024, HD), lambda s, c: (s, 0, 0)), blocks, blocks]
-            + [edge(0), edge(4), edge(16), edge(20)],
+            in_specs=[pl.BlockSpec((1, 1024, HD), lambda s, c: (s % 2, 0, 0))] * 2
+            + [blocks, blocks, edge(0), edge(4), edge(0), edge(4)],
             out_specs=[blocks, pl.BlockSpec((1, 8, HD), lambda s, c: (s, 0, 0))],
         ),
         out_shape=[jax.ShapeDtypeStruct((4, 8, HD, BLOCK), F32), jax.ShapeDtypeStruct((4, 8, BLOCK), F32)],
         compiler_params=params(),
         cost_estimate=BRIEF,
         name="near",
-    )(core, q, k, v, halo.reshape(8, BLOCK, HD), halo.reshape(8, BLOCK, HD), swapped.reshape(24, BLOCK, HD), swapped.reshape(24, BLOCK, HD))
+    )(core, keep, send, k, v, *[e.reshape(8, BLOCK, HD) for e in (halo, halo, swapped, swapped)])
 
 
 GROUP = 4
@@ -495,29 +518,27 @@
     def after(x, *deps):
         return lax.optimization_barrier((x, *deps))[0]
 
-    def rows_of(j, gate):
-        got = core_swap(split_cache(2 - 2 * gate + j, kv_cache))
-        return lax.dynamic_update_slice(split_cache(2 * gate + j, kv_cache, 2), got, (16, 0, 0, 0))
-
-    rows0 = rows_of(0, core)
+    normed, q_keep, q_send = query(core, tokens, norm_gain, w_query)
+    send0 = split_cache(2 - 2 * after(core, q_send), kv_cache)
+    mine = jnp.concatenate([q_keep, core_swap(q_send)], axis=0).reshape(2, 2, 8, BLOCK, HD)
+    q1, q3, q2 = query_perm(mine, -1), query_perm(mine, 1), query_perm(mine, 2)
+
+    keep0 = split_cache(2 * after(core, mine), kv_cache, 2)
+    rows0 = lax.dynamic_update_slice(keep0, core_swap(send0), (16, 0, 0, 0))
     up0, down0 = rows_perm(rows0, 1), rows_perm(rows0, -1)
-    rows1 = rows_of(1, after(core, rows0))
-
-    gain, rows1 = lax.optimization_barrier((norm_gain, rows1))
-    q_all, swap, k_all, v_all, edge = project(core, tokens, gain, w_query, w_key, w_value)
+    core1 = after(core, rows0)
+    send1, keep1 = split_cache(3 - 2 * core1, kv_cache), split_cache(1 + 2 * core1, kv_cache, 2)
+    normed, keep1, send1 = lax.optimization_barrier((normed, keep1, send1))
+    k_all, v_all, swap, edge = project(core, normed, w_key, w_value)
+    send1, swap, edge, q1, q2, q3 = lax.optimization_barrier((send1, swap, edge, q1, q2, q3))
     swapped, halo = core_swap(swap), halo_perm(edge)
-    mine = jnp.concatenate([q_all[:2], swapped[:2048].reshape(2, 1024, HD)], axis=0).reshape(2, 2, 8, BLOCK, HD)
-    mine, halo, up0, down0 = lax.optimization_barrier((mine, halo, up0, down0))
+    rows1 = lax.dynamic_update_slice(keep1, core_swap(send1), (16, 0, 0, 0))
+    code, cnt = line_codes(wake_blocks, wake_frames, wake_counts, y, z, c)
+    halo, *lists = lax.optimization_barrier((halo, *plan(cnt, code)))
+    near_o, near_lse = near(core, q_keep, q_send, k_all, v_all, halo, swapped)
+    up0, down0, near_o, near_lse, rows1 = lax.optimization_barrier((up0, down0, near_o, near_lse, rows1))
     up20, down20 = rows_perm(up0[:16], 1), rows_perm(down0[16:], -1)
-    q1, q3, q2 = query_perm(mine, -1), query_perm(mine, 1), query_perm(mine, 2)
-
-    near_o, near_lse = near(core, q_all, k_all, v_all, after(halo, mine), swapped)
-    code, cnt = line_codes(wake_blocks, wake_frames, wake_counts, y, z, c)
-    lists = plan(cnt, code)
-    weights = pick(after(place, mine), w_out)
-    held = (*weights, rows1, near_o, near_lse, up20, down20, q1, q2, q3, *lists)
-    *weights, rows1, near_o, near_lse, up20, down20, q1, q2, q3, e, f, g, h = lax.optimization_barrier(held)
-    lists = [e, f, g, h]
+    rows1, up20, down20 = lax.optimization_barrier((rows1, up20, down20))
     up1, down1 = rows_perm(rows1, 1), rows_perm(rows1, -1)
     qs = [mine, q1, q2, q3]
 
@@ -528,10 +549,11 @@
         return [heads, mp_perm(heads, -1), mp_perm(heads, 2), mp_perm(heads, 1)]
 
     parts = far(0, cnt, lists, [rows0, down0, up20, down20, up0], qs)
+    weights = pick(after(place, parts[0]), w_out)
     back = returned(parts)
     back[1], back[3], up1, down1 = lax.optimization_barrier((back[1], back[3], up1, down1))
     up21, down21 = rows_perm(up1[:16], 1), rows_perm(down1[16:], -1)
-    near_lse, up21, down21 = lax.optimization_barrier((near_lse, up21, down21))
+    back[0], *weights = lax.optimization_barrier((back[0], *weights))
     own, other = merge(back)
     heads = finish(0, near_o, near_lse, own, core_swap(other))
     gathered = gather(heads)
@@ -539,11 +561,11 @@
     parts = far(1, cnt, lists, [after(rows1, heads), down1, up21, down21, up1], qs)
     *parts, gathered[1], gathered[3] = lax.optimization_barrier((*parts, gathered[1], gathered[3]))
     back = returned(parts)
-    gathered[0] = after(gathered[0], parts[0])
-    acc = mix(place, gathered, weights[0], tokens, F32)
-    back[0], acc = lax.optimization_barrier((back[0], acc))
+    back[0], gathered[2] = lax.optimization_barrier((back[0], gathered[2]))
     own, other = merge(back)
     heads = finish(1, near_o, near_lse, own, core_swap(other))
+    gathered[0] = after(gathered[0], heads)
+    acc = mix(place, gathered, weights[0], tokens, F32)
     return mix(place, gather(heads), weights[1], acc, BF16)
 
 

time: 228 us -> 238 us (1.044)
  Pallas kernels: 80.4 us -> 88.1 us
  local copies, waits for them, and re-layouts: 18.7 us -> 22.2 us
  waiting for transfers between devices: 82.6 us -> 80.2 us
    ppermute x8, waiting for transfers between devices: 32.1 us -> 20.7 us  [rows_perm(): return lax.ppermute(x, 'tok', pairs)]
    ppermute x9, waiting for transfers between devices: 11.7 us -> 21.4 us  [query_perm(): return lax.ppermute(x, 'tok', pairs)]
    pallas_call x0 -> x1, Pallas kernels: none -> 7.21 us  [query(): pl.pallas_call(query_kernel, grid_spec=pltpu.PrefetchScalarGridSpec(num_s...]
    unnamed x36 -> x46, local copies, waits for them, and re-layouts: 7.6 us -> 13 us
    pallas_call x1, Pallas kernels: 15.7 us -> 10.4 us  [project(): pl.pallas_call(project_kernel, grid_spec=pltpu.PrefetchScalarGridSpec(num...]
    pallas_call x2, Pallas kernels: 18.5 us -> 22.3 us  [far(): pl.pallas_call(functools.partial(far_kernel, j), in_specs=[SMEM] * 5 + [A...]
    ppermute x5 -> x6, waiting for transfers between devices: 1.96 us -> 4.49 us  [core_swap(): lax.ppermute(x, 'tok', [(tok_of(y, z, c), tok_of(y, z, 1 - c)) for y, z,...]
    ppermute x1, waiting for transfers between devices: 2.52 us -> 0.01 us  [halo_perm(): lax.ppermute(x, 'tok', [(i, (i + (1 if i % 2 else -1)) % n) for i in rang...]
  transfers between devices with their start and end apart: 29 -> 30, of which waited for: 14 -> 13; matrix products, arithmetic and copies ran while one was open for 5% -> 4% of each run, Pallas kernels for 29% -> 30%
where the time goes in v5:
time: 238 us
  Pallas kernels  88.1 us (37%)
  waiting for transfers between devices  80.2 us (34%)
  starting transfers between devices  46.3 us (19%)
  local copies, waits for them, and re-layouts  22.2 us (9%)
    ppermute x6, waiting for transfers between devices, mp_perm(): return lax.ppermute(x, 'mp', [(i, (i + d) % NX) for i in range(NX)])  33.6 us
    pallas_call x4, Pallas kernels, split_cache(): pl.pallas_call(split_cache_kernel, grid_spec=pltpu.PrefetchScalarGridSpec...  23.7 us
    pallas_call x2, Pallas kernels, far(): pl.pallas_call(functools.partial(far_kernel, j), in_specs=[SMEM] * 5 + [A...  22.3 us
    ppermute x9, waiting for transfers between devices, query_perm(): return lax.ppermute(x, 'tok', pairs)  21.4 us
    ppermute x8, waiting for transfers between devices, rows_perm(): return lax.ppermute(x, 'tok', pairs)  20.7 us
    ppermute x9, starting transfers between devices, query_perm(): return lax.ppermute(x, 'tok', pairs)  14.7 us
    unnamed x46, local copies, waits for them, and re-layouts  13 us
    ppermute x8, starting transfers between devices, rows_perm(): return lax.ppermute(x, 'tok', pairs)  12.5 us
  transfers between devices with their start and end apart: 30, of which 13 were waited for; matrix products, arithmetic and copies ran while one was open for 4% of the time, Pallas kernels for 30%

profile of v5, /device:TPU:1, one launch (start us, length us, event | category | flops | bytes accessed | tf_op | source)
XLA Modules:
  0.0 237.6 jit_solution(14296491605568380538)
XLA Ops:
  2.3 7.2 %query.1 = (bf16[1024,2048]{1,0:T(8,128)(2,1)}, bf16[2,1024,128]{2,1,0:T(8,128)(2,1)S(1)}, bf16[2,1024,128]{2,1,0:T(8,128)(2,1)S(1)}) custom-call(s32[1]{0:T(128)} %bitcast.core_ref, bf16[1024,2048]{1,0:T(8,128)(2,1)} %carried.1, f32[1,2048]{1,0:T(1,128)S(1)} %bitcast.23, bf16[2048,512]{1,0:T(8,128)(2,1)S(1)} %copy-done.2), custom_call_target="tpu_custom_call" | custom-call | flops 1 | bytes 1 | tf_op jit(solution)/shard_map/query/pallas_call | solution.py:120
  9.5 4.5 %split_cache.5 = bf16[16,2,128,128]{3,2,1,0:T(8,128)(2,1)S(1)} custom-call(s32[1]{0:T(128)S(6)} %sub.20.head_ref, bf16[2,1024,2,512]{3,2,1,0:T(2,128)(2,1)S(1)} %copy-done), custom_call_target="tpu_custom_call" | custom-call | flops 1 | bytes 1 | tf_op jit(solution)/shard_map/split_cache/pallas_call | solution.py:76
  15.6 2.9 %collective-permute-done = bf16[2,1024,128]{2,1,0:T(8,128)(2,1)S(1)} collective-permute-done((bf16[2,1024,128]{2,1,0:T(8,128)(2,1)S(1)}, bf16[2,1024,128]{2,1,0:T(8,128)(2,1)S(1)}, u32[]{:S(2)}, u32[]{:S(2)}) %collective-permute-start) | collective-permute-done | bytes 524320 | tf_op jit(solution)/shard_map/ppermute | solution.py:48
  18.7 2.9 %collective-permute-start.4 = (bf16[2,2,8,128,128]{4,3,2,1,0:T(8,128)(2,1)S(1)}, bf16[2,2,8,128,128]{4,3,2,1,0:T(8,128)(2,1)S(1)}, u32[]{:S(2)}, u32[]{:S(2)}) collective-permute-start(bf16[2,2,8,128,128]{4,3,2,1,0:T(8,128)(2,1)S(1)} %bitcast.14), channel_id=1, source_target_pairs={{0,24},{4,100},{8,0},{12,108},{16,8},{20,116},{24,16},{28,124},{32... | collective-permute-start | bytes 3145736 | tf_op jit(solution)/shard_map/ppermute | solution.py:44
  22.6 6.9 %split_cache.4 = bf16[32,2,128,128]{3,2,1,0:T(8,128)(2,1)} custom-call(s32[1]{0:T(128)S(6)} %mul.37.head_ref, bf16[2,1024,2,512]{3,2,1,0:T(2,128)(2,1)} %src.7), custom_call_target="tpu_custom_call" | custom-call | flops 1 | bytes 1 | tf_op jit(solution)/shard_map/split_cache/pallas_call | solution.py:76
  34.4 7.0 %split_cache.6 = bf16[32,2,128,128]{3,2,1,0:T(8,128)(2,1)} custom-call(s32[1]{0:T(128)S(6)} %add.42.head_ref, bf16[2,1024,2,512]{3,2,1,0:T(2,128)(2,1)} %src.7), custom_call_target="tpu_custom_call" | custom-call | flops 1 | bytes 1 | tf_op jit(solution)/shard_map/split_cache/pallas_call | solution.py:76
  41.4 5.4 %split_cache.7 = bf16[16,2,128,128]{3,2,1,0:T(8,128)(2,1)} custom-call(s32[1]{0:T(128)S(6)} %sub.21.head_ref, bf16[2,1024,2,512]{3,2,1,0:T(2,128)(2,1)S(1)} %copy-done.1), custom_call_target="tpu_custom_call" | custom-call | flops 1 | bytes 1 | tf_op jit(solution)/shard_map/split_cache/pallas_call | solution.py:76
  46.8 10.4 %project.1 = (bf16[4,8,128,128]{3,2,1,0:T(8,128)(2,1)S(1)}, bf16[4,8,128,128]{3,2,1,0:T(8,128)(2,1)S(1)}, bf16[1024,128]{1,0:T(8,128)(2,1)S(1)}, bf16[1024,128]{1,0:T(8,128)(2,1)S(1)}) custom-call(s32[1]{0:T(128)} %bitcast.core_ref, bf16[1024,2048]{1,0:T(8,128)(2,1)} %get-tuple-element.81.normed_ref, bf16[2048,512]{1,0:T(8,128)(2,1)S(1)} %copy-done.5, ...), custom_call_target="tpu_custom_call" | custom-call | flops 1 | bytes 1 | tf_op jit(solution)/shard_map/project/pallas_call | solution.py:172
  64.7 4.9 %collective-permute-start.8 = (bf16[1024,128]{1,0:T(8,128)(2,1)S(1)}, bf16[1024,128]{1,0:T(8,128)(2,1)S(1)}, u32[]{:S(2)}, u32[]{:S(2)}) collective-permute-start(bf16[1024,128]{1,0:T(8,128)(2,1)S(1)} %get-tuple-element.93), channel_id=1, source_target_pairs={{0,4},{4,0},{8,12},{12,8},{16,20},{20,16},{24,28},{28,24},{32,36},... | collective-permute-start | bytes 786440 | tf_op jit(solution)/shard_map/ppermute | solution.py:48
  70.1 2.9 %plan.1 = (s32[100]{0:T(128)S(1)}, s32[64]{0:T(128)S(1)}, s32[64]{0:T(128)S(1)}, s32[2]{0:T(128)S(1)}) custom-call(s32[64]{0:T(128)S(1)} %reduce_sum.12.cnt_ref, s32[512]{0:T(512)S(1)} %reshape.73.code_ref), custom_call_target="tpu_custom_call" | custom-call | flops 1 | bytes 1 | tf_op jit(solution)/shard_map/plan/pallas_call | solution.py:272
  79.3 8.7 %near.1 = (f32[4,8,128,128]{3,2,1,0:T(8,128)S(1)}, f32[4,8,128]{2,1,0:T(8,128)S(1)}) custom-call(s32[1]{0:T(128)} %bitcast.core_ref, bf16[2,1024,128]{2,1,0:T(8,128)(2,1)S(1)} %copy-done.4, bf16[2,1024,128]{2,1,0:T(8,128)(2,1)S(1)} %copy-done.15, bf16[4,8,128,128]{3,2,1,0:T(8,128)(2,1)S(1)} %copy-done.7, bf16[4,8,128,128]{3,2,1,0:T(8,128)(2,1)S(1)} %copy-done.9, ...), custom_call_target="tpu_custom_call" | custom-call | flops 1 | bytes 1 | tf_op jit(solution)/shard_map/near/pallas_call | solution.py:217
  95.7 11.1 %collective-permute-done.10.rest_2_ = bf16[16,2,128,128]{3,2,1,0:T(8,128)(2,1)S(1)} collective-permute-done((bf16[16,2,128,128]{3,2,1,0:T(8,128)(2,1)S(1)}, bf16[16,2,128,128]{3,2,1,0:T(8,128)(2,1)S(1)}, u32[]{:S(2)}, u32[]{:S(2)}) %collective-permute-start.10) | collective-permute-done | bytes 1048608 | tf_op jit(solution)/shard_map/ppermute | solution.py:39
  110.6 11.6 %far.2 = (bf16[2096,128]{1,0:T(8,128)(2,1)S(1)}, bf16[2096,128]{1,0:T(8,128)(2,1)}, bf16[2096,128]{1,0:T(8,128)(2,1)}, bf16[2096,128]{1,0:T(8,128)(2,1)}) custom-call(s32[64]{0:T(128)S(1)} %reduce_sum.12.cnt_ref, s32[100]{0:T(128)S(1)} %get-tuple-element.100.unit_ref, s32[64]{0:T(128)S(1)} %get-tuple-element.101.first_ref, ...), custom_call_target="tpu_custom_call" | custom-call | flops 1 | bytes 1 | tf_op jit(solution)/shard_map/far/pallas_call | solution.py:357
  124.4 3.3 %collective-permute-start.13 = (bf16[2096,128]{1,0:T(8,128)(2,1)}, bf16[2096,128]{1,0:T(8,128)(2,1)}, u32[]{:S(2)}, u32[]{:S(2)}) collective-permute-start(bf16[2096,128]{1,0:T(8,128)(2,1)} %get-tuple-element.119), channel_id=1, source_target_pairs={{0,24},{4,100},{8,0},{12,108},{16,8},{20,116},{24,16},{28,124},{32... | collective-permute-start | bytes 1609736 | tf_op jit(solution)/shard_map/ppermute | solution.py:44
  131.3 9.5 %collective-permute-done.12.b = bf16[2096,128]{1,0:T(8,128)(2,1)} collective-permute-done((bf16[2096,128]{1,0:T(8,128)(2,1)}, bf16[2096,128]{1,0:T(8,128)(2,1)}, u32[]{:S(2)}, u32[]{:S(2)}) %collective-permute-start.12) | collective-permute-done | bytes 536608 | tf_op jit(solution)/shard_map/ppermute | solution.py:44
  141.7 10.6 %collective-permute-done.16.c = bf16[2096,128]{1,0:T(8,128)(2,1)} collective-permute-done((bf16[2096,128]{1,0:T(8,128)(2,1)}, bf16[2096,128]{1,0:T(8,128)(2,1)}, u32[]{:S(2)}, u32[]{:S(2)}) %collective-permute-start.16) | collective-permute-done | bytes 536608 | tf_op jit(solution)/shard_map/ppermute | solution.py:44
  162.7 8.3 %collective-permute-done.18.rest_2_ = bf16[16,2,128,128]{3,2,1,0:T(8,128)(2,1)S(1)} collective-permute-done((bf16[16,2,128,128]{3,2,1,0:T(8,128)(2,1)S(1)}, bf16[16,2,128,128]{3,2,1,0:T(8,128)(2,1)S(1)}, u32[]{:S(2)}, u32[]{:S(2)}) %collective-permute-start.18) | collective-permute-done | bytes 1048608 | tf_op jit(solution)/shard_map/ppermute | solution.py:39
  171.6 10.7 %far.3 = (bf16[2096,128]{1,0:T(8,128)(2,1)S(1)}, bf16[2096,128]{1,0:T(8,128)(2,1)S(1)}, bf16[2096,128]{1,0:T(8,128)(2,1)S(1)}, bf16[2096,128]{1,0:T(8,128)(2,1)S(1)}) custom-call(s32[64]{0:T(128)S(1)} %reduce_sum.12.cnt_ref, s32[100]{0:T(128)S(1)} %get-tuple-element.100.unit_ref, s32[64]{0:T(128)S(1)} %get-tuple-element.101.first_ref, ...), custom_call_target="tpu_custom_call" | custom-call | flops 1 | bytes 1 | tf_op jit(solution)/shard_map/far/pallas_call | solution.py:357
  184.4 2.9 %collective-permute-start.24 = (bf16[2096,128]{1,0:T(8,128)(2,1)S(1)}, bf16[2096,128]{1,0:T(8,128)(2,1)S(1)}, u32[]{:S(2)}, u32[]{:S(2)}) collective-permute-start(bf16[2096,128]{1,0:T(8,128)(2,1)S(1)} %get-tuple-element.135), channel_id=1, source_target_pairs={{0,16},{4,68},{8,24},{12,76},{16,0},{20,84},{24,8},{28,92},{32,48}... | collective-permute-start | bytes 1609736 | tf_op jit(solution)/shard_map/ppermute | solution.py:44
  190.0 12.2 %collective-permute-done.22.a2 = bf16[2,1024,128]{2,1,0:T(8,128)(2,1)S(1)} collective-permute-done((bf16[2,1024,128]{2,1,0:T(8,128)(2,1)S(1)}, bf16[2,1024,128]{2,1,0:T(8,128)(2,1)S(1)}, u32[]{:S(2)}, u32[]{:S(2)}) %collective-permute-start.22) | collective-permute-done | bytes 524320 | tf_op jit(solution)/shard_map/ppermute | solution.py:57
  208.7 4.0 %mix.2.carried = f32[1024,512]{1,0:T(8,128)S(1)} custom-call(s32[2]{0:T(128)S(1)} %pad_add_fusion.place_ref, bf16[2,1024,128]{2,1,0:T(8,128)(2,1)S(1)} %finish.2.a0, bf16[2,1024,128]{2,1,0:T(8,128)(2,1)S(1)} %collective-permute-done.20.a1, bf16[2,1024,128]{2,1,0:T(8,128)(2,1)S(1)} %collective-permute-done.22.a2, ...), custom_call_target="tpu_custom_call" | custom-call | flops 1 | bytes 1 | tf_op jit(solution)/shard_map/mix/pallas_call | solution.py:476
  212.7 16.9 %collective-permute-done.27.a1 = bf16[2,1024,128]{2,1,0:T(8,128)(2,1)S(1)} collective-permute-done((bf16[2,1024,128]{2,1,0:T(8,128)(2,1)S(1)}, bf16[2,1024,128]{2,1,0:T(8,128)(2,1)S(1)}, u32[]{:S(2)}, u32[]{:S(2)}) %collective-permute-start.27) | collective-permute-done | bytes 524320 | tf_op jit(solution)/shard_map/ppermute | solution.py:57
  229.6 4.6 %collective-permute-done.29.a3 = bf16[2,1024,128]{2,1,0:T(8,128)(2,1)S(1)} collective-permute-done((bf16[2,1024,128]{2,1,0:T(8,128)(2,1)S(1)}, bf16[2,1024,128]{2,1,0:T(8,128)(2,1)S(1)}, u32[]{:S(2)}, u32[]{:S(2)}) %collective-permute-start.29) | collective-permute-done | bytes 524320 | tf_op jit(solution)/shard_map/ppermute | solution.py:57
  234.2 3.4 %mix.3 = bf16[1024,512]{1,0:T(8,128)(2,1)} custom-call(s32[2]{0:T(128)S(1)} %pad_add_fusion.place_ref, bf16[2,1024,128]{2,1,0:T(8,128)(2,1)S(1)} %finish.3.a0, bf16[2,1024,128]{2,1,0:T(8,128)(2,1)S(1)} %collective-permute-done.27.a1, bf16[2,1024,128]{2,1,0:T(8,128)(2,1)S(1)} %collective-permute-done.28.a2, ...), custom_call_target="tpu_custom_call" | custom-call | flops 1 | bytes 1 | tf_op jit(solution)/shard_map/mix/pallas_call | solution.py:476
  (119 shorter events, 64.4 us)
Async XLA Ops:
  14.0 15.4 %collective-permute-start.1 = (bf16[16,2,128,128]{3,2,1,0:T(8,128)(2,1)S(1)}, bf16[16,2,128,128]{3,2,1,0:T(8,128)(2,1)S(1)}, u32[]{:S(2)}, u32[]{:S(2)}) collective-permute-start(bf16[16,2,128,128]{3,2,1,0:T(8,128)(2,1)S(1)} %split_cache.5), channel_id=1, source_target_pairs={{0,4},{4,0},{8,12},{12,8},{16,20},{20,16},{24,28},{28,24},{32,36},... | collective-permute-start | bytes 3145736 | tf_op jit(solution)/shard_map/ppermute | solution.py:48
  18.7 40.5 %collective-permute-start.4 = (bf16[2,2,8,128,128]{4,3,2,1,0:T(8,128)(2,1)S(1)}, bf16[2,2,8,128,128]{4,3,2,1,0:T(8,128)(2,1)S(1)}, u32[]{:S(2)}, u32[]{:S(2)}) collective-permute-start(bf16[2,2,8,128,128]{4,3,2,1,0:T(8,128)(2,1)S(1)} %bitcast.14), channel_id=1, source_target_pairs={{0,24},{4,100},{8,0},{12,108},{16,8},{20,116},{24,16},{28,124},{32... | collective-permute-start | bytes 3145736 | tf_op jit(solution)/shard_map/ppermute | solution.py:44
  21.6 37.6 %collective-permute-start.5 = (bf16[2,2,8,128,128]{4,3,2,1,0:T(8,128)(2,1)S(1)}, bf16[2,2,8,128,128]{4,3,2,1,0:T(8,128)(2,1)S(1)}, u32[]{:S(2)}, u32[]{:S(2)}) collective-permute-start(bf16[2,2,8,128,128]{4,3,2,1,0:T(8,128)(2,1)S(1)} %bitcast.15), channel_id=1, source_target_pairs={{0,16},{4,68},{8,24},{12,76},{16,0},{20,84},{24,8},{28,92},{32,48}... | collective-permute-start | bytes 3145736 | tf_op jit(solution)/shard_map/ppermute | solution.py:44
  21.9 37.6 %collective-permute-start.6 = (bf16[2,2,8,128,128]{4,3,2,1,0:T(8,128)(2,1)S(1)}, bf16[2,2,8,128,128]{4,3,2,1,0:T(8,128)(2,1)S(1)}, u32[]{:S(2)}, u32[]{:S(2)}) collective-permute-start(bf16[2,2,8,128,128]{4,3,2,1,0:T(8,128)(2,1)S(1)} %bitcast.16), channel_id=1, source_target_pairs={{0,8},{4,36},{8,16},{12,44},{16,24},{20,52},{24,0},{28,60},{32,40}... | collective-permute-start | bytes 3145736 | tf_op jit(solution)/shard_map/ppermute | solution.py:44
  30.6 59.7 %collective-permute-start.2 = (bf16[32,2,128,128]{3,2,1,0:T(8,128)(2,1)}, bf16[32,2,128,128]{3,2,1,0:T(8,128)(2,1)}, u32[]{:S(2)}, u32[]{:S(2)}) collective-permute-start(bf16[32,2,128,128]{3,2,1,0:T(8,128)(2,1)} %constant_dynamic-update-slice_fusion.1.rest_0_), channel_id=1, source_target_pairs={{0,32},{4,12},{8,40},{12,20},{16,48},{20,28},{24,56},{28,4},{32,64... | collective-permute-start | bytes 6291464 | tf_op jit(solution)/shard_map/ppermute | solution.py:39
  32.3 58.0 %collective-permute-start.3 = (bf16[32,2,128,128]{3,2,1,0:T(8,128)(2,1)}, bf16[32,2,128,128]{3,2,1,0:T(8,128)(2,1)}, u32[]{:S(2)}, u32[]{:S(2)}) collective-permute-start(bf16[32,2,128,128]{3,2,1,0:T(8,128)(2,1)} %constant_dynamic-update-slice_fusion.1.rest_0_), channel_id=1, source_target_pairs={{0,96},{4,28},{8,104},{12,4},{16,112},{20,12},{24,120},{28,20},{32... | collective-permute-start | bytes 6291464 | tf_op jit(solution)/shard_map/ppermute | solution.py:39
  61.2 26.8 %collective-permute-start.9 = (bf16[16,2,128,128]{3,2,1,0:T(8,128)(2,1)}, bf16[16,2,128,128]{3,2,1,0:T(8,128)(2,1)}, u32[]{:S(2)}, u32[]{:S(2)}) collective-permute-start(bf16[16,2,128,128]{3,2,1,0:T(8,128)(2,1)} %split_cache.7), channel_id=1, source_target_pairs={{0,4},{4,0},{8,12},{12,8},{16,20},{20,16},{24,28},{28,24},{32,36},... | collective-permute-start | bytes 3145736 | tf_op jit(solution)/shard_map/ppermute | solution.py:48
  91.6 15.2 %collective-permute-start.10 = (bf16[16,2,128,128]{3,2,1,0:T(8,128)(2,1)S(1)}, bf16[16,2,128,128]{3,2,1,0:T(8,128)(2,1)S(1)}, u32[]{:S(2)}, u32[]{:S(2)}) collective-permute-start(bf16[16,2,128,128]{3,2,1,0:T(8,128)(2,1)S(1)} %slice.12), channel_id=1, source_target_pairs={{0,32},{4,12},{8,40},{12,20},{16,48},{20,28},{24,56},{28,4},{32,64... | collective-permute-start | bytes 3145736 | tf_op jit(solution)/shard_map/ppermute | solution.py:39
  107.5 34.3 %collective-permute-start.14 = (bf16[32,2,128,128]{3,2,1,0:T(8,128)(2,1)}, bf16[32,2,128,128]{3,2,1,0:T(8,128)(2,1)}, u32[]{:S(2)}, u32[]{:S(2)}) collective-permute-start(bf16[32,2,128,128]{3,2,1,0:T(8,128)(2,1)} %constant_dynamic-update-slice_fusion.rest_0_), channel_id=1, source_target_pairs={{0,32},{4,12},{8,40},{12,20},{16,48},{20,28},{24,56},{28,4},{32,64... | collective-permute-start | bytes 6291464 | tf_op jit(solution)/shard_map/ppermute | solution.py:39
  108.6 33.2 %collective-permute-start.15 = (bf16[32,2,128,128]{3,2,1,0:T(8,128)(2,1)}, bf16[32,2,128,128]{3,2,1,0:T(8,128)(2,1)}, u32[]{:S(2)}, u32[]{:S(2)}) collective-permute-start(bf16[32,2,128,128]{3,2,1,0:T(8,128)(2,1)} %constant_dynamic-update-slice_fusion.rest_0_), channel_id=1, source_target_pairs={{0,96},{4,28},{8,104},{12,4},{16,112},{20,12},{24,120},{28,20},{32... | collective-permute-start | bytes 6291464 | tf_op jit(solution)/shard_map/ppermute | solution.py:39
  123.1 17.8 %collective-permute-start.12 = (bf16[2096,128]{1,0:T(8,128)(2,1)}, bf16[2096,128]{1,0:T(8,128)(2,1)}, u32[]{:S(2)}, u32[]{:S(2)}) collective-permute-start(bf16[2096,128]{1,0:T(8,128)(2,1)} %get-tuple-element.118), channel_id=1, source_target_pairs={{0,8},{4,36},{8,16},{12,44},{16,24},{20,52},{24,0},{28,60},{32,40}... | collective-permute-start | bytes 1609736 | tf_op jit(solution)/shard_map/ppermute | solution.py:44
  124.4 17.4 %collective-permute-start.13 = (bf16[2096,128]{1,0:T(8,128)(2,1)}, bf16[2096,128]{1,0:T(8,128)(2,1)}, u32[]{:S(2)}, u32[]{:S(2)}) collective-permute-start(bf16[2096,128]{1,0:T(8,128)(2,1)} %get-tuple-element.119), channel_id=1, source_target_pairs={{0,24},{4,100},{8,0},{12,108},{16,8},{20,116},{24,16},{28,124},{32... | collective-permute-start | bytes 1609736 | tf_op jit(solution)/shard_map/ppermute | solution.py:44
  127.7 24.7 %collective-permute-start.16 = (bf16[2096,128]{1,0:T(8,128)(2,1)}, bf16[2096,128]{1,0:T(8,128)(2,1)}, u32[]{:S(2)}, u32[]{:S(2)}) collective-permute-start(bf16[2096,128]{1,0:T(8,128)(2,1)} %get-tuple-element.121), channel_id=1, source_target_pairs={{0,16},{4,68},{8,24},{12,76},{16,0},{20,84},{24,8},{28,92},{32,48}... | collective-permute-start | bytes 1609736 | tf_op jit(solution)/shard_map/ppermute | solution.py:44
  155.8 15.2 %collective-permute-start.18 = (bf16[16,2,128,128]{3,2,1,0:T(8,128)(2,1)S(1)}, bf16[16,2,128,128]{3,2,1,0:T(8,128)(2,1)S(1)}, u32[]{:S(2)}, u32[]{:S(2)}) collective-permute-start(bf16[16,2,128,128]{3,2,1,0:T(8,128)(2,1)S(1)} %slice.14), channel_id=1, source_target_pairs={{0,32},{4,12},{8,40},{12,20},{16,48},{20,28},{24,56},{28,4},{32,64... | collective-permute-start | bytes 3145736 | tf_op jit(solution)/shard_map/ppermute | solution.py:39
  157.1 14.5 %collective-permute-start.19 = (bf16[16,2,128,128]{3,2,1,0:T(8,128)(2,1)S(1)}, bf16[16,2,128,128]{3,2,1,0:T(8,128)(2,1)S(1)}, u32[]{:S(2)}, u32[]{:S(2)}) collective-permute-start(bf16[16,2,128,128]{3,2,1,0:T(8,128)(2,1)S(1)} %slice.15), channel_id=1, source_target_pairs={{0,96},{4,28},{8,104},{12,4},{16,112},{20,12},{24,120},{28,20},{32... | collective-permute-start | bytes 3145736 | tf_op jit(solution)/shard_map/ppermute | solution.py:39
  160.1 22.1 %collective-permute-start.20 = (bf16[2,1024,128]{2,1,0:T(8,128)(2,1)S(1)}, bf16[2,1024,128]{2,1,0:T(8,128)(2,1)S(1)}, u32[]{:S(2)}, u32[]{:S(2)}) collective-permute-start(bf16[2,1024,128]{2,1,0:T(8,128)(2,1)S(1)} %finish.2.a0), channel_id=1, source_target_pairs={{0,3},{1,0},{2,1},{3,2},{4,7},{5,4},{6,5},{7,6},{8,11},{9,8},{10,9... | collective-permute-start | bytes 1572872 | tf_op jit(solution)/shard_map/ppermute | solution.py:57
  162.7 19.6 %collective-permute-start.21 = (bf16[2,1024,128]{2,1,0:T(8,128)(2,1)S(1)}, bf16[2,1024,128]{2,1,0:T(8,128)(2,1)S(1)}, u32[]{:S(2)}, u32[]{:S(2)}) collective-permute-start(bf16[2,1024,128]{2,1,0:T(8,128)(2,1)S(1)} %finish.2.a0), channel_id=1, source_target_pairs={{0,1},{1,2},{2,3},{3,0},{4,5},{5,6},{6,7},{7,4},{8,9},{9,10},{10,1... | collective-permute-start | bytes 1572872 | tf_op jit(solution)/shard_map/ppermute | solution.py:57
  182.3 19.9 %collective-permute-start.23 = (bf16[2096,128]{1,0:T(8,128)(2,1)S(1)}, bf16[2096,128]{1,0:T(8,128)(2,1)S(1)}, u32[]{:S(2)}, u32[]{:S(2)}) collective-permute-start(bf16[2096,128]{1,0:T(8,128)(2,1)S(1)} %get-tuple-element.134), channel_id=1, source_target_pairs={{0,8},{4,36},{8,16},{12,44},{16,24},{20,52},{24,0},{28,60},{32,40}... | collective-permute-start | bytes 1609736 | tf_op jit(solution)/shard_map/ppermute | solution.py:44
  184.4 17.8 %collective-permute-start.24 = (bf16[2096,128]{1,0:T(8,128)(2,1)S(1)}, bf16[2096,128]{1,0:T(8,128)(2,1)S(1)}, u32[]{:S(2)}, u32[]{:S(2)}) collective-permute-start(bf16[2096,128]{1,0:T(8,128)(2,1)S(1)} %get-tuple-element.135), channel_id=1, source_target_pairs={{0,16},{4,68},{8,24},{12,76},{16,0},{20,84},{24,8},{28,92},{32,48}... | collective-permute-start | bytes 1609736 | tf_op jit(solution)/shard_map/ppermute | solution.py:44
  187.2 14.9 %collective-permute-start.25 = (bf16[2096,128]{1,0:T(8,128)(2,1)S(1)}, bf16[2096,128]{1,0:T(8,128)(2,1)S(1)}, u32[]{:S(2)}, u32[]{:S(2)}) collective-permute-start(bf16[2096,128]{1,0:T(8,128)(2,1)S(1)} %get-tuple-element.136), channel_id=1, source_target_pairs={{0,24},{4,100},{8,0},{12,108},{16,8},{20,116},{24,16},{28,124},{32... | collective-permute-start | bytes 1609736 | tf_op jit(solution)/shard_map/ppermute | solution.py:44
  187.2 14.9 %collective-permute-start.22 = (bf16[2,1024,128]{2,1,0:T(8,128)(2,1)S(1)}, bf16[2,1024,128]{2,1,0:T(8,128)(2,1)S(1)}, u32[]{:S(2)}, u32[]{:S(2)}) collective-permute-start(bf16[2,1024,128]{2,1,0:T(8,128)(2,1)S(1)} %finish.2.a0), channel_id=1, source_target_pairs={{0,2},{1,3},{2,0},{3,1},{4,6},{5,7},{6,4},{7,5},{8,10},{9,11},{10,... | collective-permute-start | bytes 1572872 | tf_op jit(solution)/shard_map/ppermute | solution.py:57
  205.1 24.6 %collective-permute-start.27 = (bf16[2,1024,128]{2,1,0:T(8,128)(2,1)S(1)}, bf16[2,1024,128]{2,1,0:T(8,128)(2,1)S(1)}, u32[]{:S(2)}, u32[]{:S(2)}) collective-permute-start(bf16[2,1024,128]{2,1,0:T(8,128)(2,1)S(1)} %finish.3.a0), channel_id=1, source_target_pairs={{0,3},{1,0},{2,1},{3,2},{4,7},{5,4},{6,5},{7,6},{8,11},{9,8},{10,9... | collective-permute-start | bytes 1572872 | tf_op jit(solution)/shard_map/ppermute | solution.py:57
  207.6 22.0 %collective-permute-start.28 = (bf16[2,1024,128]{2,1,0:T(8,128)(2,1)S(1)}, bf16[2,1024,128]{2,1,0:T(8,128)(2,1)S(1)}, u32[]{:S(2)}, u32[]{:S(2)}) collective-permute-start(bf16[2,1024,128]{2,1,0:T(8,128)(2,1)S(1)} %finish.3.a0), channel_id=1, source_target_pairs={{0,2},{1,3},{2,0},{3,1},{4,6},{5,7},{6,4},{7,5},{8,10},{9,11},{10,... | collective-permute-start | bytes 1572872 | tf_op jit(solution)/shard_map/ppermute | solution.py:57
  208.1 26.1 %collective-permute-start.29 = (bf16[2,1024,128]{2,1,0:T(8,128)(2,1)S(1)}, bf16[2,1024,128]{2,1,0:T(8,128)(2,1)S(1)}, u32[]{:S(2)}, u32[]{:S(2)}) collective-permute-start(bf16[2,1024,128]{2,1,0:T(8,128)(2,1)S(1)} %finish.3.a0), channel_id=1, source_target_pairs={{0,1},{1,2},{2,3},{3,0},{4,5},{5,6},{6,7},{7,4},{8,9},{9,10},{10,1... | collective-permute-start | bytes 1572872 | tf_op jit(solution)/shard_map/ppermute | solution.py:57
  (29 other events, 176.3 us)

commit v6 on v5

--- a/solution.py
+++ b/solution.py
@@ -518,27 +518,24 @@
     def after(x, *deps):
         return lax.optimization_barrier((x, *deps))[0]
 
-    normed, q_keep, q_send = query(core, tokens, norm_gain, w_query)
-    send0 = split_cache(2 - 2 * after(core, q_send), kv_cache)
+    got0 = core_swap(split_cache(2 - 2 * core, kv_cache))
+    rows0 = lax.dynamic_update_slice(split_cache(2 * core, kv_cache, 2), got0, (16, 0, 0, 0))
+    up0, down0 = rows_perm(rows0, 1), rows_perm(rows0, -1)
+
+    normed, q_keep, q_send = query(core, tokens, after(norm_gain, rows0), w_query)
     mine = jnp.concatenate([q_keep, core_swap(q_send)], axis=0).reshape(2, 2, 8, BLOCK, HD)
     q1, q3, q2 = query_perm(mine, -1), query_perm(mine, 1), query_perm(mine, 2)
-
-    keep0 = split_cache(2 * after(core, mine), kv_cache, 2)
-    rows0 = lax.dynamic_update_slice(keep0, core_swap(send0), (16, 0, 0, 0))
-    up0, down0 = rows_perm(rows0, 1), rows_perm(rows0, -1)
-    core1 = after(core, rows0)
+    core1 = after(core, mine)
     send1, keep1 = split_cache(3 - 2 * core1, kv_cache), split_cache(1 + 2 * core1, kv_cache, 2)
     normed, keep1, send1 = lax.optimization_barrier((normed, keep1, send1))
     k_all, v_all, swap, edge = project(core, normed, w_key, w_value)
     send1, swap, edge, q1, q2, q3 = lax.optimization_barrier((send1, swap, edge, q1, q2, q3))
     swapped, halo = core_swap(swap), halo_perm(edge)
     rows1 = lax.dynamic_update_slice(keep1, core_swap(send1), (16, 0, 0, 0))
+    up20, down20 = rows_perm(up0[:16], 1), rows_perm(down0[16:], -1)
     code, cnt = line_codes(wake_blocks, wake_frames, wake_counts, y, z, c)
-    halo, *lists = lax.optimization_barrier((halo, *plan(cnt, code)))
-    near_o, near_lse = near(core, q_keep, q_send, k_all, v_all, halo, swapped)
-    up0, down0, near_o, near_lse, rows1 = lax.optimization_barrier((up0, down0, near_o, near_lse, rows1))
-    up20, down20 = rows_perm(up0[:16], 1), rows_perm(down0[16:], -1)
-    rows1, up20, down20 = lax.optimization_barrier((rows1, up20, down20))
+    lists = plan(cnt, code)
+    rows1, up20, down20, *lists = lax.optimization_barrier((rows1, up20, down20, *lists))
     up1, down1 = rows_perm(rows1, 1), rows_perm(rows1, -1)
     qs = [mine, q1, q2, q3]
 
@@ -550,10 +547,12 @@
 
     parts = far(0, cnt, lists, [rows0, down0, up20, down20, up0], qs)
     weights = pick(after(place, parts[0]), w_out)
+    halo, swapped, *_ = lax.optimization_barrier((halo, swapped, parts[0]))
+    near_o, near_lse = near(core, q_keep, q_send, k_all, v_all, halo, swapped)
     back = returned(parts)
     back[1], back[3], up1, down1 = lax.optimization_barrier((back[1], back[3], up1, down1))
     up21, down21 = rows_perm(up1[:16], 1), rows_perm(down1[16:], -1)
-    back[0], *weights = lax.optimization_barrier((back[0], *weights))
+    back[0], near_lse, *weights = lax.optimization_barrier((back[0], near_lse, *weights))
     own, other = merge(back)
     heads = finish(0, near_o, near_lse, own, core_swap(other))
     gathered = gather(heads)

time: 238 us -> 227 us (0.954)
  waiting for transfers between devices: 80.2 us -> 74.9 us
  local copies, waits for them, and re-layouts: 22.2 us -> 18.7 us
    ppermute x9, waiting for transfers between devices: 21.4 us -> 7.69 us  [query_perm(): return lax.ppermute(x, 'tok', pairs)]
    ppermute x1, waiting for transfers between devices: 0.01 us -> 13.1 us  [halo_perm(): lax.ppermute(x, 'tok', [(i, (i + (1 if i % 2 else -1)) % n) for i in rang...]
    unnamed x46 -> x52, local copies, waits for them, and re-layouts: 13 us -> 8.16 us
    ppermute x8, waiting for transfers between devices: 20.7 us -> 17.3 us  [rows_perm(): return lax.ppermute(x, 'tok', pairs)]
  transfers between devices with their start and end apart: 30 -> 30, of which waited for: 13 -> 11; matrix products, arithmetic and copies ran while one was open for 4% -> 4% of each run, Pallas kernels for 30% -> 33%
where the time goes in v6:
time: 227 us; the launch traced here: 226 us
  Pallas kernels  86.4 us (38%)
  waiting for transfers between devices  74.9 us (33%)
  starting transfers between devices  45.1 us (20%)
  local copies, waits for them, and re-layouts  18.7 us (8%)
    ppermute x6, waiting for transfers between devices, mp_perm(): return lax.ppermute(x, 'mp', [(i, (i + d) % NX) for i in range(NX)])  33.4 us
    pallas_call x4, Pallas kernels, split_cache(): pl.pallas_call(split_cache_kernel, grid_spec=pltpu.PrefetchScalarGridSpec...  22.9 us
    pallas_call x2, Pallas kernels, far(): pl.pallas_call(functools.partial(far_kernel, j), in_specs=[SMEM] * 5 + [A...  21.6 us
    ppermute x8, waiting for transfers between devices, rows_perm(): return lax.ppermute(x, 'tok', pairs)  17.3 us
    ppermute x8, starting transfers between devices, rows_perm(): return lax.ppermute(x, 'tok', pairs)  13.5 us
    ppermute x1, waiting for transfers between devices, halo_perm(): lax.ppermute(x, 'tok', [(i, (i + (1 if i % 2 else -1)) % n) for i in rang...  13.1 us
    ppermute x9, starting transfers between devices, query_perm(): return lax.ppermute(x, 'tok', pairs)  12.9 us
    pallas_call x1, Pallas kernels, project(): pl.pallas_call(project_kernel, grid_spec=pltpu.PrefetchScalarGridSpec(num...  10.3 us
  transfers between devices with their start and end apart: 30, of which 11 were waited for; matrix products, arithmetic and copies ran while one was open for 4% of the time, Pallas kernels for 33%

profile of v6, /device:TPU:1, one launch (start us, length us, event | category | flops | bytes accessed | tf_op | source)
XLA Modules:
  0.0 226.0 jit_solution(4399670015756774506)
XLA Ops:
  2.2 4.5 %split_cache.5 = bf16[16,2,128,128]{3,2,1,0:T(8,128)(2,1)S(1)} custom-call(s32[1]{0:T(128)S(6)} %sub.20.head_ref, bf16[2,1024,2,512]{3,2,1,0:T(2,128)(2,1)S(1)} %copy-done), custom_call_target="tpu_custom_call" | custom-call | flops 1 | bytes 1 | tf_op jit(solution)/shard_map/split_cache/pallas_call | solution.py:76
  8.2 6.9 %split_cache.4 = bf16[32,2,128,128]{3,2,1,0:T(8,128)(2,1)} custom-call(s32[1]{0:T(128)S(6)} %mul.35.head_ref, bf16[2,1024,2,512]{3,2,1,0:T(2,128)(2,1)} %src.7), custom_call_target="tpu_custom_call" | custom-call | flops 1 | bytes 1 | tf_op jit(solution)/shard_map/split_cache/pallas_call | solution.py:76
  20.1 6.9 %query.1 = (bf16[1024,2048]{1,0:T(8,128)(2,1)}, bf16[2,1024,128]{2,1,0:T(8,128)(2,1)S(1)}, bf16[2,1024,128]{2,1,0:T(8,128)(2,1)S(1)}) custom-call(s32[1]{0:T(128)} %bitcast.core_ref, bf16[1024,2048]{1,0:T(8,128)(2,1)} %carried.1, f32[1,2048]{1,0:T(1,128)S(1)} %bitcast.23, bf16[2048,512]{1,0:T(8,128)(2,1)S(1)} %copy-done.3), custom_call_target="tpu_custom_call" | custom-call | flops 1 | bytes 1 | tf_op jit(solution)/shard_map/query/pallas_call | solution.py:120
  29.0 2.8 %collective-permute-start.2 = (bf16[2,2,8,128,128]{4,3,2,1,0:T(8,128)(2,1)S(1)}, bf16[2,2,8,128,128]{4,3,2,1,0:T(8,128)(2,1)S(1)}, u32[]{:S(2)}, u32[]{:S(2)}) collective-permute-start(bf16[2,2,8,128,128]{4,3,2,1,0:T(8,128)(2,1)S(1)} %bitcast.14), channel_id=1, source_target_pairs={{0,24},{4,100},{8,0},{12,108},{16,8},{20,116},{24,16},{28,124},{32... | collective-permute-start | bytes 3145736 | tf_op jit(solution)/shard_map/ppermute | solution.py:44
  32.8 6.1 %split_cache.6 = bf16[32,2,128,128]{3,2,1,0:T(8,128)(2,1)S(1)} custom-call(s32[1]{0:T(128)S(6)} %add.42.head_ref, bf16[2,1024,2,512]{3,2,1,0:T(2,128)(2,1)} %src.7), custom_call_target="tpu_custom_call" | custom-call | flops 1 | bytes 1 | tf_op jit(solution)/shard_map/split_cache/pallas_call | solution.py:76
  39.0 5.4 %split_cache.7 = bf16[16,2,128,128]{3,2,1,0:T(8,128)(2,1)} custom-call(s32[1]{0:T(128)S(6)} %sub.21.head_ref, bf16[2,1024,2,512]{3,2,1,0:T(2,128)(2,1)S(1)} %copy-done.1), custom_call_target="tpu_custom_call" | custom-call | flops 1 | bytes 1 | tf_op jit(solution)/shard_map/split_cache/pallas_call | solution.py:76
  44.4 10.3 %project.1 = (bf16[4,8,128,128]{3,2,1,0:T(8,128)(2,1)S(1)}, bf16[4,8,128,128]{3,2,1,0:T(8,128)(2,1)S(1)}, bf16[1024,128]{1,0:T(8,128)(2,1)S(1)}, bf16[1024,128]{1,0:T(8,128)(2,1)S(1)}) custom-call(s32[1]{0:T(128)} %bitcast.core_ref, bf16[1024,2048]{1,0:T(8,128)(2,1)} %get-tuple-element.76.normed_ref, bf16[2048,512]{1,0:T(8,128)(2,1)S(1)} %copy-done.6, ...), custom_call_target="tpu_custom_call" | custom-call | flops 1 | bytes 1 | tf_op jit(solution)/shard_map/project/pallas_call | solution.py:172
  58.2 7.7 %collective-permute-done.4.rest_8_ = bf16[2,2,8,128,128]{4,3,2,1,0:T(8,128)(2,1)S(1)} collective-permute-done((bf16[2,2,8,128,128]{4,3,2,1,0:T(8,128)(2,1)S(1)}, bf16[2,2,8,128,128]{4,3,2,1,0:T(8,128)(2,1)S(1)}, u32[]{:S(2)}, u32[]{:S(2)}) %collective-permute-start.4) | collective-permute-done | bytes 1048608 | tf_op jit(solution)/shard_map/ppermute | solution.py:44
  77.2 2.9 %plan.1 = (s32[100]{0:T(128)S(1)}, s32[64]{0:T(128)S(1)}, s32[64]{0:T(128)S(1)}, s32[2]{0:T(128)S(1)}) custom-call(s32[64]{0:T(128)S(1)} %reduce_sum.12.cnt_ref, s32[512]{0:T(512)S(1)} %reshape.73.code_ref), custom_call_target="tpu_custom_call" | custom-call | flops 1 | bytes 1 | tf_op jit(solution)/shard_map/plan/pallas_call | solution.py:272
  81.5 5.1 %collective-permute-done.9.rest_2_ = bf16[16,2,128,128]{3,2,1,0:T(8,128)(2,1)} collective-permute-done((bf16[16,2,128,128]{3,2,1,0:T(8,128)(2,1)}, bf16[16,2,128,128]{3,2,1,0:T(8,128)(2,1)}, u32[]{:S(2)}, u32[]{:S(2)}) %collective-permute-start.9) | collective-permute-done | bytes 1048608 | tf_op jit(solution)/shard_map/ppermute | solution.py:39
  91.9 3.0 %collective-permute-start.5 = (bf16[1024,128]{1,0:T(8,128)(2,1)}, bf16[1024,128]{1,0:T(8,128)(2,1)S(1)}, u32[]{:S(2)}, u32[]{:S(2)}) collective-permute-start(bf16[1024,128]{1,0:T(8,128)(2,1)} %copy-done.19), channel_id=1, source_target_pairs={{0,124},{4,8},{8,4},{12,16},{16,12},{20,24},{24,20},{28,32},{32,28... | collective-permute-start | bytes 786440 | tf_op jit(solution)/shard_map/ppermute | solution.py:53
  96.0 11.6 %far.2 = (bf16[2096,128]{1,0:T(8,128)(2,1)S(1)}, bf16[2096,128]{1,0:T(8,128)(2,1)}, bf16[2096,128]{1,0:T(8,128)(2,1)}, bf16[2096,128]{1,0:T(8,128)(2,1)}) custom-call(s32[64]{0:T(128)S(1)} %reduce_sum.12.cnt_ref, s32[100]{0:T(128)S(1)} %get-tuple-element.90.unit_ref, s32[64]{0:T(128)S(1)} %get-tuple-element.91.first_ref, s32[64]{0:T(128)S(1)} %get-tuple-element.92.long_ref, ...), custom_call_target="tpu_custom_call" | custom-call | flops 1 | bytes 1 | tf_op jit(solution)/shard_map/far/pallas_call | solution.py:357
  108.4 13.1 %collective-permute-done.5 = bf16[1024,128]{1,0:T(8,128)(2,1)S(1)} collective-permute-done((bf16[1024,128]{1,0:T(8,128)(2,1)}, bf16[1024,128]{1,0:T(8,128)(2,1)S(1)}, u32[]{:S(2)}, u32[]{:S(2)}) %collective-permute-start.5) | collective-permute-done | bytes 262176 | tf_op jit(solution)/shard_map/ppermute | solution.py:53
  121.5 2.7 %collective-permute-start.13 = (bf16[2096,128]{1,0:T(8,128)(2,1)}, bf16[2096,128]{1,0:T(8,128)(2,1)}, u32[]{:S(2)}, u32[]{:S(2)}) collective-permute-start(bf16[2096,128]{1,0:T(8,128)(2,1)} %get-tuple-element.111), channel_id=1, source_target_pairs={{0,24},{4,100},{8,0},{12,108},{16,8},{20,116},{24,16},{28,124},{32... | collective-permute-start | bytes 1609736 | tf_op jit(solution)/shard_map/ppermute | solution.py:44
  128.5 8.7 %near.1 = (f32[4,8,128,128]{3,2,1,0:T(8,128)S(1)}, f32[4,8,128]{2,1,0:T(8,128)S(1)}) custom-call(s32[1]{0:T(128)} %bitcast.core_ref, bf16[2,1024,128]{2,1,0:T(8,128)(2,1)S(1)} %copy-done.5, bf16[2,1024,128]{2,1,0:T(8,128)(2,1)S(1)} %copy-done.16, bf16[4,8,128,128]{3,2,1,0:T(8,128)(2,1)S(1)} %copy-done.8, bf16[4,8,128,128]{3,2,1,0:T(8,128)(2,1)S(1)} %copy-done.10, ...), custom_call_target="tpu_custom_call" | custom-call | flops 1 | bytes 1 | tf_op jit(solution)/shard_map/near/pallas_call | solution.py:217
  149.9 8.2 %collective-permute-done.18.rest_2_ = bf16[16,2,128,128]{3,2,1,0:T(8,128)(2,1)S(1)} collective-permute-done((bf16[16,2,128,128]{3,2,1,0:T(8,128)(2,1)S(1)}, bf16[16,2,128,128]{3,2,1,0:T(8,128)(2,1)S(1)}, u32[]{:S(2)}, u32[]{:S(2)}) %collective-permute-start.18) | collective-permute-done | bytes 1048608 | tf_op jit(solution)/shard_map/ppermute | solution.py:39
  159.4 10.1 %far.3 = (bf16[2096,128]{1,0:T(8,128)(2,1)S(1)}, bf16[2096,128]{1,0:T(8,128)(2,1)S(1)}, bf16[2096,128]{1,0:T(8,128)(2,1)S(1)}, bf16[2096,128]{1,0:T(8,128)(2,1)S(1)}) custom-call(s32[64]{0:T(128)S(1)} %reduce_sum.12.cnt_ref, s32[100]{0:T(128)S(1)} %get-tuple-element.90.unit_ref, s32[64]{0:T(128)S(1)} %get-tuple-element.91.first_ref, ...), custom_call_target="tpu_custom_call" | custom-call | flops 1 | bytes 1 | tf_op jit(solution)/shard_map/far/pallas_call | solution.py:357
  170.1 3.4 %collective-permute-start.24 = (bf16[2096,128]{1,0:T(8,128)(2,1)S(1)}, bf16[2096,128]{1,0:T(8,128)(2,1)S(1)}, u32[]{:S(2)}, u32[]{:S(2)}) collective-permute-start(bf16[2096,128]{1,0:T(8,128)(2,1)S(1)} %get-tuple-element.127), channel_id=1, source_target_pairs={{0,16},{4,68},{8,24},{12,76},{16,0},{20,84},{24,8},{28,92},{32,48}... | collective-permute-start | bytes 1609736 | tf_op jit(solution)/shard_map/ppermute | solution.py:44
  175.1 2.7 %collective-permute-start.22 = (bf16[2,1024,128]{2,1,0:T(8,128)(2,1)S(1)}, bf16[2,1024,128]{2,1,0:T(8,128)(2,1)S(1)}, u32[]{:S(2)}, u32[]{:S(2)}) collective-permute-start(bf16[2,1024,128]{2,1,0:T(8,128)(2,1)S(1)} %finish.2.a0), channel_id=1, source_target_pairs={{0,2},{1,3},{2,0},{3,1},{4,6},{5,7},{6,4},{7,5},{8,10},{9,11},{10,... | collective-permute-start | bytes 1572872 | tf_op jit(solution)/shard_map/ppermute | solution.py:57
  177.8 11.9 %collective-permute-done.22.a2 = bf16[2,1024,128]{2,1,0:T(8,128)(2,1)S(1)} collective-permute-done((bf16[2,1024,128]{2,1,0:T(8,128)(2,1)S(1)}, bf16[2,1024,128]{2,1,0:T(8,128)(2,1)S(1)}, u32[]{:S(2)}, u32[]{:S(2)}) %collective-permute-start.22) | collective-permute-done | bytes 524320 | tf_op jit(solution)/shard_map/ppermute | solution.py:57
  197.1 4.0 %mix.2.carried = f32[1024,512]{1,0:T(8,128)S(1)} custom-call(s32[2]{0:T(128)S(1)} %pad_add_fusion.place_ref, bf16[2,1024,128]{2,1,0:T(8,128)(2,1)S(1)} %finish.2.a0, bf16[2,1024,128]{2,1,0:T(8,128)(2,1)S(1)} %collective-permute-done.20.a1, bf16[2,1024,128]{2,1,0:T(8,128)(2,1)S(1)} %collective-permute-done.22.a2, ...), custom_call_target="tpu_custom_call" | custom-call | flops 1 | bytes 1 | tf_op jit(solution)/shard_map/mix/pallas_call | solution.py:476
  201.1 16.9 %collective-permute-done.27.a1 = bf16[2,1024,128]{2,1,0:T(8,128)(2,1)S(1)} collective-permute-done((bf16[2,1024,128]{2,1,0:T(8,128)(2,1)S(1)}, bf16[2,1024,128]{2,1,0:T(8,128)(2,1)S(1)}, u32[]{:S(2)}, u32[]{:S(2)}) %collective-permute-start.27) | collective-permute-done | bytes 524320 | tf_op jit(solution)/shard_map/ppermute | solution.py:57
  218.0 4.6 %collective-permute-done.29.a3 = bf16[2,1024,128]{2,1,0:T(8,128)(2,1)S(1)} collective-permute-done((bf16[2,1024,128]{2,1,0:T(8,128)(2,1)S(1)}, bf16[2,1024,128]{2,1,0:T(8,128)(2,1)S(1)}, u32[]{:S(2)}, u32[]{:S(2)}) %collective-permute-start.29) | collective-permute-done | bytes 524320 | tf_op jit(solution)/shard_map/ppermute | solution.py:57
  222.6 3.4 %mix.3 = bf16[1024,512]{1,0:T(8,128)(2,1)} custom-call(s32[2]{0:T(128)S(1)} %pad_add_fusion.place_ref, bf16[2,1024,128]{2,1,0:T(8,128)(2,1)S(1)} %finish.3.a0, bf16[2,1024,128]{2,1,0:T(8,128)(2,1)S(1)} %collective-permute-done.27.a1, bf16[2,1024,128]{2,1,0:T(8,128)(2,1)S(1)} %collective-permute-done.28.a2, ...), custom_call_target="tpu_custom_call" | custom-call | flops 1 | bytes 1 | tf_op jit(solution)/shard_map/mix/pallas_call | solution.py:476
  (125 shorter events, 62.7 us)
Async XLA Ops:
  16.2 51.9 %collective-permute-start.8 = (bf16[32,2,128,128]{3,2,1,0:T(8,128)(2,1)}, bf16[32,2,128,128]{3,2,1,0:T(8,128)(2,1)}, u32[]{:S(2)}, u32[]{:S(2)}) collective-permute-start(bf16[32,2,128,128]{3,2,1,0:T(8,128)(2,1)} %constant_dynamic-update-slice_fusion.1.rest_0_), channel_id=1, source_target_pairs={{0,32},{4,12},{8,40},{12,20},{16,48},{20,28},{24,56},{28,4},{32,64... | collective-permute-start | bytes 6291464 | tf_op jit(solution)/shard_map/ppermute | solution.py:39
  18.0 54.7 %collective-permute-start.10 = (bf16[32,2,128,128]{3,2,1,0:T(8,128)(2,1)}, bf16[32,2,128,128]{3,2,1,0:T(8,128)(2,1)}, u32[]{:S(2)}, u32[]{:S(2)}) collective-permute-start(bf16[32,2,128,128]{3,2,1,0:T(8,128)(2,1)} %constant_dynamic-update-slice_fusion.1.rest_0_), channel_id=1, source_target_pairs={{0,96},{4,28},{8,104},{12,4},{16,112},{20,12},{24,120},{28,20},{32... | collective-permute-start | bytes 6291464 | tf_op jit(solution)/shard_map/ppermute | solution.py:39
  29.0 29.1 %collective-permute-start.2 = (bf16[2,2,8,128,128]{4,3,2,1,0:T(8,128)(2,1)S(1)}, bf16[2,2,8,128,128]{4,3,2,1,0:T(8,128)(2,1)S(1)}, u32[]{:S(2)}, u32[]{:S(2)}) collective-permute-start(bf16[2,2,8,128,128]{4,3,2,1,0:T(8,128)(2,1)S(1)} %bitcast.14), channel_id=1, source_target_pairs={{0,24},{4,100},{8,0},{12,108},{16,8},{20,116},{24,16},{28,124},{32... | collective-permute-start | bytes 3145736 | tf_op jit(solution)/shard_map/ppermute | solution.py:44
  31.8 26.3 %collective-permute-start.3 = (bf16[2,2,8,128,128]{4,3,2,1,0:T(8,128)(2,1)S(1)}, bf16[2,2,8,128,128]{4,3,2,1,0:T(8,128)(2,1)S(1)}, u32[]{:S(2)}, u32[]{:S(2)}) collective-permute-start(bf16[2,2,8,128,128]{4,3,2,1,0:T(8,128)(2,1)S(1)} %bitcast.15), channel_id=1, source_target_pairs={{0,16},{4,68},{8,24},{12,76},{16,0},{20,84},{24,8},{28,92},{32,48}... | collective-permute-start | bytes 3145736 | tf_op jit(solution)/shard_map/ppermute | solution.py:44
  32.2 33.7 %collective-permute-start.4 = (bf16[2,2,8,128,128]{4,3,2,1,0:T(8,128)(2,1)S(1)}, bf16[2,2,8,128,128]{4,3,2,1,0:T(8,128)(2,1)S(1)}, u32[]{:S(2)}, u32[]{:S(2)}) collective-permute-start(bf16[2,2,8,128,128]{4,3,2,1,0:T(8,128)(2,1)S(1)} %bitcast.16), channel_id=1, source_target_pairs={{0,8},{4,36},{8,16},{12,44},{16,24},{20,52},{24,0},{28,60},{32,40}... | collective-permute-start | bytes 3145736 | tf_op jit(solution)/shard_map/ppermute | solution.py:44
  70.5 16.1 %collective-permute-start.9 = (bf16[16,2,128,128]{3,2,1,0:T(8,128)(2,1)}, bf16[16,2,128,128]{3,2,1,0:T(8,128)(2,1)}, u32[]{:S(2)}, u32[]{:S(2)}) collective-permute-start(bf16[16,2,128,128]{3,2,1,0:T(8,128)(2,1)} %slice.16), channel_id=1, source_target_pairs={{0,32},{4,12},{8,40},{12,20},{16,48},{20,28},{24,56},{28,4},{32,64... | collective-permute-start | bytes 3145736 | tf_op jit(solution)/shard_map/ppermute | solution.py:39
  75.0 14.3 %collective-permute-start.11 = (bf16[16,2,128,128]{3,2,1,0:T(8,128)(2,1)}, bf16[16,2,128,128]{3,2,1,0:T(8,128)(2,1)}, u32[]{:S(2)}, u32[]{:S(2)}) collective-permute-start(bf16[16,2,128,128]{3,2,1,0:T(8,128)(2,1)} %slice.17), channel_id=1, source_target_pairs={{0,96},{4,28},{8,104},{12,4},{16,112},{20,12},{24,120},{28,20},{32... | collective-permute-start | bytes 3145736 | tf_op jit(solution)/shard_map/ppermute | solution.py:39
  89.2 48.0 %collective-permute-start.14 = (bf16[32,2,128,128]{3,2,1,0:T(8,128)(2,1)S(1)}, bf16[32,2,128,128]{3,2,1,0:T(8,128)(2,1)}, u32[]{:S(2)}, u32[]{:S(2)}) collective-permute-start(bf16[32,2,128,128]{3,2,1,0:T(8,128)(2,1)S(1)} %constant_dynamic-update-slice_fusion.rest_0_), channel_id=1, source_target_pairs={{0,32},{4,12},{8,40},{12,20},{16,48},{20,28},{24,56},{28,4},{32,64... | collective-permute-start | bytes 6291464 | tf_op jit(solution)/shard_map/ppermute | solution.py:39
  89.9 47.3 %collective-permute-start.15 = (bf16[32,2,128,128]{3,2,1,0:T(8,128)(2,1)S(1)}, bf16[32,2,128,128]{3,2,1,0:T(8,128)(2,1)}, u32[]{:S(2)}, u32[]{:S(2)}) collective-permute-start(bf16[32,2,128,128]{3,2,1,0:T(8,128)(2,1)S(1)} %constant_dynamic-update-slice_fusion.rest_0_), channel_id=1, source_target_pairs={{0,96},{4,28},{8,104},{12,4},{16,112},{20,12},{24,120},{28,20},{32... | collective-permute-start | bytes 6291464 | tf_op jit(solution)/shard_map/ppermute | solution.py:39
  91.9 29.6 %collective-permute-start.5 = (bf16[1024,128]{1,0:T(8,128)(2,1)}, bf16[1024,128]{1,0:T(8,128)(2,1)S(1)}, u32[]{:S(2)}, u32[]{:S(2)}) collective-permute-start(bf16[1024,128]{1,0:T(8,128)(2,1)} %copy-done.19), channel_id=1, source_target_pairs={{0,124},{4,8},{8,4},{12,16},{16,12},{20,24},{24,20},{28,32},{32,28... | collective-permute-start | bytes 786440 | tf_op jit(solution)/shard_map/ppermute | solution.py:53
  94.9 29.4 %collective-permute-start.6 = (bf16[1024,128]{1,0:T(8,128)(2,1)}, bf16[1024,128]{1,0:T(8,128)(2,1)S(1)}, u32[]{:S(2)}, u32[]{:S(2)}) collective-permute-start(bf16[1024,128]{1,0:T(8,128)(2,1)} %copy-done.18), channel_id=1, source_target_pairs={{0,4},{4,0},{8,12},{12,8},{16,20},{20,16},{24,28},{28,24},{32,36},... | collective-permute-start | bytes 786440 | tf_op jit(solution)/shard_map/ppermute | solution.py:48
  108.4 28.8 %collective-permute-start.12 = (bf16[2096,128]{1,0:T(8,128)(2,1)}, bf16[2096,128]{1,0:T(8,128)(2,1)}, u32[]{:S(2)}, u32[]{:S(2)}) collective-permute-start(bf16[2096,128]{1,0:T(8,128)(2,1)} %get-tuple-element.110), channel_id=1, source_target_pairs={{0,8},{4,36},{8,16},{12,44},{16,24},{20,52},{24,0},{28,60},{32,40}... | collective-permute-start | bytes 1609736 | tf_op jit(solution)/shard_map/ppermute | solution.py:44
  121.5 15.7 %collective-permute-start.13 = (bf16[2096,128]{1,0:T(8,128)(2,1)}, bf16[2096,128]{1,0:T(8,128)(2,1)}, u32[]{:S(2)}, u32[]{:S(2)}) collective-permute-start(bf16[2096,128]{1,0:T(8,128)(2,1)} %get-tuple-element.111), channel_id=1, source_target_pairs={{0,24},{4,100},{8,0},{12,108},{16,8},{20,116},{24,16},{28,124},{32... | collective-permute-start | bytes 1609736 | tf_op jit(solution)/shard_map/ppermute | solution.py:44
  142.1 16.0 %collective-permute-start.18 = (bf16[16,2,128,128]{3,2,1,0:T(8,128)(2,1)S(1)}, bf16[16,2,128,128]{3,2,1,0:T(8,128)(2,1)S(1)}, u32[]{:S(2)}, u32[]{:S(2)}) collective-permute-start(bf16[16,2,128,128]{3,2,1,0:T(8,128)(2,1)S(1)} %slice.14), channel_id=1, source_target_pairs={{0,32},{4,12},{8,40},{12,20},{16,48},{20,28},{24,56},{28,4},{32,64... | collective-permute-start | bytes 3145736 | tf_op jit(solution)/shard_map/ppermute | solution.py:39
  145.4 14.0 %collective-permute-start.19 = (bf16[16,2,128,128]{3,2,1,0:T(8,128)(2,1)S(1)}, bf16[16,2,128,128]{3,2,1,0:T(8,128)(2,1)S(1)}, u32[]{:S(2)}, u32[]{:S(2)}) collective-permute-start(bf16[16,2,128,128]{3,2,1,0:T(8,128)(2,1)S(1)} %slice.15), channel_id=1, source_target_pairs={{0,96},{4,28},{8,104},{12,4},{16,112},{20,12},{24,120},{28,20},{32... | collective-permute-start | bytes 3145736 | tf_op jit(solution)/shard_map/ppermute | solution.py:39
  147.3 22.1 %collective-permute-start.20 = (bf16[2,1024,128]{2,1,0:T(8,128)(2,1)S(1)}, bf16[2,1024,128]{2,1,0:T(8,128)(2,1)S(1)}, u32[]{:S(2)}, u32[]{:S(2)}) collective-permute-start(bf16[2,1024,128]{2,1,0:T(8,128)(2,1)S(1)} %finish.2.a0), channel_id=1, source_target_pairs={{0,3},{1,0},{2,1},{3,2},{4,7},{5,4},{6,5},{7,6},{8,11},{9,8},{10,9... | collective-permute-start | bytes 1572872 | tf_op jit(solution)/shard_map/ppermute | solution.py:57
  149.9 19.6 %collective-permute-start.21 = (bf16[2,1024,128]{2,1,0:T(8,128)(2,1)S(1)}, bf16[2,1024,128]{2,1,0:T(8,128)(2,1)S(1)}, u32[]{:S(2)}, u32[]{:S(2)}) collective-permute-start(bf16[2,1024,128]{2,1,0:T(8,128)(2,1)S(1)} %finish.2.a0), channel_id=1, source_target_pairs={{0,1},{1,2},{2,3},{3,0},{4,5},{5,6},{6,7},{7,4},{8,9},{9,10},{10,1... | collective-permute-start | bytes 1572872 | tf_op jit(solution)/shard_map/ppermute | solution.py:57
  169.5 20.3 %collective-permute-start.23 = (bf16[2096,128]{1,0:T(8,128)(2,1)S(1)}, bf16[2096,128]{1,0:T(8,128)(2,1)S(1)}, u32[]{:S(2)}, u32[]{:S(2)}) collective-permute-start(bf16[2096,128]{1,0:T(8,128)(2,1)S(1)} %get-tuple-element.126), channel_id=1, source_target_pairs={{0,8},{4,36},{8,16},{12,44},{16,24},{20,52},{24,0},{28,60},{32,40}... | collective-permute-start | bytes 1609736 | tf_op jit(solution)/shard_map/ppermute | solution.py:44
  170.1 19.7 %collective-permute-start.24 = (bf16[2096,128]{1,0:T(8,128)(2,1)S(1)}, bf16[2096,128]{1,0:T(8,128)(2,1)S(1)}, u32[]{:S(2)}, u32[]{:S(2)}) collective-permute-start(bf16[2096,128]{1,0:T(8,128)(2,1)S(1)} %get-tuple-element.127), channel_id=1, source_target_pairs={{0,16},{4,68},{8,24},{12,76},{16,0},{20,84},{24,8},{28,92},{32,48}... | collective-permute-start | bytes 1609736 | tf_op jit(solution)/shard_map/ppermute | solution.py:44
  173.5 16.3 %collective-permute-start.25 = (bf16[2096,128]{1,0:T(8,128)(2,1)S(1)}, bf16[2096,128]{1,0:T(8,128)(2,1)S(1)}, u32[]{:S(2)}, u32[]{:S(2)}) collective-permute-start(bf16[2096,128]{1,0:T(8,128)(2,1)S(1)} %get-tuple-element.128), channel_id=1, source_target_pairs={{0,24},{4,100},{8,0},{12,108},{16,8},{20,116},{24,16},{28,124},{32... | collective-permute-start | bytes 1609736 | tf_op jit(solution)/shard_map/ppermute | solution.py:44
  175.1 14.7 %collective-permute-start.22 = (bf16[2,1024,128]{2,1,0:T(8,128)(2,1)S(1)}, bf16[2,1024,128]{2,1,0:T(8,128)(2,1)S(1)}, u32[]{:S(2)}, u32[]{:S(2)}) collective-permute-start(bf16[2,1024,128]{2,1,0:T(8,128)(2,1)S(1)} %finish.2.a0), channel_id=1, source_target_pairs={{0,2},{1,3},{2,0},{3,1},{4,6},{5,7},{6,4},{7,5},{8,10},{9,11},{10,... | collective-permute-start | bytes 1572872 | tf_op jit(solution)/shard_map/ppermute | solution.py:57
  193.4 24.6 %collective-permute-start.27 = (bf16[2,1024,128]{2,1,0:T(8,128)(2,1)S(1)}, bf16[2,1024,128]{2,1,0:T(8,128)(2,1)S(1)}, u32[]{:S(2)}, u32[]{:S(2)}) collective-permute-start(bf16[2,1024,128]{2,1,0:T(8,128)(2,1)S(1)} %finish.3.a0), channel_id=1, source_target_pairs={{0,3},{1,0},{2,1},{3,2},{4,7},{5,4},{6,5},{7,6},{8,11},{9,8},{10,9... | collective-permute-start | bytes 1572872 | tf_op jit(solution)/shard_map/ppermute | solution.py:57
  196.0 22.0 %collective-permute-start.28 = (bf16[2,1024,128]{2,1,0:T(8,128)(2,1)S(1)}, bf16[2,1024,128]{2,1,0:T(8,128)(2,1)S(1)}, u32[]{:S(2)}, u32[]{:S(2)}) collective-permute-start(bf16[2,1024,128]{2,1,0:T(8,128)(2,1)S(1)} %finish.3.a0), channel_id=1, source_target_pairs={{0,2},{1,3},{2,0},{3,1},{4,6},{5,7},{6,4},{7,5},{8,10},{9,11},{10,... | collective-permute-start | bytes 1572872 | tf_op jit(solution)/shard_map/ppermute | solution.py:57
  196.5 26.1 %collective-permute-start.29 = (bf16[2,1024,128]{2,1,0:T(8,128)(2,1)S(1)}, bf16[2,1024,128]{2,1,0:T(8,128)(2,1)S(1)}, u32[]{:S(2)}, u32[]{:S(2)}) collective-permute-start(bf16[2,1024,128]{2,1,0:T(8,128)(2,1)S(1)} %finish.3.a0), channel_id=1, source_target_pairs={{0,1},{1,2},{2,3},{3,0},{4,5},{5,6},{6,7},{7,4},{8,9},{9,10},{10,1... | collective-permute-start | bytes 1572872 | tf_op jit(solution)/shard_map/ppermute | solution.py:57
  (32 other events, 194.7 us)

commit v7 on v6

--- a/solution.py
+++ b/solution.py
@@ -527,15 +527,19 @@
     q1, q3, q2 = query_perm(mine, -1), query_perm(mine, 1), query_perm(mine, 2)
     core1 = after(core, mine)
     send1, keep1 = split_cache(3 - 2 * core1, kv_cache), split_cache(1 + 2 * core1, kv_cache, 2)
-    normed, keep1, send1 = lax.optimization_barrier((normed, keep1, send1))
+    code, cnt = line_codes(wake_blocks, wake_frames, wake_counts, y, z, c)
+    tops, bottoms = up0[:16], down0[16:]
+    held = (normed, keep1, send1, code, cnt, tops, bottoms)
+    normed, keep1, send1, code, cnt, tops, bottoms = lax.optimization_barrier(held)
     k_all, v_all, swap, edge = project(core, normed, w_key, w_value)
     send1, swap, edge, q1, q2, q3 = lax.optimization_barrier((send1, swap, edge, q1, q2, q3))
     swapped, halo = core_swap(swap), halo_perm(edge)
     rows1 = lax.dynamic_update_slice(keep1, core_swap(send1), (16, 0, 0, 0))
-    up20, down20 = rows_perm(up0[:16], 1), rows_perm(down0[16:], -1)
-    code, cnt = line_codes(wake_blocks, wake_frames, wake_counts, y, z, c)
+    up20, down20 = rows_perm(tops, 1), rows_perm(bottoms, -1)
     lists = plan(cnt, code)
-    rows1, up20, down20, *lists = lax.optimization_barrier((rows1, up20, down20, *lists))
+    near_o, near_lse = near(core, q_keep, q_send, k_all, v_all, halo, swapped)
+    held = (rows1, up20, down20, near_o, near_lse, *lists)
+    rows1, up20, down20, near_o, near_lse, *lists = lax.optimization_barrier(held)
     up1, down1 = rows_perm(rows1, 1), rows_perm(rows1, -1)
     qs = [mine, q1, q2, q3]
 
@@ -547,8 +551,6 @@
 
     parts = far(0, cnt, lists, [rows0, down0, up20, down20, up0], qs)
     weights = pick(after(place, parts[0]), w_out)
-    halo, swapped, *_ = lax.optimization_barrier((halo, swapped, parts[0]))
-    near_o, near_lse = near(core, q_keep, q_send, k_all, v_all, halo, swapped)
     back = returned(parts)
     back[1], back[3], up1, down1 = lax.optimization_barrier((back[1], back[3], up1, down1))
     up21, down21 = rows_perm(up1[:16], 1), rows_perm(down1[16:], -1)

time: 227 us -> 226 us (level)
  waiting for transfers between devices: 74.9 us -> 81.4 us
  local copies, waits for them, and re-layouts: 18.7 us -> 12.6 us
  starting transfers between devices: 45.1 us -> 42 us
    ppermute x8, waiting for transfers between devices: 17.3 us -> 26 us  [rows_perm(): return lax.ppermute(x, 'tok', pairs)]
    ppermute x1, waiting for transfers between devices: 13.1 us -> 8.09 us  [halo_perm(): lax.ppermute(x, 'tok', [(i, (i + (1 if i % 2 else -1)) % n) for i in rang...]
    ppermute x8, starting transfers between devices: 13.5 us -> 17 us  [rows_perm(): return lax.ppermute(x, 'tok', pairs)]
    ppermute x9, waiting for transfers between devices: 7.69 us -> 11.1 us  [query_perm(): return lax.ppermute(x, 'tok', pairs)]
    ppermute x6, starting transfers between devices: 6.77 us -> 3.36 us  [core_swap(): lax.ppermute(x, 'tok', [(tok_of(y, z, c), tok_of(y, z, 1 - c)) for y, z,...]
    unnamed x52 -> x32, local copies, waits for them, and re-layouts: 8.16 us -> 5.39 us
  transfers between devices with their start and end apart: 30 -> 30, of which waited for: 11 -> 13; matrix products, arithmetic and copies ran while one was open for 4% -> 4% of each run, Pallas kernels for 33% -> 34%
where the time goes in v7:
time: 226 us
  Pallas kernels  87.6 us (39%)
  waiting for transfers between devices  81.4 us (36%)
  starting transfers between devices  42 us (19%)
  local copies, waits for them, and re-layouts  12.6 us (6%)
    ppermute x6, waiting for transfers between devices, mp_perm(): return lax.ppermute(x, 'mp', [(i, (i + d) % NX) for i in range(NX)])  33.6 us
    ppermute x8, waiting for transfers between devices, rows_perm(): return lax.ppermute(x, 'tok', pairs)  26 us
    pallas_call x2, Pallas kernels, far(): pl.pallas_call(functools.partial(far_kernel, j), in_specs=[SMEM] * 5 + [A...  23.8 us
    pallas_call x4, Pallas kernels, split_cache(): pl.pallas_call(split_cache_kernel, grid_spec=pltpu.PrefetchScalarGridSpec...  22 us
    ppermute x8, starting transfers between devices, rows_perm(): return lax.ppermute(x, 'tok', pairs)  17 us
    ppermute x9, starting transfers between devices, query_perm(): return lax.ppermute(x, 'tok', pairs)  11.6 us
    ppermute x9, waiting for transfers between devices, query_perm(): return lax.ppermute(x, 'tok', pairs)  11.1 us
    pallas_call x1, Pallas kernels, project(): pl.pallas_call(project_kernel, grid_spec=pltpu.PrefetchScalarGridSpec(num...  10.4 us
  transfers between devices with their start and end apart: 30, of which 13 were waited for; matrix products, arithmetic and copies ran while one was open for 4% of the time, Pallas kernels for 34%

profile of v7, /device:TPU:1, one launch (start us, length us, event | category | flops | bytes accessed | tf_op | source)
XLA Modules:
  0.0 225.7 jit_solution(4481745414277369231)
XLA Ops:
  2.2 4.5 %split_cache.5 = bf16[16,2,128,128]{3,2,1,0:T(8,128)(2,1)S(1)} custom-call(s32[1]{0:T(128)S(6)} %sub.20.head_ref, bf16[2,1024,2,512]{3,2,1,0:T(2,128)(2,1)S(1)} %copy-done), custom_call_target="tpu_custom_call" | custom-call | flops 1 | bytes 1 | tf_op jit(solution)/shard_map/split_cache/pallas_call | solution.py:76
  8.2 6.0 %split_cache.4 = bf16[32,2,128,128]{3,2,1,0:T(8,128)(2,1)S(1)} custom-call(s32[1]{0:T(128)S(6)} %mul.35.head_ref, bf16[2,1024,2,512]{3,2,1,0:T(2,128)(2,1)} %src.7), custom_call_target="tpu_custom_call" | custom-call | flops 1 | bytes 1 | tf_op jit(solution)/shard_map/split_cache/pallas_call | solution.py:76
  18.4 6.9 %query.1 = (bf16[1024,2048]{1,0:T(8,128)(2,1)}, bf16[2,1024,128]{2,1,0:T(8,128)(2,1)S(1)}, bf16[2,1024,128]{2,1,0:T(8,128)(2,1)S(1)}) custom-call(s32[1]{0:T(128)} %bitcast.core_ref, bf16[1024,2048]{1,0:T(8,128)(2,1)} %carried.1, f32[1,2048]{1,0:T(1,128)S(1)} %bitcast.23, bf16[2048,512]{1,0:T(8,128)(2,1)S(1)} %copy-done.3), custom_call_target="tpu_custom_call" | custom-call | flops 1 | bytes 1 | tf_op jit(solution)/shard_map/query/pallas_call | solution.py:120
  30.1 2.8 %collective-permute-start.4 = (bf16[2,2,8,128,128]{4,3,2,1,0:T(8,128)(2,1)S(1)}, bf16[2,2,8,128,128]{4,3,2,1,0:T(8,128)(2,1)}, u32[]{:S(2)}, u32[]{:S(2)}) collective-permute-start(bf16[2,2,8,128,128]{4,3,2,1,0:T(8,128)(2,1)S(1)} %bitcast.14), channel_id=1, source_target_pairs={{0,24},{4,100},{8,0},{12,108},{16,8},{20,116},{24,16},{28,124},{32... | collective-permute-start | bytes 3145736 | tf_op jit(solution)/shard_map/ppermute | solution.py:44
  34.9 7.0 %split_cache.6 = bf16[32,2,128,128]{3,2,1,0:T(8,128)(2,1)} custom-call(s32[1]{0:T(128)S(6)} %add.42.head_ref, bf16[2,1024,2,512]{3,2,1,0:T(2,128)(2,1)} %src.7), custom_call_target="tpu_custom_call" | custom-call | flops 1 | bytes 1 | tf_op jit(solution)/shard_map/split_cache/pallas_call | solution.py:76
  42.0 4.5 %split_cache.7 = bf16[16,2,128,128]{3,2,1,0:T(8,128)(2,1)S(1)} custom-call(s32[1]{0:T(128)S(6)} %sub.21.head_ref, bf16[2,1024,2,512]{3,2,1,0:T(2,128)(2,1)S(1)} %copy-done.1), custom_call_target="tpu_custom_call" | custom-call | flops 1 | bytes 1 | tf_op jit(solution)/shard_map/split_cache/pallas_call | solution.py:76
  46.5 10.9 %collective-permute-done.2.rest_4_ = bf16[32,2,128,128]{3,2,1,0:T(8,128)(2,1)} collective-permute-done((bf16[32,2,128,128]{3,2,1,0:T(8,128)(2,1)S(1)}, bf16[32,2,128,128]{3,2,1,0:T(8,128)(2,1)}, u32[]{:S(2)}, u32[]{:S(2)}) %collective-permute-start.2) | collective-permute-done | bytes 2097184 | tf_op jit(solution)/shard_map/ppermute | solution.py:39
  60.0 10.4 %project.1 = (bf16[4,8,128,128]{3,2,1,0:T(8,128)(2,1)S(1)}, bf16[4,8,128,128]{3,2,1,0:T(8,128)(2,1)S(1)}, bf16[1024,128]{1,0:T(8,128)(2,1)S(1)}, bf16[1024,128]{1,0:T(8,128)(2,1)S(1)}) custom-call(s32[1]{0:T(128)} %bitcast.core_ref, bf16[1024,2048]{1,0:T(8,128)(2,1)} %get-tuple-element.82.normed_ref, bf16[2048,512]{1,0:T(8,128)(2,1)S(1)} %copy-done.6, ...), custom_call_target="tpu_custom_call" | custom-call | flops 1 | bytes 1 | tf_op jit(solution)/shard_map/project/pallas_call | solution.py:172
  70.6 3.2 %collective-permute-start.8 = (bf16[16,2,128,128]{3,2,1,0:T(8,128)(2,1)S(1)}, bf16[16,2,128,128]{3,2,1,0:T(8,128)(2,1)S(1)}, u32[]{:S(2)}, u32[]{:S(2)}) collective-permute-start(bf16[16,2,128,128]{3,2,1,0:T(8,128)(2,1)S(1)} %slice.16), channel_id=1, source_target_pairs={{0,32},{4,12},{8,40},{12,20},{16,48},{20,28},{24,56},{28,4},{32,64... | collective-permute-start | bytes 3145736 | tf_op jit(solution)/shard_map/ppermute | solution.py:39
  77.3 3.0 %plan.1 = (s32[100]{0:T(128)S(1)}, s32[64]{0:T(128)S(1)}, s32[64]{0:T(128)S(1)}, s32[2]{0:T(128)S(1)}) custom-call(s32[64]{0:T(128)S(1)} %reduce_sum.12.cnt_ref, s32[512]{0:T(512)S(1)} %reshape.73.code_ref), custom_call_target="tpu_custom_call" | custom-call | flops 1 | bytes 1 | tf_op jit(solution)/shard_map/plan/pallas_call | solution.py:272
  80.3 8.1 %collective-permute-done.10 = bf16[1024,128]{1,0:T(8,128)(2,1)S(1)} collective-permute-done((bf16[1024,128]{1,0:T(8,128)(2,1)S(1)}, bf16[1024,128]{1,0:T(8,128)(2,1)S(1)}, u32[]{:S(2)}, u32[]{:S(2)}) %collective-permute-start.10) | collective-permute-done | bytes 262176 | tf_op jit(solution)/shard_map/ppermute | solution.py:53
  88.4 8.7 %near.1 = (f32[4,8,128,128]{3,2,1,0:T(8,128)S(1)}, f32[4,8,128]{2,1,0:T(8,128)S(1)}) custom-call(s32[1]{0:T(128)} %bitcast.core_ref, bf16[2,1024,128]{2,1,0:T(8,128)(2,1)S(1)} %copy-done.5, bf16[2,1024,128]{2,1,0:T(8,128)(2,1)S(1)} %copy-done.10, bf16[4,8,128,128]{3,2,1,0:T(8,128)(2,1)S(1)} %get-tuple-element.88.k_ref, ...), custom_call_target="tpu_custom_call" | custom-call | flops 1 | bytes 1 | tf_op jit(solution)/shard_map/near/pallas_call | solution.py:217
  99.9 3.3 %collective-permute-start.15 = (bf16[32,2,128,128]{3,2,1,0:T(8,128)(2,1)}, bf16[32,2,128,128]{3,2,1,0:T(8,128)(2,1)}, u32[]{:S(2)}, u32[]{:S(2)}) collective-permute-start(bf16[32,2,128,128]{3,2,1,0:T(8,128)(2,1)} %constant_dynamic-update-slice_fusion.rest_0_), channel_id=1, source_target_pairs={{0,96},{4,28},{8,104},{12,4},{16,112},{20,12},{24,120},{28,20},{32... | collective-permute-start | bytes 6291464 | tf_op jit(solution)/shard_map/ppermute | solution.py:39
  103.1 12.4 %far.2 = (bf16[2096,128]{1,0:T(8,128)(2,1)S(1)}, bf16[2096,128]{1,0:T(8,128)(2,1)}, bf16[2096,128]{1,0:T(8,128)(2,1)}, bf16[2096,128]{1,0:T(8,128)(2,1)}) custom-call(s32[64]{0:T(128)S(1)} %reduce_sum.12.cnt_ref, s32[100]{0:T(128)S(1)} %get-tuple-element.101.unit_ref, s32[64]{0:T(128)S(1)} %get-tuple-element.102.first_ref, ...), custom_call_target="tpu_custom_call" | custom-call | flops 1 | bytes 1 | tf_op jit(solution)/shard_map/far/pallas_call | solution.py:357
  122.2 9.9 %collective-permute-done.12.b = bf16[2096,128]{1,0:T(8,128)(2,1)} collective-permute-done((bf16[2096,128]{1,0:T(8,128)(2,1)}, bf16[2096,128]{1,0:T(8,128)(2,1)}, u32[]{:S(2)}, u32[]{:S(2)}) %collective-permute-start.12) | collective-permute-done | bytes 536608 | tf_op jit(solution)/shard_map/ppermute | solution.py:44
  134.4 3.6 %collective-permute-done.15.rest_1_ = bf16[32,2,128,128]{3,2,1,0:T(8,128)(2,1)} collective-permute-done((bf16[32,2,128,128]{3,2,1,0:T(8,128)(2,1)}, bf16[32,2,128,128]{3,2,1,0:T(8,128)(2,1)}, u32[]{:S(2)}, u32[]{:S(2)}) %collective-permute-start.15) | collective-permute-done | bytes 2097184 | tf_op jit(solution)/shard_map/ppermute | solution.py:39
  150.6 8.2 %collective-permute-done.18.rest_2_ = bf16[16,2,128,128]{3,2,1,0:T(8,128)(2,1)S(1)} collective-permute-done((bf16[16,2,128,128]{3,2,1,0:T(8,128)(2,1)S(1)}, bf16[16,2,128,128]{3,2,1,0:T(8,128)(2,1)S(1)}, u32[]{:S(2)}, u32[]{:S(2)}) %collective-permute-start.18) | collective-permute-done | bytes 1048608 | tf_op jit(solution)/shard_map/ppermute | solution.py:39
  159.8 11.4 %far.3 = (bf16[2096,128]{1,0:T(8,128)(2,1)S(1)}, bf16[2096,128]{1,0:T(8,128)(2,1)S(1)}, bf16[2096,128]{1,0:T(8,128)(2,1)S(1)}, bf16[2096,128]{1,0:T(8,128)(2,1)S(1)}) custom-call(s32[64]{0:T(128)S(1)} %reduce_sum.12.cnt_ref, s32[100]{0:T(128)S(1)} %get-tuple-element.101.unit_ref, s32[64]{0:T(128)S(1)} %get-tuple-element.102.first_ref, ...), custom_call_target="tpu_custom_call" | custom-call | flops 1 | bytes 1 | tf_op jit(solution)/shard_map/far/pallas_call | solution.py:357
  175.5 2.7 %collective-permute-start.22 = (bf16[2,1024,128]{2,1,0:T(8,128)(2,1)S(1)}, bf16[2,1024,128]{2,1,0:T(8,128)(2,1)S(1)}, u32[]{:S(2)}, u32[]{:S(2)}) collective-permute-start(bf16[2,1024,128]{2,1,0:T(8,128)(2,1)S(1)} %finish.2.a0), channel_id=1, source_target_pairs={{0,2},{1,3},{2,0},{3,1},{4,6},{5,7},{6,4},{7,5},{8,10},{9,11},{10,... | collective-permute-start | bytes 1572872 | tf_op jit(solution)/shard_map/ppermute | solution.py:57
  178.2 12.1 %collective-permute-done.22.a2 = bf16[2,1024,128]{2,1,0:T(8,128)(2,1)S(1)} collective-permute-done((bf16[2,1024,128]{2,1,0:T(8,128)(2,1)S(1)}, bf16[2,1024,128]{2,1,0:T(8,128)(2,1)S(1)}, u32[]{:S(2)}, u32[]{:S(2)}) %collective-permute-start.22) | collective-permute-done | bytes 524320 | tf_op jit(solution)/shard_map/ppermute | solution.py:57
  196.9 4.0 %mix.2.carried = f32[1024,512]{1,0:T(8,128)S(1)} custom-call(s32[2]{0:T(128)S(1)} %pad_add_fusion.place_ref, bf16[2,1024,128]{2,1,0:T(8,128)(2,1)S(1)} %finish.2.a0, bf16[2,1024,128]{2,1,0:T(8,128)(2,1)S(1)} %collective-permute-done.20.a1, bf16[2,1024,128]{2,1,0:T(8,128)(2,1)S(1)} %collective-permute-done.22.a2, ...), custom_call_target="tpu_custom_call" | custom-call | flops 1 | bytes 1 | tf_op jit(solution)/shard_map/mix/pallas_call | solution.py:476
  200.8 16.9 %collective-permute-done.27.a1 = bf16[2,1024,128]{2,1,0:T(8,128)(2,1)S(1)} collective-permute-done((bf16[2,1024,128]{2,1,0:T(8,128)(2,1)S(1)}, bf16[2,1024,128]{2,1,0:T(8,128)(2,1)S(1)}, u32[]{:S(2)}, u32[]{:S(2)}) %collective-permute-start.27) | collective-permute-done | bytes 524320 | tf_op jit(solution)/shard_map/ppermute | solution.py:57
  217.8 4.6 %collective-permute-done.29.a3 = bf16[2,1024,128]{2,1,0:T(8,128)(2,1)S(1)} collective-permute-done((bf16[2,1024,128]{2,1,0:T(8,128)(2,1)S(1)}, bf16[2,1024,128]{2,1,0:T(8,128)(2,1)S(1)}, u32[]{:S(2)}, u32[]{:S(2)}) %collective-permute-start.29) | collective-permute-done | bytes 524320 | tf_op jit(solution)/shard_map/ppermute | solution.py:57
  222.3 3.4 %mix.3 = bf16[1024,512]{1,0:T(8,128)(2,1)} custom-call(s32[2]{0:T(128)S(1)} %pad_add_fusion.place_ref, bf16[2,1024,128]{2,1,0:T(8,128)(2,1)S(1)} %finish.3.a0, bf16[2,1024,128]{2,1,0:T(8,128)(2,1)S(1)} %collective-permute-done.27.a1, bf16[2,1024,128]{2,1,0:T(8,128)(2,1)S(1)} %collective-permute-done.28.a2, ...), custom_call_target="tpu_custom_call" | custom-call | flops 1 | bytes 1 | tf_op jit(solution)/shard_map/mix/pallas_call | solution.py:476
  (105 shorter events, 57.0 us)
Async XLA Ops:
  14.4 42.9 %collective-permute-start.2 = (bf16[32,2,128,128]{3,2,1,0:T(8,128)(2,1)S(1)}, bf16[32,2,128,128]{3,2,1,0:T(8,128)(2,1)}, u32[]{:S(2)}, u32[]{:S(2)}) collective-permute-start(bf16[32,2,128,128]{3,2,1,0:T(8,128)(2,1)S(1)} %constant_dynamic-update-slice_fusion.1.rest_0_), channel_id=1, source_target_pairs={{0,32},{4,12},{8,40},{12,20},{16,48},{20,28},{24,56},{28,4},{32,64... | collective-permute-start | bytes 6291464 | tf_op jit(solution)/shard_map/ppermute | solution.py:39
  16.2 42.5 %collective-permute-start.3 = (bf16[32,2,128,128]{3,2,1,0:T(8,128)(2,1)S(1)}, bf16[32,2,128,128]{3,2,1,0:T(8,128)(2,1)}, u32[]{:S(2)}, u32[]{:S(2)}) collective-permute-start(bf16[32,2,128,128]{3,2,1,0:T(8,128)(2,1)S(1)} %constant_dynamic-update-slice_fusion.1.rest_0_), channel_id=1, source_target_pairs={{0,96},{4,28},{8,104},{12,4},{16,112},{20,12},{24,120},{28,20},{32... | collective-permute-start | bytes 6291464 | tf_op jit(solution)/shard_map/ppermute | solution.py:39
  30.1 40.4 %collective-permute-start.4 = (bf16[2,2,8,128,128]{4,3,2,1,0:T(8,128)(2,1)S(1)}, bf16[2,2,8,128,128]{4,3,2,1,0:T(8,128)(2,1)}, u32[]{:S(2)}, u32[]{:S(2)}) collective-permute-start(bf16[2,2,8,128,128]{4,3,2,1,0:T(8,128)(2,1)S(1)} %bitcast.14), channel_id=1, source_target_pairs={{0,24},{4,100},{8,0},{12,108},{16,8},{20,116},{24,16},{28,124},{32... | collective-permute-start | bytes 3145736 | tf_op jit(solution)/shard_map/ppermute | solution.py:44
  32.9 37.6 %collective-permute-start.5 = (bf16[2,2,8,128,128]{4,3,2,1,0:T(8,128)(2,1)S(1)}, bf16[2,2,8,128,128]{4,3,2,1,0:T(8,128)(2,1)}, u32[]{:S(2)}, u32[]{:S(2)}) collective-permute-start(bf16[2,2,8,128,128]{4,3,2,1,0:T(8,128)(2,1)S(1)} %bitcast.15), channel_id=1, source_target_pairs={{0,16},{4,68},{8,24},{12,76},{16,0},{20,84},{24,8},{28,92},{32,48}... | collective-permute-start | bytes 3145736 | tf_op jit(solution)/shard_map/ppermute | solution.py:44
  33.3 37.2 %collective-permute-start.6 = (bf16[2,2,8,128,128]{4,3,2,1,0:T(8,128)(2,1)S(1)}, bf16[2,2,8,128,128]{4,3,2,1,0:T(8,128)(2,1)}, u32[]{:S(2)}, u32[]{:S(2)}) collective-permute-start(bf16[2,2,8,128,128]{4,3,2,1,0:T(8,128)(2,1)S(1)} %bitcast.16), channel_id=1, source_target_pairs={{0,8},{4,36},{8,16},{12,44},{16,24},{20,52},{24,0},{28,60},{32,40}... | collective-permute-start | bytes 3145736 | tf_op jit(solution)/shard_map/ppermute | solution.py:44
  70.5 26.6 %collective-permute-start.7 = (bf16[16,2,128,128]{3,2,1,0:T(8,128)(2,1)S(1)}, bf16[16,2,128,128]{3,2,1,0:T(8,128)(2,1)S(1)}, u32[]{:S(2)}, u32[]{:S(2)}) collective-permute-start(bf16[16,2,128,128]{3,2,1,0:T(8,128)(2,1)S(1)} %split_cache.7), channel_id=1, source_target_pairs={{0,4},{4,0},{8,12},{12,8},{16,20},{20,16},{24,28},{28,24},{32,36},... | collective-permute-start | bytes 3145736 | tf_op jit(solution)/shard_map/ppermute | solution.py:48
  70.6 27.6 %collective-permute-start.8 = (bf16[16,2,128,128]{3,2,1,0:T(8,128)(2,1)S(1)}, bf16[16,2,128,128]{3,2,1,0:T(8,128)(2,1)S(1)}, u32[]{:S(2)}, u32[]{:S(2)}) collective-permute-start(bf16[16,2,128,128]{3,2,1,0:T(8,128)(2,1)S(1)} %slice.16), channel_id=1, source_target_pairs={{0,32},{4,12},{8,40},{12,20},{16,48},{20,28},{24,56},{28,4},{32,64... | collective-permute-start | bytes 3145736 | tf_op jit(solution)/shard_map/ppermute | solution.py:39
  73.8 24.4 %collective-permute-start.9 = (bf16[16,2,128,128]{3,2,1,0:T(8,128)(2,1)S(1)}, bf16[16,2,128,128]{3,2,1,0:T(8,128)(2,1)S(1)}, u32[]{:S(2)}, u32[]{:S(2)}) collective-permute-start(bf16[16,2,128,128]{3,2,1,0:T(8,128)(2,1)S(1)} %slice.17), channel_id=1, source_target_pairs={{0,96},{4,28},{8,104},{12,4},{16,112},{20,12},{24,120},{28,20},{32... | collective-permute-start | bytes 3145736 | tf_op jit(solution)/shard_map/ppermute | solution.py:39
  98.2 36.1 %collective-permute-start.14 = (bf16[32,2,128,128]{3,2,1,0:T(8,128)(2,1)}, bf16[32,2,128,128]{3,2,1,0:T(8,128)(2,1)}, u32[]{:S(2)}, u32[]{:S(2)}) collective-permute-start(bf16[32,2,128,128]{3,2,1,0:T(8,128)(2,1)} %constant_dynamic-update-slice_fusion.rest_0_), channel_id=1, source_target_pairs={{0,32},{4,12},{8,40},{12,20},{16,48},{20,28},{24,56},{28,4},{32,64... | collective-permute-start | bytes 6291464 | tf_op jit(solution)/shard_map/ppermute | solution.py:39
  99.9 38.1 %collective-permute-start.15 = (bf16[32,2,128,128]{3,2,1,0:T(8,128)(2,1)}, bf16[32,2,128,128]{3,2,1,0:T(8,128)(2,1)}, u32[]{:S(2)}, u32[]{:S(2)}) collective-permute-start(bf16[32,2,128,128]{3,2,1,0:T(8,128)(2,1)} %constant_dynamic-update-slice_fusion.rest_0_), channel_id=1, source_target_pairs={{0,96},{4,28},{8,104},{12,4},{16,112},{20,12},{24,120},{28,20},{32... | collective-permute-start | bytes 6291464 | tf_op jit(solution)/shard_map/ppermute | solution.py:39
  116.3 15.8 %collective-permute-start.12 = (bf16[2096,128]{1,0:T(8,128)(2,1)}, bf16[2096,128]{1,0:T(8,128)(2,1)}, u32[]{:S(2)}, u32[]{:S(2)}) collective-permute-start(bf16[2096,128]{1,0:T(8,128)(2,1)} %get-tuple-element.118), channel_id=1, source_target_pairs={{0,8},{4,36},{8,16},{12,44},{16,24},{20,52},{24,0},{28,60},{32,40}... | collective-permute-start | bytes 1609736 | tf_op jit(solution)/shard_map/ppermute | solution.py:44
  117.5 14.6 %collective-permute-start.13 = (bf16[2096,128]{1,0:T(8,128)(2,1)}, bf16[2096,128]{1,0:T(8,128)(2,1)}, u32[]{:S(2)}, u32[]{:S(2)}) collective-permute-start(bf16[2096,128]{1,0:T(8,128)(2,1)} %get-tuple-element.119), channel_id=1, source_target_pairs={{0,24},{4,100},{8,0},{12,108},{16,8},{20,116},{24,16},{28,124},{32... | collective-permute-start | bytes 1609736 | tf_op jit(solution)/shard_map/ppermute | solution.py:44
  119.0 20.2 %collective-permute-start.16 = (bf16[2096,128]{1,0:T(8,128)(2,1)}, bf16[2096,128]{1,0:T(8,128)(2,1)}, u32[]{:S(2)}, u32[]{:S(2)}) collective-permute-start(bf16[2096,128]{1,0:T(8,128)(2,1)} %get-tuple-element.121), channel_id=1, source_target_pairs={{0,16},{4,68},{8,24},{12,76},{16,0},{20,84},{24,8},{28,92},{32,48}... | collective-permute-start | bytes 1609736 | tf_op jit(solution)/shard_map/ppermute | solution.py:44
  143.6 15.2 %collective-permute-start.18 = (bf16[16,2,128,128]{3,2,1,0:T(8,128)(2,1)S(1)}, bf16[16,2,128,128]{3,2,1,0:T(8,128)(2,1)S(1)}, u32[]{:S(2)}, u32[]{:S(2)}) collective-permute-start(bf16[16,2,128,128]{3,2,1,0:T(8,128)(2,1)S(1)} %slice.14), channel_id=1, source_target_pairs={{0,32},{4,12},{8,40},{12,20},{16,48},{20,28},{24,56},{28,4},{32,64... | collective-permute-start | bytes 3145736 | tf_op jit(solution)/shard_map/ppermute | solution.py:39
  145.8 14.0 %collective-permute-start.19 = (bf16[16,2,128,128]{3,2,1,0:T(8,128)(2,1)S(1)}, bf16[16,2,128,128]{3,2,1,0:T(8,128)(2,1)S(1)}, u32[]{:S(2)}, u32[]{:S(2)}) collective-permute-start(bf16[16,2,128,128]{3,2,1,0:T(8,128)(2,1)S(1)} %slice.15), channel_id=1, source_target_pairs={{0,96},{4,28},{8,104},{12,4},{16,112},{20,12},{24,120},{28,20},{32... | collective-permute-start | bytes 3145736 | tf_op jit(solution)/shard_map/ppermute | solution.py:39
  148.0 23.2 %collective-permute-start.20 = (bf16[2,1024,128]{2,1,0:T(8,128)(2,1)S(1)}, bf16[2,1024,128]{2,1,0:T(8,128)(2,1)S(1)}, u32[]{:S(2)}, u32[]{:S(2)}) collective-permute-start(bf16[2,1024,128]{2,1,0:T(8,128)(2,1)S(1)} %finish.2.a0), channel_id=1, source_target_pairs={{0,3},{1,0},{2,1},{3,2},{4,7},{5,4},{6,5},{7,6},{8,11},{9,8},{10,9... | collective-permute-start | bytes 1572872 | tf_op jit(solution)/shard_map/ppermute | solution.py:57
  150.6 20.7 %collective-permute-start.21 = (bf16[2,1024,128]{2,1,0:T(8,128)(2,1)S(1)}, bf16[2,1024,128]{2,1,0:T(8,128)(2,1)S(1)}, u32[]{:S(2)}, u32[]{:S(2)}) collective-permute-start(bf16[2,1024,128]{2,1,0:T(8,128)(2,1)S(1)} %finish.2.a0), channel_id=1, source_target_pairs={{0,1},{1,2},{2,3},{3,0},{4,5},{5,6},{6,7},{7,4},{8,9},{9,10},{10,1... | collective-permute-start | bytes 1572872 | tf_op jit(solution)/shard_map/ppermute | solution.py:57
  171.3 19.0 %collective-permute-start.23 = (bf16[2096,128]{1,0:T(8,128)(2,1)S(1)}, bf16[2096,128]{1,0:T(8,128)(2,1)S(1)}, u32[]{:S(2)}, u32[]{:S(2)}) collective-permute-start(bf16[2096,128]{1,0:T(8,128)(2,1)S(1)} %get-tuple-element.134), channel_id=1, source_target_pairs={{0,8},{4,36},{8,16},{12,44},{16,24},{20,52},{24,0},{28,60},{32,40}... | collective-permute-start | bytes 1609736 | tf_op jit(solution)/shard_map/ppermute | solution.py:44
  172.5 17.8 %collective-permute-start.24 = (bf16[2096,128]{1,0:T(8,128)(2,1)S(1)}, bf16[2096,128]{1,0:T(8,128)(2,1)S(1)}, u32[]{:S(2)}, u32[]{:S(2)}) collective-permute-start(bf16[2096,128]{1,0:T(8,128)(2,1)S(1)} %get-tuple-element.135), channel_id=1, source_target_pairs={{0,16},{4,68},{8,24},{12,76},{16,0},{20,84},{24,8},{28,92},{32,48}... | collective-permute-start | bytes 1609736 | tf_op jit(solution)/shard_map/ppermute | solution.py:44
  174.9 15.4 %collective-permute-start.25 = (bf16[2096,128]{1,0:T(8,128)(2,1)S(1)}, bf16[2096,128]{1,0:T(8,128)(2,1)S(1)}, u32[]{:S(2)}, u32[]{:S(2)}) collective-permute-start(bf16[2096,128]{1,0:T(8,128)(2,1)S(1)} %get-tuple-element.136), channel_id=1, source_target_pairs={{0,24},{4,100},{8,0},{12,108},{16,8},{20,116},{24,16},{28,124},{32... | collective-permute-start | bytes 1609736 | tf_op jit(solution)/shard_map/ppermute | solution.py:44
  175.5 14.8 %collective-permute-start.22 = (bf16[2,1024,128]{2,1,0:T(8,128)(2,1)S(1)}, bf16[2,1024,128]{2,1,0:T(8,128)(2,1)S(1)}, u32[]{:S(2)}, u32[]{:S(2)}) collective-permute-start(bf16[2,1024,128]{2,1,0:T(8,128)(2,1)S(1)} %finish.2.a0), channel_id=1, source_target_pairs={{0,2},{1,3},{2,0},{3,1},{4,6},{5,7},{6,4},{7,5},{8,10},{9,11},{10,... | collective-permute-start | bytes 1572872 | tf_op jit(solution)/shard_map/ppermute | solution.py:57
  193.2 24.6 %collective-permute-start.27 = (bf16[2,1024,128]{2,1,0:T(8,128)(2,1)S(1)}, bf16[2,1024,128]{2,1,0:T(8,128)(2,1)S(1)}, u32[]{:S(2)}, u32[]{:S(2)}) collective-permute-start(bf16[2,1024,128]{2,1,0:T(8,128)(2,1)S(1)} %finish.3.a0), channel_id=1, source_target_pairs={{0,3},{1,0},{2,1},{3,2},{4,7},{5,4},{6,5},{7,6},{8,11},{9,8},{10,9... | collective-permute-start | bytes 1572872 | tf_op jit(solution)/shard_map/ppermute | solution.py:57
  195.7 22.0 %collective-permute-start.28 = (bf16[2,1024,128]{2,1,0:T(8,128)(2,1)S(1)}, bf16[2,1024,128]{2,1,0:T(8,128)(2,1)S(1)}, u32[]{:S(2)}, u32[]{:S(2)}) collective-permute-start(bf16[2,1024,128]{2,1,0:T(8,128)(2,1)S(1)} %finish.3.a0), channel_id=1, source_target_pairs={{0,2},{1,3},{2,0},{3,1},{4,6},{5,7},{6,4},{7,5},{8,10},{9,11},{10,... | collective-permute-start | bytes 1572872 | tf_op jit(solution)/shard_map/ppermute | solution.py:57
  196.2 26.1 %collective-permute-start.29 = (bf16[2,1024,128]{2,1,0:T(8,128)(2,1)S(1)}, bf16[2,1024,128]{2,1,0:T(8,128)(2,1)S(1)}, u32[]{:S(2)}, u32[]{:S(2)}) collective-permute-start(bf16[2,1024,128]{2,1,0:T(8,128)(2,1)S(1)} %finish.3.a0), channel_id=1, source_target_pairs={{0,1},{1,2},{2,3},{3,0},{4,5},{5,6},{6,7},{7,4},{8,9},{9,10},{10,1... | collective-permute-start | bytes 1572872 | tf_op jit(solution)/shard_map/ppermute | solution.py:57
  (22 other events, 192.6 us)

commit v8 on v7

--- a/solution.py
+++ b/solution.py
@@ -529,17 +529,17 @@
     send1, keep1 = split_cache(3 - 2 * core1, kv_cache), split_cache(1 + 2 * core1, kv_cache, 2)
     code, cnt = line_codes(wake_blocks, wake_frames, wake_counts, y, z, c)
     tops, bottoms = up0[:16], down0[16:]
-    held = (normed, keep1, send1, code, cnt, tops, bottoms)
-    normed, keep1, send1, code, cnt, tops, bottoms = lax.optimization_barrier(held)
+    normed, keep1, send1, code, cnt = lax.optimization_barrier((normed, keep1, send1, code, cnt))
     k_all, v_all, swap, edge = project(core, normed, w_key, w_value)
-    send1, swap, edge, q1, q2, q3 = lax.optimization_barrier((send1, swap, edge, q1, q2, q3))
+    held = (send1, swap, edge, q1, q2, q3, tops, bottoms)
+    send1, swap, edge, q1, q2, q3, tops, bottoms = lax.optimization_barrier(held)
     swapped, halo = core_swap(swap), halo_perm(edge)
     rows1 = lax.dynamic_update_slice(keep1, core_swap(send1), (16, 0, 0, 0))
     up20, down20 = rows_perm(tops, 1), rows_perm(bottoms, -1)
     lists = plan(cnt, code)
+    held = (rows1, up20, down20, halo, swapped, *lists)
+    rows1, up20, down20, halo, swapped, *lists = lax.optimization_barrier(held)
     near_o, near_lse = near(core, q_keep, q_send, k_all, v_all, halo, swapped)
-    held = (rows1, up20, down20, near_o, near_lse, *lists)
-    rows1, up20, down20, near_o, near_lse, *lists = lax.optimization_barrier(held)
     up1, down1 = rows_perm(rows1, 1), rows_perm(rows1, -1)
     qs = [mine, q1, q2, q3]
 
@@ -549,7 +549,7 @@
     def gather(heads):
         return [heads, mp_perm(heads, -1), mp_perm(heads, 2), mp_perm(heads, 1)]
 
-    parts = far(0, cnt, lists, [rows0, down0, up20, down20, up0], qs)
+    parts = far(0, cnt, lists, [after(rows0, near_o), down0, up20, down20, up0], qs)
     weights = pick(after(place, parts[0]), w_out)
     back = returned(parts)
     back[1], back[3], up1, down1 = lax.optimization_barrier((back[1], back[3], up1, down1))

time: 226 us -> 212 us (0.938)
  waiting for transfers between devices: 81.4 us -> 67.3 us
    ppermute x8, waiting for transfers between devices: 26 us -> 12 us  [rows_perm(): return lax.ppermute(x, 'tok', pairs)]
    ppermute x8, starting transfers between devices: 17 us -> 12.4 us  [rows_perm(): return lax.ppermute(x, 'tok', pairs)]
    ppermute x9, waiting for transfers between devices: 11.1 us -> 14.1 us  [query_perm(): return lax.ppermute(x, 'tok', pairs)]
    ppermute x1, waiting for transfers between devices: 8.09 us -> 5.32 us  [halo_perm(): lax.ppermute(x, 'tok', [(i, (i + (1 if i % 2 else -1)) % n) for i in rang...]
    ppermute x6, starting transfers between devices: 3.36 us -> 5.9 us  [core_swap(): lax.ppermute(x, 'tok', [(tok_of(y, z, c), tok_of(y, z, 1 - c)) for y, z,...]
  transfers between devices with their start and end apart: 30 -> 30, of which waited for: 13 -> 15; matrix products, arithmetic and copies ran while one was open for 4% -> 4% of each run, Pallas kernels for 34% -> 36%
where the time goes in v8:
time: 212 us
  Pallas kernels  87.5 us (41%)
  waiting for transfers between devices  67.3 us (32%)
  starting transfers between devices  42.5 us (20%)
  local copies, waits for them, and re-layouts  12.6 us (6%)
    ppermute x6, waiting for transfers between devices, mp_perm(): return lax.ppermute(x, 'mp', [(i, (i + d) % NX) for i in range(NX)])  32.9 us
    pallas_call x2, Pallas kernels, far(): pl.pallas_call(functools.partial(far_kernel, j), in_specs=[SMEM] * 5 + [A...  23.7 us
    pallas_call x4, Pallas kernels, split_cache(): pl.pallas_call(split_cache_kernel, grid_spec=pltpu.PrefetchScalarGridSpec...  22 us
    ppermute x9, waiting for transfers between devices, query_perm(): return lax.ppermute(x, 'tok', pairs)  14.1 us
    ppermute x9, starting transfers between devices, query_perm(): return lax.ppermute(x, 'tok', pairs)  12.7 us
    ppermute x8, starting transfers between devices, rows_perm(): return lax.ppermute(x, 'tok', pairs)  12.4 us
    ppermute x8, waiting for transfers between devices, rows_perm(): return lax.ppermute(x, 'tok', pairs)  12 us
    pallas_call x1, Pallas kernels, project(): pl.pallas_call(project_kernel, grid_spec=pltpu.PrefetchScalarGridSpec(num...  10.4 us
  transfers between devices with their start and end apart: 30, of which 15 were waited for; matrix products, arithmetic and copies ran while one was open for 4% of the time, Pallas kernels for 36%

profile of v8, /device:TPU:1, one launch (start us, length us, event | category | flops | bytes accessed | tf_op | source)
XLA Modules:
  0.0 212.0 jit_solution(7675610511135994248)
XLA Ops:
  2.2 4.5 %split_cache.5 = bf16[16,2,128,128]{3,2,1,0:T(8,128)(2,1)S(1)} custom-call(s32[1]{0:T(128)S(6)} %sub.20.head_ref, bf16[2,1024,2,512]{3,2,1,0:T(2,128)(2,1)S(1)} %copy-done), custom_call_target="tpu_custom_call" | custom-call | flops 1 | bytes 1 | tf_op jit(solution)/shard_map/split_cache/pallas_call | solution.py:76
  8.2 6.0 %split_cache.4 = bf16[32,2,128,128]{3,2,1,0:T(8,128)(2,1)S(1)} custom-call(s32[1]{0:T(128)S(6)} %mul.35.head_ref, bf16[2,1024,2,512]{3,2,1,0:T(2,128)(2,1)} %src.7), custom_call_target="tpu_custom_call" | custom-call | flops 1 | bytes 1 | tf_op jit(solution)/shard_map/split_cache/pallas_call | solution.py:76
  18.4 6.9 %query.1 = (bf16[1024,2048]{1,0:T(8,128)(2,1)}, bf16[2,1024,128]{2,1,0:T(8,128)(2,1)S(1)}, bf16[2,1024,128]{2,1,0:T(8,128)(2,1)S(1)}) custom-call(s32[1]{0:T(128)} %bitcast.core_ref, bf16[1024,2048]{1,0:T(8,128)(2,1)} %carried.1, f32[1,2048]{1,0:T(1,128)S(1)} %bitcast.23, bf16[2048,512]{1,0:T(8,128)(2,1)S(1)} %copy-done.3), custom_call_target="tpu_custom_call" | custom-call | flops 1 | bytes 1 | tf_op jit(solution)/shard_map/query/pallas_call | solution.py:120
  30.1 2.8 %collective-permute-start.2 = (bf16[2,2,8,128,128]{4,3,2,1,0:T(8,128)(2,1)S(1)}, bf16[2,2,8,128,128]{4,3,2,1,0:T(8,128)(2,1)}, u32[]{:S(2)}, u32[]{:S(2)}) collective-permute-start(bf16[2,2,8,128,128]{4,3,2,1,0:T(8,128)(2,1)S(1)} %bitcast.14), channel_id=1, source_target_pairs={{0,24},{4,100},{8,0},{12,108},{16,8},{20,116},{24,16},{28,124},{32... | collective-permute-start | bytes 3145736 | tf_op jit(solution)/shard_map/ppermute | solution.py:44
  34.9 7.0 %split_cache.6 = bf16[32,2,128,128]{3,2,1,0:T(8,128)(2,1)} custom-call(s32[1]{0:T(128)S(6)} %add.42.head_ref, bf16[2,1024,2,512]{3,2,1,0:T(2,128)(2,1)} %src.7), custom_call_target="tpu_custom_call" | custom-call | flops 1 | bytes 1 | tf_op jit(solution)/shard_map/split_cache/pallas_call | solution.py:76
  42.0 4.5 %split_cache.7 = bf16[16,2,128,128]{3,2,1,0:T(8,128)(2,1)S(1)} custom-call(s32[1]{0:T(128)S(6)} %sub.21.head_ref, bf16[2,1024,2,512]{3,2,1,0:T(2,128)(2,1)S(1)} %copy-done.1), custom_call_target="tpu_custom_call" | custom-call | flops 1 | bytes 1 | tf_op jit(solution)/shard_map/split_cache/pallas_call | solution.py:76
  46.5 10.4 %project.1 = (bf16[4,8,128,128]{3,2,1,0:T(8,128)(2,1)S(1)}, bf16[4,8,128,128]{3,2,1,0:T(8,128)(2,1)S(1)}, bf16[1024,128]{1,0:T(8,128)(2,1)S(1)}, bf16[1024,128]{1,0:T(8,128)(2,1)S(1)}) custom-call(s32[1]{0:T(128)} %bitcast.core_ref, bf16[1024,2048]{1,0:T(8,128)(2,1)} %get-tuple-element.81.normed_ref, bf16[2048,512]{1,0:T(8,128)(2,1)S(1)} %copy-done.6, ...), custom_call_target="tpu_custom_call" | custom-call | flops 1 | bytes 1 | tf_op jit(solution)/shard_map/project/pallas_call | solution.py:172
  60.1 3.8 %collective-permute-done.4.rest_8_ = bf16[2,2,8,128,128]{4,3,2,1,0:T(8,128)(2,1)} collective-permute-done((bf16[2,2,8,128,128]{4,3,2,1,0:T(8,128)(2,1)S(1)}, bf16[2,2,8,128,128]{4,3,2,1,0:T(8,128)(2,1)}, u32[]{:S(2)}, u32[]{:S(2)}) %collective-permute-start.4) | collective-permute-done | bytes 1048608 | tf_op jit(solution)/shard_map/ppermute | solution.py:44
  72.1 3.0 %plan.1 = (s32[100]{0:T(128)S(1)}, s32[64]{0:T(128)S(1)}, s32[64]{0:T(128)S(1)}, s32[2]{0:T(128)S(1)}) custom-call(s32[64]{0:T(128)S(1)} %reduce_sum.12.cnt_ref, s32[512]{0:T(512)S(1)} %reshape.73.code_ref), custom_call_target="tpu_custom_call" | custom-call | flops 1 | bytes 1 | tf_op jit(solution)/shard_map/plan/pallas_call | solution.py:272
  76.3 5.3 %collective-permute-done.10 = bf16[1024,128]{1,0:T(8,128)(2,1)S(1)} collective-permute-done((bf16[1024,128]{1,0:T(8,128)(2,1)S(1)}, bf16[1024,128]{1,0:T(8,128)(2,1)S(1)}, u32[]{:S(2)}, u32[]{:S(2)}) %collective-permute-start.10) | collective-permute-done | bytes 262176 | tf_op jit(solution)/shard_map/ppermute | solution.py:53
  86.4 8.7 %near.1 = (f32[4,8,128,128]{3,2,1,0:T(8,128)S(1)}, f32[4,8,128]{2,1,0:T(8,128)S(1)}) custom-call(s32[1]{0:T(128)} %bitcast.core_ref, bf16[2,1024,128]{2,1,0:T(8,128)(2,1)S(1)} %copy-done.5, bf16[2,1024,128]{2,1,0:T(8,128)(2,1)S(1)} %copy-done.10, bf16[4,8,128,128]{3,2,1,0:T(8,128)(2,1)S(1)} %get-tuple-element.82.k_ref, ...), custom_call_target="tpu_custom_call" | custom-call | flops 1 | bytes 1 | tf_op jit(solution)/shard_map/near/pallas_call | solution.py:217
  95.1 12.3 %far.2 = (bf16[2096,128]{1,0:T(8,128)(2,1)S(1)}, bf16[2096,128]{1,0:T(8,128)(2,1)}, bf16[2096,128]{1,0:T(8,128)(2,1)}, bf16[2096,128]{1,0:T(8,128)(2,1)}) custom-call(s32[64]{0:T(128)S(1)} %reduce_sum.12.cnt_ref, s32[100]{0:T(128)S(1)} %get-tuple-element.102.unit_ref, s32[64]{0:T(128)S(1)} %get-tuple-element.103.first_ref, ...), custom_call_target="tpu_custom_call" | custom-call | flops 1 | bytes 1 | tf_op jit(solution)/shard_map/far/pallas_call | solution.py:357
  108.2 2.7 %collective-permute-start.13 = (bf16[2096,128]{1,0:T(8,128)(2,1)}, bf16[2096,128]{1,0:T(8,128)(2,1)}, u32[]{:S(2)}, u32[]{:S(2)}) collective-permute-start(bf16[2096,128]{1,0:T(8,128)(2,1)} %get-tuple-element.121), channel_id=1, source_target_pairs={{0,24},{4,100},{8,0},{12,108},{16,8},{20,116},{24,16},{28,124},{32... | collective-permute-start | bytes 1609736 | tf_op jit(solution)/shard_map/ppermute | solution.py:44
  114.1 3.9 %collective-permute-done.12.b = bf16[2096,128]{1,0:T(8,128)(2,1)} collective-permute-done((bf16[2096,128]{1,0:T(8,128)(2,1)}, bf16[2096,128]{1,0:T(8,128)(2,1)}, u32[]{:S(2)}, u32[]{:S(2)}) %collective-permute-start.12) | collective-permute-done | bytes 536608 | tf_op jit(solution)/shard_map/ppermute | solution.py:44
  118.0 5.2 %collective-permute-done.13.d = bf16[2096,128]{1,0:T(8,128)(2,1)} collective-permute-done((bf16[2096,128]{1,0:T(8,128)(2,1)}, bf16[2096,128]{1,0:T(8,128)(2,1)}, u32[]{:S(2)}, u32[]{:S(2)}) %collective-permute-start.13) | collective-permute-done | bytes 536608 | tf_op jit(solution)/shard_map/ppermute | solution.py:44
  136.0 8.2 %collective-permute-done.18.rest_2_ = bf16[16,2,128,128]{3,2,1,0:T(8,128)(2,1)S(1)} collective-permute-done((bf16[16,2,128,128]{3,2,1,0:T(8,128)(2,1)S(1)}, bf16[16,2,128,128]{3,2,1,0:T(8,128)(2,1)S(1)}, u32[]{:S(2)}, u32[]{:S(2)}) %collective-permute-start.18) | collective-permute-done | bytes 1048608 | tf_op jit(solution)/shard_map/ppermute | solution.py:39
  145.5 11.4 %far.3 = (bf16[2096,128]{1,0:T(8,128)(2,1)S(1)}, bf16[2096,128]{1,0:T(8,128)(2,1)S(1)}, bf16[2096,128]{1,0:T(8,128)(2,1)S(1)}, bf16[2096,128]{1,0:T(8,128)(2,1)S(1)}) custom-call(s32[64]{0:T(128)S(1)} %reduce_sum.12.cnt_ref, s32[100]{0:T(128)S(1)} %get-tuple-element.102.unit_ref, s32[64]{0:T(128)S(1)} %get-tuple-element.103.first_ref, ...), custom_call_target="tpu_custom_call" | custom-call | flops 1 | bytes 1 | tf_op jit(solution)/shard_map/far/pallas_call | solution.py:357
  157.0 3.3 %collective-permute-start.24 = (bf16[2096,128]{1,0:T(8,128)(2,1)S(1)}, bf16[2096,128]{1,0:T(8,128)(2,1)S(1)}, u32[]{:S(2)}, u32[]{:S(2)}) collective-permute-start(bf16[2096,128]{1,0:T(8,128)(2,1)S(1)} %get-tuple-element.137), channel_id=1, source_target_pairs={{0,16},{4,68},{8,24},{12,76},{16,0},{20,84},{24,8},{28,92},{32,48}... | collective-permute-start | bytes 1609736 | tf_op jit(solution)/shard_map/ppermute | solution.py:44
  162.3 2.7 %collective-permute-start.22 = (bf16[2,1024,128]{2,1,0:T(8,128)(2,1)S(1)}, bf16[2,1024,128]{2,1,0:T(8,128)(2,1)S(1)}, u32[]{:S(2)}, u32[]{:S(2)}) collective-permute-start(bf16[2,1024,128]{2,1,0:T(8,128)(2,1)S(1)} %finish.2.a0), channel_id=1, source_target_pairs={{0,2},{1,3},{2,0},{3,1},{4,6},{5,7},{6,4},{7,5},{8,10},{9,11},{10,... | collective-permute-start | bytes 1572872 | tf_op jit(solution)/shard_map/ppermute | solution.py:57
  165.0 11.5 %collective-permute-done.22.a2 = bf16[2,1024,128]{2,1,0:T(8,128)(2,1)S(1)} collective-permute-done((bf16[2,1024,128]{2,1,0:T(8,128)(2,1)S(1)}, bf16[2,1024,128]{2,1,0:T(8,128)(2,1)S(1)}, u32[]{:S(2)}, u32[]{:S(2)}) %collective-permute-start.22) | collective-permute-done | bytes 524320 | tf_op jit(solution)/shard_map/ppermute | solution.py:57
  183.1 4.0 %mix.2.carried = f32[1024,512]{1,0:T(8,128)S(1)} custom-call(s32[2]{0:T(128)S(1)} %pad_add_fusion.place_ref, bf16[2,1024,128]{2,1,0:T(8,128)(2,1)S(1)} %finish.2.a0, bf16[2,1024,128]{2,1,0:T(8,128)(2,1)S(1)} %collective-permute-done.20.a1, bf16[2,1024,128]{2,1,0:T(8,128)(2,1)S(1)} %collective-permute-done.22.a2, ...), custom_call_target="tpu_custom_call" | custom-call | flops 1 | bytes 1 | tf_op jit(solution)/shard_map/mix/pallas_call | solution.py:476
  187.1 17.2 %collective-permute-done.27.a1 = bf16[2,1024,128]{2,1,0:T(8,128)(2,1)S(1)} collective-permute-done((bf16[2,1024,128]{2,1,0:T(8,128)(2,1)S(1)}, bf16[2,1024,128]{2,1,0:T(8,128)(2,1)S(1)}, u32[]{:S(2)}, u32[]{:S(2)}) %collective-permute-start.27) | collective-permute-done | bytes 524320 | tf_op jit(solution)/shard_map/ppermute | solution.py:57
  204.2 4.3 %collective-permute-done.29.a3 = bf16[2,1024,128]{2,1,0:T(8,128)(2,1)S(1)} collective-permute-done((bf16[2,1024,128]{2,1,0:T(8,128)(2,1)S(1)}, bf16[2,1024,128]{2,1,0:T(8,128)(2,1)S(1)}, u32[]{:S(2)}, u32[]{:S(2)}) %collective-permute-start.29) | collective-permute-done | bytes 524320 | tf_op jit(solution)/shard_map/ppermute | solution.py:57
  208.5 3.4 %mix.3 = bf16[1024,512]{1,0:T(8,128)(2,1)} custom-call(s32[2]{0:T(128)S(1)} %pad_add_fusion.place_ref, bf16[2,1024,128]{2,1,0:T(8,128)(2,1)S(1)} %finish.3.a0, bf16[2,1024,128]{2,1,0:T(8,128)(2,1)S(1)} %collective-permute-done.27.a1, bf16[2,1024,128]{2,1,0:T(8,128)(2,1)S(1)} %collective-permute-done.28.a2, ...), custom_call_target="tpu_custom_call" | custom-call | flops 1 | bytes 1 | tf_op jit(solution)/shard_map/mix/pallas_call | solution.py:476
  (105 shorter events, 58.5 us)
Async XLA Ops:
  14.4 42.9 %collective-permute-start.5 = (bf16[32,2,128,128]{3,2,1,0:T(8,128)(2,1)S(1)}, bf16[32,2,128,128]{3,2,1,0:T(8,128)(2,1)}, u32[]{:S(2)}, u32[]{:S(2)}) collective-permute-start(bf16[32,2,128,128]{3,2,1,0:T(8,128)(2,1)S(1)} %constant_dynamic-update-slice_fusion.1.rest_0_), channel_id=1, source_target_pairs={{0,32},{4,12},{8,40},{12,20},{16,48},{20,28},{24,56},{28,4},{32,64... | collective-permute-start | bytes 6291464 | tf_op jit(solution)/shard_map/ppermute | solution.py:39
  16.2 42.5 %collective-permute-start.6 = (bf16[32,2,128,128]{3,2,1,0:T(8,128)(2,1)S(1)}, bf16[32,2,128,128]{3,2,1,0:T(8,128)(2,1)}, u32[]{:S(2)}, u32[]{:S(2)}) collective-permute-start(bf16[32,2,128,128]{3,2,1,0:T(8,128)(2,1)S(1)} %constant_dynamic-update-slice_fusion.1.rest_0_), channel_id=1, source_target_pairs={{0,96},{4,28},{8,104},{12,4},{16,112},{20,12},{24,120},{28,20},{32... | collective-permute-start | bytes 6291464 | tf_op jit(solution)/shard_map/ppermute | solution.py:39
  30.1 30.0 %collective-permute-start.2 = (bf16[2,2,8,128,128]{4,3,2,1,0:T(8,128)(2,1)S(1)}, bf16[2,2,8,128,128]{4,3,2,1,0:T(8,128)(2,1)}, u32[]{:S(2)}, u32[]{:S(2)}) collective-permute-start(bf16[2,2,8,128,128]{4,3,2,1,0:T(8,128)(2,1)S(1)} %bitcast.14), channel_id=1, source_target_pairs={{0,24},{4,100},{8,0},{12,108},{16,8},{20,116},{24,16},{28,124},{32... | collective-permute-start | bytes 3145736 | tf_op jit(solution)/shard_map/ppermute | solution.py:44
  32.9 27.2 %collective-permute-start.3 = (bf16[2,2,8,128,128]{4,3,2,1,0:T(8,128)(2,1)S(1)}, bf16[2,2,8,128,128]{4,3,2,1,0:T(8,128)(2,1)}, u32[]{:S(2)}, u32[]{:S(2)}) collective-permute-start(bf16[2,2,8,128,128]{4,3,2,1,0:T(8,128)(2,1)S(1)} %bitcast.15), channel_id=1, source_target_pairs={{0,16},{4,68},{8,24},{12,76},{16,0},{20,84},{24,8},{28,92},{32,48}... | collective-permute-start | bytes 3145736 | tf_op jit(solution)/shard_map/ppermute | solution.py:44
  33.3 30.7 %collective-permute-start.4 = (bf16[2,2,8,128,128]{4,3,2,1,0:T(8,128)(2,1)S(1)}, bf16[2,2,8,128,128]{4,3,2,1,0:T(8,128)(2,1)}, u32[]{:S(2)}, u32[]{:S(2)}) collective-permute-start(bf16[2,2,8,128,128]{4,3,2,1,0:T(8,128)(2,1)S(1)} %bitcast.16), channel_id=1, source_target_pairs={{0,8},{4,36},{8,16},{12,44},{16,24},{20,52},{24,0},{28,60},{32,40}... | collective-permute-start | bytes 3145736 | tf_op jit(solution)/shard_map/ppermute | solution.py:44
  65.0 17.8 %collective-permute-start.8 = (bf16[16,2,128,128]{3,2,1,0:T(8,128)(2,1)S(1)}, bf16[16,2,128,128]{3,2,1,0:T(8,128)(2,1)S(1)}, u32[]{:S(2)}, u32[]{:S(2)}) collective-permute-start(bf16[16,2,128,128]{3,2,1,0:T(8,128)(2,1)S(1)} %slice.16), channel_id=1, source_target_pairs={{0,32},{4,12},{8,40},{12,20},{16,48},{20,28},{24,56},{28,4},{32,64... | collective-permute-start | bytes 3145736 | tf_op jit(solution)/shard_map/ppermute | solution.py:39
  67.1 16.5 %collective-permute-start.9 = (bf16[16,2,128,128]{3,2,1,0:T(8,128)(2,1)S(1)}, bf16[16,2,128,128]{3,2,1,0:T(8,128)(2,1)S(1)}, u32[]{:S(2)}, u32[]{:S(2)}) collective-permute-start(bf16[16,2,128,128]{3,2,1,0:T(8,128)(2,1)S(1)} %slice.17), channel_id=1, source_target_pairs={{0,96},{4,28},{8,104},{12,4},{16,112},{20,12},{24,120},{28,20},{32... | collective-permute-start | bytes 3145736 | tf_op jit(solution)/shard_map/ppermute | solution.py:39
  67.8 13.8 %collective-permute-start.10 = (bf16[1024,128]{1,0:T(8,128)(2,1)S(1)}, bf16[1024,128]{1,0:T(8,128)(2,1)S(1)}, u32[]{:S(2)}, u32[]{:S(2)}) collective-permute-start(bf16[1024,128]{1,0:T(8,128)(2,1)S(1)} %get-tuple-element.91), channel_id=1, source_target_pairs={{0,124},{4,8},{8,4},{12,16},{16,12},{20,24},{24,20},{28,32},{32,28... | collective-permute-start | bytes 786440 | tf_op jit(solution)/shard_map/ppermute | solution.py:53
  70.2 11.4 %collective-permute-start.11 = (bf16[1024,128]{1,0:T(8,128)(2,1)S(1)}, bf16[1024,128]{1,0:T(8,128)(2,1)S(1)}, u32[]{:S(2)}, u32[]{:S(2)}) collective-permute-start(bf16[1024,128]{1,0:T(8,128)(2,1)S(1)} %get-tuple-element.92), channel_id=1, source_target_pairs={{0,4},{4,0},{8,12},{12,8},{16,20},{20,16},{24,28},{28,24},{32,36},... | collective-permute-start | bytes 786440 | tf_op jit(solution)/shard_map/ppermute | solution.py:48
  83.5 39.7 %collective-permute-start.14 = (bf16[32,2,128,128]{3,2,1,0:T(8,128)(2,1)}, bf16[32,2,128,128]{3,2,1,0:T(8,128)(2,1)}, u32[]{:S(2)}, u32[]{:S(2)}) collective-permute-start(bf16[32,2,128,128]{3,2,1,0:T(8,128)(2,1)} %constant_dynamic-update-slice_fusion.rest_0_), channel_id=1, source_target_pairs={{0,32},{4,12},{8,40},{12,20},{16,48},{20,28},{24,56},{28,4},{32,64... | collective-permute-start | bytes 6291464 | tf_op jit(solution)/shard_map/ppermute | solution.py:39
  83.8 39.4 %collective-permute-start.15 = (bf16[32,2,128,128]{3,2,1,0:T(8,128)(2,1)}, bf16[32,2,128,128]{3,2,1,0:T(8,128)(2,1)}, u32[]{:S(2)}, u32[]{:S(2)}) collective-permute-start(bf16[32,2,128,128]{3,2,1,0:T(8,128)(2,1)} %constant_dynamic-update-slice_fusion.rest_0_), channel_id=1, source_target_pairs={{0,96},{4,28},{8,104},{12,4},{16,112},{20,12},{24,120},{28,20},{32... | collective-permute-start | bytes 6291464 | tf_op jit(solution)/shard_map/ppermute | solution.py:39
  108.2 15.0 %collective-permute-start.13 = (bf16[2096,128]{1,0:T(8,128)(2,1)}, bf16[2096,128]{1,0:T(8,128)(2,1)}, u32[]{:S(2)}, u32[]{:S(2)}) collective-permute-start(bf16[2096,128]{1,0:T(8,128)(2,1)} %get-tuple-element.121), channel_id=1, source_target_pairs={{0,24},{4,100},{8,0},{12,108},{16,8},{20,116},{24,16},{28,124},{32... | collective-permute-start | bytes 1609736 | tf_op jit(solution)/shard_map/ppermute | solution.py:44
  110.9 13.5 %collective-permute-start.16 = (bf16[2096,128]{1,0:T(8,128)(2,1)}, bf16[2096,128]{1,0:T(8,128)(2,1)}, u32[]{:S(2)}, u32[]{:S(2)}) collective-permute-start(bf16[2096,128]{1,0:T(8,128)(2,1)} %get-tuple-element.123), channel_id=1, source_target_pairs={{0,16},{4,68},{8,24},{12,76},{16,0},{20,84},{24,8},{28,92},{32,48}... | collective-permute-start | bytes 1609736 | tf_op jit(solution)/shard_map/ppermute | solution.py:44
  129.0 15.2 %collective-permute-start.18 = (bf16[16,2,128,128]{3,2,1,0:T(8,128)(2,1)S(1)}, bf16[16,2,128,128]{3,2,1,0:T(8,128)(2,1)S(1)}, u32[]{:S(2)}, u32[]{:S(2)}) collective-permute-start(bf16[16,2,128,128]{3,2,1,0:T(8,128)(2,1)S(1)} %slice.14), channel_id=1, source_target_pairs={{0,32},{4,12},{8,40},{12,20},{16,48},{20,28},{24,56},{28,4},{32,64... | collective-permute-start | bytes 3145736 | tf_op jit(solution)/shard_map/ppermute | solution.py:39
  131.5 14.0 %collective-permute-start.19 = (bf16[16,2,128,128]{3,2,1,0:T(8,128)(2,1)S(1)}, bf16[16,2,128,128]{3,2,1,0:T(8,128)(2,1)S(1)}, u32[]{:S(2)}, u32[]{:S(2)}) collective-permute-start(bf16[16,2,128,128]{3,2,1,0:T(8,128)(2,1)S(1)} %slice.15), channel_id=1, source_target_pairs={{0,96},{4,28},{8,104},{12,4},{16,112},{20,12},{24,120},{28,20},{32... | collective-permute-start | bytes 3145736 | tf_op jit(solution)/shard_map/ppermute | solution.py:39
  133.4 23.5 %collective-permute-start.20 = (bf16[2,1024,128]{2,1,0:T(8,128)(2,1)S(1)}, bf16[2,1024,128]{2,1,0:T(8,128)(2,1)S(1)}, u32[]{:S(2)}, u32[]{:S(2)}) collective-permute-start(bf16[2,1024,128]{2,1,0:T(8,128)(2,1)S(1)} %finish.2.a0), channel_id=1, source_target_pairs={{0,3},{1,0},{2,1},{3,2},{4,7},{5,4},{6,5},{7,6},{8,11},{9,8},{10,9... | collective-permute-start | bytes 1572872 | tf_op jit(solution)/shard_map/ppermute | solution.py:57
  136.0 21.0 %collective-permute-start.21 = (bf16[2,1024,128]{2,1,0:T(8,128)(2,1)S(1)}, bf16[2,1024,128]{2,1,0:T(8,128)(2,1)S(1)}, u32[]{:S(2)}, u32[]{:S(2)}) collective-permute-start(bf16[2,1024,128]{2,1,0:T(8,128)(2,1)S(1)} %finish.2.a0), channel_id=1, source_target_pairs={{0,1},{1,2},{2,3},{3,0},{4,5},{5,6},{6,7},{7,4},{8,9},{9,10},{10,1... | collective-permute-start | bytes 1572872 | tf_op jit(solution)/shard_map/ppermute | solution.py:57
  156.9 19.6 %collective-permute-start.23 = (bf16[2096,128]{1,0:T(8,128)(2,1)S(1)}, bf16[2096,128]{1,0:T(8,128)(2,1)S(1)}, u32[]{:S(2)}, u32[]{:S(2)}) collective-permute-start(bf16[2096,128]{1,0:T(8,128)(2,1)S(1)} %get-tuple-element.136), channel_id=1, source_target_pairs={{0,8},{4,36},{8,16},{12,44},{16,24},{20,52},{24,0},{28,60},{32,40}... | collective-permute-start | bytes 1609736 | tf_op jit(solution)/shard_map/ppermute | solution.py:44
  157.0 19.5 %collective-permute-start.24 = (bf16[2096,128]{1,0:T(8,128)(2,1)S(1)}, bf16[2096,128]{1,0:T(8,128)(2,1)S(1)}, u32[]{:S(2)}, u32[]{:S(2)}) collective-permute-start(bf16[2096,128]{1,0:T(8,128)(2,1)S(1)} %get-tuple-element.137), channel_id=1, source_target_pairs={{0,16},{4,68},{8,24},{12,76},{16,0},{20,84},{24,8},{28,92},{32,48}... | collective-permute-start | bytes 1609736 | tf_op jit(solution)/shard_map/ppermute | solution.py:44
  160.3 16.2 %collective-permute-start.25 = (bf16[2096,128]{1,0:T(8,128)(2,1)S(1)}, bf16[2096,128]{1,0:T(8,128)(2,1)S(1)}, u32[]{:S(2)}, u32[]{:S(2)}) collective-permute-start(bf16[2096,128]{1,0:T(8,128)(2,1)S(1)} %get-tuple-element.138), channel_id=1, source_target_pairs={{0,24},{4,100},{8,0},{12,108},{16,8},{20,116},{24,16},{28,124},{32... | collective-permute-start | bytes 1609736 | tf_op jit(solution)/shard_map/ppermute | solution.py:44
  162.3 14.2 %collective-permute-start.22 = (bf16[2,1024,128]{2,1,0:T(8,128)(2,1)S(1)}, bf16[2,1024,128]{2,1,0:T(8,128)(2,1)S(1)}, u32[]{:S(2)}, u32[]{:S(2)}) collective-permute-start(bf16[2,1024,128]{2,1,0:T(8,128)(2,1)S(1)} %finish.2.a0), channel_id=1, source_target_pairs={{0,2},{1,3},{2,0},{3,1},{4,6},{5,7},{6,4},{7,5},{8,10},{9,11},{10,... | collective-permute-start | bytes 1572872 | tf_op jit(solution)/shard_map/ppermute | solution.py:57
  179.4 24.8 %collective-permute-start.27 = (bf16[2,1024,128]{2,1,0:T(8,128)(2,1)S(1)}, bf16[2,1024,128]{2,1,0:T(8,128)(2,1)S(1)}, u32[]{:S(2)}, u32[]{:S(2)}) collective-permute-start(bf16[2,1024,128]{2,1,0:T(8,128)(2,1)S(1)} %finish.3.a0), channel_id=1, source_target_pairs={{0,3},{1,0},{2,1},{3,2},{4,7},{5,4},{6,5},{7,6},{8,11},{9,8},{10,9... | collective-permute-start | bytes 1572872 | tf_op jit(solution)/shard_map/ppermute | solution.py:57
  182.0 22.3 %collective-permute-start.28 = (bf16[2,1024,128]{2,1,0:T(8,128)(2,1)S(1)}, bf16[2,1024,128]{2,1,0:T(8,128)(2,1)S(1)}, u32[]{:S(2)}, u32[]{:S(2)}) collective-permute-start(bf16[2,1024,128]{2,1,0:T(8,128)(2,1)S(1)} %finish.3.a0), channel_id=1, source_target_pairs={{0,2},{1,3},{2,0},{3,1},{4,6},{5,7},{6,4},{7,5},{8,10},{9,11},{10,... | collective-permute-start | bytes 1572872 | tf_op jit(solution)/shard_map/ppermute | solution.py:57
  182.5 26.1 %collective-permute-start.29 = (bf16[2,1024,128]{2,1,0:T(8,128)(2,1)S(1)}, bf16[2,1024,128]{2,1,0:T(8,128)(2,1)S(1)}, u32[]{:S(2)}, u32[]{:S(2)}) collective-permute-start(bf16[2,1024,128]{2,1,0:T(8,128)(2,1)S(1)} %finish.3.a0), channel_id=1, source_target_pairs={{0,1},{1,2},{2,3},{3,0},{4,5},{5,6},{6,7},{7,4},{8,9},{9,10},{10,1... | collective-permute-start | bytes 1572872 | tf_op jit(solution)/shard_map/ppermute | solution.py:57
  (22 other events, 173.0 us)

commit v9 on v8

--- a/solution.py
+++ b/solution.py
@@ -553,7 +553,9 @@
     weights = pick(after(place, parts[0]), w_out)
     back = returned(parts)
     back[1], back[3], up1, down1 = lax.optimization_barrier((back[1], back[3], up1, down1))
-    up21, down21 = rows_perm(up1[:16], 1), rows_perm(down1[16:], -1)
+    tops1, bottoms1 = up1[:16], down1[16:]
+    back[0], tops1, bottoms1 = lax.optimization_barrier((back[0], tops1, bottoms1))
+    up21, down21 = rows_perm(tops1, 1), rows_perm(bottoms1, -1)
     back[0], near_lse, *weights = lax.optimization_barrier((back[0], near_lse, *weights))
     own, other = merge(back)
     heads = finish(0, near_o, near_lse, own, core_swap(other))

time: 212 us -> 210 us (level)
  Pallas kernels: 87.5 us -> 81.5 us
  starting transfers between devices: 42.5 us -> 45.9 us
    pallas_call x2, Pallas kernels: 23.7 us -> 18.1 us  [far(): pl.pallas_call(functools.partial(far_kernel, j), in_specs=[SMEM] * 5 + [A...]
    ppermute x6, starting transfers between devices: 5.9 us -> 8.03 us  [core_swap(): lax.ppermute(x, 'tok', [(tok_of(y, z, c), tok_of(y, z, 1 - c)) for y, z,...]
  transfers between devices with their start and end apart: 30 -> 30, of which waited for: 15 -> 13; matrix products, arithmetic and copies ran while one was open for 4% -> 5% of each run, Pallas kernels for 36% -> 34%
where the time goes in v9:
time: 210 us
  Pallas kernels  81.5 us (39%)
  waiting for transfers between devices  66.7 us (32%)
  starting transfers between devices  45.9 us (22%)
  local copies, waits for them, and re-layouts  13.6 us (6%)
    ppermute x6, waiting for transfers between devices, mp_perm(): return lax.ppermute(x, 'mp', [(i, (i + d) % NX) for i in range(NX)])  32.9 us
    pallas_call x4, Pallas kernels, split_cache(): pl.pallas_call(split_cache_kernel, grid_spec=pltpu.PrefetchScalarGridSpec...  22 us
    pallas_call x2, Pallas kernels, far(): pl.pallas_call(functools.partial(far_kernel, j), in_specs=[SMEM] * 5 + [A...  18.1 us
    ppermute x9, starting transfers between devices, query_perm(): return lax.ppermute(x, 'tok', pairs)  14 us
    ppermute x9, waiting for transfers between devices, query_perm(): return lax.ppermute(x, 'tok', pairs)  13.2 us
    ppermute x8, starting transfers between devices, rows_perm(): return lax.ppermute(x, 'tok', pairs)  13 us
    ppermute x8, waiting for transfers between devices, rows_perm(): return lax.ppermute(x, 'tok', pairs)  12.3 us
    pallas_call x1, Pallas kernels, project(): pl.pallas_call(project_kernel, grid_spec=pltpu.PrefetchScalarGridSpec(num...  10.4 us
  transfers between devices with their start and end apart: 30, of which 13 were waited for; matrix products, arithmetic and copies ran while one was open for 5% of the time, Pallas kernels for 34%

profile of v9, /device:TPU:1, one launch (start us, length us, event | category | flops | bytes accessed | tf_op | source)
XLA Modules:
  0.0 209.8 jit_solution(4349105146028433638)
XLA Ops:
  2.2 4.5 %split_cache.5 = bf16[16,2,128,128]{3,2,1,0:T(8,128)(2,1)S(1)} custom-call(s32[1]{0:T(128)S(6)} %sub.20.head_ref, bf16[2,1024,2,512]{3,2,1,0:T(2,128)(2,1)S(1)} %copy-done), custom_call_target="tpu_custom_call" | custom-call | flops 1 | bytes 1 | tf_op jit(solution)/shard_map/split_cache/pallas_call | solution.py:76
  8.2 6.0 %split_cache.4 = bf16[32,2,128,128]{3,2,1,0:T(8,128)(2,1)S(1)} custom-call(s32[1]{0:T(128)S(6)} %mul.35.head_ref, bf16[2,1024,2,512]{3,2,1,0:T(2,128)(2,1)} %src.7), custom_call_target="tpu_custom_call" | custom-call | flops 1 | bytes 1 | tf_op jit(solution)/shard_map/split_cache/pallas_call | solution.py:76
  18.4 6.9 %query.1 = (bf16[1024,2048]{1,0:T(8,128)(2,1)}, bf16[2,1024,128]{2,1,0:T(8,128)(2,1)S(1)}, bf16[2,1024,128]{2,1,0:T(8,128)(2,1)S(1)}) custom-call(s32[1]{0:T(128)} %bitcast.core_ref, bf16[1024,2048]{1,0:T(8,128)(2,1)} %carried.1, f32[1,2048]{1,0:T(1,128)S(1)} %bitcast.23, bf16[2048,512]{1,0:T(8,128)(2,1)S(1)} %copy-done.3), custom_call_target="tpu_custom_call" | custom-call | flops 1 | bytes 1 | tf_op jit(solution)/shard_map/query/pallas_call | solution.py:120
  30.1 2.8 %collective-permute-start.2 = (bf16[2,2,8,128,128]{4,3,2,1,0:T(8,128)(2,1)S(1)}, bf16[2,2,8,128,128]{4,3,2,1,0:T(8,128)(2,1)}, u32[]{:S(2)}, u32[]{:S(2)}) collective-permute-start(bf16[2,2,8,128,128]{4,3,2,1,0:T(8,128)(2,1)S(1)} %bitcast.14), channel_id=1, source_target_pairs={{0,24},{4,100},{8,0},{12,108},{16,8},{20,116},{24,16},{28,124},{32... | collective-permute-start | bytes 3145736 | tf_op jit(solution)/shard_map/ppermute | solution.py:44
  34.9 7.0 %split_cache.6 = bf16[32,2,128,128]{3,2,1,0:T(8,128)(2,1)} custom-call(s32[1]{0:T(128)S(6)} %add.42.head_ref, bf16[2,1024,2,512]{3,2,1,0:T(2,128)(2,1)} %src.7), custom_call_target="tpu_custom_call" | custom-call | flops 1 | bytes 1 | tf_op jit(solution)/shard_map/split_cache/pallas_call | solution.py:76
  42.0 4.5 %split_cache.7 = bf16[16,2,128,128]{3,2,1,0:T(8,128)(2,1)S(1)} custom-call(s32[1]{0:T(128)S(6)} %sub.21.head_ref, bf16[2,1024,2,512]{3,2,1,0:T(2,128)(2,1)S(1)} %copy-done.1), custom_call_target="tpu_custom_call" | custom-call | flops 1 | bytes 1 | tf_op jit(solution)/shard_map/split_cache/pallas_call | solution.py:76
  46.5 10.4 %project.1 = (bf16[4,8,128,128]{3,2,1,0:T(8,128)(2,1)S(1)}, bf16[4,8,128,128]{3,2,1,0:T(8,128)(2,1)S(1)}, bf16[1024,128]{1,0:T(8,128)(2,1)S(1)}, bf16[1024,128]{1,0:T(8,128)(2,1)S(1)}) custom-call(s32[1]{0:T(128)} %bitcast.core_ref, bf16[1024,2048]{1,0:T(8,128)(2,1)} %get-tuple-element.84.normed_ref, bf16[2048,512]{1,0:T(8,128)(2,1)S(1)} %copy-done.6, ...), custom_call_target="tpu_custom_call" | custom-call | flops 1 | bytes 1 | tf_op jit(solution)/shard_map/project/pallas_call | solution.py:172
  60.1 3.8 %collective-permute-done.4.rest_8_ = bf16[2,2,8,128,128]{4,3,2,1,0:T(8,128)(2,1)} collective-permute-done((bf16[2,2,8,128,128]{4,3,2,1,0:T(8,128)(2,1)S(1)}, bf16[2,2,8,128,128]{4,3,2,1,0:T(8,128)(2,1)}, u32[]{:S(2)}, u32[]{:S(2)}) %collective-permute-start.4) | collective-permute-done | bytes 1048608 | tf_op jit(solution)/shard_map/ppermute | solution.py:44
  72.1 2.7 %plan.1 = (s32[100]{0:T(128)S(1)}, s32[64]{0:T(128)S(1)}, s32[64]{0:T(128)S(1)}, s32[2]{0:T(128)S(1)}) custom-call(s32[64]{0:T(128)S(1)} %reduce_sum.12.cnt_ref, s32[512]{0:T(512)S(1)} %reshape.73.code_ref), custom_call_target="tpu_custom_call" | custom-call | flops 1 | bytes 1 | tf_op jit(solution)/shard_map/plan/pallas_call | solution.py:272
  76.0 5.6 %collective-permute-done.10 = bf16[1024,128]{1,0:T(8,128)(2,1)S(1)} collective-permute-done((bf16[1024,128]{1,0:T(8,128)(2,1)S(1)}, bf16[1024,128]{1,0:T(8,128)(2,1)S(1)}, u32[]{:S(2)}, u32[]{:S(2)}) %collective-permute-start.10) | collective-permute-done | bytes 262176 | tf_op jit(solution)/shard_map/ppermute | solution.py:53
  83.8 2.6 %collective-permute-start.15 = (bf16[32,2,128,128]{3,2,1,0:T(8,128)(2,1)}, bf16[32,2,128,128]{3,2,1,0:T(8,128)(2,1)}, u32[]{:S(2)}, u32[]{:S(2)}) collective-permute-start(bf16[32,2,128,128]{3,2,1,0:T(8,128)(2,1)} %constant_dynamic-update-slice_fusion.rest_0_), channel_id=1, source_target_pairs={{0,96},{4,28},{8,104},{12,4},{16,112},{20,12},{24,120},{28,20},{32... | collective-permute-start | bytes 6291464 | tf_op jit(solution)/shard_map/ppermute | solution.py:39
  86.4 8.7 %near.1 = (f32[4,8,128,128]{3,2,1,0:T(8,128)S(1)}, f32[4,8,128]{2,1,0:T(8,128)S(1)}) custom-call(s32[1]{0:T(128)} %bitcast.core_ref, bf16[2,1024,128]{2,1,0:T(8,128)(2,1)S(1)} %copy-done.5, bf16[2,1024,128]{2,1,0:T(8,128)(2,1)S(1)} %copy-done.10, bf16[4,8,128,128]{3,2,1,0:T(8,128)(2,1)S(1)} %get-tuple-element.85.k_ref, ...), custom_call_target="tpu_custom_call" | custom-call | flops 1 | bytes 1 | tf_op jit(solution)/shard_map/near/pallas_call | solution.py:217
  95.1 9.5 %far.2 = (bf16[2096,128]{1,0:T(8,128)(2,1)S(1)}, bf16[2096,128]{1,0:T(8,128)(2,1)}, bf16[2096,128]{1,0:T(8,128)(2,1)}, bf16[2096,128]{1,0:T(8,128)(2,1)}) custom-call(s32[64]{0:T(128)S(1)} %reduce_sum.12.cnt_ref, s32[100]{0:T(128)S(1)} %get-tuple-element.105.unit_ref, s32[64]{0:T(128)S(1)} %get-tuple-element.106.first_ref, ...), custom_call_target="tpu_custom_call" | custom-call | flops 1 | bytes 1 | tf_op jit(solution)/shard_map/far/pallas_call | solution.py:357
  112.3 4.1 %collective-permute-done.12.b = bf16[2096,128]{1,0:T(8,128)(2,1)} collective-permute-done((bf16[2096,128]{1,0:T(8,128)(2,1)}, bf16[2096,128]{1,0:T(8,128)(2,1)}, u32[]{:S(2)}, u32[]{:S(2)}) %collective-permute-start.12) | collective-permute-done | bytes 536608 | tf_op jit(solution)/shard_map/ppermute | solution.py:44
  116.4 5.3 %collective-permute-done.13.d = bf16[2096,128]{1,0:T(8,128)(2,1)} collective-permute-done((bf16[2096,128]{1,0:T(8,128)(2,1)}, bf16[2096,128]{1,0:T(8,128)(2,1)}, u32[]{:S(2)}, u32[]{:S(2)}) %collective-permute-start.13) | collective-permute-done | bytes 536608 | tf_op jit(solution)/shard_map/ppermute | solution.py:44
  128.7 3.4 %collective-permute-start.19 = (bf16[16,2,128,128]{3,2,1,0:T(8,128)(2,1)S(1)}, bf16[16,2,128,128]{3,2,1,0:T(8,128)(2,1)S(1)}, u32[]{:S(2)}, u32[]{:S(2)}) collective-permute-start(bf16[16,2,128,128]{3,2,1,0:T(8,128)(2,1)S(1)} %slice.15), channel_id=1, source_target_pairs={{0,96},{4,28},{8,104},{12,4},{16,112},{20,12},{24,120},{28,20},{32... | collective-permute-start | bytes 3145736 | tf_op jit(solution)/shard_map/ppermute | solution.py:39
  135.0 9.9 %collective-permute-done.18.rest_2_ = bf16[16,2,128,128]{3,2,1,0:T(8,128)(2,1)S(1)} collective-permute-done((bf16[16,2,128,128]{3,2,1,0:T(8,128)(2,1)}, bf16[16,2,128,128]{3,2,1,0:T(8,128)(2,1)S(1)}, u32[]{:S(2)}, u32[]{:S(2)}) %collective-permute-start.18) | collective-permute-done | bytes 1048608 | tf_op jit(solution)/shard_map/ppermute | solution.py:39
  144.8 8.5 %far.3 = (bf16[2096,128]{1,0:T(8,128)(2,1)S(1)}, bf16[2096,128]{1,0:T(8,128)(2,1)S(1)}, bf16[2096,128]{1,0:T(8,128)(2,1)S(1)}, bf16[2096,128]{1,0:T(8,128)(2,1)S(1)}) custom-call(s32[64]{0:T(128)S(1)} %reduce_sum.12.cnt_ref, s32[100]{0:T(128)S(1)} %get-tuple-element.105.unit_ref, s32[64]{0:T(128)S(1)} %get-tuple-element.106.first_ref, ...), custom_call_target="tpu_custom_call" | custom-call | flops 1 | bytes 1 | tf_op jit(solution)/shard_map/far/pallas_call | solution.py:357
  153.5 5.6 %collective-permute-start.24 = (bf16[2096,128]{1,0:T(8,128)(2,1)S(1)}, bf16[2096,128]{1,0:T(8,128)(2,1)S(1)}, u32[]{:S(2)}, u32[]{:S(2)}) collective-permute-start(bf16[2096,128]{1,0:T(8,128)(2,1)S(1)} %get-tuple-element.143), channel_id=1, source_target_pairs={{0,16},{4,68},{8,24},{12,76},{16,0},{20,84},{24,8},{28,92},{32,48}... | collective-permute-start | bytes 1609736 | tf_op jit(solution)/shard_map/ppermute | solution.py:44
  161.5 11.3 %collective-permute-done.22.a2 = bf16[2,1024,128]{2,1,0:T(8,128)(2,1)S(1)} collective-permute-done((bf16[2,1024,128]{2,1,0:T(8,128)(2,1)S(1)}, bf16[2,1024,128]{2,1,0:T(8,128)(2,1)S(1)}, u32[]{:S(2)}, u32[]{:S(2)}) %collective-permute-start.22) | collective-permute-done | bytes 524320 | tf_op jit(solution)/shard_map/ppermute | solution.py:57
  180.8 4.0 %mix.2.carried = f32[1024,512]{1,0:T(8,128)S(1)} custom-call(s32[2]{0:T(128)S(1)} %pad_add_fusion.place_ref, bf16[2,1024,128]{2,1,0:T(8,128)(2,1)S(1)} %finish.2.a0, bf16[2,1024,128]{2,1,0:T(8,128)(2,1)S(1)} %collective-permute-done.20.a1, bf16[2,1024,128]{2,1,0:T(8,128)(2,1)S(1)} %collective-permute-done.22.a2, ...), custom_call_target="tpu_custom_call" | custom-call | flops 1 | bytes 1 | tf_op jit(solution)/shard_map/mix/pallas_call | solution.py:476
  184.8 17.2 %collective-permute-done.27.a1 = bf16[2,1024,128]{2,1,0:T(8,128)(2,1)S(1)} collective-permute-done((bf16[2,1024,128]{2,1,0:T(8,128)(2,1)S(1)}, bf16[2,1024,128]{2,1,0:T(8,128)(2,1)S(1)}, u32[]{:S(2)}, u32[]{:S(2)}) %collective-permute-start.27) | collective-permute-done | bytes 524320 | tf_op jit(solution)/shard_map/ppermute | solution.py:57
  202.0 4.4 %collective-permute-done.29.a3 = bf16[2,1024,128]{2,1,0:T(8,128)(2,1)S(1)} collective-permute-done((bf16[2,1024,128]{2,1,0:T(8,128)(2,1)S(1)}, bf16[2,1024,128]{2,1,0:T(8,128)(2,1)S(1)}, u32[]{:S(2)}, u32[]{:S(2)}) %collective-permute-start.29) | collective-permute-done | bytes 524320 | tf_op jit(solution)/shard_map/ppermute | solution.py:57
  206.4 3.4 %mix.3 = bf16[1024,512]{1,0:T(8,128)(2,1)} custom-call(s32[2]{0:T(128)S(1)} %pad_add_fusion.place_ref, bf16[2,1024,128]{2,1,0:T(8,128)(2,1)S(1)} %finish.3.a0, bf16[2,1024,128]{2,1,0:T(8,128)(2,1)S(1)} %collective-permute-done.27.a1, bf16[2,1024,128]{2,1,0:T(8,128)(2,1)S(1)} %collective-permute-done.28.a2, ...), custom_call_target="tpu_custom_call" | custom-call | flops 1 | bytes 1 | tf_op jit(solution)/shard_map/mix/pallas_call | solution.py:476
  (105 shorter events, 57.3 us)
Async XLA Ops:
  14.4 42.9 %collective-permute-start.5 = (bf16[32,2,128,128]{3,2,1,0:T(8,128)(2,1)S(1)}, bf16[32,2,128,128]{3,2,1,0:T(8,128)(2,1)}, u32[]{:S(2)}, u32[]{:S(2)}) collective-permute-start(bf16[32,2,128,128]{3,2,1,0:T(8,128)(2,1)S(1)} %constant_dynamic-update-slice_fusion.1.rest_0_), channel_id=1, source_target_pairs={{0,32},{4,12},{8,40},{12,20},{16,48},{20,28},{24,56},{28,4},{32,64... | collective-permute-start | bytes 6291464 | tf_op jit(solution)/shard_map/ppermute | solution.py:39
  16.2 42.5 %collective-permute-start.6 = (bf16[32,2,128,128]{3,2,1,0:T(8,128)(2,1)S(1)}, bf16[32,2,128,128]{3,2,1,0:T(8,128)(2,1)}, u32[]{:S(2)}, u32[]{:S(2)}) collective-permute-start(bf16[32,2,128,128]{3,2,1,0:T(8,128)(2,1)S(1)} %constant_dynamic-update-slice_fusion.1.rest_0_), channel_id=1, source_target_pairs={{0,96},{4,28},{8,104},{12,4},{16,112},{20,12},{24,120},{28,20},{32... | collective-permute-start | bytes 6291464 | tf_op jit(solution)/shard_map/ppermute | solution.py:39
  30.1 30.0 %collective-permute-start.2 = (bf16[2,2,8,128,128]{4,3,2,1,0:T(8,128)(2,1)S(1)}, bf16[2,2,8,128,128]{4,3,2,1,0:T(8,128)(2,1)}, u32[]{:S(2)}, u32[]{:S(2)}) collective-permute-start(bf16[2,2,8,128,128]{4,3,2,1,0:T(8,128)(2,1)S(1)} %bitcast.14), channel_id=1, source_target_pairs={{0,24},{4,100},{8,0},{12,108},{16,8},{20,116},{24,16},{28,124},{32... | collective-permute-start | bytes 3145736 | tf_op jit(solution)/shard_map/ppermute | solution.py:44
  32.9 27.2 %collective-permute-start.3 = (bf16[2,2,8,128,128]{4,3,2,1,0:T(8,128)(2,1)S(1)}, bf16[2,2,8,128,128]{4,3,2,1,0:T(8,128)(2,1)}, u32[]{:S(2)}, u32[]{:S(2)}) collective-permute-start(bf16[2,2,8,128,128]{4,3,2,1,0:T(8,128)(2,1)S(1)} %bitcast.15), channel_id=1, source_target_pairs={{0,16},{4,68},{8,24},{12,76},{16,0},{20,84},{24,8},{28,92},{32,48}... | collective-permute-start | bytes 3145736 | tf_op jit(solution)/shard_map/ppermute | solution.py:44
  33.3 30.7 %collective-permute-start.4 = (bf16[2,2,8,128,128]{4,3,2,1,0:T(8,128)(2,1)S(1)}, bf16[2,2,8,128,128]{4,3,2,1,0:T(8,128)(2,1)}, u32[]{:S(2)}, u32[]{:S(2)}) collective-permute-start(bf16[2,2,8,128,128]{4,3,2,1,0:T(8,128)(2,1)S(1)} %bitcast.16), channel_id=1, source_target_pairs={{0,8},{4,36},{8,16},{12,44},{16,24},{20,52},{24,0},{28,60},{32,40}... | collective-permute-start | bytes 3145736 | tf_op jit(solution)/shard_map/ppermute | solution.py:44
  65.0 17.8 %collective-permute-start.8 = (bf16[16,2,128,128]{3,2,1,0:T(8,128)(2,1)S(1)}, bf16[16,2,128,128]{3,2,1,0:T(8,128)(2,1)S(1)}, u32[]{:S(2)}, u32[]{:S(2)}) collective-permute-start(bf16[16,2,128,128]{3,2,1,0:T(8,128)(2,1)S(1)} %slice.16), channel_id=1, source_target_pairs={{0,32},{4,12},{8,40},{12,20},{16,48},{20,28},{24,56},{28,4},{32,64... | collective-permute-start | bytes 3145736 | tf_op jit(solution)/shard_map/ppermute | solution.py:39
  67.1 16.5 %collective-permute-start.9 = (bf16[16,2,128,128]{3,2,1,0:T(8,128)(2,1)S(1)}, bf16[16,2,128,128]{3,2,1,0:T(8,128)(2,1)S(1)}, u32[]{:S(2)}, u32[]{:S(2)}) collective-permute-start(bf16[16,2,128,128]{3,2,1,0:T(8,128)(2,1)S(1)} %slice.17), channel_id=1, source_target_pairs={{0,96},{4,28},{8,104},{12,4},{16,112},{20,12},{24,120},{28,20},{32... | collective-permute-start | bytes 3145736 | tf_op jit(solution)/shard_map/ppermute | solution.py:39
  67.8 13.8 %collective-permute-start.10 = (bf16[1024,128]{1,0:T(8,128)(2,1)S(1)}, bf16[1024,128]{1,0:T(8,128)(2,1)S(1)}, u32[]{:S(2)}, u32[]{:S(2)}) collective-permute-start(bf16[1024,128]{1,0:T(8,128)(2,1)S(1)} %get-tuple-element.94), channel_id=1, source_target_pairs={{0,124},{4,8},{8,4},{12,16},{16,12},{20,24},{24,20},{28,32},{32,28... | collective-permute-start | bytes 786440 | tf_op jit(solution)/shard_map/ppermute | solution.py:53
  70.2 11.4 %collective-permute-start.11 = (bf16[1024,128]{1,0:T(8,128)(2,1)S(1)}, bf16[1024,128]{1,0:T(8,128)(2,1)S(1)}, u32[]{:S(2)}, u32[]{:S(2)}) collective-permute-start(bf16[1024,128]{1,0:T(8,128)(2,1)S(1)} %get-tuple-element.95), channel_id=1, source_target_pairs={{0,4},{4,0},{8,12},{12,8},{16,20},{20,16},{24,28},{28,24},{32,36},... | collective-permute-start | bytes 786440 | tf_op jit(solution)/shard_map/ppermute | solution.py:48
  83.5 38.2 %collective-permute-start.14 = (bf16[32,2,128,128]{3,2,1,0:T(8,128)(2,1)}, bf16[32,2,128,128]{3,2,1,0:T(8,128)(2,1)}, u32[]{:S(2)}, u32[]{:S(2)}) collective-permute-start(bf16[32,2,128,128]{3,2,1,0:T(8,128)(2,1)} %constant_dynamic-update-slice_fusion.rest_0_), channel_id=1, source_target_pairs={{0,32},{4,12},{8,40},{12,20},{16,48},{20,28},{24,56},{28,4},{32,64... | collective-permute-start | bytes 6291464 | tf_op jit(solution)/shard_map/ppermute | solution.py:39
  83.8 37.9 %collective-permute-start.15 = (bf16[32,2,128,128]{3,2,1,0:T(8,128)(2,1)}, bf16[32,2,128,128]{3,2,1,0:T(8,128)(2,1)}, u32[]{:S(2)}, u32[]{:S(2)}) collective-permute-start(bf16[32,2,128,128]{3,2,1,0:T(8,128)(2,1)} %constant_dynamic-update-slice_fusion.rest_0_), channel_id=1, source_target_pairs={{0,96},{4,28},{8,104},{12,4},{16,112},{20,12},{24,120},{28,20},{32... | collective-permute-start | bytes 6291464 | tf_op jit(solution)/shard_map/ppermute | solution.py:39
  106.7 15.0 %collective-permute-start.13 = (bf16[2096,128]{1,0:T(8,128)(2,1)}, bf16[2096,128]{1,0:T(8,128)(2,1)}, u32[]{:S(2)}, u32[]{:S(2)}) collective-permute-start(bf16[2096,128]{1,0:T(8,128)(2,1)} %get-tuple-element.117), channel_id=1, source_target_pairs={{0,24},{4,100},{8,0},{12,108},{16,8},{20,116},{24,16},{28,124},{32... | collective-permute-start | bytes 1609736 | tf_op jit(solution)/shard_map/ppermute | solution.py:44
  108.7 16.6 %collective-permute-start.16 = (bf16[2096,128]{1,0:T(8,128)(2,1)}, bf16[2096,128]{1,0:T(8,128)(2,1)}, u32[]{:S(2)}, u32[]{:S(2)}) collective-permute-start(bf16[2096,128]{1,0:T(8,128)(2,1)} %get-tuple-element.129), channel_id=1, source_target_pairs={{0,16},{4,68},{8,24},{12,76},{16,0},{20,84},{24,8},{28,92},{32,48}... | collective-permute-start | bytes 1609736 | tf_op jit(solution)/shard_map/ppermute | solution.py:44
  128.7 16.1 %collective-permute-start.18 = (bf16[16,2,128,128]{3,2,1,0:T(8,128)(2,1)}, bf16[16,2,128,128]{3,2,1,0:T(8,128)(2,1)S(1)}, u32[]{:S(2)}, u32[]{:S(2)}) collective-permute-start(bf16[16,2,128,128]{3,2,1,0:T(8,128)(2,1)} %slice.14), channel_id=1, source_target_pairs={{0,32},{4,12},{8,40},{12,20},{16,48},{20,28},{24,56},{28,4},{32,64... | collective-permute-start | bytes 3145736 | tf_op jit(solution)/shard_map/ppermute | solution.py:39
  128.7 16.1 %collective-permute-start.19 = (bf16[16,2,128,128]{3,2,1,0:T(8,128)(2,1)S(1)}, bf16[16,2,128,128]{3,2,1,0:T(8,128)(2,1)S(1)}, u32[]{:S(2)}, u32[]{:S(2)}) collective-permute-start(bf16[16,2,128,128]{3,2,1,0:T(8,128)(2,1)S(1)} %slice.15), channel_id=1, source_target_pairs={{0,96},{4,28},{8,104},{12,4},{16,112},{20,12},{24,120},{28,20},{32... | collective-permute-start | bytes 3145736 | tf_op jit(solution)/shard_map/ppermute | solution.py:39
  132.4 21.0 %collective-permute-start.20 = (bf16[2,1024,128]{2,1,0:T(8,128)(2,1)S(1)}, bf16[2,1024,128]{2,1,0:T(8,128)(2,1)S(1)}, u32[]{:S(2)}, u32[]{:S(2)}) collective-permute-start(bf16[2,1024,128]{2,1,0:T(8,128)(2,1)S(1)} %finish.2.a0), channel_id=1, source_target_pairs={{0,3},{1,0},{2,1},{3,2},{4,7},{5,4},{6,5},{7,6},{8,11},{9,8},{10,9... | collective-permute-start | bytes 1572872 | tf_op jit(solution)/shard_map/ppermute | solution.py:57
  135.0 18.4 %collective-permute-start.21 = (bf16[2,1024,128]{2,1,0:T(8,128)(2,1)S(1)}, bf16[2,1024,128]{2,1,0:T(8,128)(2,1)S(1)}, u32[]{:S(2)}, u32[]{:S(2)}) collective-permute-start(bf16[2,1024,128]{2,1,0:T(8,128)(2,1)S(1)} %finish.2.a0), channel_id=1, source_target_pairs={{0,1},{1,2},{2,3},{3,0},{4,5},{5,6},{6,7},{7,4},{8,9},{9,10},{10,1... | collective-permute-start | bytes 1572872 | tf_op jit(solution)/shard_map/ppermute | solution.py:57
  153.4 19.4 %collective-permute-start.23 = (bf16[2096,128]{1,0:T(8,128)(2,1)S(1)}, bf16[2096,128]{1,0:T(8,128)(2,1)S(1)}, u32[]{:S(2)}, u32[]{:S(2)}) collective-permute-start(bf16[2096,128]{1,0:T(8,128)(2,1)S(1)} %get-tuple-element.142), channel_id=1, source_target_pairs={{0,8},{4,36},{8,16},{12,44},{16,24},{20,52},{24,0},{28,60},{32,40}... | collective-permute-start | bytes 1609736 | tf_op jit(solution)/shard_map/ppermute | solution.py:44
  153.5 19.3 %collective-permute-start.24 = (bf16[2096,128]{1,0:T(8,128)(2,1)S(1)}, bf16[2096,128]{1,0:T(8,128)(2,1)S(1)}, u32[]{:S(2)}, u32[]{:S(2)}) collective-permute-start(bf16[2096,128]{1,0:T(8,128)(2,1)S(1)} %get-tuple-element.143), channel_id=1, source_target_pairs={{0,16},{4,68},{8,24},{12,76},{16,0},{20,84},{24,8},{28,92},{32,48}... | collective-permute-start | bytes 1609736 | tf_op jit(solution)/shard_map/ppermute | solution.py:44
  159.0 13.8 %collective-permute-start.25 = (bf16[2096,128]{1,0:T(8,128)(2,1)S(1)}, bf16[2096,128]{1,0:T(8,128)(2,1)S(1)}, u32[]{:S(2)}, u32[]{:S(2)}) collective-permute-start(bf16[2096,128]{1,0:T(8,128)(2,1)S(1)} %get-tuple-element.144), channel_id=1, source_target_pairs={{0,24},{4,100},{8,0},{12,108},{16,8},{20,116},{24,16},{28,124},{32... | collective-permute-start | bytes 1609736 | tf_op jit(solution)/shard_map/ppermute | solution.py:44
  159.1 13.8 %collective-permute-start.22 = (bf16[2,1024,128]{2,1,0:T(8,128)(2,1)S(1)}, bf16[2,1024,128]{2,1,0:T(8,128)(2,1)S(1)}, u32[]{:S(2)}, u32[]{:S(2)}) collective-permute-start(bf16[2,1024,128]{2,1,0:T(8,128)(2,1)S(1)} %finish.2.a0), channel_id=1, source_target_pairs={{0,2},{1,3},{2,0},{3,1},{4,6},{5,7},{6,4},{7,5},{8,10},{9,11},{10,... | collective-permute-start | bytes 1572872 | tf_op jit(solution)/shard_map/ppermute | solution.py:57
  177.4 24.6 %collective-permute-start.27 = (bf16[2,1024,128]{2,1,0:T(8,128)(2,1)S(1)}, bf16[2,1024,128]{2,1,0:T(8,128)(2,1)S(1)}, u32[]{:S(2)}, u32[]{:S(2)}) collective-permute-start(bf16[2,1024,128]{2,1,0:T(8,128)(2,1)S(1)} %finish.3.a0), channel_id=1, source_target_pairs={{0,3},{1,0},{2,1},{3,2},{4,7},{5,4},{6,5},{7,6},{8,11},{9,8},{10,9... | collective-permute-start | bytes 1572872 | tf_op jit(solution)/shard_map/ppermute | solution.py:57
  180.0 22.0 %collective-permute-start.28 = (bf16[2,1024,128]{2,1,0:T(8,128)(2,1)S(1)}, bf16[2,1024,128]{2,1,0:T(8,128)(2,1)S(1)}, u32[]{:S(2)}, u32[]{:S(2)}) collective-permute-start(bf16[2,1024,128]{2,1,0:T(8,128)(2,1)S(1)} %finish.3.a0), channel_id=1, source_target_pairs={{0,2},{1,3},{2,0},{3,1},{4,6},{5,7},{6,4},{7,5},{8,10},{9,11},{10,... | collective-permute-start | bytes 1572872 | tf_op jit(solution)/shard_map/ppermute | solution.py:57
  180.2 26.2 %collective-permute-start.29 = (bf16[2,1024,128]{2,1,0:T(8,128)(2,1)S(1)}, bf16[2,1024,128]{2,1,0:T(8,128)(2,1)S(1)}, u32[]{:S(2)}, u32[]{:S(2)}) collective-permute-start(bf16[2,1024,128]{2,1,0:T(8,128)(2,1)S(1)} %finish.3.a0), channel_id=1, source_target_pairs={{0,1},{1,2},{2,3},{3,0},{4,5},{5,6},{6,7},{7,4},{8,9},{9,10},{10,1... | collective-permute-start | bytes 1572872 | tf_op jit(solution)/shard_map/ppermute | solution.py:57
  (22 other events, 174.1 us)

commit v10 on v9

--- a/solution.py
+++ b/solution.py
@@ -539,7 +539,6 @@
     lists = plan(cnt, code)
     held = (rows1, up20, down20, halo, swapped, *lists)
     rows1, up20, down20, halo, swapped, *lists = lax.optimization_barrier(held)
-    near_o, near_lse = near(core, q_keep, q_send, k_all, v_all, halo, swapped)
     up1, down1 = rows_perm(rows1, 1), rows_perm(rows1, -1)
     qs = [mine, q1, q2, q3]
 
@@ -549,8 +548,9 @@
     def gather(heads):
         return [heads, mp_perm(heads, -1), mp_perm(heads, 2), mp_perm(heads, 1)]
 
-    parts = far(0, cnt, lists, [after(rows0, near_o), down0, up20, down20, up0], qs)
+    parts = far(0, cnt, lists, [rows0, down0, up20, down20, up0], qs)
     weights = pick(after(place, parts[0]), w_out)
+    near_o, near_lse = near(core, q_keep, q_send, k_all, v_all, after(halo, parts[0]), swapped)
     back = returned(parts)
     back[1], back[3], up1, down1 = lax.optimization_barrier((back[1], back[3], up1, down1))
     tops1, bottoms1 = up1[:16], down1[16:]

time: 210 us -> 213 us (1.014)
  starting transfers between devices: 45.9 us -> 51 us
  Pallas kernels: 81.5 us -> 85 us
  waiting for transfers between devices: 66.7 us -> 63.4 us
    ppermute x9, waiting for transfers between devices: 13.2 us -> 5.75 us  [query_perm(): return lax.ppermute(x, 'tok', pairs)]
    ppermute x8, waiting for transfers between devices: 12.3 us -> 18.1 us  [rows_perm(): return lax.ppermute(x, 'tok', pairs)]
    ppermute x6, starting transfers between devices: 8.03 us -> 10.9 us  [core_swap(): lax.ppermute(x, 'tok', [(tok_of(y, z, c), tok_of(y, z, 1 - c)) for y, z,...]
    pallas_call x2, Pallas kernels: 18.1 us -> 20.9 us  [far(): pl.pallas_call(functools.partial(far_kernel, j), in_specs=[SMEM] * 5 + [A...]
    ppermute x8, starting transfers between devices: 13 us -> 15.4 us  [rows_perm(): return lax.ppermute(x, 'tok', pairs)]
    unnamed x32 -> x42, local copies, waits for them, and re-layouts: 5.39 us -> 4.56 us
  transfers between devices with their start and end apart: 30 -> 30, of which waited for: 13 -> 14; matrix products, arithmetic and copies ran while one was open for 5% -> 3% of each run, Pallas kernels for 34% -> 35%
where the time goes in v10:
time: 213 us; the launch traced here: 212 us
  Pallas kernels  85 us (40%)
  waiting for transfers between devices  63.4 us (30%)
  starting transfers between devices  51 us (24%)
  local copies, waits for them, and re-layouts  11.6 us (5%)
    ppermute x6, waiting for transfers between devices, mp_perm(): return lax.ppermute(x, 'mp', [(i, (i + d) % NX) for i in range(NX)])  32.6 us
    pallas_call x4, Pallas kernels, split_cache(): pl.pallas_call(split_cache_kernel, grid_spec=pltpu.PrefetchScalarGridSpec...  22 us
    pallas_call x2, Pallas kernels, far(): pl.pallas_call(functools.partial(far_kernel, j), in_specs=[SMEM] * 5 + [A...  20.9 us
    ppermute x8, waiting for transfers between devices, rows_perm(): return lax.ppermute(x, 'tok', pairs)  18.1 us
    ppermute x8, starting transfers between devices, rows_perm(): return lax.ppermute(x, 'tok', pairs)  15.4 us
    ppermute x9, starting transfers between devices, query_perm(): return lax.ppermute(x, 'tok', pairs)  14.4 us
    ppermute x6, starting transfers between devices, core_swap(): lax.ppermute(x, 'tok', [(tok_of(y, z, c), tok_of(y, z, 1 - c)) for y, z,...  10.9 us
    pallas_call x1, Pallas kernels, project(): pl.pallas_call(project_kernel, grid_spec=pltpu.PrefetchScalarGridSpec(num...  10.4 us
  transfers between devices with their start and end apart: 30, of which 14 were waited for; matrix products, arithmetic and copies ran while one was open for 3% of the time, Pallas kernels for 35%

profile of v10, /device:TPU:1, one launch (start us, length us, event | category | flops | bytes accessed | tf_op | source)
XLA Modules:
  0.0 212.0 jit_solution(15768707078058871545)
XLA Ops:
  2.2 4.5 %split_cache.5 = bf16[16,2,128,128]{3,2,1,0:T(8,128)(2,1)S(1)} custom-call(s32[1]{0:T(128)S(6)} %sub.20.head_ref, bf16[2,1024,2,512]{3,2,1,0:T(2,128)(2,1)S(1)} %copy-done), custom_call_target="tpu_custom_call" | custom-call | flops 1 | bytes 1 | tf_op jit(solution)/shard_map/split_cache/pallas_call | solution.py:76
  8.2 6.9 %split_cache.4 = bf16[32,2,128,128]{3,2,1,0:T(8,128)(2,1)} custom-call(s32[1]{0:T(128)S(6)} %mul.35.head_ref, bf16[2,1024,2,512]{3,2,1,0:T(2,128)(2,1)} %src.7), custom_call_target="tpu_custom_call" | custom-call | flops 1 | bytes 1 | tf_op jit(solution)/shard_map/split_cache/pallas_call | solution.py:76
  20.0 7.0 %query.1 = (bf16[1024,2048]{1,0:T(8,128)(2,1)}, bf16[2,1024,128]{2,1,0:T(8,128)(2,1)S(1)}, bf16[2,1024,128]{2,1,0:T(8,128)(2,1)S(1)}) custom-call(s32[1]{0:T(128)} %bitcast.core_ref, bf16[1024,2048]{1,0:T(8,128)(2,1)} %carried.1, f32[1,2048]{1,0:T(1,128)S(1)} %bitcast.23, bf16[2048,512]{1,0:T(8,128)(2,1)S(1)} %copy-done.3), custom_call_target="tpu_custom_call" | custom-call | flops 1 | bytes 1 | tf_op jit(solution)/shard_map/query/pallas_call | solution.py:120
  29.2 2.8 %collective-permute-start.2 = (bf16[2,2,8,128,128]{4,3,2,1,0:T(8,128)(2,1)S(1)}, bf16[2,2,8,128,128]{4,3,2,1,0:T(8,128)(2,1)}, u32[]{:S(2)}, u32[]{:S(2)}) collective-permute-start(bf16[2,2,8,128,128]{4,3,2,1,0:T(8,128)(2,1)S(1)} %bitcast.14), channel_id=1, source_target_pairs={{0,24},{4,100},{8,0},{12,108},{16,8},{20,116},{24,16},{28,124},{32... | collective-permute-start | bytes 3145736 | tf_op jit(solution)/shard_map/ppermute | solution.py:44
  34.0 6.1 %split_cache.6 = bf16[32,2,128,128]{3,2,1,0:T(8,128)(2,1)S(1)} custom-call(s32[1]{0:T(128)S(6)} %add.42.head_ref, bf16[2,1024,2,512]{3,2,1,0:T(2,128)(2,1)} %src.7), custom_call_target="tpu_custom_call" | custom-call | flops 1 | bytes 1 | tf_op jit(solution)/shard_map/split_cache/pallas_call | solution.py:76
  40.2 4.5 %split_cache.7 = bf16[16,2,128,128]{3,2,1,0:T(8,128)(2,1)S(1)} custom-call(s32[1]{0:T(128)S(6)} %sub.21.head_ref, bf16[2,1024,2,512]{3,2,1,0:T(2,128)(2,1)S(1)} %copy-done.1), custom_call_target="tpu_custom_call" | custom-call | flops 1 | bytes 1 | tf_op jit(solution)/shard_map/split_cache/pallas_call | solution.py:76
  44.7 10.4 %project.1 = (bf16[4,8,128,128]{3,2,1,0:T(8,128)(2,1)S(1)}, bf16[4,8,128,128]{3,2,1,0:T(8,128)(2,1)S(1)}, bf16[1024,128]{1,0:T(8,128)(2,1)S(1)}, bf16[1024,128]{1,0:T(8,128)(2,1)S(1)}) custom-call(s32[1]{0:T(128)} %bitcast.core_ref, bf16[1024,2048]{1,0:T(8,128)(2,1)} %get-tuple-element.84.normed_ref, bf16[2048,512]{1,0:T(8,128)(2,1)S(1)} %copy-done.6, ...), custom_call_target="tpu_custom_call" | custom-call | flops 1 | bytes 1 | tf_op jit(solution)/shard_map/project/pallas_call | solution.py:172
  55.2 6.8 %collective-permute-done.5.rest_4_ = bf16[32,2,128,128]{3,2,1,0:T(8,128)(2,1)} collective-permute-done((bf16[32,2,128,128]{3,2,1,0:T(8,128)(2,1)}, bf16[32,2,128,128]{3,2,1,0:T(8,128)(2,1)}, u32[]{:S(2)}, u32[]{:S(2)}) %collective-permute-start.5) | collective-permute-done | bytes 2097184 | tf_op jit(solution)/shard_map/ppermute | solution.py:39
  72.7 3.4 %collective-permute-start.11 = (bf16[1024,128]{1,0:T(8,128)(2,1)S(1)}, bf16[1024,128]{1,0:T(8,128)(2,1)S(1)}, u32[]{:S(2)}, u32[]{:S(2)}) collective-permute-start(bf16[1024,128]{1,0:T(8,128)(2,1)S(1)} %get-tuple-element.95), channel_id=1, source_target_pairs={{0,4},{4,0},{8,12},{12,8},{16,20},{20,16},{24,28},{28,24},{32,36},... | collective-permute-start | bytes 786440 | tf_op jit(solution)/shard_map/ppermute | solution.py:48
  76.1 2.9 %plan.1 = (s32[100]{0:T(128)S(1)}, s32[64]{0:T(128)S(1)}, s32[64]{0:T(128)S(1)}, s32[2]{0:T(128)S(1)}) custom-call(s32[64]{0:T(128)S(1)} %reduce_sum.12.cnt_ref, s32[512]{0:T(512)S(1)} %reshape.73.code_ref), custom_call_target="tpu_custom_call" | custom-call | flops 1 | bytes 1 | tf_op jit(solution)/shard_map/plan/pallas_call | solution.py:272
  79.1 4.4 %collective-permute-done.10 = bf16[1024,128]{1,0:T(8,128)(2,1)S(1)} collective-permute-done((bf16[1024,128]{1,0:T(8,128)(2,1)S(1)}, bf16[1024,128]{1,0:T(8,128)(2,1)S(1)}, u32[]{:S(2)}, u32[]{:S(2)}) %collective-permute-start.10) | collective-permute-done | bytes 262176 | tf_op jit(solution)/shard_map/ppermute | solution.py:53
  89.0 10.9 %far.2 = (bf16[2096,128]{1,0:T(8,128)(2,1)S(1)}, bf16[2096,128]{1,0:T(8,128)(2,1)}, bf16[2096,128]{1,0:T(8,128)(2,1)}, bf16[2096,128]{1,0:T(8,128)(2,1)}) custom-call(s32[64]{0:T(128)S(1)} %reduce_sum.12.cnt_ref, s32[100]{0:T(128)S(1)} %get-tuple-element.103.unit_ref, s32[64]{0:T(128)S(1)} %get-tuple-element.104.first_ref, ...), custom_call_target="tpu_custom_call" | custom-call | flops 1 | bytes 1 | tf_op jit(solution)/shard_map/far/pallas_call | solution.py:357
  101.1 3.6 %collective-permute-start.13 = (bf16[2096,128]{1,0:T(8,128)(2,1)}, bf16[2096,128]{1,0:T(8,128)(2,1)}, u32[]{:S(2)}, u32[]{:S(2)}) collective-permute-start(bf16[2096,128]{1,0:T(8,128)(2,1)} %get-tuple-element.117), channel_id=1, source_target_pairs={{0,24},{4,100},{8,0},{12,108},{16,8},{20,116},{24,16},{28,124},{32... | collective-permute-start | bytes 1609736 | tf_op jit(solution)/shard_map/ppermute | solution.py:44
  108.6 8.7 %near.1 = (f32[4,8,128,128]{3,2,1,0:T(8,128)S(1)}, f32[4,8,128]{2,1,0:T(8,128)S(1)}) custom-call(s32[1]{0:T(128)} %bitcast.core_ref, bf16[2,1024,128]{2,1,0:T(8,128)(2,1)S(1)} %copy-done.5, bf16[2,1024,128]{2,1,0:T(8,128)(2,1)S(1)} %copy-done.16, bf16[4,8,128,128]{3,2,1,0:T(8,128)(2,1)S(1)} %copy-done.8, bf16[4,8,128,128]{3,2,1,0:T(8,128)(2,1)S(1)} %copy-done.10, ...), custom_call_target="tpu_custom_call" | custom-call | flops 1 | bytes 1 | tf_op jit(solution)/shard_map/near/pallas_call | solution.py:217
  121.5 3.0 %collective-permute-done.16.c = bf16[2096,128]{1,0:T(8,128)(2,1)} collective-permute-done((bf16[2096,128]{1,0:T(8,128)(2,1)}, bf16[2096,128]{1,0:T(8,128)(2,1)}, u32[]{:S(2)}, u32[]{:S(2)}) %collective-permute-start.16) | collective-permute-done | bytes 536608 | tf_op jit(solution)/shard_map/ppermute | solution.py:44
  136.2 9.7 %collective-permute-done.18.rest_2_ = bf16[16,2,128,128]{3,2,1,0:T(8,128)(2,1)S(1)} collective-permute-done((bf16[16,2,128,128]{3,2,1,0:T(8,128)(2,1)S(1)}, bf16[16,2,128,128]{3,2,1,0:T(8,128)(2,1)S(1)}, u32[]{:S(2)}, u32[]{:S(2)}) %collective-permute-start.18) | collective-permute-done | bytes 1048608 | tf_op jit(solution)/shard_map/ppermute | solution.py:39
  145.9 9.9 %far.3 = (bf16[2096,128]{1,0:T(8,128)(2,1)S(1)}, bf16[2096,128]{1,0:T(8,128)(2,1)S(1)}, bf16[2096,128]{1,0:T(8,128)(2,1)S(1)}, bf16[2096,128]{1,0:T(8,128)(2,1)S(1)}) custom-call(s32[64]{0:T(128)S(1)} %reduce_sum.12.cnt_ref, s32[100]{0:T(128)S(1)} %get-tuple-element.103.unit_ref, s32[64]{0:T(128)S(1)} %get-tuple-element.104.first_ref, ...), custom_call_target="tpu_custom_call" | custom-call | flops 1 | bytes 1 | tf_op jit(solution)/shard_map/far/pallas_call | solution.py:357
  156.0 5.4 %collective-permute-start.24 = (bf16[2096,128]{1,0:T(8,128)(2,1)S(1)}, bf16[2096,128]{1,0:T(8,128)(2,1)S(1)}, u32[]{:S(2)}, u32[]{:S(2)}) collective-permute-start(bf16[2096,128]{1,0:T(8,128)(2,1)S(1)} %get-tuple-element.143), channel_id=1, source_target_pairs={{0,16},{4,68},{8,24},{12,76},{16,0},{20,84},{24,8},{28,92},{32,48}... | collective-permute-start | bytes 1609736 | tf_op jit(solution)/shard_map/ppermute | solution.py:44
  163.8 11.1 %collective-permute-done.22.a2 = bf16[2,1024,128]{2,1,0:T(8,128)(2,1)S(1)} collective-permute-done((bf16[2,1024,128]{2,1,0:T(8,128)(2,1)S(1)}, bf16[2,1024,128]{2,1,0:T(8,128)(2,1)S(1)}, u32[]{:S(2)}, u32[]{:S(2)}) %collective-permute-start.22) | collective-permute-done | bytes 524320 | tf_op jit(solution)/shard_map/ppermute | solution.py:57
  183.1 4.0 %mix.2.carried = f32[1024,512]{1,0:T(8,128)S(1)} custom-call(s32[2]{0:T(128)S(1)} %pad_add_fusion.place_ref, bf16[2,1024,128]{2,1,0:T(8,128)(2,1)S(1)} %finish.2.a0, bf16[2,1024,128]{2,1,0:T(8,128)(2,1)S(1)} %collective-permute-done.20.a1, bf16[2,1024,128]{2,1,0:T(8,128)(2,1)S(1)} %collective-permute-done.22.a2, ...), custom_call_target="tpu_custom_call" | custom-call | flops 1 | bytes 1 | tf_op jit(solution)/shard_map/mix/pallas_call | solution.py:476
  187.1 6.3 %collective-permute-done.27.a1 = bf16[2,1024,128]{2,1,0:T(8,128)(2,1)S(1)} collective-permute-done((bf16[2,1024,128]{2,1,0:T(8,128)(2,1)S(1)}, bf16[2,1024,128]{2,1,0:T(8,128)(2,1)S(1)}, u32[]{:S(2)}, u32[]{:S(2)}) %collective-permute-start.27) | collective-permute-done | bytes 524320 | tf_op jit(solution)/shard_map/ppermute | solution.py:57
  193.4 2.9 %collective-permute-done.28.a2 = bf16[2,1024,128]{2,1,0:T(8,128)(2,1)S(1)} collective-permute-done((bf16[2,1024,128]{2,1,0:T(8,128)(2,1)S(1)}, bf16[2,1024,128]{2,1,0:T(8,128)(2,1)S(1)}, u32[]{:S(2)}, u32[]{:S(2)}) %collective-permute-start.28) | collective-permute-done | bytes 524320 | tf_op jit(solution)/shard_map/ppermute | solution.py:57
  196.4 12.2 %collective-permute-done.29.a3 = bf16[2,1024,128]{2,1,0:T(8,128)(2,1)S(1)} collective-permute-done((bf16[2,1024,128]{2,1,0:T(8,128)(2,1)S(1)}, bf16[2,1024,128]{2,1,0:T(8,128)(2,1)S(1)}, u32[]{:S(2)}, u32[]{:S(2)}) %collective-permute-start.29) | collective-permute-done | bytes 524320 | tf_op jit(solution)/shard_map/ppermute | solution.py:57
  208.6 3.4 %mix.3 = bf16[1024,512]{1,0:T(8,128)(2,1)} custom-call(s32[2]{0:T(128)S(1)} %pad_add_fusion.place_ref, bf16[2,1024,128]{2,1,0:T(8,128)(2,1)S(1)} %finish.3.a0, bf16[2,1024,128]{2,1,0:T(8,128)(2,1)S(1)} %collective-permute-done.27.a1, bf16[2,1024,128]{2,1,0:T(8,128)(2,1)S(1)} %collective-permute-done.28.a2, ...), custom_call_target="tpu_custom_call" | custom-call | flops 1 | bytes 1 | tf_op jit(solution)/shard_map/mix/pallas_call | solution.py:476
  (115 shorter events, 60.6 us)
Async XLA Ops:
  16.2 45.8 %collective-permute-start.5 = (bf16[32,2,128,128]{3,2,1,0:T(8,128)(2,1)}, bf16[32,2,128,128]{3,2,1,0:T(8,128)(2,1)}, u32[]{:S(2)}, u32[]{:S(2)}) collective-permute-start(bf16[32,2,128,128]{3,2,1,0:T(8,128)(2,1)} %constant_dynamic-update-slice_fusion.1.rest_0_), channel_id=1, source_target_pairs={{0,32},{4,12},{8,40},{12,20},{16,48},{20,28},{24,56},{28,4},{32,64... | collective-permute-start | bytes 6291464 | tf_op jit(solution)/shard_map/ppermute | solution.py:39
  17.9 45.4 %collective-permute-start.6 = (bf16[32,2,128,128]{3,2,1,0:T(8,128)(2,1)}, bf16[32,2,128,128]{3,2,1,0:T(8,128)(2,1)}, u32[]{:S(2)}, u32[]{:S(2)}) collective-permute-start(bf16[32,2,128,128]{3,2,1,0:T(8,128)(2,1)} %constant_dynamic-update-slice_fusion.1.rest_0_), channel_id=1, source_target_pairs={{0,96},{4,28},{8,104},{12,4},{16,112},{20,12},{24,120},{28,20},{32... | collective-permute-start | bytes 6291464 | tf_op jit(solution)/shard_map/ppermute | solution.py:39
  29.2 35.5 %collective-permute-start.2 = (bf16[2,2,8,128,128]{4,3,2,1,0:T(8,128)(2,1)S(1)}, bf16[2,2,8,128,128]{4,3,2,1,0:T(8,128)(2,1)}, u32[]{:S(2)}, u32[]{:S(2)}) collective-permute-start(bf16[2,2,8,128,128]{4,3,2,1,0:T(8,128)(2,1)S(1)} %bitcast.14), channel_id=1, source_target_pairs={{0,24},{4,100},{8,0},{12,108},{16,8},{20,116},{24,16},{28,124},{32... | collective-permute-start | bytes 3145736 | tf_op jit(solution)/shard_map/ppermute | solution.py:44
  32.0 32.7 %collective-permute-start.3 = (bf16[2,2,8,128,128]{4,3,2,1,0:T(8,128)(2,1)S(1)}, bf16[2,2,8,128,128]{4,3,2,1,0:T(8,128)(2,1)}, u32[]{:S(2)}, u32[]{:S(2)}) collective-permute-start(bf16[2,2,8,128,128]{4,3,2,1,0:T(8,128)(2,1)S(1)} %bitcast.15), channel_id=1, source_target_pairs={{0,16},{4,68},{8,24},{12,76},{16,0},{20,84},{24,8},{28,92},{32,48}... | collective-permute-start | bytes 3145736 | tf_op jit(solution)/shard_map/ppermute | solution.py:44
  32.3 33.5 %collective-permute-start.4 = (bf16[2,2,8,128,128]{4,3,2,1,0:T(8,128)(2,1)S(1)}, bf16[2,2,8,128,128]{4,3,2,1,0:T(8,128)(2,1)}, u32[]{:S(2)}, u32[]{:S(2)}) collective-permute-start(bf16[2,2,8,128,128]{4,3,2,1,0:T(8,128)(2,1)S(1)} %bitcast.16), channel_id=1, source_target_pairs={{0,8},{4,36},{8,16},{12,44},{16,24},{20,52},{24,0},{28,60},{32,40}... | collective-permute-start | bytes 3145736 | tf_op jit(solution)/shard_map/ppermute | solution.py:44
  65.9 13.1 %collective-permute-start.7 = (bf16[16,2,128,128]{3,2,1,0:T(8,128)(2,1)S(1)}, bf16[16,2,128,128]{3,2,1,0:T(8,128)(2,1)S(1)}, u32[]{:S(2)}, u32[]{:S(2)}) collective-permute-start(bf16[16,2,128,128]{3,2,1,0:T(8,128)(2,1)S(1)} %split_cache.7), channel_id=1, source_target_pairs={{0,4},{4,0},{8,12},{12,8},{16,20},{20,16},{24,28},{28,24},{32,36},... | collective-permute-start | bytes 3145736 | tf_op jit(solution)/shard_map/ppermute | solution.py:48
  66.9 18.9 %collective-permute-start.8 = (bf16[16,2,128,128]{3,2,1,0:T(8,128)(2,1)S(1)}, bf16[16,2,128,128]{3,2,1,0:T(8,128)(2,1)S(1)}, u32[]{:S(2)}, u32[]{:S(2)}) collective-permute-start(bf16[16,2,128,128]{3,2,1,0:T(8,128)(2,1)S(1)} %slice.16), channel_id=1, source_target_pairs={{0,32},{4,12},{8,40},{12,20},{16,48},{20,28},{24,56},{28,4},{32,64... | collective-permute-start | bytes 3145736 | tf_op jit(solution)/shard_map/ppermute | solution.py:39
  69.0 16.8 %collective-permute-start.9 = (bf16[16,2,128,128]{3,2,1,0:T(8,128)(2,1)S(1)}, bf16[16,2,128,128]{3,2,1,0:T(8,128)(2,1)S(1)}, u32[]{:S(2)}, u32[]{:S(2)}) collective-permute-start(bf16[16,2,128,128]{3,2,1,0:T(8,128)(2,1)S(1)} %slice.17), channel_id=1, source_target_pairs={{0,96},{4,28},{8,104},{12,4},{16,112},{20,12},{24,120},{28,20},{32... | collective-permute-start | bytes 3145736 | tf_op jit(solution)/shard_map/ppermute | solution.py:39
  85.8 33.1 %collective-permute-start.14 = (bf16[32,2,128,128]{3,2,1,0:T(8,128)(2,1)S(1)}, bf16[32,2,128,128]{3,2,1,0:T(8,128)(2,1)}, u32[]{:S(2)}, u32[]{:S(2)}) collective-permute-start(bf16[32,2,128,128]{3,2,1,0:T(8,128)(2,1)S(1)} %constant_dynamic-update-slice_fusion.rest_0_), channel_id=1, source_target_pairs={{0,32},{4,12},{8,40},{12,20},{16,48},{20,28},{24,56},{28,4},{32,64... | collective-permute-start | bytes 6291464 | tf_op jit(solution)/shard_map/ppermute | solution.py:39
  86.8 32.2 %collective-permute-start.15 = (bf16[32,2,128,128]{3,2,1,0:T(8,128)(2,1)S(1)}, bf16[32,2,128,128]{3,2,1,0:T(8,128)(2,1)}, u32[]{:S(2)}, u32[]{:S(2)}) collective-permute-start(bf16[32,2,128,128]{3,2,1,0:T(8,128)(2,1)S(1)} %constant_dynamic-update-slice_fusion.rest_0_), channel_id=1, source_target_pairs={{0,96},{4,28},{8,104},{12,4},{16,112},{20,12},{24,120},{28,20},{32... | collective-permute-start | bytes 6291464 | tf_op jit(solution)/shard_map/ppermute | solution.py:39
  100.8 17.0 %collective-permute-start.12 = (bf16[2096,128]{1,0:T(8,128)(2,1)}, bf16[2096,128]{1,0:T(8,128)(2,1)}, u32[]{:S(2)}, u32[]{:S(2)}) collective-permute-start(bf16[2096,128]{1,0:T(8,128)(2,1)} %get-tuple-element.116), channel_id=1, source_target_pairs={{0,8},{4,36},{8,16},{12,44},{16,24},{20,52},{24,0},{28,60},{32,40}... | collective-permute-start | bytes 1609736 | tf_op jit(solution)/shard_map/ppermute | solution.py:44
  101.1 17.8 %collective-permute-start.13 = (bf16[2096,128]{1,0:T(8,128)(2,1)}, bf16[2096,128]{1,0:T(8,128)(2,1)}, u32[]{:S(2)}, u32[]{:S(2)}) collective-permute-start(bf16[2096,128]{1,0:T(8,128)(2,1)} %get-tuple-element.117), channel_id=1, source_target_pairs={{0,24},{4,100},{8,0},{12,108},{16,8},{20,116},{24,16},{28,124},{32... | collective-permute-start | bytes 1609736 | tf_op jit(solution)/shard_map/ppermute | solution.py:44
  104.7 19.9 %collective-permute-start.16 = (bf16[2096,128]{1,0:T(8,128)(2,1)}, bf16[2096,128]{1,0:T(8,128)(2,1)}, u32[]{:S(2)}, u32[]{:S(2)}) collective-permute-start(bf16[2096,128]{1,0:T(8,128)(2,1)} %get-tuple-element.129), channel_id=1, source_target_pairs={{0,16},{4,68},{8,24},{12,76},{16,0},{20,84},{24,8},{28,92},{32,48}... | collective-permute-start | bytes 1609736 | tf_op jit(solution)/shard_map/ppermute | solution.py:44
  129.0 16.9 %collective-permute-start.18 = (bf16[16,2,128,128]{3,2,1,0:T(8,128)(2,1)S(1)}, bf16[16,2,128,128]{3,2,1,0:T(8,128)(2,1)S(1)}, u32[]{:S(2)}, u32[]{:S(2)}) collective-permute-start(bf16[16,2,128,128]{3,2,1,0:T(8,128)(2,1)S(1)} %slice.14), channel_id=1, source_target_pairs={{0,32},{4,12},{8,40},{12,20},{16,48},{20,28},{24,56},{28,4},{32,64... | collective-permute-start | bytes 3145736 | tf_op jit(solution)/shard_map/ppermute | solution.py:39
  130.7 15.2 %collective-permute-start.19 = (bf16[16,2,128,128]{3,2,1,0:T(8,128)(2,1)S(1)}, bf16[16,2,128,128]{3,2,1,0:T(8,128)(2,1)S(1)}, u32[]{:S(2)}, u32[]{:S(2)}) collective-permute-start(bf16[16,2,128,128]{3,2,1,0:T(8,128)(2,1)S(1)} %slice.15), channel_id=1, source_target_pairs={{0,96},{4,28},{8,104},{12,4},{16,112},{20,12},{24,120},{28,20},{32... | collective-permute-start | bytes 3145736 | tf_op jit(solution)/shard_map/ppermute | solution.py:39
  133.7 22.2 %collective-permute-start.20 = (bf16[2,1024,128]{2,1,0:T(8,128)(2,1)S(1)}, bf16[2,1024,128]{2,1,0:T(8,128)(2,1)S(1)}, u32[]{:S(2)}, u32[]{:S(2)}) collective-permute-start(bf16[2,1024,128]{2,1,0:T(8,128)(2,1)S(1)} %finish.2.a0), channel_id=1, source_target_pairs={{0,3},{1,0},{2,1},{3,2},{4,7},{5,4},{6,5},{7,6},{8,11},{9,8},{10,9... | collective-permute-start | bytes 1572872 | tf_op jit(solution)/shard_map/ppermute | solution.py:57
  136.2 19.6 %collective-permute-start.21 = (bf16[2,1024,128]{2,1,0:T(8,128)(2,1)S(1)}, bf16[2,1024,128]{2,1,0:T(8,128)(2,1)S(1)}, u32[]{:S(2)}, u32[]{:S(2)}) collective-permute-start(bf16[2,1024,128]{2,1,0:T(8,128)(2,1)S(1)} %finish.2.a0), channel_id=1, source_target_pairs={{0,1},{1,2},{2,3},{3,0},{4,5},{5,6},{6,7},{7,4},{8,9},{9,10},{10,1... | collective-permute-start | bytes 1572872 | tf_op jit(solution)/shard_map/ppermute | solution.py:57
  155.9 19.1 %collective-permute-start.23 = (bf16[2096,128]{1,0:T(8,128)(2,1)S(1)}, bf16[2096,128]{1,0:T(8,128)(2,1)S(1)}, u32[]{:S(2)}, u32[]{:S(2)}) collective-permute-start(bf16[2096,128]{1,0:T(8,128)(2,1)S(1)} %get-tuple-element.142), channel_id=1, source_target_pairs={{0,8},{4,36},{8,16},{12,44},{16,24},{20,52},{24,0},{28,60},{32,40}... | collective-permute-start | bytes 1609736 | tf_op jit(solution)/shard_map/ppermute | solution.py:44
  156.0 19.0 %collective-permute-start.24 = (bf16[2096,128]{1,0:T(8,128)(2,1)S(1)}, bf16[2096,128]{1,0:T(8,128)(2,1)S(1)}, u32[]{:S(2)}, u32[]{:S(2)}) collective-permute-start(bf16[2096,128]{1,0:T(8,128)(2,1)S(1)} %get-tuple-element.143), channel_id=1, source_target_pairs={{0,16},{4,68},{8,24},{12,76},{16,0},{20,84},{24,8},{28,92},{32,48}... | collective-permute-start | bytes 1609736 | tf_op jit(solution)/shard_map/ppermute | solution.py:44
  161.4 13.6 %collective-permute-start.25 = (bf16[2096,128]{1,0:T(8,128)(2,1)S(1)}, bf16[2096,128]{1,0:T(8,128)(2,1)S(1)}, u32[]{:S(2)}, u32[]{:S(2)}) collective-permute-start(bf16[2096,128]{1,0:T(8,128)(2,1)S(1)} %get-tuple-element.144), channel_id=1, source_target_pairs={{0,24},{4,100},{8,0},{12,108},{16,8},{20,116},{24,16},{28,124},{32... | collective-permute-start | bytes 1609736 | tf_op jit(solution)/shard_map/ppermute | solution.py:44
  161.4 13.6 %collective-permute-start.22 = (bf16[2,1024,128]{2,1,0:T(8,128)(2,1)S(1)}, bf16[2,1024,128]{2,1,0:T(8,128)(2,1)S(1)}, u32[]{:S(2)}, u32[]{:S(2)}) collective-permute-start(bf16[2,1024,128]{2,1,0:T(8,128)(2,1)S(1)} %finish.2.a0), channel_id=1, source_target_pairs={{0,2},{1,3},{2,0},{3,1},{4,6},{5,7},{6,4},{7,5},{8,10},{9,11},{10,... | collective-permute-start | bytes 1572872 | tf_op jit(solution)/shard_map/ppermute | solution.py:57
  179.7 13.7 %collective-permute-start.27 = (bf16[2,1024,128]{2,1,0:T(8,128)(2,1)S(1)}, bf16[2,1024,128]{2,1,0:T(8,128)(2,1)S(1)}, u32[]{:S(2)}, u32[]{:S(2)}) collective-permute-start(bf16[2,1024,128]{2,1,0:T(8,128)(2,1)S(1)} %finish.3.a0), channel_id=1, source_target_pairs={{0,3},{1,0},{2,1},{3,2},{4,7},{5,4},{6,5},{7,6},{8,11},{9,8},{10,9... | collective-permute-start | bytes 1572872 | tf_op jit(solution)/shard_map/ppermute | solution.py:57
  182.0 14.4 %collective-permute-start.28 = (bf16[2,1024,128]{2,1,0:T(8,128)(2,1)S(1)}, bf16[2,1024,128]{2,1,0:T(8,128)(2,1)S(1)}, u32[]{:S(2)}, u32[]{:S(2)}) collective-permute-start(bf16[2,1024,128]{2,1,0:T(8,128)(2,1)S(1)} %finish.3.a0), channel_id=1, source_target_pairs={{0,2},{1,3},{2,0},{3,1},{4,6},{5,7},{6,4},{7,5},{8,10},{9,11},{10,... | collective-permute-start | bytes 1572872 | tf_op jit(solution)/shard_map/ppermute | solution.py:57
  182.5 26.1 %collective-permute-start.29 = (bf16[2,1024,128]{2,1,0:T(8,128)(2,1)S(1)}, bf16[2,1024,128]{2,1,0:T(8,128)(2,1)S(1)}, u32[]{:S(2)}, u32[]{:S(2)}) collective-permute-start(bf16[2,1024,128]{2,1,0:T(8,128)(2,1)S(1)} %finish.3.a0), channel_id=1, source_target_pairs={{0,1},{1,2},{2,3},{3,0},{4,5},{5,6},{6,7},{7,4},{8,9},{9,10},{10,1... | collective-permute-start | bytes 1572872 | tf_op jit(solution)/shard_map/ppermute | solution.py:57
  (27 other events, 161.8 us)

commit v11 on v9

--- a/solution.py
+++ b/solution.py
@@ -552,7 +552,6 @@
     parts = far(0, cnt, lists, [after(rows0, near_o), down0, up20, down20, up0], qs)
     weights = pick(after(place, parts[0]), w_out)
     back = returned(parts)
-    back[1], back[3], up1, down1 = lax.optimization_barrier((back[1], back[3], up1, down1))
     tops1, bottoms1 = up1[:16], down1[16:]
     back[0], tops1, bottoms1 = lax.optimization_barrier((back[0], tops1, bottoms1))
     up21, down21 = rows_perm(tops1, 1), rows_perm(bottoms1, -1)

time: 210 us -> 208 us (level)
  waiting for transfers between devices: 66.7 us -> 60.9 us
  starting transfers between devices: 45.9 us -> 50.8 us
    ppermute x9, waiting for transfers between devices: 13.2 us -> 8.98 us  [query_perm(): return lax.ppermute(x, 'tok', pairs)]
    ppermute x6, starting transfers between devices: 8.03 us -> 11.3 us  [core_swap(): lax.ppermute(x, 'tok', [(tok_of(y, z, c), tok_of(y, z, 1 - c)) for y, z,...]
  transfers between devices with their start and end apart: 30 -> 30, of which waited for: 13 -> 12; matrix products, arithmetic and copies ran while one was open for 5% -> 5% of each run, Pallas kernels for 34% -> 33%
where the time goes in v11:
time: 208 us; the launch traced here: 207 us
  Pallas kernels  80 us (38%)
  waiting for transfers between devices  60.9 us (29%)
  starting transfers between devices  50.8 us (24%)
  local copies, waits for them, and re-layouts  13.7 us (7%)
    ppermute x6, waiting for transfers between devices, mp_perm(): return lax.ppermute(x, 'mp', [(i, (i + d) % NX) for i in range(NX)])  31.4 us
    pallas_call x4, Pallas kernels, split_cache(): pl.pallas_call(split_cache_kernel, grid_spec=pltpu.PrefetchScalarGridSpec...  22 us
    pallas_call x2, Pallas kernels, far(): pl.pallas_call(functools.partial(far_kernel, j), in_specs=[SMEM] * 5 + [A...  16.6 us
    ppermute x9, starting transfers between devices, query_perm(): return lax.ppermute(x, 'tok', pairs)  15.9 us
    ppermute x8, starting transfers between devices, rows_perm(): return lax.ppermute(x, 'tok', pairs)  12.3 us
    ppermute x8, waiting for transfers between devices, rows_perm(): return lax.ppermute(x, 'tok', pairs)  12 us
    ppermute x6, starting transfers between devices, core_swap(): lax.ppermute(x, 'tok', [(tok_of(y, z, c), tok_of(y, z, 1 - c)) for y, z,...  11.3 us
    pallas_call x1, Pallas kernels, project(): pl.pallas_call(project_kernel, grid_spec=pltpu.PrefetchScalarGridSpec(num...  10.4 us
  transfers between devices with their start and end apart: 30, of which 12 were waited for; matrix products, arithmetic and copies ran while one was open for 5% of the time, Pallas kernels for 33%

profile of v11, /device:TPU:1, one launch (start us, length us, event | category | flops | bytes accessed | tf_op | source)
XLA Modules:
  0.0 207.4 jit_solution(13724602953506626664)
XLA Ops:
  2.2 4.5 %split_cache.5 = bf16[16,2,128,128]{3,2,1,0:T(8,128)(2,1)S(1)} custom-call(s32[1]{0:T(128)S(6)} %sub.20.head_ref, bf16[2,1024,2,512]{3,2,1,0:T(2,128)(2,1)S(1)} %copy-done), custom_call_target="tpu_custom_call" | custom-call | flops 1 | bytes 1 | tf_op jit(solution)/shard_map/split_cache/pallas_call | solution.py:76
  8.2 6.0 %split_cache.4 = bf16[32,2,128,128]{3,2,1,0:T(8,128)(2,1)S(1)} custom-call(s32[1]{0:T(128)S(6)} %mul.35.head_ref, bf16[2,1024,2,512]{3,2,1,0:T(2,128)(2,1)} %src.7), custom_call_target="tpu_custom_call" | custom-call | flops 1 | bytes 1 | tf_op jit(solution)/shard_map/split_cache/pallas_call | solution.py:76
  18.4 6.9 %query.1 = (bf16[1024,2048]{1,0:T(8,128)(2,1)}, bf16[2,1024,128]{2,1,0:T(8,128)(2,1)S(1)}, bf16[2,1024,128]{2,1,0:T(8,128)(2,1)S(1)}) custom-call(s32[1]{0:T(128)} %bitcast.core_ref, bf16[1024,2048]{1,0:T(8,128)(2,1)} %carried.1, f32[1,2048]{1,0:T(1,128)S(1)} %bitcast.23, bf16[2048,512]{1,0:T(8,128)(2,1)S(1)} %copy-done.3), custom_call_target="tpu_custom_call" | custom-call | flops 1 | bytes 1 | tf_op jit(solution)/shard_map/query/pallas_call | solution.py:120
  30.1 2.8 %collective-permute-start.2 = (bf16[2,2,8,128,128]{4,3,2,1,0:T(8,128)(2,1)S(1)}, bf16[2,2,8,128,128]{4,3,2,1,0:T(8,128)(2,1)}, u32[]{:S(2)}, u32[]{:S(2)}) collective-permute-start(bf16[2,2,8,128,128]{4,3,2,1,0:T(8,128)(2,1)S(1)} %bitcast.14), channel_id=1, source_target_pairs={{0,24},{4,100},{8,0},{12,108},{16,8},{20,116},{24,16},{28,124},{32... | collective-permute-start | bytes 3145736 | tf_op jit(solution)/shard_map/ppermute | solution.py:44
  34.9 7.0 %split_cache.6 = bf16[32,2,128,128]{3,2,1,0:T(8,128)(2,1)} custom-call(s32[1]{0:T(128)S(6)} %add.42.head_ref, bf16[2,1024,2,512]{3,2,1,0:T(2,128)(2,1)} %src.7), custom_call_target="tpu_custom_call" | custom-call | flops 1 | bytes 1 | tf_op jit(solution)/shard_map/split_cache/pallas_call | solution.py:76
  42.0 4.5 %split_cache.7 = bf16[16,2,128,128]{3,2,1,0:T(8,128)(2,1)S(1)} custom-call(s32[1]{0:T(128)S(6)} %sub.21.head_ref, bf16[2,1024,2,512]{3,2,1,0:T(2,128)(2,1)S(1)} %copy-done.1), custom_call_target="tpu_custom_call" | custom-call | flops 1 | bytes 1 | tf_op jit(solution)/shard_map/split_cache/pallas_call | solution.py:76
  46.5 10.4 %project.1 = (bf16[4,8,128,128]{3,2,1,0:T(8,128)(2,1)S(1)}, bf16[4,8,128,128]{3,2,1,0:T(8,128)(2,1)S(1)}, bf16[1024,128]{1,0:T(8,128)(2,1)S(1)}, bf16[1024,128]{1,0:T(8,128)(2,1)S(1)}) custom-call(s32[1]{0:T(128)} %bitcast.core_ref, bf16[1024,2048]{1,0:T(8,128)(2,1)} %get-tuple-element.80.normed_ref, bf16[2048,512]{1,0:T(8,128)(2,1)S(1)} %copy-done.6, ...), custom_call_target="tpu_custom_call" | custom-call | flops 1 | bytes 1 | tf_op jit(solution)/shard_map/project/pallas_call | solution.py:172
  60.1 3.8 %collective-permute-done.4.rest_8_ = bf16[2,2,8,128,128]{4,3,2,1,0:T(8,128)(2,1)} collective-permute-done((bf16[2,2,8,128,128]{4,3,2,1,0:T(8,128)(2,1)S(1)}, bf16[2,2,8,128,128]{4,3,2,1,0:T(8,128)(2,1)}, u32[]{:S(2)}, u32[]{:S(2)}) %collective-permute-start.4) | collective-permute-done | bytes 1048608 | tf_op jit(solution)/shard_map/ppermute | solution.py:44
  75.8 5.8 %collective-permute-done.10 = bf16[1024,128]{1,0:T(8,128)(2,1)S(1)} collective-permute-done((bf16[1024,128]{1,0:T(8,128)(2,1)S(1)}, bf16[1024,128]{1,0:T(8,128)(2,1)S(1)}, u32[]{:S(2)}, u32[]{:S(2)}) %collective-permute-start.10) | collective-permute-done | bytes 262176 | tf_op jit(solution)/shard_map/ppermute | solution.py:53
  86.4 8.7 %near.1 = (f32[4,8,128,128]{3,2,1,0:T(8,128)S(1)}, f32[4,8,128]{2,1,0:T(8,128)S(1)}) custom-call(s32[1]{0:T(128)} %bitcast.core_ref, bf16[2,1024,128]{2,1,0:T(8,128)(2,1)S(1)} %copy-done.5, bf16[2,1024,128]{2,1,0:T(8,128)(2,1)S(1)} %copy-done.10, bf16[4,8,128,128]{3,2,1,0:T(8,128)(2,1)S(1)} %get-tuple-element.81.k_ref, ...), custom_call_target="tpu_custom_call" | custom-call | flops 1 | bytes 1 | tf_op jit(solution)/shard_map/near/pallas_call | solution.py:217
  95.1 8.8 %far.2 = (bf16[2096,128]{1,0:T(8,128)(2,1)S(1)}, bf16[2096,128]{1,0:T(8,128)(2,1)}, bf16[2096,128]{1,0:T(8,128)(2,1)}, bf16[2096,128]{1,0:T(8,128)(2,1)}) custom-call(s32[64]{0:T(128)S(1)} %reduce_sum.12.cnt_ref, s32[100]{0:T(128)S(1)} %get-tuple-element.101.unit_ref, s32[64]{0:T(128)S(1)} %get-tuple-element.102.first_ref, ...), custom_call_target="tpu_custom_call" | custom-call | flops 1 | bytes 1 | tf_op jit(solution)/shard_map/far/pallas_call | solution.py:357
  104.7 3.3 %collective-permute-start.14 = (bf16[2096,128]{1,0:T(8,128)(2,1)}, bf16[2096,128]{1,0:T(8,128)(2,1)}, u32[]{:S(2)}, u32[]{:S(2)}) collective-permute-start(bf16[2096,128]{1,0:T(8,128)(2,1)} %get-tuple-element.120), channel_id=1, source_target_pairs={{0,8},{4,36},{8,16},{12,44},{16,24},{20,52},{24,0},{28,60},{32,40}... | collective-permute-start | bytes 1609736 | tf_op jit(solution)/shard_map/ppermute | solution.py:44
  117.1 5.1 %collective-permute-done.15.c = bf16[2096,128]{1,0:T(8,128)(2,1)} collective-permute-done((bf16[2096,128]{1,0:T(8,128)(2,1)}, bf16[2096,128]{1,0:T(8,128)(2,1)}, u32[]{:S(2)}, u32[]{:S(2)}) %collective-permute-start.15) | collective-permute-done | bytes 536608 | tf_op jit(solution)/shard_map/ppermute | solution.py:44
  124.1 3.3 %collective-permute-start.17 = (f32[1032,128]{1,0:T(8,128)S(1)}, f32[1032,128]{1,0:T(8,128)S(1)}, u32[]{:S(2)}, u32[]{:S(2)}) collective-permute-start(f32[1032,128]{1,0:T(8,128)S(1)} %get-tuple-element.124), channel_id=1, source_target_pairs={{0,4},{4,0},{8,12},{12,8},{16,20},{20,16},{24,28},{28,24},{32,36},... | collective-permute-start | bytes 1585160 | tf_op jit(solution)/shard_map/ppermute | solution.py:48
  132.9 9.7 %collective-permute-done.18.rest_2_ = bf16[16,2,128,128]{3,2,1,0:T(8,128)(2,1)S(1)} collective-permute-done((bf16[16,2,128,128]{3,2,1,0:T(8,128)(2,1)S(1)}, bf16[16,2,128,128]{3,2,1,0:T(8,128)(2,1)S(1)}, u32[]{:S(2)}, u32[]{:S(2)}) %collective-permute-start.18) | collective-permute-done | bytes 1048608 | tf_op jit(solution)/shard_map/ppermute | solution.py:39
  142.6 7.8 %far.3 = (bf16[2096,128]{1,0:T(8,128)(2,1)S(1)}, bf16[2096,128]{1,0:T(8,128)(2,1)S(1)}, bf16[2096,128]{1,0:T(8,128)(2,1)S(1)}, bf16[2096,128]{1,0:T(8,128)(2,1)S(1)}) custom-call(s32[64]{0:T(128)S(1)} %reduce_sum.12.cnt_ref, s32[100]{0:T(128)S(1)} %get-tuple-element.101.unit_ref, s32[64]{0:T(128)S(1)} %get-tuple-element.102.first_ref, ...), custom_call_target="tpu_custom_call" | custom-call | flops 1 | bytes 1 | tf_op jit(solution)/shard_map/far/pallas_call | solution.py:357
  152.8 3.4 %collective-permute-start.24 = (bf16[2096,128]{1,0:T(8,128)(2,1)S(1)}, bf16[2096,128]{1,0:T(8,128)(2,1)S(1)}, u32[]{:S(2)}, u32[]{:S(2)}) collective-permute-start(bf16[2096,128]{1,0:T(8,128)(2,1)S(1)} %get-tuple-element.135), channel_id=1, source_target_pairs={{0,16},{4,68},{8,24},{12,76},{16,0},{20,84},{24,8},{28,92},{32,48}... | collective-permute-start | bytes 1609736 | tf_op jit(solution)/shard_map/ppermute | solution.py:44
  156.2 2.7 %collective-permute-start.22 = (bf16[2,1024,128]{2,1,0:T(8,128)(2,1)S(1)}, bf16[2,1024,128]{2,1,0:T(8,128)(2,1)S(1)}, u32[]{:S(2)}, u32[]{:S(2)}) collective-permute-start(bf16[2,1024,128]{2,1,0:T(8,128)(2,1)S(1)} %finish.2.a0), channel_id=1, source_target_pairs={{0,2},{1,3},{2,0},{3,1},{4,6},{5,7},{6,4},{7,5},{8,10},{9,11},{10,... | collective-permute-start | bytes 1572872 | tf_op jit(solution)/shard_map/ppermute | solution.py:57
  158.9 10.0 %collective-permute-done.22.a2 = bf16[2,1024,128]{2,1,0:T(8,128)(2,1)S(1)} collective-permute-done((bf16[2,1024,128]{2,1,0:T(8,128)(2,1)S(1)}, bf16[2,1024,128]{2,1,0:T(8,128)(2,1)S(1)}, u32[]{:S(2)}, u32[]{:S(2)}) %collective-permute-start.22) | collective-permute-done | bytes 524320 | tf_op jit(solution)/shard_map/ppermute | solution.py:57
  169.5 3.5 %collective-permute-start.26 = (f32[1032,128]{1,0:T(8,128)S(1)}, f32[1032,128]{1,0:T(8,128)S(1)}, u32[]{:S(2)}, u32[]{:S(2)}) collective-permute-start(f32[1032,128]{1,0:T(8,128)S(1)} %get-tuple-element.138), channel_id=1, source_target_pairs={{0,4},{4,0},{8,12},{12,8},{16,20},{20,16},{24,28},{28,24},{32,36},... | collective-permute-start | bytes 1585160 | tf_op jit(solution)/shard_map/ppermute | solution.py:48
  178.5 4.0 %mix.2.carried = f32[1024,512]{1,0:T(8,128)S(1)} custom-call(s32[2]{0:T(128)S(1)} %pad_add_fusion.place_ref, bf16[2,1024,128]{2,1,0:T(8,128)(2,1)S(1)} %finish.2.a0, bf16[2,1024,128]{2,1,0:T(8,128)(2,1)S(1)} %collective-permute-done.20.a1, bf16[2,1024,128]{2,1,0:T(8,128)(2,1)S(1)} %collective-permute-done.22.a2, ...), custom_call_target="tpu_custom_call" | custom-call | flops 1 | bytes 1 | tf_op jit(solution)/shard_map/mix/pallas_call | solution.py:476
  182.5 16.9 %collective-permute-done.27.a1 = bf16[2,1024,128]{2,1,0:T(8,128)(2,1)S(1)} collective-permute-done((bf16[2,1024,128]{2,1,0:T(8,128)(2,1)S(1)}, bf16[2,1024,128]{2,1,0:T(8,128)(2,1)S(1)}, u32[]{:S(2)}, u32[]{:S(2)}) %collective-permute-start.27) | collective-permute-done | bytes 524320 | tf_op jit(solution)/shard_map/ppermute | solution.py:57
  199.4 4.6 %collective-permute-done.29.a3 = bf16[2,1024,128]{2,1,0:T(8,128)(2,1)S(1)} collective-permute-done((bf16[2,1024,128]{2,1,0:T(8,128)(2,1)S(1)}, bf16[2,1024,128]{2,1,0:T(8,128)(2,1)S(1)}, u32[]{:S(2)}, u32[]{:S(2)}) %collective-permute-start.29) | collective-permute-done | bytes 524320 | tf_op jit(solution)/shard_map/ppermute | solution.py:57
  204.0 3.4 %mix.3 = bf16[1024,512]{1,0:T(8,128)(2,1)} custom-call(s32[2]{0:T(128)S(1)} %pad_add_fusion.place_ref, bf16[2,1024,128]{2,1,0:T(8,128)(2,1)S(1)} %finish.3.a0, bf16[2,1024,128]{2,1,0:T(8,128)(2,1)S(1)} %collective-permute-done.27.a1, bf16[2,1024,128]{2,1,0:T(8,128)(2,1)S(1)} %collective-permute-done.28.a2, ...), custom_call_target="tpu_custom_call" | custom-call | flops 1 | bytes 1 | tf_op jit(solution)/shard_map/mix/pallas_call | solution.py:476
  (105 shorter events, 60.3 us)
Async XLA Ops:
  14.4 42.9 %collective-permute-start.5 = (bf16[32,2,128,128]{3,2,1,0:T(8,128)(2,1)S(1)}, bf16[32,2,128,128]{3,2,1,0:T(8,128)(2,1)}, u32[]{:S(2)}, u32[]{:S(2)}) collective-permute-start(bf16[32,2,128,128]{3,2,1,0:T(8,128)(2,1)S(1)} %constant_dynamic-update-slice_fusion.1.rest_0_), channel_id=1, source_target_pairs={{0,32},{4,12},{8,40},{12,20},{16,48},{20,28},{24,56},{28,4},{32,64... | collective-permute-start | bytes 6291464 | tf_op jit(solution)/shard_map/ppermute | solution.py:39
  16.2 42.5 %collective-permute-start.6 = (bf16[32,2,128,128]{3,2,1,0:T(8,128)(2,1)S(1)}, bf16[32,2,128,128]{3,2,1,0:T(8,128)(2,1)}, u32[]{:S(2)}, u32[]{:S(2)}) collective-permute-start(bf16[32,2,128,128]{3,2,1,0:T(8,128)(2,1)S(1)} %constant_dynamic-update-slice_fusion.1.rest_0_), channel_id=1, source_target_pairs={{0,96},{4,28},{8,104},{12,4},{16,112},{20,12},{24,120},{28,20},{32... | collective-permute-start | bytes 6291464 | tf_op jit(solution)/shard_map/ppermute | solution.py:39
  30.1 30.0 %collective-permute-start.2 = (bf16[2,2,8,128,128]{4,3,2,1,0:T(8,128)(2,1)S(1)}, bf16[2,2,8,128,128]{4,3,2,1,0:T(8,128)(2,1)}, u32[]{:S(2)}, u32[]{:S(2)}) collective-permute-start(bf16[2,2,8,128,128]{4,3,2,1,0:T(8,128)(2,1)S(1)} %bitcast.14), channel_id=1, source_target_pairs={{0,24},{4,100},{8,0},{12,108},{16,8},{20,116},{24,16},{28,124},{32... | collective-permute-start | bytes 3145736 | tf_op jit(solution)/shard_map/ppermute | solution.py:44
  32.9 27.2 %collective-permute-start.3 = (bf16[2,2,8,128,128]{4,3,2,1,0:T(8,128)(2,1)S(1)}, bf16[2,2,8,128,128]{4,3,2,1,0:T(8,128)(2,1)}, u32[]{:S(2)}, u32[]{:S(2)}) collective-permute-start(bf16[2,2,8,128,128]{4,3,2,1,0:T(8,128)(2,1)S(1)} %bitcast.15), channel_id=1, source_target_pairs={{0,16},{4,68},{8,24},{12,76},{16,0},{20,84},{24,8},{28,92},{32,48}... | collective-permute-start | bytes 3145736 | tf_op jit(solution)/shard_map/ppermute | solution.py:44
  33.3 30.7 %collective-permute-start.4 = (bf16[2,2,8,128,128]{4,3,2,1,0:T(8,128)(2,1)S(1)}, bf16[2,2,8,128,128]{4,3,2,1,0:T(8,128)(2,1)}, u32[]{:S(2)}, u32[]{:S(2)}) collective-permute-start(bf16[2,2,8,128,128]{4,3,2,1,0:T(8,128)(2,1)S(1)} %bitcast.16), channel_id=1, source_target_pairs={{0,8},{4,36},{8,16},{12,44},{16,24},{20,52},{24,0},{28,60},{32,40}... | collective-permute-start | bytes 3145736 | tf_op jit(solution)/shard_map/ppermute | solution.py:44
  65.0 17.8 %collective-permute-start.8 = (bf16[16,2,128,128]{3,2,1,0:T(8,128)(2,1)S(1)}, bf16[16,2,128,128]{3,2,1,0:T(8,128)(2,1)S(1)}, u32[]{:S(2)}, u32[]{:S(2)}) collective-permute-start(bf16[16,2,128,128]{3,2,1,0:T(8,128)(2,1)S(1)} %slice.16), channel_id=1, source_target_pairs={{0,32},{4,12},{8,40},{12,20},{16,48},{20,28},{24,56},{28,4},{32,64... | collective-permute-start | bytes 3145736 | tf_op jit(solution)/shard_map/ppermute | solution.py:39
  67.1 16.5 %collective-permute-start.9 = (bf16[16,2,128,128]{3,2,1,0:T(8,128)(2,1)S(1)}, bf16[16,2,128,128]{3,2,1,0:T(8,128)(2,1)S(1)}, u32[]{:S(2)}, u32[]{:S(2)}) collective-permute-start(bf16[16,2,128,128]{3,2,1,0:T(8,128)(2,1)S(1)} %slice.17), channel_id=1, source_target_pairs={{0,96},{4,28},{8,104},{12,4},{16,112},{20,12},{24,120},{28,20},{32... | collective-permute-start | bytes 3145736 | tf_op jit(solution)/shard_map/ppermute | solution.py:39
  67.8 13.8 %collective-permute-start.10 = (bf16[1024,128]{1,0:T(8,128)(2,1)S(1)}, bf16[1024,128]{1,0:T(8,128)(2,1)S(1)}, u32[]{:S(2)}, u32[]{:S(2)}) collective-permute-start(bf16[1024,128]{1,0:T(8,128)(2,1)S(1)} %get-tuple-element.90), channel_id=1, source_target_pairs={{0,124},{4,8},{8,4},{12,16},{16,12},{20,24},{24,20},{28,32},{32,28... | collective-permute-start | bytes 786440 | tf_op jit(solution)/shard_map/ppermute | solution.py:53
  83.5 29.8 %collective-permute-start.12 = (bf16[32,2,128,128]{3,2,1,0:T(8,128)(2,1)}, bf16[32,2,128,128]{3,2,1,0:T(8,128)(2,1)}, u32[]{:S(2)}, u32[]{:S(2)}) collective-permute-start(bf16[32,2,128,128]{3,2,1,0:T(8,128)(2,1)} %constant_dynamic-update-slice_fusion.rest_0_), channel_id=1, source_target_pairs={{0,32},{4,12},{8,40},{12,20},{16,48},{20,28},{24,56},{28,4},{32,64... | collective-permute-start | bytes 6291464 | tf_op jit(solution)/shard_map/ppermute | solution.py:39
  83.8 30.9 %collective-permute-start.13 = (bf16[32,2,128,128]{3,2,1,0:T(8,128)(2,1)}, bf16[32,2,128,128]{3,2,1,0:T(8,128)(2,1)}, u32[]{:S(2)}, u32[]{:S(2)}) collective-permute-start(bf16[32,2,128,128]{3,2,1,0:T(8,128)(2,1)} %constant_dynamic-update-slice_fusion.rest_0_), channel_id=1, source_target_pairs={{0,96},{4,28},{8,104},{12,4},{16,112},{20,12},{24,120},{28,20},{32... | collective-permute-start | bytes 6291464 | tf_op jit(solution)/shard_map/ppermute | solution.py:39
  104.7 12.4 %collective-permute-start.14 = (bf16[2096,128]{1,0:T(8,128)(2,1)}, bf16[2096,128]{1,0:T(8,128)(2,1)}, u32[]{:S(2)}, u32[]{:S(2)}) collective-permute-start(bf16[2096,128]{1,0:T(8,128)(2,1)} %get-tuple-element.120), channel_id=1, source_target_pairs={{0,8},{4,36},{8,16},{12,44},{16,24},{20,52},{24,0},{28,60},{32,40}... | collective-permute-start | bytes 1609736 | tf_op jit(solution)/shard_map/ppermute | solution.py:44
  108.0 14.2 %collective-permute-start.15 = (bf16[2096,128]{1,0:T(8,128)(2,1)}, bf16[2096,128]{1,0:T(8,128)(2,1)}, u32[]{:S(2)}, u32[]{:S(2)}) collective-permute-start(bf16[2096,128]{1,0:T(8,128)(2,1)} %get-tuple-element.121), channel_id=1, source_target_pairs={{0,16},{4,68},{8,24},{12,76},{16,0},{20,84},{24,8},{28,92},{32,48}... | collective-permute-start | bytes 1609736 | tf_op jit(solution)/shard_map/ppermute | solution.py:44
  109.1 13.1 %collective-permute-start.16 = (bf16[2096,128]{1,0:T(8,128)(2,1)}, bf16[2096,128]{1,0:T(8,128)(2,1)}, u32[]{:S(2)}, u32[]{:S(2)}) collective-permute-start(bf16[2096,128]{1,0:T(8,128)(2,1)} %get-tuple-element.122), channel_id=1, source_target_pairs={{0,24},{4,100},{8,0},{12,108},{16,8},{20,116},{24,16},{28,124},{32... | collective-permute-start | bytes 1609736 | tf_op jit(solution)/shard_map/ppermute | solution.py:44
  127.4 15.2 %collective-permute-start.18 = (bf16[16,2,128,128]{3,2,1,0:T(8,128)(2,1)S(1)}, bf16[16,2,128,128]{3,2,1,0:T(8,128)(2,1)S(1)}, u32[]{:S(2)}, u32[]{:S(2)}) collective-permute-start(bf16[16,2,128,128]{3,2,1,0:T(8,128)(2,1)S(1)} %slice.18), channel_id=1, source_target_pairs={{0,32},{4,12},{8,40},{12,20},{16,48},{20,28},{24,56},{28,4},{32,64... | collective-permute-start | bytes 3145736 | tf_op jit(solution)/shard_map/ppermute | solution.py:39
  127.7 14.9 %collective-permute-start.19 = (bf16[16,2,128,128]{3,2,1,0:T(8,128)(2,1)}, bf16[16,2,128,128]{3,2,1,0:T(8,128)(2,1)S(1)}, u32[]{:S(2)}, u32[]{:S(2)}) collective-permute-start(bf16[16,2,128,128]{3,2,1,0:T(8,128)(2,1)} %slice.19), channel_id=1, source_target_pairs={{0,96},{4,28},{8,104},{12,4},{16,112},{20,12},{24,120},{28,20},{32... | collective-permute-start | bytes 3145736 | tf_op jit(solution)/shard_map/ppermute | solution.py:39
  130.4 20.0 %collective-permute-start.20 = (bf16[2,1024,128]{2,1,0:T(8,128)(2,1)S(1)}, bf16[2,1024,128]{2,1,0:T(8,128)(2,1)S(1)}, u32[]{:S(2)}, u32[]{:S(2)}) collective-permute-start(bf16[2,1024,128]{2,1,0:T(8,128)(2,1)S(1)} %finish.2.a0), channel_id=1, source_target_pairs={{0,3},{1,0},{2,1},{3,2},{4,7},{5,4},{6,5},{7,6},{8,11},{9,8},{10,9... | collective-permute-start | bytes 1572872 | tf_op jit(solution)/shard_map/ppermute | solution.py:57
  132.9 17.5 %collective-permute-start.21 = (bf16[2,1024,128]{2,1,0:T(8,128)(2,1)S(1)}, bf16[2,1024,128]{2,1,0:T(8,128)(2,1)S(1)}, u32[]{:S(2)}, u32[]{:S(2)}) collective-permute-start(bf16[2,1024,128]{2,1,0:T(8,128)(2,1)S(1)} %finish.2.a0), channel_id=1, source_target_pairs={{0,1},{1,2},{2,3},{3,0},{4,5},{5,6},{6,7},{7,4},{8,9},{9,10},{10,1... | collective-permute-start | bytes 1572872 | tf_op jit(solution)/shard_map/ppermute | solution.py:57
  150.4 18.5 %collective-permute-start.23 = (bf16[2096,128]{1,0:T(8,128)(2,1)S(1)}, bf16[2096,128]{1,0:T(8,128)(2,1)S(1)}, u32[]{:S(2)}, u32[]{:S(2)}) collective-permute-start(bf16[2096,128]{1,0:T(8,128)(2,1)S(1)} %get-tuple-element.134), channel_id=1, source_target_pairs={{0,8},{4,36},{8,16},{12,44},{16,24},{20,52},{24,0},{28,60},{32,40}... | collective-permute-start | bytes 1609736 | tf_op jit(solution)/shard_map/ppermute | solution.py:44
  152.8 16.1 %collective-permute-start.24 = (bf16[2096,128]{1,0:T(8,128)(2,1)S(1)}, bf16[2096,128]{1,0:T(8,128)(2,1)S(1)}, u32[]{:S(2)}, u32[]{:S(2)}) collective-permute-start(bf16[2096,128]{1,0:T(8,128)(2,1)S(1)} %get-tuple-element.135), channel_id=1, source_target_pairs={{0,16},{4,68},{8,24},{12,76},{16,0},{20,84},{24,8},{28,92},{32,48}... | collective-permute-start | bytes 1609736 | tf_op jit(solution)/shard_map/ppermute | solution.py:44
  156.2 12.7 %collective-permute-start.25 = (bf16[2096,128]{1,0:T(8,128)(2,1)S(1)}, bf16[2096,128]{1,0:T(8,128)(2,1)S(1)}, u32[]{:S(2)}, u32[]{:S(2)}) collective-permute-start(bf16[2096,128]{1,0:T(8,128)(2,1)S(1)} %get-tuple-element.136), channel_id=1, source_target_pairs={{0,24},{4,100},{8,0},{12,108},{16,8},{20,116},{24,16},{28,124},{32... | collective-permute-start | bytes 1609736 | tf_op jit(solution)/shard_map/ppermute | solution.py:44
  156.2 12.7 %collective-permute-start.22 = (bf16[2,1024,128]{2,1,0:T(8,128)(2,1)S(1)}, bf16[2,1024,128]{2,1,0:T(8,128)(2,1)S(1)}, u32[]{:S(2)}, u32[]{:S(2)}) collective-permute-start(bf16[2,1024,128]{2,1,0:T(8,128)(2,1)S(1)} %finish.2.a0), channel_id=1, source_target_pairs={{0,2},{1,3},{2,0},{3,1},{4,6},{5,7},{6,4},{7,5},{8,10},{9,11},{10,... | collective-permute-start | bytes 1572872 | tf_op jit(solution)/shard_map/ppermute | solution.py:57
  174.8 24.6 %collective-permute-start.27 = (bf16[2,1024,128]{2,1,0:T(8,128)(2,1)S(1)}, bf16[2,1024,128]{2,1,0:T(8,128)(2,1)S(1)}, u32[]{:S(2)}, u32[]{:S(2)}) collective-permute-start(bf16[2,1024,128]{2,1,0:T(8,128)(2,1)S(1)} %finish.3.a0), channel_id=1, source_target_pairs={{0,3},{1,0},{2,1},{3,2},{4,7},{5,4},{6,5},{7,6},{8,11},{9,8},{10,9... | collective-permute-start | bytes 1572872 | tf_op jit(solution)/shard_map/ppermute | solution.py:57
  177.4 22.0 %collective-permute-start.28 = (bf16[2,1024,128]{2,1,0:T(8,128)(2,1)S(1)}, bf16[2,1024,128]{2,1,0:T(8,128)(2,1)S(1)}, u32[]{:S(2)}, u32[]{:S(2)}) collective-permute-start(bf16[2,1024,128]{2,1,0:T(8,128)(2,1)S(1)} %finish.3.a0), channel_id=1, source_target_pairs={{0,2},{1,3},{2,0},{3,1},{4,6},{5,7},{6,4},{7,5},{8,10},{9,11},{10,... | collective-permute-start | bytes 1572872 | tf_op jit(solution)/shard_map/ppermute | solution.py:57
  177.9 26.1 %collective-permute-start.29 = (bf16[2,1024,128]{2,1,0:T(8,128)(2,1)S(1)}, bf16[2,1024,128]{2,1,0:T(8,128)(2,1)S(1)}, u32[]{:S(2)}, u32[]{:S(2)}) collective-permute-start(bf16[2,1024,128]{2,1,0:T(8,128)(2,1)S(1)} %finish.3.a0), channel_id=1, source_target_pairs={{0,1},{1,2},{2,3},{3,0},{4,5},{5,6},{6,7},{7,4},{8,9},{9,10},{10,1... | collective-permute-start | bytes 1572872 | tf_op jit(solution)/shard_map/ppermute | solution.py:57
  (22 other events, 172.7 us)
